TPU v7x, 256 devices: a whole 4x4x8 slice. The times are simulated.
256 devices in a mesh: gx: 8 (over y, core), gy: 16 (over x_hi, z), pa: 2 (over x_lo).
Axes of the slice: x: 4 (x_hi: 2, x_lo: 2; x = x_hi * 2 + x_lo), y: 4, z: 8, core: 2. Of those that a mesh axis runs over, the one named last changes fastest.
Arguments:
- volume: bfloat16 [4, 4096, 4096], P('pa', 'gx', 'gy'), may hold values from -6 to 6
- view_slopes: int32 [2, 16], replicated, may hold values from -14 to 14, as said below
- measured_x: float32 [16, 4, 4096], P(None, 'pa', 'gy'), may hold values from -6 to 6
- measured_y: float32 [16, 4, 4096], P(None, 'pa', 'gx'), may hold values from -6 to 6
Outputs:
- gradient: float32 [4, 4096, 4096], P('pa', 'gx', 'gy')
- residual_x: float32 [16, 4, 4096], P(None, 'pa', 'gy')
- residual_y: float32 [16, 4, 4096], P(None, 'pa', 'gx')
Inputs may be any that keep to these rules, and one draw needn't show every extreme that they name: `view_slopes`: row 0 holds the near-x slopes in units of 1/512, row 1 the near-y slopes in units of 1/256; in each row both 14 and its negative occur.
All inputs are finite; a program needn't handle non-finite values.
Results may differ from a plain program's by a relative error of at most 0.0025.
Values may be sent and summed in bfloat16 or wider, within the bound.
No kernel may reach another device: no remote copies, remote signals or barrier semaphores. Data moves between devices by JAX's collectives and lax.ppermute only.
A program may use at most 128 MiB of HBM per device.

v0:
```python
import jax
import jax.numpy as jnp
from jax import lax
from jax.sharding import PartitionSpec as P

SHEAR = 14


def padded_2(value, sides, width):
    for axis, dim in sides:
        size, length = (lax.axis_size(axis), value.shape[dim])
        up = [(i, (i + 1) % size) for i in range(size - 1)]
        down = [(j, i) for i, j in up]
        last = lax.slice_in_dim(value, length - width, length, axis=dim)
        leading = lax.slice_in_dim(value, 0, width, axis=dim)
        before = lax.ppermute(last, axis, up)
        after = lax.ppermute(leading, axis, down)
        value = jnp.concatenate([before, value, after], axis=dim)
    return value


def lane_round(value):
    return -(-value // 128) * 128


def shear_table(slopes, positions, cells, shift_levels):
    product = slopes[:, None] * positions[None, :]
    shifts = jnp.floor_divide(product, cells)
    fraction = (product - shifts * cells).astype(jnp.float32) / cells
    lowest = jnp.min(shifts, axis=1)
    offsets = shifts - lowest[:, None]
    levels = jnp.arange(shift_levels, dtype=jnp.int32)
    lower = (1.0 - fraction).astype(jnp.bfloat16)
    upper = fraction.astype(jnp.bfloat16)
    nothing = jnp.zeros((), jnp.bfloat16)
    table = jnp.where(levels[None, :, None] == offsets[:, None, :], lower[:, None, :], nothing)
    table = table + jnp.where(
        levels[None, :, None] == offsets[:, None, :] + 1, upper[:, None, :], nothing
    )
    return (table, lowest)


def shear_sum(summands, lowest, leading, number, pad_cells):
    planes, shift_levels, length = summands.shape
    natural_row = length + 2 * pad_cells
    right_pad = pad_cells + lane_round(natural_row + 1) - (natural_row + 1)
    row_length = length + pad_cells + right_pad
    padded = jnp.pad(summands, ((0, 0), (0, 0), (pad_cells, right_pad)))
    flattened = jnp.pad(
        padded.reshape(planes, shift_levels * row_length), ((0, 0), (0, shift_levels))
    )
    skewed = jnp.sum(flattened.reshape(planes, shift_levels, row_length + 1), axis=1)
    return lax.dynamic_slice_in_dim(skewed, leading + lowest + pad_cells, number, 1)


def spread(values, lowest, leading, number, pad_cells, shift_levels):
    planes, length = values.shape
    natural_row = length + 2 * pad_cells
    right_pad = pad_cells + lane_round(natural_row - 1) - (natural_row - 1)
    row_length = length + pad_cells + right_pad
    padded = jnp.pad(values, ((0, 0), (pad_cells, right_pad)))
    repeated = jnp.broadcast_to(padded[:, None, :], (planes, shift_levels, row_length))
    repeated = repeated.reshape(planes, shift_levels * row_length)
    skewed = repeated[:, : shift_levels * (row_length - 1)].reshape(
        planes, shift_levels, row_length - 1
    )
    return lax.dynamic_slice_in_dim(skewed, leading - lowest + pad_cells, number, 2)


def sheared_views(summands, lowest, leading, number, pad_cells):
    return jax.vmap(lambda pieces, low: shear_sum(pieces, low, leading, number, pad_cells))(
        summands, lowest
    )


def spread_views(values, lowest, leading, number, pad_cells, shift_levels):
    return jax.vmap(
        lambda pieces, low: spread(pieces, low, leading, number, pad_cells, shift_levels)
    )(values, lowest)


def fold_edges(inner, outer, ghost_width, length, dim):
    lead_pads = [(0, 0)] * inner.ndim
    tail_pads = [(0, 0)] * inner.ndim
    lead_pads[dim] = (0, length - ghost_width)
    tail_pads[dim] = (length - ghost_width, 0)
    head = lax.slice_in_dim(outer, 0, ghost_width, 1, dim)
    tail = lax.slice_in_dim(outer, length + 3 * ghost_width, length + 4 * ghost_width, 1, dim)
    return inner + jnp.pad(head, lead_pads) + jnp.pad(tail, tail_pads)


def on_device(volume, view_slopes, measured_x, measured_y):
    planes, cells_x, cells_y = volume.shape
    count_x = lax.axis_size("gx")
    count_y = lax.axis_size("gy")
    ghost_width = SHEAR * max(count_x, count_y) // 2 + 2
    shift_levels = SHEAR + 2
    pad_cells = 2 * ghost_width + shift_levels
    positions_x = (
        lax.axis_index("gx") * cells_x
        + jnp.arange(cells_x, dtype=jnp.int32)
        - cells_x * count_x // 2
    )
    positions_y = (
        lax.axis_index("gy") * cells_y
        + jnp.arange(cells_y, dtype=jnp.int32)
        - cells_y * count_y // 2
    )
    table_x, lowest_x = shear_table(view_slopes[0], positions_x, cells_x, shift_levels)
    table_y, lowest_y = shear_table(view_slopes[1], positions_y, cells_y, shift_levels)
    scale_x = float(cells_x * count_x) ** (-0.5)
    scale_y = float(cells_y * count_y) ** (-0.5)
    layered = padded_2(volume, (("pa", 0),), 1).astype(jnp.float32)
    coupling = 0.02 * (2.0 * layered[1:-1] - layered[:-2] - layered[2:])
    extended = padded_2(volume, (("gx", 1), ("gy", 2)), ghost_width)
    source_x = extended[:, ghost_width : ghost_width + cells_x, :]
    source_y = extended[:, :, ghost_width : ghost_width + cells_y]
    summands_x = jnp.einsum("vsx,pxy->vpsy", table_x, source_x, preferred_element_type=jnp.float32)
    summands_x = sheared_views(summands_x, lowest_x, ghost_width, cells_y, pad_cells)
    summands_y = jnp.einsum("vsy,pxy->vpsx", table_y, source_y, preferred_element_type=jnp.float32)
    summands_y = sheared_views(summands_y, lowest_y, ghost_width, cells_x, pad_cells)
    total_x = lax.psum(summands_x, "gx")
    total_y = lax.psum(summands_y, "gy")
    residual_x = total_x * scale_x - measured_x
    residual_y = total_y * scale_y - measured_y
    back_rx = residual_x.astype(jnp.bfloat16)
    back_ry = residual_y.astype(jnp.bfloat16)
    spread_x = spread_views(
        back_rx, lowest_x, -ghost_width, cells_y + 2 * ghost_width, pad_cells, shift_levels
    )
    spread_y = spread_views(
        back_ry, lowest_y, -ghost_width, cells_x + 2 * ghost_width, pad_cells, shift_levels
    )
    wide_x = jnp.einsum("vsx,vpsy->pxy", table_x, spread_x, preferred_element_type=jnp.float32)
    wide_y = jnp.einsum("vsy,vpsx->pxy", table_y, spread_y, preferred_element_type=jnp.float32)
    combined = jnp.pad(wide_x * scale_x, ((0, 0), (ghost_width, ghost_width), (0, 0)))
    combined = combined + jnp.pad(wide_y * scale_y, ((0, 0), (0, 0), (ghost_width, ghost_width)))
    outer = padded_2(combined.astype(jnp.bfloat16), (("gx", 1), ("gy", 2)), ghost_width).astype(
        combined.dtype
    )
    backed = combined[:, ghost_width : ghost_width + cells_x, ghost_width : ghost_width + cells_y]
    rows_band = outer[:, :, 2 * ghost_width : 2 * ghost_width + cells_y]
    columns_band = outer[:, 2 * ghost_width : 2 * ghost_width + cells_x, :]
    backed = fold_edges(backed, rows_band, ghost_width, cells_x, 1)
    backed = fold_edges(backed, columns_band, ghost_width, cells_y, 2)
    gradient = backed + coupling
    return (gradient, residual_x, residual_y)


def solution(mesh):
    return jax.shard_map(
        on_device,
        mesh=mesh,
        in_specs=(P("pa", "gx", "gy"), P(), P(None, "pa", "gy"), P(None, "pa", "gx")),
        out_specs=(P("pa", "gx", "gy"), P(None, "pa", "gy"), P(None, "pa", "gx")),
        check_vma=False,
    )
```

profile of v0, /device:TPU:10, one launch (start us, length us, event | category | flops | bytes accessed | tf_op | source)
XLA Modules:
  0.0 452.8 jit_solution(3947259791864831188)
XLA Ops:
  10.5 3.6 collective-permute-start.1
  15.8 3.2 copy.52
  19.0 3.4 copy.59
  24.6 2.1 pad.56
  26.7 3.9 reshape.412
  32.5 2.3 copy.81
  34.8 2.2 reduce_sum.19
  36.9 5.6 %copy.58 = f32[16,2,1280]{1,0,2:T(8,128)} copy(f32[16,2,1280]{2,0,1:T(8,128)S(1)} %reduce_sum.19) | data formatting | bytes 327680 | tf_op jit(solution)/shard_map/vmap()/reduce_sum | solution.py:52
  42.5 7.8 %gather_fusion.2 = f32[16,2,512]{1,0,2:T(8,128)} fusion(f32[16,2,1280]{1,0,2:T(8,128)} %copy.58, s32[16]{0:T(128)S(1)} %get-tuple-element.41), kind=kCustom, calls=%fused_computation.2 | custom fusion | bytes 131264 | tf_op jit(solution)/shard_map/vmap()/gather | solution.py:53
  51.6 4.6 %collective-permute-start.2 = (bf16[2,740,114]{1,2,0:T(8,128)(2,1)}, bf16[2,740,114]{1,2,0:T(8,128)(2,1)}, u32[]{:S(2)}, u32[]{:S(2)}) collective-permute-start(bf16[2,740,114]{1,2,0:T(8,128)(2,1)} %get-tuple-element.24), channel_id=1, source_target_pairs={{0,2},{2,4},{4,6},{6,8},{8,10},{10,12},{12,14},{14,16},{16,18},{18... | collective-permute-start | bytes 1012328 | tf_op jit(solution)/shard_map/ppermute | solution.py:16
  57.7 169.6 %all-reduce.18.cloned.1.call-done = f32[16,2,512]{1,0,2:T(8,128)} async-done(((f32[16,2,512]{1,0,2:T(8,128)}), f32[16,2,512]{1,0,2:T(8,128)}) %all-reduce.18.cloned.1.call-update) | async-done | bytes 65552 | tf_op jit(solution)/shard_map/psum | solution.py:123
  227.3 6.6 %fusion.51 = (bf16[16,2,512]{1,0,2:T(8,128)(2,1)}, f32[16,2,512]{1,0,2:T(8,128)}) fusion(f32[16,2,512]{1,0,2:T(8,128)} %copy.59, f32[16,2,512]{1,0,2:T(8,128)} %all-reduce.18.cloned.1.call-done), kind=kLoop, calls=%fused_computation.119 | loop fusion | flops 49152 | bytes 229376 | tf_op jit(solution)/shard_map/convert_element_type | solution.py:127
  233.9 2.7 copy.78
  238.6 15.0 %copy.61 = bf16[16,2,16,1024]{2,1,0,3:T(2,128)(2,1)} copy(bf16[16,2,16,1024]{3,2,0,1:T(8,128)(2,1)S(1)} %bitcast.125) | data formatting | bytes 2097152 | tf_op jit(solution)/shard_map/vmap()/reshape | solution.py:64
  253.6 21.1 %gather_fusion.3 = bf16[16,2,16,740]{2,1,3,0:T(2,128)(2,1)} fusion(bf16[16,2,16,1024]{2,1,0,3:T(2,128)(2,1)} %copy.61, s32[16]{0:T(128)S(1)} %get-tuple-element.40), kind=kCustom, calls=%fused_computation.3 | custom fusion | bytes 1515776 | tf_op jit(solution)/shard_map/vmap()/gather | solution.py:67
  274.7 8.9 %copy.62 = bf16[16,2,16,740]{3,0,2,1:T(8,128)(2,1)S(1)} copy(bf16[16,2,16,740]{2,1,3,0:T(2,128)(2,1)} %gather_fusion.3) | data formatting | bytes 1515520 | tf_op jit(solution)/shard_map/vmap()/gather | solution.py:67
  288.4 3.4 reshape.408
  293.5 2.5 copy.79
  298.1 6.0 %copy.51 = f32[16,2,1024]{1,0,2:T(8,128)} copy(f32[16,2,1024]{2,0,1:T(8,128)S(1)} %reduce_sum.18) | data formatting | bytes 262144 | tf_op jit(solution)/shard_map/vmap()/reduce_sum | solution.py:52
  304.0 5.1 %gather_fusion = f32[16,2,256]{1,0,2:T(8,128)} fusion(f32[16,2,1024]{1,0,2:T(8,128)} %copy.51, s32[16]{0:T(128)S(1)} %copy-done.13), kind=kCustom, calls=%fused_computation | custom fusion | bytes 65728 | tf_op jit(solution)/shard_map/vmap()/gather | solution.py:53
  309.1 49.5 %psum.14 = f32[16,2,256]{1,0,2:T(8,128)} all-reduce(f32[16,2,256]{1,0,2:T(8,128)} %gather_fusion), channel_id=1, replica_groups=mesh['gx'=8,'gy'=16,'pa'=2] {'gx'}, use_global_device_ids=true, to_apply=%region_2.3 | all-reduce | flops 8192 | bytes 65536 | tf_op jit(solution)/shard_map/psum | solution.py:122
  358.6 3.9 fusion.52
  364.7 11.2 %copy.54 = bf16[16,2,16,768]{2,1,0,3:T(2,128)(2,1)} copy(bf16[16,2,16,768]{3,2,0,1:T(8,128)(2,1)S(1)} %bitcast.127) | data formatting | bytes 1572864 | tf_op jit(solution)/shard_map/vmap()/reshape | solution.py:64
  375.9 14.9 %gather_fusion.1 = bf16[16,2,16,484]{2,1,3,0:T(2,128)(2,1)} fusion(bf16[16,2,16,768]{2,1,0,3:T(2,128)(2,1)} %copy.54, s32[16]{0:T(128)S(1)} %copy-done.8), kind=kCustom, calls=%fused_computation.1 | custom fusion | bytes 991488 | tf_op jit(solution)/shard_map/vmap()/gather | solution.py:67
  390.8 6.1 %copy.55 = bf16[16,2,16,484]{3,0,2,1:T(8,128)(2,1)S(1)} copy(bf16[16,2,16,484]{2,1,3,0:T(2,128)(2,1)} %gather_fusion.1) | data formatting | bytes 991232 | tf_op jit(solution)/shard_map/vmap()/gather | solution.py:67
  400.9 4.8 %collective-permute-start.5 = (bf16[2,114,484]{1,2,0:T(8,128)(2,1)S(1)}, bf16[2,114,484]{1,2,0:T(8,128)(2,1)S(1)}, u32[]{:S(2)}, u32[]{:S(2)}) collective-permute-start(bf16[2,114,484]{1,2,0:T(8,128)(2,1)S(1)} %get-tuple-element.23), channel_id=1, source_target_pairs={{32,0},{64,32},{96,64},{128,96},{160,128},{192,160},{224,192},{33,... | collective-permute-start | bytes 662120 | tf_op jit(solution)/shard_map/ppermute | solution.py:17
  411.0 3.1 collective-permute-start.6
  417.6 6.0 %collective-permute-start.9 = (bf16[1,512,256]{1,2,0:T(8,128)(2,1)}, bf16[1,512,256]{1,2,0:T(8,128)(2,1)}, u32[]{:S(2)}, u32[]{:S(2)}) collective-permute-start(bf16[1,512,256]{1,2,0:T(8,128)(2,1)} %get-tuple-element.27), channel_id=1, source_target_pairs={{1,0},{3,2},{5,4},{7,6},{9,8},{11,10},{13,12},{15,14},{17,16},{19,... | collective-permute-start | bytes 786440 | tf_op jit(solution)/shard_map/ppermute | solution.py:17
  423.5 3.5 copy.69
  427.0 7.9 %collective-permute-done.8 = bf16[1,512,256]{1,2,0:T(8,128)(2,1)} collective-permute-done((bf16[1,512,256]{1,2,0:T(8,128)(2,1)}, bf16[1,512,256]{1,2,0:T(8,128)(2,1)}, u32[]{:S(2)}, u32[]{:S(2)}) %collective-permute-start.8) | collective-permute-done | bytes 262176 | tf_op jit(solution)/shard_map/ppermute | solution.py:16
  434.9 2.7 maximum_convert_fusion
  437.6 3.1 copy.68
  (112 shorter events, 42.0 us)
Async XLA Ops:
  7.2 11.9 %copy-start.21 = (f32[16,2,512]{2,1,0:T(2,128)S(1)}, f32[16,2,512]{2,1,0:T(2,128)}, u32[]{:S(2)}) copy-start(f32[16,2,512]{2,1,0:T(2,128)} %param.7) | copy-start | bytes 196612
  7.2 220.1 %all-reduce.18.cloned.1.call-start = ((), (), s32[]{:S(2)}) async-start(), calls=%async_computation | async-start | bytes 8388608 | tf_op jit(solution)/shard_map/psum | solution.py:123
  8.5 276.3 %copy-start.1 = (bf16[2,512,256]{1,2,0:T(8,128)(2,1)}, bf16[2,512,256]{1,2,0:T(8,128)(2,1)S(1)}, u32[]{:S(2)}) copy-start(bf16[2,512,256]{1,2,0:T(8,128)(2,1)S(1)} %copy.47) | copy-start | bytes 1572868
  8.6 15.4 %collective-permute-start = (bf16[2,114,256]{1,2,0:T(8,128)(2,1)S(1)}, bf16[2,114,256]{1,2,0:T(8,128)(2,1)S(1)}, u32[]{:S(2)}, u32[]{:S(2)}) collective-permute-start(bf16[2,114,256]{1,2,0:T(8,128)(2,1)S(1)} %get-tuple-element.28), channel_id=1, source_target_pairs={{0,32},{32,64},{64,96},{96,128},{128,160},{160,192},{192,224},{1,3... | collective-permute-start | bytes 350216 | tf_op jit(solution)/shard_map/ppermute | solution.py:16
  10.5 13.5 %collective-permute-start.1 = (bf16[2,114,256]{1,2,0:T(8,128)(2,1)S(1)}, bf16[2,114,256]{1,2,0:T(8,128)(2,1)S(1)}, u32[]{:S(2)}, u32[]{:S(2)}) collective-permute-start(bf16[2,114,256]{1,2,0:T(8,128)(2,1)S(1)} %get-tuple-element.29), channel_id=1, source_target_pairs={{32,0},{64,32},{96,64},{128,96},{160,128},{192,160},{224,192},{33,... | collective-permute-start | bytes 350216 | tf_op jit(solution)/shard_map/ppermute | solution.py:17
  15.2 7.2 %copy-start.18 = (bf16[16,256]{1,0:T(8,128)(2,1)}, bf16[16,256]{1,0:T(8,128)(2,1)S(1)}, u32[]{:S(2)}) copy-start(bf16[16,256]{1,0:T(8,128)(2,1)S(1)} %get-tuple-element.36) | copy-start | bytes 24580
  15.3 7.2 %copy-start.20 = (bf16[16,256]{1,0:T(8,128)(2,1)}, bf16[16,256]{1,0:T(8,128)(2,1)S(1)}, u32[]{:S(2)}) copy-start(bf16[16,256]{1,0:T(8,128)(2,1)S(1)} %get-tuple-element.37) | copy-start | bytes 24580
  15.7 6.8 %copy-start.22 = (bf16[16,512]{1,0:T(8,128)(2,1)}, bf16[16,512]{1,0:T(8,128)(2,1)S(1)}, u32[]{:S(2)}) copy-start(bf16[16,512]{1,0:T(8,128)(2,1)S(1)} %get-tuple-element.32) | copy-start | bytes 49156
  15.7 6.8 %copy-start.24 = (bf16[16,512]{1,0:T(8,128)(2,1)}, bf16[16,512]{1,0:T(8,128)(2,1)S(1)}, u32[]{:S(2)}) copy-start(bf16[16,512]{1,0:T(8,128)(2,1)S(1)} %get-tuple-element.33) | copy-start | bytes 49156
  15.8 6.7 %copy-start.14 = (s32[16,512]{1,0:T(8,128)}, s32[16,512]{1,0:T(8,128)S(1)}, u32[]{:S(2)}) copy-start(s32[16,512]{1,0:T(8,128)S(1)} %get-tuple-element.30) | copy-start | bytes 98308
  15.8 6.7 %copy-start.16 = (s32[16,512]{1,0:T(8,128)}, s32[16,512]{1,0:T(8,128)S(1)}, u32[]{:S(2)}) copy-start(s32[16,512]{1,0:T(8,128)S(1)} %get-tuple-element.31) | copy-start | bytes 98308
  24.0 26.4 %copy-start.9 = (bf16[2,114,256]{1,2,0:T(8,128)(2,1)}, bf16[2,114,256]{1,2,0:T(8,128)(2,1)S(1)}, u32[]{:S(2)}) copy-start(bf16[2,114,256]{1,2,0:T(8,128)(2,1)S(1)} %collective-permute-done) | copy-start | bytes 350212
  24.0 26.4 %copy-start.11 = (bf16[2,114,256]{1,2,0:T(8,128)(2,1)}, bf16[2,114,256]{1,2,0:T(8,128)(2,1)S(1)}, u32[]{:S(2)}) copy-start(bf16[2,114,256]{1,2,0:T(8,128)(2,1)S(1)} %collective-permute-done.1) | copy-start | bytes 350212
  51.6 233.2 %collective-permute-start.2 = (bf16[2,740,114]{1,2,0:T(8,128)(2,1)}, bf16[2,740,114]{1,2,0:T(8,128)(2,1)}, u32[]{:S(2)}, u32[]{:S(2)}) collective-permute-start(bf16[2,740,114]{1,2,0:T(8,128)(2,1)} %get-tuple-element.24), channel_id=1, source_target_pairs={{0,2},{2,4},{4,6},{6,8},{8,10},{10,12},{12,14},{14,16},{16,18},{18... | collective-permute-start | bytes 1012328 | tf_op jit(solution)/shard_map/ppermute | solution.py:16
  56.2 228.6 %collective-permute-start.3 = (bf16[2,740,114]{1,2,0:T(8,128)(2,1)S(1)}, bf16[2,740,114]{1,2,0:T(8,128)(2,1)}, u32[]{:S(2)}, u32[]{:S(2)}) collective-permute-start(bf16[2,740,114]{1,2,0:T(8,128)(2,1)S(1)} %get-tuple-element.25), channel_id=1, source_target_pairs={{2,0},{4,2},{6,4},{8,6},{10,8},{12,10},{14,12},{16,14},{18,16},{20... | collective-permute-start | bytes 1012328 | tf_op jit(solution)/shard_map/ppermute | solution.py:17
  274.7 8.9 %copy-start.19 = (bf16[16,256]{1,0:T(8,128)(2,1)S(1)}, bf16[16,256]{1,0:T(8,128)(2,1)}, u32[]{:S(2)}) copy-start(bf16[16,256]{1,0:T(8,128)(2,1)} %copy-done.18) | copy-start | bytes 24580
  298.0 6.0 %copy-start.13 = (s32[16]{0:T(128)S(1)}, s32[16]{0:T(128)}, u32[]{:S(2)}) copy-start(s32[16]{0:T(128)} %get-tuple-element.43) | copy-start | bytes 196
  364.6 11.2 %copy-start.8 = (s32[16]{0:T(128)S(1)}, s32[16]{0:T(128)}, u32[]{:S(2)}) copy-start(s32[16]{0:T(128)} %get-tuple-element.42) | copy-start | bytes 196
  390.8 6.1 %copy-start.15 = (s32[16,512]{1,0:T(8,128)S(1)}, s32[16,512]{1,0:T(8,128)}, u32[]{:S(2)}) copy-start(s32[16,512]{1,0:T(8,128)} %copy-done.14) | copy-start | bytes 98308
  390.8 6.1 %copy-start.17 = (s32[16,512]{1,0:T(8,128)S(1)}, s32[16,512]{1,0:T(8,128)}, u32[]{:S(2)}) copy-start(s32[16,512]{1,0:T(8,128)} %copy-done.16) | copy-start | bytes 98308
  390.8 6.1 %copy-start.23 = (bf16[16,512]{1,0:T(8,128)(2,1)S(1)}, bf16[16,512]{1,0:T(8,128)(2,1)}, u32[]{:S(2)}) copy-start(bf16[16,512]{1,0:T(8,128)(2,1)} %copy-done.22) | copy-start | bytes 49156
  390.8 6.1 %copy-start.25 = (bf16[16,512]{1,0:T(8,128)(2,1)S(1)}, bf16[16,512]{1,0:T(8,128)(2,1)}, u32[]{:S(2)}) copy-start(bf16[16,512]{1,0:T(8,128)(2,1)} %copy-done.24) | copy-start | bytes 49156
  398.7 16.7 %copy-start.2 = (bf16[2,512,256]{1,2,0:T(8,128)(2,1)S(1)}, bf16[2,512,256]{1,2,0:T(8,128)(2,1)}, u32[]{:S(2)}) copy-start(bf16[2,512,256]{1,2,0:T(8,128)(2,1)} %copy-done.1) | copy-start | bytes 1572868
  398.9 8.8 %collective-permute-start.4 = (bf16[2,114,484]{1,2,0:T(8,128)(2,1)S(1)}, bf16[2,114,484]{1,2,0:T(8,128)(2,1)S(1)}, u32[]{:S(2)}, u32[]{:S(2)}) collective-permute-start(bf16[2,114,484]{1,2,0:T(8,128)(2,1)S(1)} %get-tuple-element.22), channel_id=1, source_target_pairs={{0,32},{32,64},{64,96},{96,128},{128,160},{160,192},{192,224},{1,3... | collective-permute-start | bytes 662120 | tf_op jit(solution)/shard_map/ppermute | solution.py:16
  400.9 8.5 %collective-permute-start.5 = (bf16[2,114,484]{1,2,0:T(8,128)(2,1)S(1)}, bf16[2,114,484]{1,2,0:T(8,128)(2,1)S(1)}, u32[]{:S(2)}, u32[]{:S(2)}) collective-permute-start(bf16[2,114,484]{1,2,0:T(8,128)(2,1)S(1)} %get-tuple-element.23), channel_id=1, source_target_pairs={{32,0},{64,32},{96,64},{128,96},{160,128},{192,160},{224,192},{33,... | collective-permute-start | bytes 662120 | tf_op jit(solution)/shard_map/ppermute | solution.py:17
  409.5 6.8 %copy-start.5 = (bf16[2,114,484]{1,2,0:T(8,128)(2,1)}, bf16[2,114,484]{1,2,0:T(8,128)(2,1)S(1)}, u32[]{:S(2)}) copy-start(bf16[2,114,484]{1,2,0:T(8,128)(2,1)S(1)} %collective-permute-done.5) | copy-start | bytes 662116
  411.0 29.7 %collective-permute-start.6 = (bf16[2,968,114]{1,2,0:T(8,128)(2,1)}, bf16[2,968,114]{1,2,0:T(8,128)(2,1)}, u32[]{:S(2)}, u32[]{:S(2)}) collective-permute-start(bf16[2,968,114]{1,2,0:T(8,128)(2,1)} %get-tuple-element.20), channel_id=1, source_target_pairs={{0,2},{2,4},{4,6},{6,8},{8,10},{10,12},{12,14},{14,16},{16,18},{18... | collective-permute-start | bytes 1324232 | tf_op jit(solution)/shard_map/ppermute | solution.py:16
  414.2 26.6 %collective-permute-start.7 = (bf16[2,968,114]{1,2,0:T(8,128)(2,1)}, bf16[2,968,114]{1,2,0:T(8,128)(2,1)}, u32[]{:S(2)}, u32[]{:S(2)}) collective-permute-start(bf16[2,968,114]{1,2,0:T(8,128)(2,1)} %get-tuple-element.21), channel_id=1, source_target_pairs={{2,0},{4,2},{6,4},{8,6},{10,8},{12,10},{14,12},{16,14},{18,16},{20... | collective-permute-start | bytes 1324232 | tf_op jit(solution)/shard_map/ppermute | solution.py:17
  416.3 18.6 %collective-permute-start.8 = (bf16[1,512,256]{1,2,0:T(8,128)(2,1)}, bf16[1,512,256]{1,2,0:T(8,128)(2,1)}, u32[]{:S(2)}, u32[]{:S(2)}) collective-permute-start(bf16[1,512,256]{1,2,0:T(8,128)(2,1)} %get-tuple-element.26), channel_id=1, source_target_pairs={{0,1},{2,3},{4,5},{6,7},{8,9},{10,11},{12,13},{14,15},{16,17},{18,... | collective-permute-start | bytes 786440 | tf_op jit(solution)/shard_map/ppermute | solution.py:16
  417.6 17.3 %collective-permute-start.9 = (bf16[1,512,256]{1,2,0:T(8,128)(2,1)}, bf16[1,512,256]{1,2,0:T(8,128)(2,1)}, u32[]{:S(2)}, u32[]{:S(2)}) collective-permute-start(bf16[1,512,256]{1,2,0:T(8,128)(2,1)} %get-tuple-element.27), channel_id=1, source_target_pairs={{1,0},{3,2},{5,4},{7,6},{9,8},{11,10},{13,12},{15,14},{17,16},{19,... | collective-permute-start | bytes 786440 | tf_op jit(solution)/shard_map/ppermute | solution.py:17
  440.8 2.8 copy-start.4
  442.1 1.9 copy-start
  (5 other events, 6.4 us)
Sparse Core Ops, SparseCore 0:
  50.5 176.7 all-reduce.17
where the time goes:
time: 454 us; the launch traced here: 453 us
  waiting for transfers between devices  181 us (40%)
  local copies, waits for them, and re-layouts  148 us (33%)
  blocking collectives  49.5 us (11%)
  starting transfers between devices  30.1 us (7%)
  other arithmetic  25.5 us (6%)
  between operations  14.6 us (3%)
    psum x1, waiting for transfers between devices, on_device(): total_y = lax.psum(summands_y, 'gy')  170 us
    gather x4, local copies, waits for them, and re-layouts, spread(): lax.dynamic_slice_in_dim(skewed, leading - lowest + pad_cells, number, 2)  50.9 us
    psum x1, blocking collectives, on_device(): total_x = lax.psum(summands_x, 'gx')  49.5 us
    reshape x2, local copies, waits for them, and re-layouts, spread(): repeated[:, :shift_levels * (row_length - 1)]  26.2 us
    unnamed x64, local copies, waits for them, and re-layouts  26.1 us
    ppermute x5, starting transfers between devices, padded_2(): after = lax.ppermute(leading, axis, down)  17.1 us
    gather x2, local copies, waits for them, and re-layouts, shear_sum(): lax.dynamic_slice_in_dim(skewed, leading + lowest + pad_cells, number, 1)  13 us
    ppermute x5, starting transfers between devices, padded_2(): before = lax.ppermute(last, axis, up)  13 us
  transfers between devices with their start and end apart: 11, of which 4 were waited for; matrix products, arithmetic and copies ran while one was open for 17% of the time, Pallas kernels for 0%

commit v1 on v0

v1 whole, which is shorter than its diff:
```python
import jax
import jax.numpy as jnp
from jax import lax
from jax.experimental import pallas as pl
from jax.experimental.pallas import tpu as pltpu
from jax.sharding import PartitionSpec as P

LEVELS = 16
F32 = jnp.float32
BF16 = jnp.bfloat16


def interpreted():
    return False


def fill(slopes_ref, family, shape, dim):
    views = slopes_ref.shape[1]
    view = lax.broadcasted_iota(jnp.int32, shape, dim) % views
    slopes = jnp.zeros(shape, jnp.int32)
    for v in range(views):
        slopes = jnp.where(view == v, slopes_ref[family, v], slopes)
    return slopes


def lowest_shift(slopes, block, blocks):
    return slopes * (block - blocks // 2) + jnp.minimum(slopes, 0)


def barrel(value, amounts, bits):
    for bit in range(bits):
        taken = ((amounts >> bit) & 1) == 1
        value = jnp.where(taken, pltpu.roll(value, 1 << bit, 1), value)
    return value


def offsets(slopes_ref, family, block, blocks, cells):
    views = slopes_ref.shape[1]
    slopes = fill(slopes_ref, family, (views, cells), 0)
    cell = lax.broadcasted_iota(jnp.int32, (views, cells), 1) + (block * cells - blocks * cells // 2)
    lowest = lowest_shift(slopes, block, blocks)
    return (slopes * cell - lowest * cells).astype(F32) * (1.0 / cells)


def hat(offset, level):
    return jnp.maximum(1.0 - jnp.abs(offset - level), 0.0)


def forward_kernel(slopes_ref, block_ref, volume_ref, measured_ref, out_ref, table_ref, rows_ref, *, family, blocks, pad, scale):
    views = slopes_ref.shape[1]
    planes = volume_ref.shape[0]
    bins = volume_ref.shape[2 - family]
    cells = volume_ref.shape[1 + family]
    width = out_ref.shape[1]
    block = block_ref[0]
    first = (block == 0).astype(F32)
    offset = offsets(slopes_ref, family, block, blocks, cells)
    for level in range(LEVELS):
        table_ref[level * views : (level + 1) * views, :] = hat(offset, float(LEVELS - 1 - level)).astype(BF16)
    for plane in range(planes):
        for v in range(views):
            rows_ref[plane * views + v : plane * views + v + 1, :] = measured_ref[v, plane : plane + 1, :]
    slopes = fill(slopes_ref, family, (views, width), 0)
    amounts = pad - LEVELS + 1 - lowest_shift(slopes, block, blocks)
    bits = max(1, (2 * pad).bit_length() - 1)
    empty = jnp.zeros((views, width - bins), F32)
    for plane in range(planes):
        dims = (((1,), (family,)), ((), ()))
        summands = lax.dot_general(table_ref[...], volume_ref[plane], dims, preferred_element_type=F32)
        total = None
        for level in reversed(range(LEVELS)):
            piece = jnp.concatenate([summands[level * views : (level + 1) * views, :], empty], axis=1)
            total = piece if total is None else pltpu.roll(total, 1, 1) + piece
        total = barrel(total, amounts, bits) * scale
        known = jnp.concatenate([rows_ref[plane * views : (plane + 1) * views, :], empty], axis=1)
        known = pltpu.roll(known, pad, 1)
        out_ref[plane * views : (plane + 1) * views, :] = total - known * first


def forward(slopes, block, volume, measured, family, blocks, pad, scale):
    views, planes, bins = measured.shape
    width = bins + 2 * pad
    cells = volume.shape[1 + family]

    def body(*refs):
        forward_kernel(*refs, family=family, blocks=blocks, pad=pad, scale=scale)

    smem = pl.BlockSpec(memory_space=pltpu.SMEM)
    vmem = pl.BlockSpec(memory_space=pltpu.VMEM)
    return pl.pallas_call(
        body,
        out_shape=jax.ShapeDtypeStruct((planes * views, width), F32),
        in_specs=[smem, smem, vmem, vmem],
        out_specs=vmem,
        scratch_shapes=[pltpu.VMEM((LEVELS * views, cells), BF16), pltpu.VMEM((planes * views, bins), F32)],
        interpret=interpreted(),
        name="forward_" + "xy"[family],
    )(slopes, block, volume, measured)


def spread_into(residual_ref, plane, slopes_ref, family, block, blocks, other, others, pad, spread_ref):
    views = slopes_ref.shape[1]
    width = residual_ref.shape[1]
    bins = width - 2 * pad
    slopes = fill(slopes_ref, family, (views, width), 0)
    bits = max(1, (2 * pad).bit_length() - 1)
    place = lax.broadcasted_iota(jnp.int32, (views, width), 1)
    inside = (place >= jnp.where(other == 0, pad, 0)) & (place < jnp.where(other == others - 1, pad + bins, width))
    value = residual_ref[plane * views : (plane + 1) * views, :]
    value = jnp.where(inside, value, 0.0).astype(BF16).astype(F32)
    amounts = lowest_shift(slopes, block, blocks) + pad
    value = pltpu.roll(barrel(value, amounts, bits), width - 2 * pad, 1)
    for level in range(LEVELS):
        spread_ref[level * views : (level + 1) * views, :] = value[:, :bins].astype(BF16)
        value = pltpu.roll(value, 1, 1)


def split_rows(residual_ref, out_ref, rows_ref, pad):
    views, planes, bins = out_ref.shape
    width = residual_ref.shape[1]
    for plane in range(planes):
        value = residual_ref[plane * views : (plane + 1) * views, :]
        rows_ref[plane * views : (plane + 1) * views, :] = pltpu.roll(value, width - pad, 1)[:, :bins]
    for plane in range(planes):
        for v in range(views):
            out_ref[v, plane : plane + 1, :] = rows_ref[plane * views + v : plane * views + v + 1, :]


def back_x_kernel(slopes_ref, blocks_ref, volume_ref, beside_ref, residual_ref, out_ref, rest_ref, table_ref, spread_ref, rows_ref, *, blocks, others, pad, scale):
    views = slopes_ref.shape[1]
    planes, cells, bins = volume_ref.shape
    block, other, band = blocks_ref[0], blocks_ref[1], blocks_ref[2]
    shape = (cells, LEVELS * views)
    slopes = fill(slopes_ref, 0, (8, shape[1]), 1)
    level = lax.broadcasted_iota(jnp.int32, (8, shape[1]), 1) // views
    base = ((lowest_shift(slopes, block, blocks) + level) * cells).astype(F32)[:1]
    slopes = slopes.astype(F32)[:1]
    cell = (lax.broadcasted_iota(jnp.int32, shape, 0) + (block * cells - blocks * cells // 2)).astype(F32)
    gap = (cell * slopes - base) * (1.0 / cells)
    table_ref[...] = jnp.maximum(1.0 - jnp.abs(gap), 0.0).astype(BF16)
    beside = beside_ref[0].astype(F32)
    for plane in range(planes):
        spread_into(residual_ref, plane, slopes_ref, 0, block, blocks, other, others, pad, spread_ref)
        value = jnp.dot(table_ref[...], spread_ref[...], preferred_element_type=F32) * scale
        here = volume_ref[plane].astype(F32)
        if plane == 0:
            before = beside * (band == 1).astype(F32)
            after = volume_ref[1].astype(F32)
        else:
            before = volume_ref[0].astype(F32)
            after = beside * (band == 0).astype(F32)
        out_ref[plane] = value + 0.02 * (2.0 * here - before - after)
    split_rows(residual_ref, rest_ref, rows_ref, pad)


def back_y_kernel(slopes_ref, blocks_ref, partial_ref, residual_ref, out_ref, rest_ref, table_ref, spread_ref, rows_ref, *, blocks, others, pad, scale):
    views = slopes_ref.shape[1]
    planes, bins, cells = partial_ref.shape
    block, other = blocks_ref[1], blocks_ref[0]
    offset = offsets(slopes_ref, 1, block, blocks, cells)
    for level in range(LEVELS):
        table_ref[level * views : (level + 1) * views, :] = hat(offset, float(level)).astype(BF16)
    for plane in range(planes):
        spread_into(residual_ref, plane, slopes_ref, 1, block, blocks, other, others, pad, spread_ref)
        dims = (((0,), (0,)), ((), ()))
        value = lax.dot_general(spread_ref[...], table_ref[...], dims, preferred_element_type=F32)
        out_ref[plane] = partial_ref[plane] + value * scale
    split_rows(residual_ref, rest_ref, rows_ref, pad)


def back_x(slopes, blocks, volume, beside, residual, count, others, pad, scale):
    planes, cells, bins = volume.shape
    views = slopes.shape[1]

    def body(*refs):
        back_x_kernel(*refs, blocks=count, others=others, pad=pad, scale=scale)

    smem = pl.BlockSpec(memory_space=pltpu.SMEM)
    vmem = pl.BlockSpec(memory_space=pltpu.VMEM)
    return pl.pallas_call(
        body,
        out_shape=(jax.ShapeDtypeStruct(volume.shape, F32), jax.ShapeDtypeStruct((views, planes, bins), F32)),
        in_specs=[smem, smem, vmem, vmem, vmem],
        out_specs=(vmem, vmem),
        scratch_shapes=[
            pltpu.VMEM((cells, LEVELS * views), BF16),
            pltpu.VMEM((LEVELS * views, bins), BF16),
            pltpu.VMEM((planes * views, bins), F32),
        ],
        interpret=interpreted(),
        name="back_x",
    )(slopes, blocks, volume, beside, residual)


def back_y(slopes, blocks, partial, residual, count, others, pad, scale):
    planes, bins, cells = partial.shape
    views = slopes.shape[1]

    def body(*refs):
        back_y_kernel(*refs, blocks=count, others=others, pad=pad, scale=scale)

    smem = pl.BlockSpec(memory_space=pltpu.SMEM)
    vmem = pl.BlockSpec(memory_space=pltpu.VMEM)
    return pl.pallas_call(
        body,
        out_shape=(jax.ShapeDtypeStruct(partial.shape, F32), jax.ShapeDtypeStruct((views, planes, bins), F32)),
        in_specs=[smem, smem, vmem, vmem],
        out_specs=(vmem, vmem),
        scratch_shapes=[
            pltpu.VMEM((LEVELS * views, cells), BF16),
            pltpu.VMEM((LEVELS * views, bins), BF16),
            pltpu.VMEM((planes * views, bins), F32),
        ],
        interpret=interpreted(),
        name="back_y",
    )(slopes, blocks, partial, residual)


def meet(value, axis, width):
    size = lax.axis_size(axis)
    up = [(i, i + 1) for i in range(size - 1)]
    down = [(i + 1, i) for i in range(size - 1)]
    length = value.shape[1]
    left = lax.ppermute(value[:, length - width :], axis, up)
    right = lax.ppermute(value[:, :width], axis, down)
    middle = value[:, width : length - width]
    return jnp.concatenate([value[:, :width] + left, middle, value[:, length - width :] + right], axis=1)


def swap(value, axis, bit):
    return lax.ppermute(value, axis, [(i, i ^ bit) for i in range(lax.axis_size(axis))])


def on_device(volume, view_slopes, measured_x, measured_y):
    planes, cells_x, cells_y = volume.shape
    count_x = lax.axis_size("gx")
    count_y = lax.axis_size("gy")
    scale_x = float(cells_x * count_x) ** (-0.5)
    scale_y = float(cells_y * count_y) ** (-0.5)
    here_x = lax.axis_index("gx")
    here_y = lax.axis_index("gy")
    band = lax.axis_index("pa")
    blocks = jnp.stack([here_x, here_y, band]).astype(jnp.int32)
    pad_x, pad_y = 64, 128
    near = lax.dynamic_index_in_dim(volume, 1 - band, 0, True)
    beside = lax.ppermute(near, "pa", [(0, 1), (1, 0)])

    sum_y = forward(view_slopes, blocks[1:2], volume, measured_y, 1, count_y, pad_y, scale_y)
    sum_y, ready = lax.optimization_barrier((sum_y, measured_x))
    sum_x = forward(view_slopes, blocks[0:1], volume, ready, 0, count_x, pad_x, scale_x)
    sum_y = meet(sum_y, "gx", 2 * pad_y)
    sum_x = meet(sum_x, "gy", 2 * pad_x)

    rows = sum_y.shape[0] // 2
    odd = here_y & 1
    kept = lax.dynamic_slice_in_dim(sum_y, odd * rows, rows, 0)
    sent = lax.dynamic_slice_in_dim(sum_y, (1 - odd) * rows, rows, 0)
    half = kept + swap(sent, "gy", 1)
    for bit in (2, 4, 8):
        half = half + swap(half, "gy", bit)
    rest = swap(half, "gy", 1)
    full_y = jnp.where(odd == 0, jnp.concatenate([half, rest]), jnp.concatenate([rest, half]))
    full_x = sum_x
    for bit in (1, 2, 4):
        full_x = full_x + swap(full_x, "gx", bit)

    partial, residual_x = back_x(view_slopes, blocks, volume, beside, full_x, count_x, count_y, pad_x, scale_x)
    gradient, residual_y = back_y(view_slopes, blocks, partial, full_y, count_y, count_x, pad_y, scale_y)
    return (gradient, residual_x, residual_y)


def solution(mesh):
    return jax.shard_map(
        on_device,
        mesh=mesh,
        in_specs=(P("pa", "gx", "gy"), P(), P(None, "pa", "gy"), P(None, "pa", "gx")),
        out_specs=(P("pa", "gx", "gy"), P(None, "pa", "gy"), P(None, "pa", "gx")),
        check_vma=False,
    )
```

time: 454 us -> 64.2 us (0.14)
  waiting for transfers between devices: 181 us -> 10.1 us
  local copies, waits for them, and re-layouts: 148 us -> 1.49 us
  blocking collectives: 49.5 us -> 0 us
  other arithmetic: 25.5 us -> 1.97 us
  Pallas kernels: 0 us -> 15.8 us
  between operations: 14.6 us -> 0.81 us
    psum x1 -> x0, waiting for transfers between devices: 170 us -> none  [on_device(): total_y = lax.psum(summands_y, 'gy')]
    gather x6 -> x0, local copies, waits for them, and re-layouts: 63.9 us -> none  [the longest x4 50.9 us: spread(): lax.dynamic_slice_in_dim(skewed, leading - lowest + pad_cells, number, 2)]
    psum x1 -> x0, blocking collectives: 49.5 us -> none  [on_device(): total_x = lax.psum(summands_x, 'gx')]
    reshape x6 -> x0, local copies, waits for them, and re-layouts: 35.5 us -> none  [the longest x2 26.2 us: spread(): repeated[:, :shift_levels * (row_length - 1)]]
    unnamed x64 -> x8, local copies, waits for them, and re-layouts: 26.1 us -> 0.72 us
    pallas_call x0 -> x4, Pallas kernels: none -> 15.8 us  [the longest x2 7.43 us: forward(): pl.pallas_call(body, out_shape=jax.ShapeDtypeStruct((planes * views, widt...]
    convert_element_type x6 -> x0, other arithmetic: 14 us -> none  [the longest x1 6.57 us: on_device(): back_ry = residual_y.astype(jnp.bfloat16)]
    reduce_sum x2 -> x0, local copies, waits for them, and re-layouts: 11.5 us -> none  [shear_sum(): jnp.sum(flattened.reshape(planes, shift_levels, row_length + 1), axis=1)]
  transfers between devices with their start and end apart: 11 -> 13, of which waited for: 4 -> 6; matrix products, arithmetic and copies ran while one was open for 17% -> 2% of each run, Pallas kernels for 0% -> 6%
where the time goes in v1:
time: 64.2 us; the launch traced here: 63.9 us
  starting transfers between devices  33.7 us (52%)
  Pallas kernels  15.8 us (25%)
  waiting for transfers between devices  10.1 us (16%)
  other arithmetic  1.97 us (3%)
  local copies, waits for them, and re-layouts  1.49 us (2%)
  between operations  0.81 us (1%)
    ppermute x8, starting transfers between devices, swap(): lax.ppermute(value, axis, [(i, i ^ bit) for i in range(lax.axis_size(axis...  22.3 us
    ppermute x8, waiting for transfers between devices, swap(): lax.ppermute(value, axis, [(i, i ^ bit) for i in range(lax.axis_size(axis...  8.58 us
    pallas_call x2, Pallas kernels, forward(): pl.pallas_call(body, out_shape=jax.ShapeDtypeStruct((planes * views, widt...  7.43 us
    ppermute x2, starting transfers between devices, meet(): left = lax.ppermute(value[:, length - width:], axis, up)  5.73 us
    ppermute x2, starting transfers between devices, meet(): right = lax.ppermute(value[:, :width], axis, down)  5.07 us
    pallas_call x1, Pallas kernels, back_y(): pl.pallas_call(body, out_shape=(jax.ShapeDtypeStruct(partial.shape, F32),...  4.22 us
    pallas_call x1, Pallas kernels, back_x(): pl.pallas_call(body, out_shape=(jax.ShapeDtypeStruct(volume.shape, F32),...  4.15 us
    ppermute x2, waiting for transfers between devices, meet(): right = lax.ppermute(value[:, :width], axis, down)  1.51 us
  transfers between devices with their start and end apart: 13, of which 6 were waited for; matrix products, arithmetic and copies ran while one was open for 2% of the time, Pallas kernels for 6%

profile of v1, /device:TPU:10, one launch (start us, length us, event | category | flops | bytes accessed | tf_op | source)
XLA Modules:
  0.0 63.9 jit_solution(682208842612091113)
XLA Ops:
  0.6 3.8 %forward_y.1 = f32[32,768]{1,0:T(8,128)} custom-call(s32[2,16]{1,0:T(2,128)} %refs_0_.7, s32[1]{0:T(128)} %bitcast.1.refs_1_, bf16[2,512,256]{2,1,0:T(8,128)(2,1)} %refs_2_.5, f32[16,2,512]{2,1,0:T(2,128)} %refs_3_.1), custom_call_target="tpu_custom_call" | custom-call | tf_op jit(solution)/shard_map/forward_y/pallas_call | solution.py:90
  4.4 3.7 %forward_x.1 = f32[32,384]{1,0:T(8,128)} custom-call(s32[2,16]{1,0:T(2,128)} %refs_0_.7, s32[1]{0:T(128)} %bitcast.refs_1_, bf16[2,512,256]{2,1,0:T(8,128)(2,1)} %refs_2_.5, f32[16,2,256]{2,1,0:T(2,128)} %refs_3_.2), custom_call_target="tpu_custom_call" | custom-call | tf_op jit(solution)/shard_map/forward_x/pallas_call | solution.py:90
  8.1 0.7 %fusion.2 = (f32[32,128]{1,0:T(8,128)S(1)}, f32[32,128]{1,0:T(8,128)S(1)}) fusion(f32[32,384]{1,0:T(8,128)} %forward_x.1), kind=kLoop, calls=%fused_computation.13 | loop fusion | bytes 65536 | tf_op jit(solution)/shard_map/slice | solution.py:224
  8.8 3.8 %collective-permute-start.1 = (f32[32,128]{1,0:T(8,128)S(1)}, f32[32,128]{1,0:T(8,128)S(1)}, u32[]{:S(2)}, u32[]{:S(2)}) collective-permute-start(f32[32,128]{1,0:T(8,128)S(1)} %get-tuple-element.23), channel_id=1, source_target_pairs={{0,2},{2,4},{4,6},{6,8},{8,10},{10,12},{12,14},{14,16},{16,18},{18... | collective-permute-start | bytes 49160 | tf_op jit(solution)/shard_map/ppermute | solution.py:224
  12.6 0.0 copy-start.2
  12.6 0.0 copy-start
  12.6 1.4 %collective-permute-start.2 = (f32[32,128]{1,0:T(8,128)S(1)}, f32[32,128]{1,0:T(8,128)S(1)}, u32[]{:S(2)}, u32[]{:S(2)}) collective-permute-start(f32[32,128]{1,0:T(8,128)S(1)} %get-tuple-element.24), channel_id=1, source_target_pairs={{2,0},{4,2},{6,4},{8,6},{10,8},{12,10},{14,12},{16,14},{18,16},{20... | collective-permute-start | bytes 49160 | tf_op jit(solution)/shard_map/ppermute | solution.py:225
  14.1 1.9 %collective-permute-start.6 = (f32[32,256]{1,0:T(8,128)S(1)}, f32[32,256]{1,0:T(8,128)S(1)}, u32[]{:S(2)}, u32[]{:S(2)}) collective-permute-start(f32[32,256]{1,0:T(8,128)S(1)} %get-tuple-element.18), channel_id=1, source_target_pairs={{0,32},{32,64},{64,96},{96,128},{128,160},{160,192},{192,224},{1,3... | collective-permute-start | bytes 98312 | tf_op jit(solution)/shard_map/ppermute | solution.py:224
  16.0 3.6 %collective-permute-start.7 = (f32[32,256]{1,0:T(8,128)S(1)}, f32[32,256]{1,0:T(8,128)S(1)}, u32[]{:S(2)}, u32[]{:S(2)}) collective-permute-start(f32[32,256]{1,0:T(8,128)S(1)} %get-tuple-element.19), channel_id=1, source_target_pairs={{32,0},{64,32},{96,64},{128,96},{160,128},{192,160},{224,192},{33,... | collective-permute-start | bytes 98312 | tf_op jit(solution)/shard_map/ppermute | solution.py:225
  19.7 0.0 collective-permute-done.2
  19.7 0.0 collective-permute-done.6
  19.7 1.5 %collective-permute-done.7 = f32[32,256]{1,0:T(8,128)S(1)} collective-permute-done((f32[32,256]{1,0:T(8,128)S(1)}, f32[32,256]{1,0:T(8,128)S(1)}, u32[]{:S(2)}, u32[]{:S(2)}) %collective-permute-start.7) | collective-permute-done | bytes 32800 | tf_op jit(solution)/shard_map/ppermute | solution.py:225
  21.3 2.7 %collective-permute-start.8 = (f32[16,768]{1,0:T(8,128)S(1)}, f32[16,768]{1,0:T(8,128)S(1)}, u32[]{:S(2)}, u32[]{:S(2)}) collective-permute-start(f32[16,768]{1,0:T(8,128)S(1)} %constant_dynamic-slice_fusion), channel_id=1, source_target_pairs={{0,2},{2,0},{4,6},{6,4},{8,10},{10,8},{12,14},{14,12},{16,18},{18,... | collective-permute-start | bytes 147464 | tf_op jit(solution)/shard_map/ppermute | solution.py:231
  24.0 1.4 %collective-permute-start.3 = (f32[32,384]{1,0:T(8,128)S(1)}, f32[32,384]{1,0:T(8,128)S(1)}, u32[]{:S(2)}, u32[]{:S(2)}) collective-permute-start(f32[32,384]{1,0:T(8,128)S(1)} %pad_maximum_fusion.1), channel_id=1, source_target_pairs={{0,32},{32,0},{64,96},{96,64},{128,160},{160,128},{192,224},{224,1... | collective-permute-start | bytes 147464 | tf_op jit(solution)/shard_map/ppermute | solution.py:231
  25.5 0.7 %collective-permute-done.8 = f32[16,768]{1,0:T(8,128)S(1)} collective-permute-done((f32[16,768]{1,0:T(8,128)S(1)}, f32[16,768]{1,0:T(8,128)S(1)}, u32[]{:S(2)}, u32[]{:S(2)}) %collective-permute-start.8) | collective-permute-done | bytes 49184 | tf_op jit(solution)/shard_map/ppermute | solution.py:231
  26.1 4.5 %collective-permute-start.9 = (f32[16,768]{1,0:T(8,128)S(1)}, f32[16,768]{1,0:T(8,128)S(1)}, u32[]{:S(2)}, u32[]{:S(2)}) collective-permute-start(f32[16,768]{1,0:T(8,128)S(1)} %dynamic-slice_add_fusion), channel_id=1, source_target_pairs={{0,4},{2,6},{4,0},{6,2},{8,12},{10,14},{12,8},{14,10},{16,20},{18,... | collective-permute-start | bytes 147464 | tf_op jit(solution)/shard_map/ppermute | solution.py:231
  30.6 0.6 collective-permute-start
  31.2 1.8 %collective-permute-done.9 = f32[16,768]{1,0:T(8,128)S(1)} collective-permute-done((f32[16,768]{1,0:T(8,128)S(1)}, f32[16,768]{1,0:T(8,128)S(1)}, u32[]{:S(2)}, u32[]{:S(2)}) %collective-permute-start.9) | collective-permute-done | bytes 49184 | tf_op jit(solution)/shard_map/ppermute | solution.py:231
  33.1 7.6 %collective-permute-start.10 = (f32[16,768]{1,0:T(8,128)S(1)}, f32[16,768]{1,0:T(8,128)S(1)}, u32[]{:S(2)}, u32[]{:S(2)}) collective-permute-start(f32[16,768]{1,0:T(8,128)S(1)} %add.55), channel_id=1, source_target_pairs={{0,8},{2,10},{4,12},{6,14},{8,0},{10,2},{12,4},{14,6},{16,24},{18,... | collective-permute-start | bytes 147464 | tf_op jit(solution)/shard_map/ppermute | solution.py:231
  40.7 0.1 collective-permute-start.4
  40.8 2.0 %collective-permute-done.10 = f32[16,768]{1,0:T(8,128)S(1)} collective-permute-done((f32[16,768]{1,0:T(8,128)S(1)}, f32[16,768]{1,0:T(8,128)S(1)}, u32[]{:S(2)}, u32[]{:S(2)}) %collective-permute-start.10) | collective-permute-done | bytes 49184 | tf_op jit(solution)/shard_map/ppermute | solution.py:231
  42.8 5.1 %collective-permute-start.11 = (f32[16,768]{1,0:T(8,128)S(1)}, f32[16,768]{1,0:T(8,128)S(1)}, u32[]{:S(2)}, u32[]{:S(2)}) collective-permute-start(f32[16,768]{1,0:T(8,128)S(1)} %add.56), channel_id=1, source_target_pairs={{0,16},{2,18},{4,20},{6,22},{8,24},{10,26},{12,28},{14,30},{16,0},... | collective-permute-start | bytes 147464 | tf_op jit(solution)/shard_map/ppermute | solution.py:231
  47.9 0.8 %collective-permute-start.5 = (f32[32,384]{1,0:T(8,128)S(1)}, f32[32,384]{1,0:T(8,128)S(1)}, u32[]{:S(2)}, u32[]{:S(2)}) collective-permute-start(f32[32,384]{1,0:T(8,128)S(1)} %add.48), channel_id=1, source_target_pairs={{0,128},{32,160},{64,192},{96,224},{128,0},{160,32},{192,64},{224,... | collective-permute-start | bytes 147464 | tf_op jit(solution)/shard_map/ppermute | solution.py:231
  48.7 1.2 %collective-permute-done.11 = f32[16,768]{1,0:T(8,128)S(1)} collective-permute-done((f32[16,768]{1,0:T(8,128)S(1)}, f32[16,768]{1,0:T(8,128)S(1)}, u32[]{:S(2)}, u32[]{:S(2)}) %collective-permute-start.11) | collective-permute-done | bytes 49184 | tf_op jit(solution)/shard_map/ppermute | solution.py:231
  49.9 0.1 collective-permute-start.12
  50.0 0.6 pad_add_fusion.refs_1_
  50.6 2.9 %collective-permute-done.5 = f32[32,384]{1,0:T(8,128)S(1)} collective-permute-done((f32[32,384]{1,0:T(8,128)S(1)}, f32[32,384]{1,0:T(8,128)S(1)}, u32[]{:S(2)}, u32[]{:S(2)}) %collective-permute-start.5) | collective-permute-done | bytes 49184 | tf_op jit(solution)/shard_map/ppermute | solution.py:231
  53.5 0.6 add.49.refs_4_
  54.2 0.7 %copy-done.3 = bf16[1,512,256]{2,1,0:T(8,128)(2,1)} copy-done((bf16[1,512,256]{2,1,0:T(8,128)(2,1)}, bf16[1,512,256]{2,1,0:T(8,128)(2,1)S(1)}, u32[]{:S(2)}) %copy-start.3) | copy-done | bytes 262168
  54.9 4.2 %back_x.1 = (f32[2,512,256]{2,1,0:T(8,128)}, f32[16,2,256]{2,1,0:T(2,128)}) custom-call(s32[2,16]{1,0:T(2,128)} %refs_0_.7, s32[3]{0:T(128)} %pad_add_fusion.refs_1_, bf16[2,512,256]{2,1,0:T(8,128)(2,1)} %refs_2_.5, bf16[1,512,256]{2,1,0:T(8,128)(2,1)} %copy-done.3, f32[32,384]{1,0:T(8,128)} %add.49.refs_4_), custom_call_target="tpu_custom_call" | custom-call | tf_op jit(solution)/shard_map/back_x/pallas_call | solution.py:180
  59.0 0.6 %maximum_select_fusion.refs_3_ = f32[32,768]{1,0:T(8,128)} fusion(f32[16,768]{1,0:T(8,128)S(1)} %collective-permute-done.12, f32[16,768]{1,0:T(8,128)S(1)} %add.57, pred[]{:T(512)S(6)} %eq.3), kind=kLoop, calls=%fused_computation.1 | loop fusion | flops 73728 | bytes 196609 | tf_op jit(solution)/shard_map/jit(_where)/select_n | solution.py:262
  59.7 4.2 %back_y.1 = (f32[2,512,256]{2,1,0:T(8,128)}, f32[16,2,512]{2,1,0:T(2,128)}) custom-call(s32[2,16]{1,0:T(2,128)} %refs_0_.7, s32[3]{0:T(128)} %pad_add_fusion.refs_1_, f32[2,512,256]{2,1,0:T(8,128)} %get-tuple-element.10.refs_2_, f32[32,768]{1,0:T(8,128)} %maximum_select_fusion.refs_3_), custom_call_target="tpu_custom_call" | custom-call | tf_op jit(solution)/shard_map/back_y/pallas_call | solution.py:204
  (23 shorter events, 0.1 us)
Async XLA Ops:
  4.4 9.7 %copy-start.1 = (f32[32,768]{1,0:T(8,128)S(1)}, f32[32,768]{1,0:T(8,128)}, u32[]{:S(2)}) copy-start(f32[32,768]{1,0:T(8,128)} %forward_y.1) | copy-start | bytes 294916
  8.8 10.9 %collective-permute-start.1 = (f32[32,128]{1,0:T(8,128)S(1)}, f32[32,128]{1,0:T(8,128)S(1)}, u32[]{:S(2)}, u32[]{:S(2)}) collective-permute-start(f32[32,128]{1,0:T(8,128)S(1)} %get-tuple-element.23), channel_id=1, source_target_pairs={{0,2},{2,4},{4,6},{6,8},{8,10},{10,12},{12,14},{14,16},{16,18},{18... | collective-permute-start | bytes 49160 | tf_op jit(solution)/shard_map/ppermute | solution.py:224
  12.6 7.1 %copy-start.2 = (f32[32,384]{1,0:T(8,128)S(1)}, f32[32,384]{1,0:T(8,128)}, u32[]{:S(2)}) copy-start(f32[32,384]{1,0:T(8,128)} %forward_x.1) | copy-start | bytes 147460
  12.6 18.0 %copy-start = (bf16[2,512,256]{2,1,0:T(8,128)(2,1)S(1)}, bf16[2,512,256]{2,1,0:T(8,128)(2,1)}, u32[]{:S(2)}) copy-start(bf16[2,512,256]{2,1,0:T(8,128)(2,1)} %refs_2_.5) | copy-start | bytes 1572868
  12.6 7.1 %collective-permute-start.2 = (f32[32,128]{1,0:T(8,128)S(1)}, f32[32,128]{1,0:T(8,128)S(1)}, u32[]{:S(2)}, u32[]{:S(2)}) collective-permute-start(f32[32,128]{1,0:T(8,128)S(1)} %get-tuple-element.24), channel_id=1, source_target_pairs={{2,0},{4,2},{6,4},{8,6},{10,8},{12,10},{14,12},{16,14},{18,16},{20... | collective-permute-start | bytes 49160 | tf_op jit(solution)/shard_map/ppermute | solution.py:225
  14.1 5.6 %collective-permute-start.6 = (f32[32,256]{1,0:T(8,128)S(1)}, f32[32,256]{1,0:T(8,128)S(1)}, u32[]{:S(2)}, u32[]{:S(2)}) collective-permute-start(f32[32,256]{1,0:T(8,128)S(1)} %get-tuple-element.18), channel_id=1, source_target_pairs={{0,32},{32,64},{64,96},{96,128},{128,160},{160,192},{192,224},{1,3... | collective-permute-start | bytes 98312 | tf_op jit(solution)/shard_map/ppermute | solution.py:224
  16.0 5.2 %collective-permute-start.7 = (f32[32,256]{1,0:T(8,128)S(1)}, f32[32,256]{1,0:T(8,128)S(1)}, u32[]{:S(2)}, u32[]{:S(2)}) collective-permute-start(f32[32,256]{1,0:T(8,128)S(1)} %get-tuple-element.19), channel_id=1, source_target_pairs={{32,0},{64,32},{96,64},{128,96},{160,128},{192,160},{224,192},{33,... | collective-permute-start | bytes 98312 | tf_op jit(solution)/shard_map/ppermute | solution.py:225
  21.3 4.8 %collective-permute-start.8 = (f32[16,768]{1,0:T(8,128)S(1)}, f32[16,768]{1,0:T(8,128)S(1)}, u32[]{:S(2)}, u32[]{:S(2)}) collective-permute-start(f32[16,768]{1,0:T(8,128)S(1)} %constant_dynamic-slice_fusion), channel_id=1, source_target_pairs={{0,2},{2,0},{4,6},{6,4},{8,10},{10,8},{12,14},{14,12},{16,18},{18,... | collective-permute-start | bytes 147464 | tf_op jit(solution)/shard_map/ppermute | solution.py:231
  24.0 16.6 %collective-permute-start.3 = (f32[32,384]{1,0:T(8,128)S(1)}, f32[32,384]{1,0:T(8,128)S(1)}, u32[]{:S(2)}, u32[]{:S(2)}) collective-permute-start(f32[32,384]{1,0:T(8,128)S(1)} %pad_maximum_fusion.1), channel_id=1, source_target_pairs={{0,32},{32,0},{64,96},{96,64},{128,160},{160,128},{192,224},{224,1... | collective-permute-start | bytes 147464 | tf_op jit(solution)/shard_map/ppermute | solution.py:231
  26.1 6.9 %collective-permute-start.9 = (f32[16,768]{1,0:T(8,128)S(1)}, f32[16,768]{1,0:T(8,128)S(1)}, u32[]{:S(2)}, u32[]{:S(2)}) collective-permute-start(f32[16,768]{1,0:T(8,128)S(1)} %dynamic-slice_add_fusion), channel_id=1, source_target_pairs={{0,4},{2,6},{4,0},{6,2},{8,12},{10,14},{12,8},{14,10},{16,20},{18,... | collective-permute-start | bytes 147464 | tf_op jit(solution)/shard_map/ppermute | solution.py:231
  30.6 23.6 %collective-permute-start = (bf16[1,512,256]{2,1,0:T(8,128)(2,1)S(1)}, bf16[1,512,256]{2,1,0:T(8,128)(2,1)S(1)}, u32[]{:S(2)}, u32[]{:S(2)}) collective-permute-start(bf16[1,512,256]{2,1,0:T(8,128)(2,1)S(1)} %constant_dynamic-slice_fusion.1), channel_id=1, source_target_pairs={{0,1},{1,0},{2,3},{3,2},{4,5},{5,4},{6,7},{7,6},{8,9},{9,8},{10,11... | collective-permute-start | bytes 786440 | tf_op jit(solution)/shard_map/ppermute | solution.py:246
  33.1 9.7 %collective-permute-start.10 = (f32[16,768]{1,0:T(8,128)S(1)}, f32[16,768]{1,0:T(8,128)S(1)}, u32[]{:S(2)}, u32[]{:S(2)}) collective-permute-start(f32[16,768]{1,0:T(8,128)S(1)} %add.55), channel_id=1, source_target_pairs={{0,8},{2,10},{4,12},{6,14},{8,0},{10,2},{12,4},{14,6},{16,24},{18,... | collective-permute-start | bytes 147464 | tf_op jit(solution)/shard_map/ppermute | solution.py:231
  40.7 7.2 %collective-permute-start.4 = (f32[32,384]{1,0:T(8,128)S(1)}, f32[32,384]{1,0:T(8,128)S(1)}, u32[]{:S(2)}, u32[]{:S(2)}) collective-permute-start(f32[32,384]{1,0:T(8,128)S(1)} %fusion), channel_id=1, source_target_pairs={{0,64},{32,96},{64,0},{96,32},{128,192},{160,224},{192,128},{224,1... | collective-permute-start | bytes 147464 | tf_op jit(solution)/shard_map/ppermute | solution.py:231
  42.8 7.2 %collective-permute-start.11 = (f32[16,768]{1,0:T(8,128)S(1)}, f32[16,768]{1,0:T(8,128)S(1)}, u32[]{:S(2)}, u32[]{:S(2)}) collective-permute-start(f32[16,768]{1,0:T(8,128)S(1)} %add.56), channel_id=1, source_target_pairs={{0,16},{2,18},{4,20},{6,22},{8,24},{10,26},{12,28},{14,30},{16,0},... | collective-permute-start | bytes 147464 | tf_op jit(solution)/shard_map/ppermute | solution.py:231
  47.9 5.7 %collective-permute-start.5 = (f32[32,384]{1,0:T(8,128)S(1)}, f32[32,384]{1,0:T(8,128)S(1)}, u32[]{:S(2)}, u32[]{:S(2)}) collective-permute-start(f32[32,384]{1,0:T(8,128)S(1)} %add.48), channel_id=1, source_target_pairs={{0,128},{32,160},{64,192},{96,224},{128,0},{160,32},{192,64},{224,... | collective-permute-start | bytes 147464 | tf_op jit(solution)/shard_map/ppermute | solution.py:231
  49.9 9.1 %collective-permute-start.12 = (f32[16,768]{1,0:T(8,128)S(1)}, f32[16,768]{1,0:T(8,128)S(1)}, u32[]{:S(2)}, u32[]{:S(2)}) collective-permute-start(f32[16,768]{1,0:T(8,128)S(1)} %add.57), channel_id=1, source_target_pairs={{0,2},{2,0},{4,6},{6,4},{8,10},{10,8},{12,14},{14,12},{16,18},{18,... | collective-permute-start | bytes 147464 | tf_op jit(solution)/shard_map/ppermute | solution.py:231
  54.2 0.7 %copy-start.3 = (bf16[1,512,256]{2,1,0:T(8,128)(2,1)}, bf16[1,512,256]{2,1,0:T(8,128)(2,1)S(1)}, u32[]{:S(2)}) copy-start(bf16[1,512,256]{2,1,0:T(8,128)(2,1)S(1)} %collective-permute-done.refs_3_) | copy-start | bytes 786436

commit v2 on v1

v2 whole, which is shorter than its diff:
```python
import jax
import jax.numpy as jnp
from jax import lax
from jax.experimental import pallas as pl
from jax.experimental.pallas import tpu as pltpu
from jax.sharding import PartitionSpec as P


LEVELS = 16
SMEM = pltpu.SMEM
VMEM = pltpu.VMEM
F32 = jnp.float32
BF16 = jnp.bfloat16


def interpreted():
    return False


def fill(slopes_ref, family, shape, dim):
    views = slopes_ref.shape[1]
    view = lax.broadcasted_iota(jnp.int32, shape, dim) % views
    slopes = jnp.zeros(shape, jnp.int32)
    for v in range(views):
        slopes = jnp.where(view == v, slopes_ref[family, v], slopes)
    return slopes


def lowest_shift(slopes, block, blocks):
    return slopes * (block - blocks // 2) + jnp.minimum(slopes, 0)


def barrel(value, amounts, bits):
    for bit in range(bits):
        taken = ((amounts >> bit) & 1) == 1
        value = jnp.where(taken, pltpu.roll(value, 1 << bit, 1), value)
    return value


def offsets(slopes_ref, family, block, blocks, cells):
    views = slopes_ref.shape[1]
    slopes = fill(slopes_ref, family, (views, cells), 0)
    cell = lax.broadcasted_iota(jnp.int32, (views, cells), 1) + (block * cells - blocks * cells // 2)
    lowest = lowest_shift(slopes, block, blocks)
    return (slopes * cell - lowest * cells).astype(F32) * (1.0 / cells)


def hat(offset, level):
    return jnp.maximum(1.0 - jnp.abs(offset - level), 0.0)


def in_vmem(value):
    if interpreted():
        return value
    return pltpu.with_memory_space_constraint(value, VMEM)


def out_vmem(shape, dtype):
    if interpreted():
        return jax.ShapeDtypeStruct(shape, dtype)
    return VMEM(shape, dtype)


def anywhere():
    return pl.BlockSpec(memory_space=pl.ANY)


def vmem():
    return pl.BlockSpec(memory_space=VMEM)


def forward_kernel(*refs, family, axis, blocks, pad, scale, views):
    slopes_hbm, volume_hbm, measured_hbm, out_ref = refs[:4]
    rest = list(refs[4:])
    if family == 1:
        table_ref, near_ref = rest.pop(0), rest.pop(0)
    else:
        table_ref = rest.pop(0)
    slopes_ref, volume_ref, measured_ref, rows_ref, sems = rest
    planes = volume_ref.shape[0]
    bins = volume_ref.shape[2 - family]
    cells = volume_ref.shape[1 + family]
    width = out_ref.shape[1]
    fetch_slopes = pltpu.make_async_copy(slopes_hbm, slopes_ref, sems.at[0])
    fetch_volume = pltpu.make_async_copy(volume_hbm, volume_ref, sems.at[1])
    fetch_measured = pltpu.make_async_copy(measured_hbm, measured_ref, sems.at[2])
    fetch_slopes.start()
    fetch_volume.start()
    fetch_measured.start()
    if family == 1:
        far = 1 - lax.axis_index("pa")
        fetch_near = pltpu.make_async_copy(volume_hbm.at[pl.ds(far, 1)], near_ref, sems.at[3])
        fetch_near.start()
    block = lax.axis_index(axis)
    first = (block == 0).astype(F32)
    fetch_slopes.wait()
    offset = offsets(slopes_ref, family, block, blocks, cells)
    for level in range(LEVELS):
        table_ref[level * views : (level + 1) * views, :] = hat(offset, float(level)).astype(BF16)
    slopes = fill(slopes_ref, family, (views, width), 0)
    amounts = pad - lowest_shift(slopes, block, blocks)
    bits = max(1, (2 * pad).bit_length() - 1)
    empty = jnp.zeros((views, width - bins), F32)
    fetch_measured.wait()
    for plane in range(planes):
        for v in range(views):
            rows_ref[plane * views + v : plane * views + v + 1, :] = measured_ref[v, plane : plane + 1, :]
    fetch_volume.wait()
    for plane in range(planes):
        dims = (((1,), (family,)), ((), ()))
        summands = lax.dot_general(table_ref[...], volume_ref[plane], dims, preferred_element_type=F32)
        total = None
        for level in reversed(range(LEVELS)):
            piece = jnp.concatenate([summands[level * views : (level + 1) * views, :], empty], axis=1)
            total = piece if total is None else pltpu.roll(total, width - 1, 1) + piece
        total = barrel(total, amounts, bits) * scale
        known = jnp.concatenate([rows_ref[plane * views : (plane + 1) * views, :] * first, empty], axis=1)
        out_ref[plane * views : (plane + 1) * views, :] = total - pltpu.roll(known, pad, 1)
    if family == 1:
        fetch_near.wait()


def forward(slopes, volume, measured, family, axis, blocks, pad, scale):
    views, planes, bins = measured.shape
    width = bins + 2 * pad
    cells = volume.shape[1 + family]

    def body(*refs):
        forward_kernel(*refs, family=family, axis=axis, blocks=blocks, pad=pad, scale=scale, views=views)

    outs = [out_vmem((planes * views, width), F32)]
    scratch = []
    if family == 1:
        outs.append(out_vmem((LEVELS * views, cells), BF16))
        outs.append(out_vmem((1,) + volume.shape[1:], BF16))
    else:
        scratch.append(VMEM((LEVELS * views, cells), BF16))
    scratch += [
        SMEM(slopes.shape, jnp.int32),
        VMEM(volume.shape, BF16),
        VMEM(measured.shape, F32),
        VMEM((planes * views, bins), F32),
        pltpu.SemaphoreType.DMA((4,)),
    ]
    return pl.pallas_call(
        body,
        out_shape=tuple(outs),
        in_specs=[anywhere(), anywhere(), anywhere()],
        out_specs=tuple(vmem() for _ in outs),
        scratch_shapes=scratch,
        interpret=interpreted(),
    )(slopes, volume, measured)


def spread_into(value, slopes_ref, family, block, blocks, other, others, pad, scale, spread_ref):
    views, width = value.shape
    bins = width - 2 * pad
    slopes = fill(slopes_ref, family, (views, width), 0)
    bits = max(1, (2 * pad).bit_length() - 1)
    place = lax.broadcasted_iota(jnp.int32, (views, width), 1)
    inside = (place >= jnp.where(other == 0, pad, 0)) & (place < jnp.where(other == others - 1, pad + bins, width))
    value = jnp.where(inside, value * scale, 0.0).astype(BF16).astype(F32)
    amounts = lowest_shift(slopes, block, blocks) + pad
    value = pltpu.roll(barrel(value, amounts, bits), width - 2 * pad, 1)
    for level in range(LEVELS):
        spread_ref[level * views : (level + 1) * views, :] = value[:, :bins].astype(BF16)
        value = pltpu.roll(value, 1, 1)


def middle(value, pad):
    width = value.shape[1]
    return pltpu.roll(value, width - pad, 1)[:, : width - 2 * pad]


def back_x_kernel(slopes_hbm, volume_hbm, beside_ref, residual_ref, out_ref, rest_ref, slopes_ref, volume_ref, table_ref, spread_ref, rows_ref, sems, *, blocks, others, pad, scale, views):
    planes, cells, _ = volume_ref.shape
    fetch_slopes = pltpu.make_async_copy(slopes_hbm, slopes_ref, sems.at[0])
    fetch_volume = pltpu.make_async_copy(volume_hbm, volume_ref, sems.at[1])
    fetch_slopes.start()
    fetch_volume.start()
    block, other, band = lax.axis_index("gx"), lax.axis_index("gy"), lax.axis_index("pa")
    shape = (cells, LEVELS * views)
    fetch_slopes.wait()
    slopes = fill(slopes_ref, 0, (8, shape[1]), 1)
    level = lax.broadcasted_iota(jnp.int32, (8, shape[1]), 1) // views
    base = (lowest_shift(slopes, block, blocks) + level).astype(F32)[:1]
    slopes = slopes.astype(F32)[:1]
    cell = lax.broadcasted_iota(jnp.int32, shape, 0).astype(F32) * (1.0 / cells) + (block - blocks // 2).astype(F32)
    table_ref[...] = jnp.maximum(1.0 - jnp.abs(cell * slopes - base), 0.0).astype(BF16)
    fetch_volume.wait()
    for plane in range(planes):
        residual = residual_ref[plane * views : (plane + 1) * views, :]
        spread_into(residual, slopes_ref, 0, block, blocks, other, others, pad, scale, spread_ref)
        value = jnp.dot(table_ref[...], spread_ref[...], preferred_element_type=F32)
        here = volume_ref[plane].astype(F32)
        beside = beside_ref[0].astype(F32) * (band == 1 - plane).astype(F32)
        within = volume_ref[1 - plane].astype(F32)
        out_ref[plane] = value + 0.02 * (2.0 * here - beside - within)
        rows_ref[plane * views : (plane + 1) * views, :] = middle(residual, pad)
    for plane in range(planes):
        for v in range(views):
            rest_ref[v, plane : plane + 1, :] = rows_ref[plane * views + v : plane * views + v + 1, :]


def back_x(slopes, volume, beside, residual, blocks, others, pad, scale):
    planes, cells, bins = volume.shape
    views = slopes.shape[1]

    def body(*refs):
        back_x_kernel(*refs, blocks=blocks, others=others, pad=pad, scale=scale, views=views)

    return pl.pallas_call(
        body,
        out_shape=(out_vmem(volume.shape, F32), jax.ShapeDtypeStruct((views, planes, bins), F32)),
        in_specs=[anywhere(), anywhere(), vmem(), vmem()],
        out_specs=(vmem(), vmem()),
        scratch_shapes=[
            SMEM(slopes.shape, jnp.int32),
            VMEM(volume.shape, BF16),
            VMEM((cells, LEVELS * views), BF16),
            VMEM((LEVELS * views, bins), BF16),
            VMEM((planes * views, bins), F32),
            pltpu.SemaphoreType.DMA((2,)),
        ],
        interpret=interpreted(),
        name="back_x",
    )(slopes, volume, in_vmem(beside), in_vmem(residual))


def back_y_kernel(*refs, last, blocks, others, pad, scale, views):
    slopes_hbm, table_ref, partial_ref, half_ref = refs[:4]
    rest = list(refs[4:])
    if last:
        other_ref = rest.pop(0)
        rest.pop(0)
        rest_ref = rest.pop(1)
    out_hbm, slopes_ref, sum_ref, spread_ref, rows_ref, sems = rest
    fetch_slopes = pltpu.make_async_copy(slopes_hbm, slopes_ref, sems.at[0])
    fetch_slopes.start()
    block, other = lax.axis_index("gy"), lax.axis_index("gx")
    mine = lax.axis_index("gy") % 2
    plane = 1 - mine if last else mine
    value = other_ref[...] if last else half_ref[...]
    fetch_slopes.wait()
    spread_into(value, slopes_ref, 1, block, blocks, other, others, pad, scale, spread_ref)
    dims = (((0,), (0,)), ((), ()))
    back = lax.dot_general(spread_ref[...], table_ref[...], dims, preferred_element_type=F32)
    sum_ref[...] = partial_ref[pl.ds(plane, 1)] + back[None]
    store = pltpu.make_async_copy(sum_ref, out_hbm.at[pl.ds(plane, 1)], sems.at[1])
    store.start()
    if last:
        odd = mine == 1
        rows_ref[:views, :] = middle(jnp.where(odd, other_ref[...], half_ref[...]), pad)
        rows_ref[views:, :] = middle(jnp.where(odd, half_ref[...], other_ref[...]), pad)
        for p in range(2):
            for v in range(views):
                rest_ref[v, p : p + 1, :] = rows_ref[p * views + v : p * views + v + 1, :]
    store.wait()


def back_y(slopes, table, partial, half, rest, blocks, others, pad, scale):
    planes, bins, cells = partial.shape
    views = slopes.shape[1]
    last = rest is not None

    def body(*refs):
        back_y_kernel(*refs, last=last, blocks=blocks, others=others, pad=pad, scale=scale, views=views)

    operands = [slopes, in_vmem(table), in_vmem(partial), in_vmem(half)]
    specs = [anywhere(), vmem(), vmem(), vmem()]
    shapes = [jax.ShapeDtypeStruct(partial.shape, F32)]
    out_specs = [anywhere()]
    aliases = {}
    if last:
        other, gradient = rest
        operands += [in_vmem(other), gradient]
        specs += [vmem(), anywhere()]
        shapes.append(jax.ShapeDtypeStruct((views, planes, bins), F32))
        out_specs.append(vmem())
        aliases = {5: 0}
    return pl.pallas_call(
        body,
        out_shape=tuple(shapes),
        in_specs=specs,
        out_specs=tuple(out_specs),
        scratch_shapes=[
            SMEM(slopes.shape, jnp.int32),
            VMEM((1, bins, cells), F32),
            VMEM((LEVELS * views, bins), BF16),
            VMEM((planes * views, bins), F32),
            pltpu.SemaphoreType.DMA((2,)),
        ],
        input_output_aliases=aliases,
        interpret=interpreted(),
        name="back_y_last" if last else "back_y_own",
    )(*operands)


def edges(value, axis, width):
    size = lax.axis_size(axis)
    up = [(i, i + 1) for i in range(size - 1)]
    down = [(i + 1, i) for i in range(size - 1)]
    length = value.shape[1]
    left = lax.ppermute(value[:, length - width :], axis, up)
    right = lax.ppermute(value[:, :width], axis, down)
    return left, right


def meet(value, left, right):
    width = left.shape[1]
    length = value.shape[1]
    return jnp.concatenate(
        [value[:, :width] + left, value[:, width : length - width], value[:, length - width :] + right], axis=1
    )


def swap(value, axis, bit):
    return lax.ppermute(value, axis, [(i, i ^ bit) for i in range(lax.axis_size(axis))])


def steps(volume, view_slopes, measured_x, measured_y):
    _, cells_x, cells_y = volume.shape
    count_x = lax.axis_size("gx")
    count_y = lax.axis_size("gy")
    scale_x = float(cells_x * count_x) ** (-0.5)
    scale_y = float(cells_y * count_y) ** (-0.5)
    pad_x, pad_y = 64, 128

    sum_y, table_y, near = forward(view_slopes, volume, measured_y, 1, "gy", count_y, pad_y, scale_y)
    sides_y = edges(sum_y, "gx", 2 * pad_y)
    beside = lax.ppermute(near, "pa", [(0, 1), (1, 0)])
    (sum_x,) = forward(view_slopes, volume, measured_x, 0, "gx", count_x, pad_x, scale_x)
    sides_x = edges(sum_x, "gy", 2 * pad_x)

    sum_y = meet(sum_y, *sides_y)
    rows = sum_y.shape[0] // 2
    odd = lax.axis_index("gy") % 2
    kept = lax.dynamic_slice_in_dim(sum_y, odd * rows, rows, 0)
    sent = lax.dynamic_slice_in_dim(sum_y, (1 - odd) * rows, rows, 0)
    half = kept + swap(sent, "gy", 1)
    sum_x, half = lax.optimization_barrier((sum_x, half))
    sum_x = meet(sum_x, *sides_x)
    half = half + swap(half, "gy", 2)
    sum_x = sum_x + swap(sum_x, "gx", 1)
    half = half + swap(half, "gy", 4)
    sum_x = sum_x + swap(sum_x, "gx", 2)
    half = half + swap(half, "gy", 8)
    sum_x = sum_x + swap(sum_x, "gx", 4)
    other = swap(half, "gy", 1)

    partial, residual_x = back_x(view_slopes, volume, beside, sum_x, count_x, count_y, pad_x, scale_x)
    (gradient,) = back_y(view_slopes, table_y, partial, half, None, count_y, count_x, pad_y, scale_y)
    gradient, residual_y = back_y(
        view_slopes, table_y, partial, half, (other, gradient), count_y, count_x, pad_y, scale_y
    )
    return (gradient, residual_x, residual_y)


def solution(mesh):
    return jax.shard_map(
        steps,
        mesh=mesh,
        in_specs=(P("pa", "gx", "gy"), P(), P(None, "pa", "gy"), P(None, "pa", "gx")),
        out_specs=(P("pa", "gx", "gy"), P(None, "pa", "gy"), P(None, "pa", "gx")),
        check_vma=False,
    )
```

time: 64.2 us -> 57.3 us (0.89); the launches traced: 63.9 us -> 56.2 us
  waiting for transfers between devices: 10.1 us -> 6.51 us
  starting transfers between devices: 33.7 us -> 31.7 us
  other arithmetic: 1.97 us -> 0.09 us
  local copies, waits for them, and re-layouts: 1.49 us -> 0.02 us
  Pallas kernels: 15.8 us -> 17.1 us
    ppermute x8, waiting for transfers between devices: 8.58 us -> 6.39 us  [swap(): lax.ppermute(value, axis, [(i, i ^ bit) for i in range(lax.axis_size(axis...]
    ppermute x5, starting transfers between devices: 11.4 us -> 9.48 us  [the longest x2 4.93 us: edges(): right = lax.ppermute(value[:, :width], axis, down)]
    ppermute x5, waiting for transfers between devices: 1.52 us -> 0.12 us  [the longest x2 0.11 us: edges(): right = lax.ppermute(value[:, :width], axis, down)]
    pallas_call x4 -> x5, Pallas kernels: 15.8 us -> 17.1 us  [the longest x2 7.37 us: back_y(): pl.pallas_call(body, out_shape=tuple(shapes), in_specs=specs, out_specs=t...]
    slice x2, local copies, waits for them, and re-layouts: 0.74 us -> 0.01 us  [edges(): left = lax.ppermute(value[:, length - width:], axis, up)]
    unnamed x8 -> x0, local copies, waits for them, and re-layouts: 0.72 us -> none
    select_n x1 -> x0, other arithmetic: 0.65 us -> none  [on_device(): jnp.where(odd == 0, jnp.concatenate([half, rest]), jnp.concatenate([rest,...]
  transfers between devices with their start and end apart: 13 -> 13, of which waited for: 6 -> 4; matrix products, arithmetic and copies ran while one was open for 2% -> 0% of each run, Pallas kernels for 6% -> 18%
where the time goes in v2:
time: 57.3 us; the launch traced here: 56.2 us
  starting transfers between devices  31.7 us (55%)
  Pallas kernels  17.1 us (30%)
  waiting for transfers between devices  6.51 us (11%)
  between operations  0.85 us (1%)
    ppermute x8, starting transfers between devices, swap(): lax.ppermute(value, axis, [(i, i ^ bit) for i in range(lax.axis_size(axis...  22.2 us
    pallas_call x2, Pallas kernels, back_y(): pl.pallas_call(body, out_shape=tuple(shapes), in_specs=specs, out_specs=t...  7.37 us
    ppermute x8, waiting for transfers between devices, swap(): lax.ppermute(value, axis, [(i, i ^ bit) for i in range(lax.axis_size(axis...  6.39 us
    pallas_call x2, Pallas kernels, forward(): pl.pallas_call(body, out_shape=tuple(outs), in_specs=[anywhere(), anywher...  6.11 us
    ppermute x2, starting transfers between devices, edges(): right = lax.ppermute(value[:, :width], axis, down)  4.93 us
    ppermute x2, starting transfers between devices, edges(): left = lax.ppermute(value[:, length - width:], axis, up)  3.92 us
    pallas_call x1, Pallas kernels, back_x(): pl.pallas_call(body, out_shape=(out_vmem(volume.shape, F32), jax.ShapeDty...  3.6 us
  transfers between devices with their start and end apart: 13, of which 4 were waited for; matrix products, arithmetic and copies ran while one was open for 0% of the time, Pallas kernels for 18%

profile of v2, /device:TPU:10, one launch (start us, length us, event | category | flops | bytes accessed | tf_op | source)
XLA Modules:
  0.0 56.2 jit_solution(13297456383695460451)
XLA Ops:
  0.6 3.1 %shard_map.67 = (f32[32,768]{1,0:T(8,128)S(1)}, bf16[256,256]{1,0:T(8,128)(2,1)S(1)}, bf16[1,512,256]{2,1,0:T(8,128)(2,1)S(1)}) custom-call(s32[2,16]{1,0:T(2,128)} %refs_0_.9, bf16[2,512,256]{2,1,0:T(8,128)(2,1)} %refs_1_.5, f32[16,2,512]{2,1,0:T(2,128)} %refs_2_.2), custom_call_target="tpu_custom_call" | custom-call | tf_op jit(solution)/shard_map/pallas_call | solution.py:145
  3.8 1.9 %collective-permute-start.1 = (f32[32,256]{1,0:T(8,128)S(1)}, f32[32,256]{1,0:T(8,128)S(1)}, u32[]{:S(2)}, u32[]{:S(2)}) collective-permute-start(f32[32,256]{1,0:T(8,128)S(1)} %get-tuple-element.24), channel_id=1, source_target_pairs={{0,32},{32,64},{64,96},{96,128},{128,160},{160,192},{192,224},{1,3... | collective-permute-start | bytes 98312 | tf_op jit(solution)/shard_map/ppermute | solution.py:304
  5.7 3.6 %collective-permute-start.2 = (f32[32,256]{1,0:T(8,128)S(1)}, f32[32,256]{1,0:T(8,128)S(1)}, u32[]{:S(2)}, u32[]{:S(2)}) collective-permute-start(f32[32,256]{1,0:T(8,128)S(1)} %get-tuple-element.25), channel_id=1, source_target_pairs={{32,0},{64,32},{96,64},{128,96},{160,128},{192,160},{224,192},{33,... | collective-permute-start | bytes 98312 | tf_op jit(solution)/shard_map/ppermute | solution.py:305
  9.4 3.0 %shard_map.68 = f32[32,384]{1,0:T(8,128)S(1)} custom-call(s32[2,16]{1,0:T(2,128)} %refs_0_.9, bf16[2,512,256]{2,1,0:T(8,128)(2,1)} %refs_1_.5, f32[16,2,256]{2,1,0:T(2,128)} %refs_2_.3), custom_call_target="tpu_custom_call" | custom-call | tf_op jit(solution)/shard_map/pallas_call | solution.py:145
  12.4 0.0 collective-permute-done.1
  12.4 0.0 collective-permute-done.2
  12.4 2.0 %collective-permute-start.3 = (f32[16,768]{1,0:T(8,128)S(1)}, f32[16,768]{1,0:T(8,128)S(1)}, u32[]{:S(2)}, u32[]{:S(2)}) collective-permute-start(f32[16,768]{1,0:T(8,128)S(1)} %constant_dynamic-slice_fusion), channel_id=1, source_target_pairs={{0,2},{2,0},{4,6},{6,4},{8,10},{10,8},{12,14},{14,12},{16,18},{18,... | collective-permute-start | bytes 147464 | tf_op jit(solution)/shard_map/ppermute | solution.py:318
  14.5 2.0 %collective-permute-start.4 = (f32[32,128]{1,0:T(8,128)S(1)}, f32[32,128]{1,0:T(8,128)S(1)}, u32[]{:S(2)}, u32[]{:S(2)}) collective-permute-start(f32[32,128]{1,0:T(8,128)S(1)} %get-tuple-element.29), channel_id=1, source_target_pairs={{0,2},{2,4},{4,6},{6,8},{8,10},{10,12},{12,14},{14,16},{16,18},{18... | collective-permute-start | bytes 49160 | tf_op jit(solution)/shard_map/ppermute | solution.py:304
  16.5 1.3 %collective-permute-start.5 = (f32[32,128]{1,0:T(8,128)S(1)}, f32[32,128]{1,0:T(8,128)S(1)}, u32[]{:S(2)}, u32[]{:S(2)}) collective-permute-start(f32[32,128]{1,0:T(8,128)S(1)} %get-tuple-element.30), channel_id=1, source_target_pairs={{2,0},{4,2},{6,4},{8,6},{10,8},{12,10},{14,12},{16,14},{18,16},{20... | collective-permute-start | bytes 49160 | tf_op jit(solution)/shard_map/ppermute | solution.py:305
  17.8 0.0 collective-permute-done.3
  17.8 5.9 %collective-permute-start.9 = (f32[16,768]{1,0:T(8,128)S(1)}, f32[16,768]{1,0:T(8,128)S(1)}, u32[]{:S(2)}, u32[]{:S(2)}) collective-permute-start(f32[16,768]{1,0:T(8,128)S(1)} %dynamic-slice_add_fusion), channel_id=1, source_target_pairs={{0,4},{2,6},{4,0},{6,2},{8,12},{10,14},{12,8},{14,10},{16,20},{18,... | collective-permute-start | bytes 147464 | tf_op jit(solution)/shard_map/ppermute | solution.py:318
  23.7 0.0 collective-permute-done.4
  23.7 0.1 collective-permute-done.5
  23.8 0.1 collective-permute-start.6
  23.9 0.6 %collective-permute-start = (bf16[1,512,256]{2,1,0:T(8,128)(2,1)S(1)}, bf16[1,512,256]{2,1,0:T(8,128)(2,1)S(1)}, u32[]{:S(2)}, u32[]{:S(2)}) collective-permute-start(bf16[1,512,256]{2,1,0:T(8,128)(2,1)S(1)} %get-tuple-element.13), channel_id=1, source_target_pairs={{0,1},{1,0},{2,3},{3,2},{4,5},{5,4},{6,7},{7,6},{8,9},{9,8},{10,11... | collective-permute-start | bytes 786440 | tf_op jit(solution)/shard_map/ppermute | solution.py:331
  24.6 1.2 %collective-permute-done.9 = f32[16,768]{1,0:T(8,128)S(1)} collective-permute-done((f32[16,768]{1,0:T(8,128)S(1)}, f32[16,768]{1,0:T(8,128)S(1)}, u32[]{:S(2)}, u32[]{:S(2)}) %collective-permute-start.9) | collective-permute-done | bytes 49184 | tf_op jit(solution)/shard_map/ppermute | solution.py:318
  25.8 7.2 %collective-permute-start.10 = (f32[16,768]{1,0:T(8,128)S(1)}, f32[16,768]{1,0:T(8,128)S(1)}, u32[]{:S(2)}, u32[]{:S(2)}) collective-permute-start(f32[16,768]{1,0:T(8,128)S(1)} %add.54), channel_id=1, source_target_pairs={{0,8},{2,10},{4,12},{6,14},{8,0},{10,2},{12,4},{14,6},{16,24},{18,... | collective-permute-start | bytes 147464 | tf_op jit(solution)/shard_map/ppermute | solution.py:318
  33.0 0.0 collective-permute-done.6
  33.0 0.1 collective-permute-start.7
  33.1 2.0 %collective-permute-done.10 = f32[16,768]{1,0:T(8,128)S(1)} collective-permute-done((f32[16,768]{1,0:T(8,128)S(1)}, f32[16,768]{1,0:T(8,128)S(1)}, u32[]{:S(2)}, u32[]{:S(2)}) %collective-permute-start.10) | collective-permute-done | bytes 49184 | tf_op jit(solution)/shard_map/ppermute | solution.py:318
  35.1 4.4 %collective-permute-start.11 = (f32[16,768]{1,0:T(8,128)S(1)}, f32[16,768]{1,0:T(8,128)S(1)}, u32[]{:S(2)}, u32[]{:S(2)}) collective-permute-start(f32[16,768]{1,0:T(8,128)S(1)} %add.55), channel_id=1, source_target_pairs={{0,16},{2,18},{4,20},{6,22},{8,24},{10,26},{12,28},{14,30},{16,0},... | collective-permute-start | bytes 147464 | tf_op jit(solution)/shard_map/ppermute | solution.py:318
  39.5 0.0 collective-permute-done.7
  39.5 2.4 %collective-permute-start.8 = (f32[32,384]{1,0:T(8,128)S(1)}, f32[32,384]{1,0:T(8,128)S(1)}, u32[]{:S(2)}, u32[]{:S(2)}) collective-permute-start(f32[32,384]{1,0:T(8,128)S(1)} %add.52), channel_id=1, source_target_pairs={{0,128},{32,160},{64,192},{96,224},{128,0},{160,32},{192,64},{224,... | collective-permute-start | bytes 147464 | tf_op jit(solution)/shard_map/ppermute | solution.py:318
  41.9 0.0 collective-permute-done.11
  41.9 0.1 collective-permute-start.12
  42.0 3.2 %collective-permute-done.8 = f32[32,384]{1,0:T(8,128)S(1)} collective-permute-done((f32[32,384]{1,0:T(8,128)S(1)}, f32[32,384]{1,0:T(8,128)S(1)}, u32[]{:S(2)}, u32[]{:S(2)}) %collective-permute-start.8) | collective-permute-done | bytes 49184 | tf_op jit(solution)/shard_map/ppermute | solution.py:318
  45.2 0.0 collective-permute-done.refs_2_
  45.2 3.6 %back_x.1 = (f32[2,512,256]{2,1,0:T(8,128)S(1)}, f32[16,2,256]{2,1,0:T(2,128)}) custom-call(s32[2,16]{1,0:T(2,128)} %refs_0_.9, bf16[2,512,256]{2,1,0:T(8,128)(2,1)} %refs_1_.5, bf16[1,512,256]{2,1,0:T(8,128)(2,1)S(1)} %collective-permute-done.refs_2_, f32[32,384]{1,0:T(8,128)S(1)} %add.53.refs_3_), custom_call_target="tpu_custom_call" | custom-call | tf_op jit(solution)/shard_map/back_x/pallas_call | solution.py:212
  48.8 3.4 %back_y_own.1.refs_5_ = f32[2,512,256]{2,1,0:T(8,128)} custom-call(s32[2,16]{1,0:T(2,128)} %refs_0_.9, bf16[256,256]{1,0:T(8,128)(2,1)S(1)} %get-tuple-element.12.refs_1_, f32[2,512,256]{2,1,0:T(8,128)S(1)} %get-tuple-element.16.refs_2_, f32[16,768]{1,0:T(8,128)S(1)} %add.56.refs_3_), custom_call_target="tpu_custom_call" | custom-call | tf_op jit(solution)/shard_map/back_y_own/pallas_call | solution.py:281
  52.2 0.0 collective-permute-done.12.refs_4_
  52.2 4.0 %back_y_last.1 = (f32[2,512,256]{2,1,0:T(8,128)}, f32[16,2,512]{2,1,0:T(2,128)}) custom-call(s32[2,16]{1,0:T(2,128)} %refs_0_.9, bf16[256,256]{1,0:T(8,128)(2,1)S(1)} %get-tuple-element.12.refs_1_, f32[2,512,256]{2,1,0:T(8,128)S(1)} %get-tuple-element.16.refs_2_, f32[16,768]{1,0:T(8,128)S(1)} %add.56.refs_3_, ...), custom_call_target="tpu_custom_call", output_to_operand_aliasing={{0}: (5, {})} | custom-call | tf_op jit(solution)/shard_map/back_y_last/pallas_call | solution.py:281
  (14 shorter events, 0.1 us)
Async XLA Ops:
  3.8 8.6 %collective-permute-start.1 = (f32[32,256]{1,0:T(8,128)S(1)}, f32[32,256]{1,0:T(8,128)S(1)}, u32[]{:S(2)}, u32[]{:S(2)}) collective-permute-start(f32[32,256]{1,0:T(8,128)S(1)} %get-tuple-element.24), channel_id=1, source_target_pairs={{0,32},{32,64},{64,96},{96,128},{128,160},{160,192},{192,224},{1,3... | collective-permute-start | bytes 98312 | tf_op jit(solution)/shard_map/ppermute | solution.py:304
  5.7 6.7 %collective-permute-start.2 = (f32[32,256]{1,0:T(8,128)S(1)}, f32[32,256]{1,0:T(8,128)S(1)}, u32[]{:S(2)}, u32[]{:S(2)}) collective-permute-start(f32[32,256]{1,0:T(8,128)S(1)} %get-tuple-element.25), channel_id=1, source_target_pairs={{32,0},{64,32},{96,64},{128,96},{160,128},{192,160},{224,192},{33,... | collective-permute-start | bytes 98312 | tf_op jit(solution)/shard_map/ppermute | solution.py:305
  12.4 5.3 %collective-permute-start.3 = (f32[16,768]{1,0:T(8,128)S(1)}, f32[16,768]{1,0:T(8,128)S(1)}, u32[]{:S(2)}, u32[]{:S(2)}) collective-permute-start(f32[16,768]{1,0:T(8,128)S(1)} %constant_dynamic-slice_fusion), channel_id=1, source_target_pairs={{0,2},{2,0},{4,6},{6,4},{8,10},{10,8},{12,14},{14,12},{16,18},{18,... | collective-permute-start | bytes 147464 | tf_op jit(solution)/shard_map/ppermute | solution.py:318
  14.5 9.2 %collective-permute-start.4 = (f32[32,128]{1,0:T(8,128)S(1)}, f32[32,128]{1,0:T(8,128)S(1)}, u32[]{:S(2)}, u32[]{:S(2)}) collective-permute-start(f32[32,128]{1,0:T(8,128)S(1)} %get-tuple-element.29), channel_id=1, source_target_pairs={{0,2},{2,4},{4,6},{6,8},{8,10},{10,12},{12,14},{14,16},{16,18},{18... | collective-permute-start | bytes 49160 | tf_op jit(solution)/shard_map/ppermute | solution.py:304
  16.5 7.3 %collective-permute-start.5 = (f32[32,128]{1,0:T(8,128)S(1)}, f32[32,128]{1,0:T(8,128)S(1)}, u32[]{:S(2)}, u32[]{:S(2)}) collective-permute-start(f32[32,128]{1,0:T(8,128)S(1)} %get-tuple-element.30), channel_id=1, source_target_pairs={{2,0},{4,2},{6,4},{8,6},{10,8},{12,10},{14,12},{16,14},{18,16},{20... | collective-permute-start | bytes 49160 | tf_op jit(solution)/shard_map/ppermute | solution.py:305
  17.8 8.0 %collective-permute-start.9 = (f32[16,768]{1,0:T(8,128)S(1)}, f32[16,768]{1,0:T(8,128)S(1)}, u32[]{:S(2)}, u32[]{:S(2)}) collective-permute-start(f32[16,768]{1,0:T(8,128)S(1)} %dynamic-slice_add_fusion), channel_id=1, source_target_pairs={{0,4},{2,6},{4,0},{6,2},{8,12},{10,14},{12,8},{14,10},{16,20},{18,... | collective-permute-start | bytes 147464 | tf_op jit(solution)/shard_map/ppermute | solution.py:318
  23.8 9.2 %collective-permute-start.6 = (f32[32,384]{1,0:T(8,128)S(1)}, f32[32,384]{1,0:T(8,128)S(1)}, u32[]{:S(2)}, u32[]{:S(2)}) collective-permute-start(f32[32,384]{1,0:T(8,128)S(1)} %pad_maximum_fusion.1), channel_id=1, source_target_pairs={{0,32},{32,0},{64,96},{96,64},{128,160},{160,128},{192,224},{224,1... | collective-permute-start | bytes 147464 | tf_op jit(solution)/shard_map/ppermute | solution.py:318
  23.9 21.3 %collective-permute-start = (bf16[1,512,256]{2,1,0:T(8,128)(2,1)S(1)}, bf16[1,512,256]{2,1,0:T(8,128)(2,1)S(1)}, u32[]{:S(2)}, u32[]{:S(2)}) collective-permute-start(bf16[1,512,256]{2,1,0:T(8,128)(2,1)S(1)} %get-tuple-element.13), channel_id=1, source_target_pairs={{0,1},{1,0},{2,3},{3,2},{4,5},{5,4},{6,7},{7,6},{8,9},{9,8},{10,11... | collective-permute-start | bytes 786440 | tf_op jit(solution)/shard_map/ppermute | solution.py:331
  25.8 9.3 %collective-permute-start.10 = (f32[16,768]{1,0:T(8,128)S(1)}, f32[16,768]{1,0:T(8,128)S(1)}, u32[]{:S(2)}, u32[]{:S(2)}) collective-permute-start(f32[16,768]{1,0:T(8,128)S(1)} %add.54), channel_id=1, source_target_pairs={{0,8},{2,10},{4,12},{6,14},{8,0},{10,2},{12,4},{14,6},{16,24},{18,... | collective-permute-start | bytes 147464 | tf_op jit(solution)/shard_map/ppermute | solution.py:318
  33.0 6.5 %collective-permute-start.7 = (f32[32,384]{1,0:T(8,128)S(1)}, f32[32,384]{1,0:T(8,128)S(1)}, u32[]{:S(2)}, u32[]{:S(2)}) collective-permute-start(f32[32,384]{1,0:T(8,128)S(1)} %fusion), channel_id=1, source_target_pairs={{0,64},{32,96},{64,0},{96,32},{128,192},{160,224},{192,128},{224,1... | collective-permute-start | bytes 147464 | tf_op jit(solution)/shard_map/ppermute | solution.py:318
  35.1 6.8 %collective-permute-start.11 = (f32[16,768]{1,0:T(8,128)S(1)}, f32[16,768]{1,0:T(8,128)S(1)}, u32[]{:S(2)}, u32[]{:S(2)}) collective-permute-start(f32[16,768]{1,0:T(8,128)S(1)} %add.55), channel_id=1, source_target_pairs={{0,16},{2,18},{4,20},{6,22},{8,24},{10,26},{12,28},{14,30},{16,0},... | collective-permute-start | bytes 147464 | tf_op jit(solution)/shard_map/ppermute | solution.py:318
  39.5 5.7 %collective-permute-start.8 = (f32[32,384]{1,0:T(8,128)S(1)}, f32[32,384]{1,0:T(8,128)S(1)}, u32[]{:S(2)}, u32[]{:S(2)}) collective-permute-start(f32[32,384]{1,0:T(8,128)S(1)} %add.52), channel_id=1, source_target_pairs={{0,128},{32,160},{64,192},{96,224},{128,0},{160,32},{192,64},{224,... | collective-permute-start | bytes 147464 | tf_op jit(solution)/shard_map/ppermute | solution.py:318
  41.9 10.3 %collective-permute-start.12 = (f32[16,768]{1,0:T(8,128)S(1)}, f32[16,768]{1,0:T(8,128)S(1)}, u32[]{:S(2)}, u32[]{:S(2)}) collective-permute-start(f32[16,768]{1,0:T(8,128)S(1)} %add.56.refs_3_), channel_id=1, source_target_pairs={{0,2},{2,0},{4,6},{6,4},{8,10},{10,8},{12,14},{14,12},{16,18},{18,... | collective-permute-start | bytes 147464 | tf_op jit(solution)/shard_map/ppermute | solution.py:318

commit v3 on v2

--- a/solution.py
+++ b/solution.py
@@ -69,43 +69,32 @@
     return pl.BlockSpec(memory_space=VMEM)
 
 
-def forward_kernel(*refs, family, axis, blocks, pad, scale, views):
-    slopes_hbm, volume_hbm, measured_hbm, out_ref = refs[:4]
-    rest = list(refs[4:])
-    if family == 1:
-        table_ref, near_ref = rest.pop(0), rest.pop(0)
-    else:
-        table_ref = rest.pop(0)
-    slopes_ref, volume_ref, measured_ref, rows_ref, sems = rest
+def in_roles(value, odd):
+    edge = value.shape[1] // 3
+    lead, mid, trail = value[:, :edge], value[:, edge : 2 * edge], value[:, 2 * edge :]
+    return jnp.concatenate([jnp.where(odd, lead, trail), mid, jnp.where(odd, trail, lead)], axis=1)
+
+
+def from_roles(value, odd):
+    edge = value.shape[1] // 3
+    a, mid, b = value[:, :edge], value[:, edge : 2 * edge], value[:, 2 * edge :]
+    return jnp.concatenate([jnp.where(odd, a, b), mid, jnp.where(odd, b, a)], axis=1)
+
+
+def on_grid(value):
+    return jnp.round(value * 32768.0) * (1.0 / 32768.0)
+
+
+def project(table_ref, volume_ref, rows_ref, slopes_ref, out_ref, family, block, blocks, odd, pad, scale):
     planes = volume_ref.shape[0]
+    views = slopes_ref.shape[1]
     bins = volume_ref.shape[2 - family]
-    cells = volume_ref.shape[1 + family]
     width = out_ref.shape[1]
-    fetch_slopes = pltpu.make_async_copy(slopes_hbm, slopes_ref, sems.at[0])
-    fetch_volume = pltpu.make_async_copy(volume_hbm, volume_ref, sems.at[1])
-    fetch_measured = pltpu.make_async_copy(measured_hbm, measured_ref, sems.at[2])
-    fetch_slopes.start()
-    fetch_volume.start()
-    fetch_measured.start()
-    if family == 1:
-        far = 1 - lax.axis_index("pa")
-        fetch_near = pltpu.make_async_copy(volume_hbm.at[pl.ds(far, 1)], near_ref, sems.at[3])
-        fetch_near.start()
-    block = lax.axis_index(axis)
     first = (block == 0).astype(F32)
-    fetch_slopes.wait()
-    offset = offsets(slopes_ref, family, block, blocks, cells)
-    for level in range(LEVELS):
-        table_ref[level * views : (level + 1) * views, :] = hat(offset, float(level)).astype(BF16)
     slopes = fill(slopes_ref, family, (views, width), 0)
     amounts = pad - lowest_shift(slopes, block, blocks)
     bits = max(1, (2 * pad).bit_length() - 1)
     empty = jnp.zeros((views, width - bins), F32)
-    fetch_measured.wait()
-    for plane in range(planes):
-        for v in range(views):
-            rows_ref[plane * views + v : plane * views + v + 1, :] = measured_ref[v, plane : plane + 1, :]
-    fetch_volume.wait()
     for plane in range(planes):
         dims = (((1,), (family,)), ((), ()))
         summands = lax.dot_general(table_ref[...], volume_ref[plane], dims, preferred_element_type=F32)
@@ -115,41 +104,89 @@
             total = piece if total is None else pltpu.roll(total, width - 1, 1) + piece
         total = barrel(total, amounts, bits) * scale
         known = jnp.concatenate([rows_ref[plane * views : (plane + 1) * views, :] * first, empty], axis=1)
-        out_ref[plane * views : (plane + 1) * views, :] = total - pltpu.roll(known, pad, 1)
-    if family == 1:
-        fetch_near.wait()
-
-
-def forward(slopes, volume, measured, family, axis, blocks, pad, scale):
-    views, planes, bins = measured.shape
-    width = bins + 2 * pad
-    cells = volume.shape[1 + family]
+        total = on_grid(total - pltpu.roll(known, pad, 1))
+        out_ref[plane * views : (plane + 1) * views, :] = in_roles(total, odd)
+
+
+def build_table(slopes_ref, family, block, blocks, cells, table_ref):
+    views = slopes_ref.shape[1]
+    offset = offsets(slopes_ref, family, block, blocks, cells)
+    for level in range(LEVELS):
+        table_ref[level * views : (level + 1) * views, :] = hat(offset, float(level)).astype(BF16)
+
+
+def gather_rows(measured_ref, rows_ref):
+    views, planes, _ = measured_ref.shape
+    for plane in range(planes):
+        for v in range(views):
+            rows_ref[plane * views + v : plane * views + v + 1, :] = measured_ref[v, plane : plane + 1, :]
+
+
+def forward_kernel(
+    slopes_hbm, volume_hbm, mx_hbm, my_hbm, x_ref, y_ref, table_y_ref, near_ref,
+    table_x_ref, slopes_ref, volume_ref, mx_ref, my_ref, rows_x_ref, rows_y_ref, sems,
+    *, count_x, count_y, pad_x, pad_y, scale_x, scale_y,
+):
+    _, cells_x, cells_y = volume_ref.shape
+    fetches = [
+        pltpu.make_async_copy(slopes_hbm, slopes_ref, sems.at[0]),
+        pltpu.make_async_copy(volume_hbm, volume_ref, sems.at[1]),
+        pltpu.make_async_copy(mx_hbm, mx_ref, sems.at[2]),
+        pltpu.make_async_copy(my_hbm, my_ref, sems.at[3]),
+        pltpu.make_async_copy(volume_hbm.at[pl.ds(1 - lax.axis_index("pa"), 1)], near_ref, sems.at[4]),
+    ]
+    for fetch in fetches:
+        fetch.start()
+    here_x, here_y = lax.axis_index("gx"), lax.axis_index("gy")
+    fetches[0].wait()
+    build_table(slopes_ref, 1, here_y, count_y, cells_y, table_y_ref)
+    build_table(slopes_ref, 0, here_x, count_x, cells_x, table_x_ref)
+    fetches[2].wait()
+    fetches[3].wait()
+    gather_rows(mx_ref, rows_x_ref)
+    gather_rows(my_ref, rows_y_ref)
+    fetches[1].wait()
+    project(table_y_ref, volume_ref, rows_y_ref, slopes_ref, y_ref, 1, here_y, count_y, here_x % 2 == 1, pad_y, scale_y)
+    project(table_x_ref, volume_ref, rows_x_ref, slopes_ref, x_ref, 0, here_x, count_x, here_y % 2 == 1, pad_x, scale_x)
+    fetches[4].wait()
+
+
+def forward(slopes, volume, measured_x, measured_y, count_x, count_y, pad_x, pad_y, scale_x, scale_y):
+    views = slopes.shape[1]
+    planes, cells_x, cells_y = volume.shape
 
     def body(*refs):
-        forward_kernel(*refs, family=family, axis=axis, blocks=blocks, pad=pad, scale=scale, views=views)
-
-    outs = [out_vmem((planes * views, width), F32)]
-    scratch = []
-    if family == 1:
-        outs.append(out_vmem((LEVELS * views, cells), BF16))
-        outs.append(out_vmem((1,) + volume.shape[1:], BF16))
-    else:
-        scratch.append(VMEM((LEVELS * views, cells), BF16))
-    scratch += [
-        SMEM(slopes.shape, jnp.int32),
-        VMEM(volume.shape, BF16),
-        VMEM(measured.shape, F32),
-        VMEM((planes * views, bins), F32),
-        pltpu.SemaphoreType.DMA((4,)),
-    ]
+        forward_kernel(
+            *refs, count_x=count_x, count_y=count_y, pad_x=pad_x, pad_y=pad_y, scale_x=scale_x, scale_y=scale_y
+        )
+
     return pl.pallas_call(
         body,
-        out_shape=tuple(outs),
-        in_specs=[anywhere(), anywhere(), anywhere()],
-        out_specs=tuple(vmem() for _ in outs),
-        scratch_shapes=scratch,
+        out_shape=(
+            out_vmem((planes * views, cells_y + 2 * pad_x), F32),
+            out_vmem((planes * views, cells_x + 2 * pad_y), F32),
+            out_vmem((LEVELS * views, cells_y), BF16),
+            out_vmem((1,) + volume.shape[1:], BF16),
+        ),
+        in_specs=[anywhere()] * 4,
+        out_specs=(vmem(),) * 4,
+        scratch_shapes=[
+            VMEM((LEVELS * views, cells_x), BF16),
+            SMEM(slopes.shape, jnp.int32),
+            VMEM(volume.shape, BF16),
+            VMEM(measured_x.shape, F32),
+            VMEM(measured_y.shape, F32),
+            VMEM((planes * views, cells_y), F32),
+            VMEM((planes * views, cells_x), F32),
+            pltpu.SemaphoreType.DMA((5,)),
+        ],
         interpret=interpreted(),
-    )(slopes, volume, measured)
+        name="forward",
+    )(slopes, volume, measured_x, measured_y)
+
+
+def half_of(index):
+    return ((index + 1) // 2) % 2
 
 
 def spread_into(value, slopes_ref, family, block, blocks, other, others, pad, scale, spread_ref):
@@ -189,7 +226,7 @@
     table_ref[...] = jnp.maximum(1.0 - jnp.abs(cell * slopes - base), 0.0).astype(BF16)
     fetch_volume.wait()
     for plane in range(planes):
-        residual = residual_ref[plane * views : (plane + 1) * views, :]
+        residual = from_roles(residual_ref[plane * views : (plane + 1) * views, :], other % 2 == 1)
         spread_into(residual, slopes_ref, 0, block, blocks, other, others, pad, scale, spread_ref)
         value = jnp.dot(table_ref[...], spread_ref[...], preferred_element_type=F32)
         here = volume_ref[plane].astype(F32)
@@ -238,9 +275,10 @@
     fetch_slopes = pltpu.make_async_copy(slopes_hbm, slopes_ref, sems.at[0])
     fetch_slopes.start()
     block, other = lax.axis_index("gy"), lax.axis_index("gx")
-    mine = lax.axis_index("gy") % 2
+    mine = half_of(lax.axis_index("gy"))
+    flip = other % 2 == 1
     plane = 1 - mine if last else mine
-    value = other_ref[...] if last else half_ref[...]
+    value = from_roles(other_ref[...] if last else half_ref[...], flip)
     fetch_slopes.wait()
     spread_into(value, slopes_ref, 1, block, blocks, other, others, pad, scale, spread_ref)
     dims = (((0,), (0,)), ((), ()))
@@ -250,8 +288,8 @@
     store.start()
     if last:
         odd = mine == 1
-        rows_ref[:views, :] = middle(jnp.where(odd, other_ref[...], half_ref[...]), pad)
-        rows_ref[views:, :] = middle(jnp.where(odd, half_ref[...], other_ref[...]), pad)
+        rows_ref[:views, :] = middle(from_roles(jnp.where(odd, other_ref[...], half_ref[...]), flip), pad)
+        rows_ref[views:, :] = middle(from_roles(jnp.where(odd, half_ref[...], other_ref[...]), flip), pad)
         for p in range(2):
             for v in range(views):
                 rest_ref[v, p : p + 1, :] = rows_ref[p * views + v : p * views + v + 1, :]
@@ -296,26 +334,18 @@
     )(*operands)
 
 
-def edges(value, axis, width):
-    size = lax.axis_size(axis)
-    up = [(i, i + 1) for i in range(size - 1)]
-    down = [(i + 1, i) for i in range(size - 1)]
-    length = value.shape[1]
-    left = lax.ppermute(value[:, length - width :], axis, up)
-    right = lax.ppermute(value[:, :width], axis, down)
-    return left, right
-
-
-def meet(value, left, right):
-    width = left.shape[1]
-    length = value.shape[1]
-    return jnp.concatenate(
-        [value[:, :width] + left, value[:, width : length - width], value[:, length - width :] + right], axis=1
-    )
-
-
 def swap(value, axis, bit):
     return lax.ppermute(value, axis, [(i, i ^ bit) for i in range(lax.axis_size(axis))])
+
+
+def swap_odd(value, axis):
+    size = lax.axis_size(axis)
+    return lax.ppermute(value, axis, [(i, (i + (1 if i % 2 else -1)) % size) for i in range(size)])
+
+
+def inner(axis):
+    index = lax.axis_index(axis)
+    return ((index > 0) & (index < lax.axis_size(axis) - 1)).astype(F32)
 
 
 def steps(volume, view_slopes, measured_x, measured_y):
@@ -326,26 +356,38 @@
     scale_y = float(cells_y * count_y) ** (-0.5)
     pad_x, pad_y = 64, 128
 
-    sum_y, table_y, near = forward(view_slopes, volume, measured_y, 1, "gy", count_y, pad_y, scale_y)
-    sides_y = edges(sum_y, "gx", 2 * pad_y)
+    sum_x, sum_y, table_y, near = forward(
+        view_slopes, volume, measured_x, measured_y, count_x, count_y, pad_x, pad_y, scale_x, scale_y
+    )
+    wide = sum_x.shape[1]
+    edge_x, edge_y = wide // 3, sum_y.shape[1] // 3
+    y_a, y_mid, y_b = sum_y[:, :edge_y], sum_y[:, edge_y : 2 * edge_y], sum_y[:, 2 * edge_y :]
+
+    got = swap(jnp.concatenate([sum_x, y_a], axis=1), "gx", 1)
+    sum_x, y_a = sum_x + got[:, :wide], y_a + got[:, wide:]
+    got = swap_odd(jnp.concatenate([sum_x, y_b], axis=1), "gx")
+    sum_x, y_b = sum_x + got[:, :wide], y_b + got[:, wide:] * inner("gx")
+    sum_y = jnp.concatenate([y_a, y_mid, y_b], axis=1)
+    x_a, x_mid, x_b = sum_x[:, :edge_x], sum_x[:, edge_x : 2 * edge_x], sum_x[:, 2 * edge_x :]
+
+    rows = sum_y.shape[0] // 2
+    long = sum_y.shape[1]
+    owns = half_of(lax.axis_index("gy")) == 0
+    kept = jnp.where(owns, sum_y[:rows], sum_y[rows:])
+    sent = jnp.where(owns, sum_y[rows:], sum_y[:rows])
+    got = swap(jnp.concatenate([sent, x_a[:rows], x_a[rows:]], axis=1), "gy", 1)
+    half = kept + got[:, :long]
+    x_a = x_a + jnp.concatenate([got[:, long : long + edge_x], got[:, long + edge_x :]], axis=0)
+    got = swap_odd(jnp.concatenate([half, x_b[:rows], x_b[rows:]], axis=1), "gy")
+    half = half + got[:, :long]
+    got = jnp.concatenate([got[:, long : long + edge_x], got[:, long + edge_x :]], axis=0)
+    x_b = x_b + got * inner("gy")
+    sum_x = jnp.concatenate([x_a, x_mid, x_b], axis=1)
+
+    half = half + swap(half, "gy", 4)
+    sum_x = sum_x + swap(sum_x, "gx", 4)
     beside = lax.ppermute(near, "pa", [(0, 1), (1, 0)])
-    (sum_x,) = forward(view_slopes, volume, measured_x, 0, "gx", count_x, pad_x, scale_x)
-    sides_x = edges(sum_x, "gy", 2 * pad_x)
-
-    sum_y = meet(sum_y, *sides_y)
-    rows = sum_y.shape[0] // 2
-    odd = lax.axis_index("gy") % 2
-    kept = lax.dynamic_slice_in_dim(sum_y, odd * rows, rows, 0)
-    sent = lax.dynamic_slice_in_dim(sum_y, (1 - odd) * rows, rows, 0)
-    half = kept + swap(sent, "gy", 1)
-    sum_x, half = lax.optimization_barrier((sum_x, half))
-    sum_x = meet(sum_x, *sides_x)
-    half = half + swap(half, "gy", 2)
-    sum_x = sum_x + swap(sum_x, "gx", 1)
-    half = half + swap(half, "gy", 4)
-    sum_x = sum_x + swap(sum_x, "gx", 2)
     half = half + swap(half, "gy", 8)
-    sum_x = sum_x + swap(sum_x, "gx", 4)
     other = swap(half, "gy", 1)
 
     partial, residual_x = back_x(view_slopes, volume, beside, sum_x, count_x, count_y, pad_x, scale_x)

time: 57.3 us -> 54.4 us (0.949)
  waiting for transfers between devices: 6.51 us -> 20.7 us
  starting transfers between devices: 31.7 us -> 17.7 us
  Pallas kernels: 17.1 us -> 14.3 us
    ppermute x8 -> x6, starting transfers between devices: 22.2 us -> 9.06 us  [swap(): lax.ppermute(value, axis, [(i, i ^ bit) for i in range(lax.axis_size(axis...]
    ppermute x4 -> x2, waiting for transfers between devices: 0.12 us -> 5.9 us  [swap_odd(): lax.ppermute(value, axis, [(i, (i + (1 if i % 2 else -1)) % size) for i i...]
    ppermute x8 -> x6, waiting for transfers between devices: 6.39 us -> 11 us  [swap(): lax.ppermute(value, axis, [(i, i ^ bit) for i in range(lax.axis_size(axis...]
    ppermute x1, waiting for transfers between devices: 0.01 us -> 3.89 us  [steps(): beside = lax.ppermute(near, 'pa', [(0, 1), (1, 0)])]
    pallas_call x2 -> x1, Pallas kernels: 6.11 us -> 3.35 us  [forward(): pl.pallas_call(body, out_shape=(out_vmem((planes * views, cells_y + 2 * p...]
    ppermute x4 -> x2, starting transfers between devices: 8.86 us -> 7.73 us  [swap_odd(): lax.ppermute(value, axis, [(i, (i + (1 if i % 2 else -1)) % size) for i i...]
  transfers between devices with their start and end apart: 13 -> 9, of which waited for: 4 -> 8; matrix products, arithmetic and copies ran while one was open for 0% -> 0% of each run, Pallas kernels for 18% -> 13%
where the time goes in v3:
time: 54.4 us; the launch traced here: 53.7 us
  waiting for transfers between devices  20.7 us (38%)
  starting transfers between devices  17.7 us (33%)
  Pallas kernels  14.3 us (26%)
  between operations  0.76 us (1%)
    ppermute x6, waiting for transfers between devices, swap(): lax.ppermute(value, axis, [(i, i ^ bit) for i in range(lax.axis_size(axis...  11 us
    ppermute x6, starting transfers between devices, swap(): lax.ppermute(value, axis, [(i, i ^ bit) for i in range(lax.axis_size(axis...  9.06 us
    ppermute x2, starting transfers between devices, swap_odd(): lax.ppermute(value, axis, [(i, (i + (1 if i % 2 else -1)) % size) for i i...  7.73 us
    pallas_call x2, Pallas kernels, back_y(): pl.pallas_call(body, out_shape=tuple(shapes), in_specs=specs, out_specs=t...  7.37 us
    ppermute x2, waiting for transfers between devices, swap_odd(): lax.ppermute(value, axis, [(i, (i + (1 if i % 2 else -1)) % size) for i i...  5.9 us
    ppermute x1, waiting for transfers between devices, steps(): beside = lax.ppermute(near, 'pa', [(0, 1), (1, 0)])  3.89 us
    pallas_call x1, Pallas kernels, back_x(): pl.pallas_call(body, out_shape=(out_vmem(volume.shape, F32), jax.ShapeDty...  3.6 us
    pallas_call x1, Pallas kernels, forward(): pl.pallas_call(body, out_shape=(out_vmem((planes * views, cells_y + 2 * p...  3.35 us
  transfers between devices with their start and end apart: 9, of which 8 were waited for; matrix products, arithmetic and copies ran while one was open for 0% of the time, Pallas kernels for 13%

profile of v3, /device:TPU:10, one launch (start us, length us, event | category | flops | bytes accessed | tf_op | source)
XLA Modules:
  0.0 53.7 jit_solution(15916806849217517604)
XLA Ops:
  0.6 3.4 %forward.1 = (f32[32,384]{1,0:T(8,128)S(1)}, f32[32,768]{1,0:T(8,128)S(1)}, bf16[256,256]{1,0:T(8,128)(2,1)S(1)}, bf16[1,512,256]{2,1,0:T(8,128)(2,1)S(1)}) custom-call(s32[2,16]{1,0:T(2,128)} %refs_0_.7, bf16[2,512,256]{2,1,0:T(8,128)(2,1)} %refs_1_.3, f32[16,2,256]{2,1,0:T(2,128)} %refs_2_.1, f32[16,2,512]{2,1,0:T(2,128)} %refs_3_.1), custom_call_target="tpu_custom_call" | custom-call | tf_op jit(solution)/shard_map/forward/pallas_call | solution.py:163
  4.0 0.1 collective-permute-start.1
  4.1 1.3 %collective-permute-done.1 = f32[32,640]{1,0:T(8,128)S(1)} collective-permute-done((f32[32,640]{1,0:T(8,128)S(1)}, f32[32,640]{1,0:T(8,128)S(1)}, u32[]{:S(2)}, u32[]{:S(2)}) %collective-permute-start.1) | collective-permute-done | bytes 81952 | tf_op jit(solution)/shard_map/ppermute | solution.py:338
  5.4 0.3 collective-permute-start.2
  5.7 3.7 %collective-permute-done.2 = f32[32,640]{1,0:T(8,128)S(1)} collective-permute-done((f32[32,640]{1,0:T(8,128)S(1)}, f32[32,640]{1,0:T(8,128)S(1)}, u32[]{:S(2)}, u32[]{:S(2)}) %collective-permute-start.2) | collective-permute-done | bytes 81952 | tf_op jit(solution)/shard_map/ppermute | solution.py:343
  9.4 2.0 %collective-permute-start.3 = (f32[16,1024]{1,0:T(8,128)S(1)}, f32[16,1024]{1,0:T(8,128)S(1)}, u32[]{:S(2)}, u32[]{:S(2)}) collective-permute-start(f32[16,1024]{1,0:T(8,128)S(1)} %pad_maximum_fusion.3), channel_id=1, source_target_pairs={{0,2},{2,0},{4,6},{6,4},{8,10},{10,8},{12,14},{14,12},{16,18},{18,... | collective-permute-start | bytes 196616 | tf_op jit(solution)/shard_map/ppermute | solution.py:338
  11.4 2.4 %collective-permute-done.3 = f32[16,1024]{1,0:T(8,128)S(1)} collective-permute-done((f32[16,1024]{1,0:T(8,128)S(1)}, f32[16,1024]{1,0:T(8,128)S(1)}, u32[]{:S(2)}, u32[]{:S(2)}) %collective-permute-start.3) | collective-permute-done | bytes 65568 | tf_op jit(solution)/shard_map/ppermute | solution.py:338
  13.9 7.4 %collective-permute-start.4 = (f32[16,1024]{1,0:T(8,128)S(1)}, f32[16,1024]{1,0:T(8,128)S(1)}, u32[]{:S(2)}, u32[]{:S(2)}) collective-permute-start(f32[16,1024]{1,0:T(8,128)S(1)} %pad_maximum_fusion.4), channel_id=1, source_target_pairs={{0,30},{2,4},{4,2},{6,8},{8,6},{10,12},{12,10},{14,16},{16,14},{18... | collective-permute-start | bytes 196616 | tf_op jit(solution)/shard_map/ppermute | solution.py:343
  21.3 2.2 %collective-permute-done.4 = f32[16,1024]{1,0:T(8,128)S(1)} collective-permute-done((f32[16,1024]{1,0:T(8,128)S(1)}, f32[16,1024]{1,0:T(8,128)S(1)}, u32[]{:S(2)}, u32[]{:S(2)}) %collective-permute-start.4) | collective-permute-done | bytes 65568 | tf_op jit(solution)/shard_map/ppermute | solution.py:343
  23.6 3.1 %collective-permute-start.6 = (f32[16,768]{1,0:T(8,128)S(1)}, f32[16,768]{1,0:T(8,128)S(1)}, u32[]{:S(2)}, u32[]{:S(2)}) collective-permute-start(f32[16,768]{1,0:T(8,128)S(1)} %slice_add_fusion), channel_id=1, source_target_pairs={{0,8},{2,10},{4,12},{6,14},{8,0},{10,2},{12,4},{14,6},{16,24},{18,... | collective-permute-start | bytes 147464 | tf_op jit(solution)/shard_map/ppermute | solution.py:338
  26.7 5.5 %collective-permute-done.6 = f32[16,768]{1,0:T(8,128)S(1)} collective-permute-done((f32[16,768]{1,0:T(8,128)S(1)}, f32[16,768]{1,0:T(8,128)S(1)}, u32[]{:S(2)}, u32[]{:S(2)}) %collective-permute-start.6) | collective-permute-done | bytes 49184 | tf_op jit(solution)/shard_map/ppermute | solution.py:338
  32.2 1.0 %collective-permute-start.7 = (f32[16,768]{1,0:T(8,128)S(1)}, f32[16,768]{1,0:T(8,128)S(1)}, u32[]{:S(2)}, u32[]{:S(2)}) collective-permute-start(f32[16,768]{1,0:T(8,128)S(1)} %add.52), channel_id=1, source_target_pairs={{0,16},{2,18},{4,20},{6,22},{8,24},{10,26},{12,28},{14,30},{16,0},... | collective-permute-start | bytes 147464 | tf_op jit(solution)/shard_map/ppermute | solution.py:338
  33.2 2.8 %collective-permute-start.5 = (f32[32,384]{1,0:T(8,128)S(1)}, f32[32,384]{1,0:T(8,128)S(1)}, u32[]{:S(2)}, u32[]{:S(2)}) collective-permute-start(f32[32,384]{1,0:T(8,128)S(1)} %pad_maximum_fusion.5), channel_id=1, source_target_pairs={{0,128},{32,160},{64,192},{96,224},{128,0},{160,32},{192,64},{224,... | collective-permute-start | bytes 147464 | tf_op jit(solution)/shard_map/ppermute | solution.py:338
  36.0 0.9 %collective-permute-start = (bf16[1,512,256]{2,1,0:T(8,128)(2,1)S(1)}, bf16[1,512,256]{2,1,0:T(8,128)(2,1)S(1)}, u32[]{:S(2)}, u32[]{:S(2)}) collective-permute-start(bf16[1,512,256]{2,1,0:T(8,128)(2,1)S(1)} %get-tuple-element.12), channel_id=1, source_target_pairs={{0,1},{1,0},{2,3},{3,2},{4,5},{5,4},{6,7},{7,6},{8,9},{9,8},{10,11... | collective-permute-start | bytes 786440 | tf_op jit(solution)/shard_map/ppermute | solution.py:389
  36.9 1.4 %collective-permute-done.7 = f32[16,768]{1,0:T(8,128)S(1)} collective-permute-done((f32[16,768]{1,0:T(8,128)S(1)}, f32[16,768]{1,0:T(8,128)S(1)}, u32[]{:S(2)}, u32[]{:S(2)}) %collective-permute-start.7) | collective-permute-done | bytes 49184 | tf_op jit(solution)/shard_map/ppermute | solution.py:338
  38.3 0.1 collective-permute-start.8
  38.4 0.4 collective-permute-done.5
  38.8 3.9 %collective-permute-done.refs_2_ = bf16[1,512,256]{2,1,0:T(8,128)(2,1)S(1)} collective-permute-done((bf16[1,512,256]{2,1,0:T(8,128)(2,1)S(1)}, bf16[1,512,256]{2,1,0:T(8,128)(2,1)S(1)}, u32[]{:S(2)}, u32[]{:S(2)}) %collective-permute-start) | collective-permute-done | bytes 262176 | tf_op jit(solution)/shard_map/ppermute | solution.py:389
  42.7 3.6 %back_x.1 = (f32[2,512,256]{2,1,0:T(8,128)S(1)}, f32[16,2,256]{2,1,0:T(2,128)}) custom-call(s32[2,16]{1,0:T(2,128)} %refs_0_.7, bf16[2,512,256]{2,1,0:T(8,128)(2,1)} %refs_1_.3, bf16[1,512,256]{2,1,0:T(8,128)(2,1)S(1)} %collective-permute-done.refs_2_, f32[32,384]{1,0:T(8,128)S(1)} %fusion.1.refs_3_), custom_call_target="tpu_custom_call" | custom-call | tf_op jit(solution)/shard_map/back_x/pallas_call | solution.py:249
  46.3 3.4 %back_y_own.1.refs_5_ = f32[2,512,256]{2,1,0:T(8,128)} custom-call(s32[2,16]{1,0:T(2,128)} %refs_0_.7, bf16[256,256]{1,0:T(8,128)(2,1)S(1)} %get-tuple-element.11.refs_1_, f32[2,512,256]{2,1,0:T(8,128)S(1)} %get-tuple-element.15.refs_2_, f32[16,768]{1,0:T(8,128)S(1)} %add.53.refs_3_), custom_call_target="tpu_custom_call" | custom-call | tf_op jit(solution)/shard_map/back_y_own/pallas_call | solution.py:319
  49.6 0.0 collective-permute-done.8.refs_4_
  49.6 4.0 %back_y_last.1 = (f32[2,512,256]{2,1,0:T(8,128)}, f32[16,2,512]{2,1,0:T(2,128)}) custom-call(s32[2,16]{1,0:T(2,128)} %refs_0_.7, bf16[256,256]{1,0:T(8,128)(2,1)S(1)} %get-tuple-element.11.refs_1_, f32[2,512,256]{2,1,0:T(8,128)S(1)} %get-tuple-element.15.refs_2_, f32[16,768]{1,0:T(8,128)S(1)} %add.53.refs_3_, ...), custom_call_target="tpu_custom_call", output_to_operand_aliasing={{0}: (5, {})} | custom-call | tf_op jit(solution)/shard_map/back_y_last/pallas_call | solution.py:319
  (20 shorter events, 0.1 us)
Async XLA Ops:
  4.0 1.4 %collective-permute-start.1 = (f32[32,640]{1,0:T(8,128)S(1)}, f32[32,640]{1,0:T(8,128)S(1)}, u32[]{:S(2)}, u32[]{:S(2)}) collective-permute-start(f32[32,640]{1,0:T(8,128)S(1)} %pad_maximum_fusion.1), channel_id=1, source_target_pairs={{0,32},{32,0},{64,96},{96,64},{128,160},{160,128},{192,224},{224,1... | collective-permute-start | bytes 245768 | tf_op jit(solution)/shard_map/ppermute | solution.py:338
  5.4 4.0 %collective-permute-start.2 = (f32[32,640]{1,0:T(8,128)S(1)}, f32[32,640]{1,0:T(8,128)S(1)}, u32[]{:S(2)}, u32[]{:S(2)}) collective-permute-start(f32[32,640]{1,0:T(8,128)S(1)} %pad_maximum_fusion.2), channel_id=1, source_target_pairs={{0,224},{32,64},{64,32},{96,128},{128,96},{160,192},{192,160},{224... | collective-permute-start | bytes 245768 | tf_op jit(solution)/shard_map/ppermute | solution.py:343
  9.4 4.4 %collective-permute-start.3 = (f32[16,1024]{1,0:T(8,128)S(1)}, f32[16,1024]{1,0:T(8,128)S(1)}, u32[]{:S(2)}, u32[]{:S(2)}) collective-permute-start(f32[16,1024]{1,0:T(8,128)S(1)} %pad_maximum_fusion.3), channel_id=1, source_target_pairs={{0,2},{2,0},{4,6},{6,4},{8,10},{10,8},{12,14},{14,12},{16,18},{18,... | collective-permute-start | bytes 196616 | tf_op jit(solution)/shard_map/ppermute | solution.py:338
  13.9 9.7 %collective-permute-start.4 = (f32[16,1024]{1,0:T(8,128)S(1)}, f32[16,1024]{1,0:T(8,128)S(1)}, u32[]{:S(2)}, u32[]{:S(2)}) collective-permute-start(f32[16,1024]{1,0:T(8,128)S(1)} %pad_maximum_fusion.4), channel_id=1, source_target_pairs={{0,30},{2,4},{4,2},{6,8},{8,6},{10,12},{12,10},{14,16},{16,14},{18... | collective-permute-start | bytes 196616 | tf_op jit(solution)/shard_map/ppermute | solution.py:343
  23.6 8.6 %collective-permute-start.6 = (f32[16,768]{1,0:T(8,128)S(1)}, f32[16,768]{1,0:T(8,128)S(1)}, u32[]{:S(2)}, u32[]{:S(2)}) collective-permute-start(f32[16,768]{1,0:T(8,128)S(1)} %slice_add_fusion), channel_id=1, source_target_pairs={{0,8},{2,10},{4,12},{6,14},{8,0},{10,2},{12,4},{14,6},{16,24},{18,... | collective-permute-start | bytes 147464 | tf_op jit(solution)/shard_map/ppermute | solution.py:338
  32.2 6.1 %collective-permute-start.7 = (f32[16,768]{1,0:T(8,128)S(1)}, f32[16,768]{1,0:T(8,128)S(1)}, u32[]{:S(2)}, u32[]{:S(2)}) collective-permute-start(f32[16,768]{1,0:T(8,128)S(1)} %add.52), channel_id=1, source_target_pairs={{0,16},{2,18},{4,20},{6,22},{8,24},{10,26},{12,28},{14,30},{16,0},... | collective-permute-start | bytes 147464 | tf_op jit(solution)/shard_map/ppermute | solution.py:338
  33.2 5.6 %collective-permute-start.5 = (f32[32,384]{1,0:T(8,128)S(1)}, f32[32,384]{1,0:T(8,128)S(1)}, u32[]{:S(2)}, u32[]{:S(2)}) collective-permute-start(f32[32,384]{1,0:T(8,128)S(1)} %pad_maximum_fusion.5), channel_id=1, source_target_pairs={{0,128},{32,160},{64,192},{96,224},{128,0},{160,32},{192,64},{224,... | collective-permute-start | bytes 147464 | tf_op jit(solution)/shard_map/ppermute | solution.py:338
  36.0 6.7 %collective-permute-start = (bf16[1,512,256]{2,1,0:T(8,128)(2,1)S(1)}, bf16[1,512,256]{2,1,0:T(8,128)(2,1)S(1)}, u32[]{:S(2)}, u32[]{:S(2)}) collective-permute-start(bf16[1,512,256]{2,1,0:T(8,128)(2,1)S(1)} %get-tuple-element.12), channel_id=1, source_target_pairs={{0,1},{1,0},{2,3},{3,2},{4,5},{5,4},{6,7},{7,6},{8,9},{9,8},{10,11... | collective-permute-start | bytes 786440 | tf_op jit(solution)/shard_map/ppermute | solution.py:389
  38.3 11.3 %collective-permute-start.8 = (f32[16,768]{1,0:T(8,128)S(1)}, f32[16,768]{1,0:T(8,128)S(1)}, u32[]{:S(2)}, u32[]{:S(2)}) collective-permute-start(f32[16,768]{1,0:T(8,128)S(1)} %add.53.refs_3_), channel_id=1, source_target_pairs={{0,2},{2,0},{4,6},{6,4},{8,10},{10,8},{12,14},{14,12},{16,18},{18,... | collective-permute-start | bytes 147464 | tf_op jit(solution)/shard_map/ppermute | solution.py:338

commit v4 on v3

v4 whole, which is shorter than its diff:
```python
import jax
import jax.numpy as jnp
from jax import lax
from jax.experimental import pallas as pl
from jax.experimental.pallas import tpu as pltpu
from jax.sharding import PartitionSpec as P


LEVELS = 16
RING = 8
SMEM = pltpu.SMEM
VMEM = pltpu.VMEM
F32 = jnp.float32
BF16 = jnp.bfloat16


def interpreted():
    return False


def fill(slopes_ref, family, shape, dim):
    views = slopes_ref.shape[1]
    view = lax.broadcasted_iota(jnp.int32, shape, dim) % views
    slopes = jnp.zeros(shape, jnp.int32)
    for v in range(views):
        slopes = jnp.where(view == v, slopes_ref[family, v], slopes)
    return slopes


def tiled(value, width):
    return jnp.concatenate([value] * (width // value.shape[1]), axis=1)


def lowest_shift(slopes, block, blocks):
    return slopes * (block - blocks // 2) + jnp.minimum(slopes, 0)


def barrel(value, amounts, bits):
    for bit in range(bits):
        taken = ((amounts >> bit) & 1) == 1
        value = jnp.where(taken, pltpu.roll(value, 1 << bit, 1), value)
    return value


def offsets(slopes, block, blocks, cells):
    views = slopes.shape[0]
    lowest = tiled(lowest_shift(slopes, block, blocks).astype(F32), cells)
    cell = lax.broadcasted_iota(jnp.int32, (views, cells), 1) + (block * cells - blocks * cells // 2)
    return tiled(slopes.astype(F32), cells) * (cell.astype(F32) * (1.0 / cells)) - lowest


def hat(offset, level):
    return jnp.maximum(1.0 - jnp.abs(offset - level), 0.0)


def in_vmem(value):
    if interpreted():
        return value
    return pltpu.with_memory_space_constraint(value, VMEM)


def out_vmem(shape, dtype):
    if interpreted():
        return jax.ShapeDtypeStruct(shape, dtype)
    return VMEM(shape, dtype)


def anywhere():
    return pl.BlockSpec(memory_space=pl.ANY)


def vmem():
    return pl.BlockSpec(memory_space=VMEM)


def in_roles(value, odd):
    edge = value.shape[1] // 3
    lead, mid, trail = value[:, :edge], value[:, edge : 2 * edge], value[:, 2 * edge :]
    return jnp.concatenate([jnp.where(odd, lead, trail), mid, jnp.where(odd, trail, lead)], axis=1)


def from_roles(value, odd):
    edge = value.shape[1] // 3
    a, mid, b = value[:, :edge], value[:, edge : 2 * edge], value[:, 2 * edge :]
    return jnp.concatenate([jnp.where(odd, a, b), mid, jnp.where(odd, b, a)], axis=1)


def on_grid(value):
    return jnp.round(value * 32768.0) * (1.0 / 32768.0)


def project(table_ref, volume_ref, rows_ref, slopes, out_ref, family, block, blocks, odd, pad, scale):
    planes = volume_ref.shape[0]
    views = slopes.shape[0]
    bins = volume_ref.shape[2 - family]
    width = out_ref.shape[1]
    first = (block == 0).astype(F32)
    amounts = tiled(pad - lowest_shift(slopes, block, blocks), width)
    bits = max(1, (2 * pad).bit_length() - 1)
    empty = jnp.zeros((views, width - bins), F32)
    for plane in range(planes):
        dims = (((1,), (family,)), ((), ()))
        summands = lax.dot_general(table_ref[...], volume_ref[plane], dims, preferred_element_type=F32)
        total = None
        for level in reversed(range(LEVELS)):
            piece = jnp.concatenate([summands[level * views : (level + 1) * views, :], empty], axis=1)
            total = piece if total is None else pltpu.roll(total, width - 1, 1) + piece
        total = barrel(total, amounts, bits) * scale
        known = jnp.concatenate([rows_ref[plane * views : (plane + 1) * views, :] * first, empty], axis=1)
        total = on_grid(total - pltpu.roll(known, pad, 1))
        out_ref[plane * views : (plane + 1) * views, :] = in_roles(total, odd)


def build_table(slopes, block, blocks, cells, table_ref):
    views = slopes.shape[0]
    offset = offsets(slopes, block, blocks, cells)
    for level in range(LEVELS):
        table_ref[level * views : (level + 1) * views, :] = hat(offset, float(level)).astype(BF16)


def gather_rows(measured_ref, rows_ref):
    views, planes, _ = measured_ref.shape
    for plane in range(planes):
        for v in range(views):
            rows_ref[plane * views + v : plane * views + v + 1, :] = measured_ref[v, plane : plane + 1, :]


def forward_kernel(
    slopes_hbm, volume_hbm, mx_hbm, my_hbm,
    x_ref, y_ref, table_y_ref, near_ref, volume_ref, column_x_ref, column_y_ref, lane_ref,
    table_x_ref, slopes_ref, mx_ref, my_ref, rows_x_ref, rows_y_ref, sems,
    *, count_x, count_y, pad_x, pad_y, scale_x, scale_y,
):
    _, cells_x, cells_y = volume_ref.shape
    fetches = [
        pltpu.make_async_copy(slopes_hbm, slopes_ref, sems.at[0]),
        pltpu.make_async_copy(volume_hbm, volume_ref, sems.at[1]),
        pltpu.make_async_copy(mx_hbm, mx_ref, sems.at[2]),
        pltpu.make_async_copy(my_hbm, my_ref, sems.at[3]),
        pltpu.make_async_copy(volume_hbm.at[pl.ds(1 - lax.axis_index("pa"), 1)], near_ref, sems.at[4]),
    ]
    for fetch in fetches:
        fetch.start()
    here_x, here_y = lax.axis_index("gx"), lax.axis_index("gy")
    fetches[0].wait()
    column_x = fill(slopes_ref, 0, column_x_ref.shape, 0)
    column_y = fill(slopes_ref, 1, column_y_ref.shape, 0)
    column_x_ref[...] = column_x
    column_y_ref[...] = column_y
    lane_ref[...] = fill(slopes_ref, 0, lane_ref.shape, 1)
    build_table(column_y, here_y, count_y, cells_y, table_y_ref)
    build_table(column_x, here_x, count_x, cells_x, table_x_ref)
    fetches[2].wait()
    fetches[3].wait()
    gather_rows(mx_ref, rows_x_ref)
    gather_rows(my_ref, rows_y_ref)
    fetches[1].wait()
    project(table_y_ref, volume_ref, rows_y_ref, column_y, y_ref, 1, here_y, count_y, here_x % 2 == 1, pad_y, scale_y)
    project(table_x_ref, volume_ref, rows_x_ref, column_x, x_ref, 0, here_x, count_x, here_y % 2 == 1, pad_x, scale_x)
    fetches[4].wait()


def forward(slopes, volume, measured_x, measured_y, count_x, count_y, pad_x, pad_y, scale_x, scale_y):
    views = slopes.shape[1]
    planes, cells_x, cells_y = volume.shape

    def body(*refs):
        forward_kernel(
            *refs, count_x=count_x, count_y=count_y, pad_x=pad_x, pad_y=pad_y, scale_x=scale_x, scale_y=scale_y
        )

    return pl.pallas_call(
        body,
        out_shape=(
            out_vmem((planes * views, cells_y + 2 * pad_x), F32),
            out_vmem((planes * views, cells_x + 2 * pad_y), F32),
            out_vmem((LEVELS * views, cells_y), BF16),
            out_vmem((1,) + volume.shape[1:], BF16),
            out_vmem(volume.shape, BF16),
            out_vmem((views, 128), jnp.int32),
            out_vmem((views, 128), jnp.int32),
            out_vmem((8, LEVELS * views), jnp.int32),
        ),
        in_specs=[anywhere()] * 4,
        out_specs=(vmem(),) * 8,
        scratch_shapes=[
            VMEM((LEVELS * views, cells_x), BF16),
            SMEM(slopes.shape, jnp.int32),
            VMEM(measured_x.shape, F32),
            VMEM(measured_y.shape, F32),
            VMEM((planes * views, cells_y), F32),
            VMEM((planes * views, cells_x), F32),
            pltpu.SemaphoreType.DMA((5,)),
        ],
        interpret=interpreted(),
        name="forward",
    )(slopes, volume, measured_x, measured_y)


def half_of(index):
    return ((index + 1) // 2) % 2


def spread_into(value, slopes, block, blocks, other, others, pad, scale, spread_ref):
    views, width = value.shape
    bins = width - 2 * pad
    bits = max(1, (2 * pad).bit_length() - 1)
    place = lax.broadcasted_iota(jnp.int32, (views, width), 1)
    inside = (place >= jnp.where(other == 0, pad, 0)) & (place < jnp.where(other == others - 1, pad + bins, width))
    value = jnp.where(inside, value * scale, 0.0).astype(BF16).astype(F32)
    amounts = tiled(lowest_shift(slopes, block, blocks) + pad, width)
    value = pltpu.roll(barrel(value, amounts, bits), width - 2 * pad, 1)
    for level in range(LEVELS):
        spread_ref[level * views : (level + 1) * views, :] = value[:, :bins].astype(BF16)
        value = pltpu.roll(value, 1, 1)


def middle(value, pad):
    width = value.shape[1]
    return pltpu.roll(value, width - pad, 1)[:, : width - 2 * pad]


def prepare_kernel(lane_ref, volume_ref, beside_ref, table_ref, base_ref, *, blocks):
    planes, cells, _ = volume_ref.shape
    block, band = lax.axis_index("gx"), lax.axis_index("pa")
    slopes = lane_ref[...]
    views = slopes.shape[1] // LEVELS
    level = lax.broadcasted_iota(jnp.int32, slopes.shape, 1) // views
    base = (lowest_shift(slopes, block, blocks) + level).astype(F32)[:1]
    slopes = slopes.astype(F32)[:1]
    shape = (cells, LEVELS * views)
    cell = lax.broadcasted_iota(jnp.int32, shape, 0).astype(F32) * (1.0 / cells) + (block - blocks // 2).astype(F32)
    table_ref[...] = jnp.maximum(1.0 - jnp.abs(cell * slopes - base), 0.0).astype(BF16)
    for plane in range(planes):
        here = volume_ref[plane].astype(F32)
        beside = beside_ref[0].astype(F32) * (band == 1 - plane).astype(F32)
        within = volume_ref[1 - plane].astype(F32)
        base_ref[plane] = 0.02 * (2.0 * here - beside - within)


def prepare(lane, volume, beside, blocks):
    def body(*refs):
        prepare_kernel(*refs, blocks=blocks)

    return pl.pallas_call(
        body,
        out_shape=(out_vmem((volume.shape[1], lane.shape[1]), BF16), out_vmem(volume.shape, F32)),
        in_specs=[vmem()] * 3,
        out_specs=(vmem(), vmem()),
        interpret=interpreted(),
        name="prepare",
    )(*(in_vmem(value) for value in (lane, volume, beside)))


def back_x_kernel(column_ref, table_ref, base_ref, residual_ref, out_ref, rest_hbm, spread_ref, rows_ref, rest_ref, sem, *, blocks, others, pad, scale):
    planes, _, _ = base_ref.shape
    views = column_ref.shape[0]
    block, other = lax.axis_index("gx"), lax.axis_index("gy")
    column = column_ref[...]
    residuals = [from_roles(residual_ref[p * views : (p + 1) * views, :], other % 2 == 1) for p in range(planes)]
    for plane in range(planes):
        rows_ref[plane * views : (plane + 1) * views, :] = middle(residuals[plane], pad)
    for plane in range(planes):
        for v in range(views):
            rest_ref[v, plane : plane + 1, :] = rows_ref[plane * views + v : plane * views + v + 1, :]
    store = pltpu.make_async_copy(rest_ref, rest_hbm, sem)
    store.start()
    for plane in range(planes):
        spread_into(residuals[plane], column, block, blocks, other, others, pad, scale, spread_ref)
        out_ref[plane] = base_ref[plane] + jnp.dot(table_ref[...], spread_ref[...], preferred_element_type=F32)
    store.wait()


def back_x(column, table, base, residual, blocks, others, pad, scale):
    planes, _, bins = base.shape
    views = column.shape[0]

    def body(*refs):
        back_x_kernel(*refs, blocks=blocks, others=others, pad=pad, scale=scale)

    return pl.pallas_call(
        body,
        out_shape=(out_vmem(base.shape, F32), jax.ShapeDtypeStruct((views, planes, bins), F32)),
        in_specs=[vmem()] * 4,
        out_specs=(vmem(), anywhere()),
        scratch_shapes=[
            VMEM((LEVELS * views, bins), BF16),
            VMEM((planes * views, bins), F32),
            VMEM((views, planes, bins), F32),
            pltpu.SemaphoreType.DMA,
        ],
        interpret=interpreted(),
        name="back_x",
    )(*(in_vmem(value) for value in (column, table, base, residual)))


def back_y_kernel(*refs, last, blocks, others, pad, scale, views):
    column_ref, table_ref, partial_ref, half_ref = refs[:4]
    rest = list(refs[4:])
    if last:
        other_ref = rest.pop(0)
        rest.pop(0)
        rest_hbm = rest.pop(1)
        rest_ref = rest.pop()
    out_hbm, sum_ref, spread_ref, rows_ref, sems = rest
    block, other = lax.axis_index("gy"), lax.axis_index("gx")
    mine = half_of(lax.axis_index("gy"))
    flip = other % 2 == 1
    plane = 1 - mine if last else mine
    value = from_roles(other_ref[...] if last else half_ref[...], flip)
    spread_into(value, column_ref[...], block, blocks, other, others, pad, scale, spread_ref)
    dims = (((0,), (0,)), ((), ()))
    back = lax.dot_general(spread_ref[...], table_ref[...], dims, preferred_element_type=F32)
    sum_ref[...] = partial_ref[pl.ds(plane, 1)] + back[None]
    store = pltpu.make_async_copy(sum_ref, out_hbm.at[pl.ds(plane, 1)], sems.at[1])
    store.start()
    if last:
        odd = mine == 1
        rows_ref[:views, :] = middle(from_roles(jnp.where(odd, other_ref[...], half_ref[...]), flip), pad)
        rows_ref[views:, :] = middle(from_roles(jnp.where(odd, half_ref[...], other_ref[...]), flip), pad)
        for p in range(2):
            for v in range(views):
                rest_ref[v, p : p + 1, :] = rows_ref[p * views + v : p * views + v + 1, :]
        also = pltpu.make_async_copy(rest_ref, rest_hbm, sems.at[0])
        also.start()
        also.wait()
    store.wait()


def back_y(column, table, partial, half, rest, blocks, others, pad, scale):
    planes, bins, cells = partial.shape
    views = column.shape[0]
    last = rest is not None

    def body(*refs):
        back_y_kernel(*refs, last=last, blocks=blocks, others=others, pad=pad, scale=scale, views=views)

    operands = [in_vmem(column), in_vmem(table), in_vmem(partial), in_vmem(half)]
    specs = [vmem()] * 4
    shapes = [jax.ShapeDtypeStruct(partial.shape, F32)]
    out_specs = [anywhere()]
    aliases = {}
    if last:
        other, gradient = rest
        operands += [in_vmem(other), gradient]
        specs += [vmem(), anywhere()]
        shapes.append(jax.ShapeDtypeStruct((views, planes, bins), F32))
        out_specs.append(anywhere())
        aliases = {5: 0}
    scratch = [
        VMEM((1, bins, cells), F32),
        VMEM((LEVELS * views, bins), BF16),
        VMEM((planes * views, bins), F32),
        pltpu.SemaphoreType.DMA((2,)),
    ]
    if last:
        scratch.append(VMEM((views, planes, bins), F32))
    return pl.pallas_call(
        body,
        out_shape=tuple(shapes),
        in_specs=specs,
        out_specs=tuple(out_specs),
        scratch_shapes=scratch,
        input_output_aliases=aliases,
        interpret=interpreted(),
        name="back_y_last" if last else "back_y_own",
    )(*operands)


def exchange(value, axis, partner):
    return lax.ppermute(value, axis, [(i, partner(i)) for i in range(lax.axis_size(axis))])


def twin(i):
    return i ^ 1


def odd_twin(i):
    return i - i % RING + (i + (1 if i % 2 else -1)) % RING


def across(i):
    return i - i % RING + (i + (-3 if i % 2 else 3)) % RING


def at_end(size, axis):
    index = lax.axis_index(axis) % size
    return (index == 0) | (index == size - 1)


def steps(volume, view_slopes, measured_x, measured_y):
    _, cells_x, cells_y = volume.shape
    count_x = lax.axis_size("gx")
    count_y = lax.axis_size("gy")
    scale_x = float(cells_x * count_x) ** (-0.5)
    scale_y = float(cells_y * count_y) ** (-0.5)
    pad_x, pad_y = 64, 128

    sum_x, sum_y, table_y, near, volume, column_x, column_y, lane = forward(
        view_slopes, volume, measured_x, measured_y, count_x, count_y, pad_x, pad_y, scale_x, scale_y
    )
    wide = sum_x.shape[1]
    edge_x, edge_y = wide // 3, sum_y.shape[1] // 3
    y_a, y_mid, y_b = sum_y[:, :edge_y], sum_y[:, edge_y : 2 * edge_y], sum_y[:, 2 * edge_y :]

    got = exchange(jnp.concatenate([sum_x, y_a], axis=1), "gx", twin)
    beside = lax.ppermute(near, "pa", [(0, 1), (1, 0)])
    sum_x, y_a = sum_x + got[:, :wide], y_a + got[:, wide:]
    got = exchange(jnp.concatenate([sum_x, y_b], axis=1), "gx", odd_twin)
    sum_x, y_b = sum_x + got[:, :wide], y_b + jnp.where(at_end(count_x, "gx"), 0.0, got[:, wide:])
    sum_y = jnp.concatenate([y_a, y_mid, y_b], axis=1)
    x_a, x_mid, x_b = sum_x[:, :edge_x], sum_x[:, edge_x : 2 * edge_x], sum_x[:, 2 * edge_x :]

    rows = sum_y.shape[0] // 2
    long = sum_y.shape[1]
    owns = half_of(lax.axis_index("gy")) == 0
    kept = jnp.where(owns, sum_y[:rows], sum_y[rows:])
    sent = jnp.where(owns, sum_y[rows:], sum_y[:rows])
    got = exchange(jnp.concatenate([sent, x_a[:rows], x_a[rows:]], axis=1), "gy", twin)
    half = kept + got[:, :long]
    x_a = x_a + jnp.concatenate([got[:, long : long + edge_x], got[:, long + edge_x :]], axis=0)
    got = exchange(jnp.concatenate([half, x_b[:rows], x_b[rows:]], axis=1), "gy", lambda i: i ^ RING)
    half = half + got[:, :long]
    sent_b = jnp.where(at_end(RING, "gy"), got[:, long:], jnp.concatenate([x_b[:rows], x_b[rows:]], axis=1))
    got = exchange(jnp.concatenate([half, sent_b], axis=1), "gy", odd_twin)
    half = half + got[:, :long]
    got = jnp.where(at_end(count_y, "gy"), 0.0, got)
    half, x_b, got = lax.optimization_barrier((half, x_b, got))
    x_b = x_b + jnp.concatenate([got[:, long : long + edge_x], got[:, long + edge_x :]], axis=0)
    sum_x = jnp.concatenate([x_a, x_mid, x_b], axis=1)

    half = half + exchange(half, "gy", across)
    sum_x = sum_x + exchange(sum_x, "gx", across)
    other = exchange(half, "gy", twin)

    table_x, base = prepare(lane, volume, beside, count_x)
    partial, residual_x = back_x(column_x, table_x, base, sum_x, count_x, count_y, pad_x, scale_x)
    (gradient,) = back_y(column_y, table_y, partial, half, None, count_y, count_x, pad_y, scale_y)
    gradient, residual_y = back_y(column_y, table_y, partial, half, (other, gradient), count_y, count_x, pad_y, scale_y)
    return (gradient, residual_x, residual_y)


def solution(mesh):
    return jax.shard_map(
        steps,
        mesh=mesh,
        in_specs=(P("pa", "gx", "gy"), P(), P(None, "pa", "gy"), P(None, "pa", "gx")),
        out_specs=(P("pa", "gx", "gy"), P(None, "pa", "gy"), P(None, "pa", "gx")),
        check_vma=False,
    )
```

time: 54.4 us -> 48.5 us (0.89)
  the two profiles are of different devices: /device:TPU:10 before, /device:TPU:1 now
where the time goes in v4:
time: 48.5 us; the launch traced here: 48.4 us
  starting transfers between devices  21.4 us (44%)
  waiting for transfers between devices  13.8 us (28%)
  Pallas kernels  11.6 us (24%)
  between operations  0.86 us (2%)
  local copies, waits for them, and re-layouts  0.64 us (1%)
    ppermute x8, starting transfers between devices, exchange(): lax.ppermute(value, axis, [(i, partner(i)) for i in range(lax.axis_size(a...  20.2 us
    ppermute x8, waiting for transfers between devices, exchange(): lax.ppermute(value, axis, [(i, partner(i)) for i in range(lax.axis_size(a...  13.8 us
    pallas_call x2, Pallas kernels, back_y(): pl.pallas_call(body, out_shape=tuple(shapes), in_specs=specs, out_specs=t...  5.43 us
    pallas_call x1, Pallas kernels, forward(): pl.pallas_call(body, out_shape=(out_vmem((planes * views, cells_y + 2 * p...  3.36 us
    pallas_call x1, Pallas kernels, back_x(): pl.pallas_call(body, out_shape=(out_vmem(base.shape, F32), jax.ShapeDtype...  2.45 us
    ppermute x1, starting transfers between devices, steps(): beside = lax.ppermute(near, 'pa', [(0, 1), (1, 0)])  1.13 us
  transfers between devices with their start and end apart: 9, of which 5 were waited for; matrix products, arithmetic and copies ran while one was open for 0% of the time, Pallas kernels for 11%

profile of v4, /device:TPU:1, one launch (start us, length us, event | category | flops | bytes accessed | tf_op | source)
XLA Modules:
  0.0 48.4 jit_solution(4692254833367737585)
XLA Ops:
  0.6 3.4 %forward.1 = (f32[32,384]{1,0:T(8,128)S(1)}, f32[32,768]{1,0:T(8,128)S(1)}, bf16[256,256]{1,0:T(8,128)(2,1)S(1)}, bf16[1,512,256]{2,1,0:T(8,128)(2,1)S(1)}, bf16...) custom-call(s32[2,16]{1,0:T(2,128)} %refs_0_.1, ...), custom_call_target="tpu_custom_call" | custom-call | tf_op jit(solution)/shard_map/forward/pallas_call | solution.py:172
  4.0 0.0 copy-start
  4.0 0.6 %copy-done = bf16[256,256]{1,0:T(8,128)(2,1)} copy-done((bf16[256,256]{1,0:T(8,128)(2,1)}, bf16[256,256]{1,0:T(8,128)(2,1)S(1)}, u32[]{:S(2)}) %copy-start) | copy-done | bytes 131096
  4.7 3.2 %collective-permute-start.1 = (f32[32,640]{1,0:T(8,128)S(1)}, f32[32,640]{1,0:T(8,128)S(1)}, u32[]{:S(2)}, u32[]{:S(2)}) collective-permute-start(f32[32,640]{1,0:T(8,128)S(1)} %pad_maximum_fusion.1), channel_id=1, source_target_pairs={{0,32},{32,0},{64,96},{96,64},{128,160},{160,128},{192,224},{224,1... | collective-permute-start | bytes 245768 | tf_op jit(solution)/shard_map/ppermute | solution.py:371
  7.9 0.9 %collective-permute-done.1 = f32[32,640]{1,0:T(8,128)S(1)} collective-permute-done((f32[32,640]{1,0:T(8,128)S(1)}, f32[32,640]{1,0:T(8,128)S(1)}, u32[]{:S(2)}, u32[]{:S(2)}) %collective-permute-start.1) | collective-permute-done | bytes 81952 | tf_op jit(solution)/shard_map/ppermute | solution.py:371
  8.8 0.1 collective-permute-start.2
  8.9 4.1 %collective-permute-done.2 = f32[32,640]{1,0:T(8,128)S(1)} collective-permute-done((f32[32,640]{1,0:T(8,128)S(1)}, f32[32,640]{1,0:T(8,128)S(1)}, u32[]{:S(2)}, u32[]{:S(2)}) %collective-permute-start.2) | collective-permute-done | bytes 81952 | tf_op jit(solution)/shard_map/ppermute | solution.py:371
  13.1 0.1 collective-permute-start.3
  13.2 1.1 %collective-permute-start = (bf16[1,512,256]{2,1,0:T(8,128)(2,1)S(1)}, bf16[1,512,256]{2,1,0:T(8,128)(2,1)S(1)}, u32[]{:S(2)}, u32[]{:S(2)}) collective-permute-start(bf16[1,512,256]{2,1,0:T(8,128)(2,1)S(1)} %get-tuple-element.25), channel_id=1, source_target_pairs={{0,1},{1,0},{2,3},{3,2},{4,5},{5,4},{6,7},{7,6},{8,9},{9,8},{10,11... | collective-permute-start | bytes 786440 | tf_op jit(solution)/shard_map/ppermute | solution.py:407
  14.4 2.0 %collective-permute-done.3 = f32[16,1024]{1,0:T(8,128)S(1)} collective-permute-done((f32[16,1024]{1,0:T(8,128)S(1)}, f32[16,1024]{1,0:T(8,128)S(1)}, u32[]{:S(2)}, u32[]{:S(2)}) %collective-permute-start.3) | collective-permute-done | bytes 65568 | tf_op jit(solution)/shard_map/ppermute | solution.py:371
  16.4 1.3 %collective-permute-start.4 = (f32[16,1024]{1,0:T(8,128)S(1)}, f32[16,1024]{1,0:T(8,128)S(1)}, u32[]{:S(2)}, u32[]{:S(2)}) collective-permute-start(f32[16,1024]{1,0:T(8,128)S(1)} %pad_maximum_fusion.4), channel_id=1, source_target_pairs={{0,16},{2,18},{4,20},{6,22},{8,24},{10,26},{12,28},{14,30},{16,0},... | collective-permute-start | bytes 196616 | tf_op jit(solution)/shard_map/ppermute | solution.py:371
  17.7 5.1 %collective-permute-done.4 = f32[16,1024]{1,0:T(8,128)S(1)} collective-permute-done((f32[16,1024]{1,0:T(8,128)S(1)}, f32[16,1024]{1,0:T(8,128)S(1)}, u32[]{:S(2)}, u32[]{:S(2)}) %collective-permute-start.4) | collective-permute-done | bytes 65568 | tf_op jit(solution)/shard_map/ppermute | solution.py:371
  22.8 4.8 %collective-permute-start.5 = (f32[16,1024]{1,0:T(8,128)S(1)}, f32[16,1024]{1,0:T(8,128)S(1)}, u32[]{:S(2)}, u32[]{:S(2)}) collective-permute-start(f32[16,1024]{1,0:T(8,128)S(1)} %pad_maximum_fusion.5), channel_id=1, source_target_pairs={{0,14},{2,4},{4,2},{6,8},{8,6},{10,12},{12,10},{14,0},{16,30},{18,... | collective-permute-start | bytes 196616 | tf_op jit(solution)/shard_map/ppermute | solution.py:371
  27.6 1.6 %collective-permute-done.5 = f32[16,1024]{1,0:T(8,128)S(1)} collective-permute-done((f32[16,1024]{1,0:T(8,128)S(1)}, f32[16,1024]{1,0:T(8,128)S(1)}, u32[]{:S(2)}, u32[]{:S(2)}) %collective-permute-start.5) | collective-permute-done | bytes 65568 | tf_op jit(solution)/shard_map/ppermute | solution.py:371
  29.2 1.7 %collective-permute-start.7 = (f32[16,768]{1,0:T(8,128)S(1)}, f32[16,768]{1,0:T(8,128)S(1)}, u32[]{:S(2)}, u32[]{:S(2)}) collective-permute-start(f32[16,768]{1,0:T(8,128)S(1)} %slice_add_fusion), channel_id=1, source_target_pairs={{0,6},{2,12},{4,10},{6,0},{8,14},{10,4},{12,2},{14,8},{16,22},{18,... | collective-permute-start | bytes 147464 | tf_op jit(solution)/shard_map/ppermute | solution.py:371
  31.0 7.4 %collective-permute-start.6 = (f32[32,384]{1,0:T(8,128)S(1)}, f32[32,384]{1,0:T(8,128)S(1)}, u32[]{:S(2)}, u32[]{:S(2)}) collective-permute-start(f32[32,384]{1,0:T(8,128)S(1)} %pad_maximum_fusion.6), channel_id=1, source_target_pairs={{0,96},{32,192},{64,160},{96,0},{128,224},{160,64},{192,32},{224,1... | collective-permute-start | bytes 147464 | tf_op jit(solution)/shard_map/ppermute | solution.py:371
  38.4 0.0 collective-permute-done.refs_2_
  38.4 0.4 prepare.1
  38.8 0.0 collective-permute-done.7
  38.8 1.7 %collective-permute-start.8 = (f32[16,768]{1,0:T(8,128)S(1)}, f32[16,768]{1,0:T(8,128)S(1)}, u32[]{:S(2)}, u32[]{:S(2)}) collective-permute-start(f32[16,768]{1,0:T(8,128)S(1)} %add.65.refs_3_), channel_id=1, source_target_pairs={{0,2},{2,0},{4,6},{6,4},{8,10},{10,8},{12,14},{14,12},{16,18},{18,... | collective-permute-start | bytes 147464 | tf_op jit(solution)/shard_map/ppermute | solution.py:371
  40.5 0.0 collective-permute-done.6
  40.5 0.0 copy-start.1
  40.5 2.5 %back_x.1 = (f32[2,512,256]{2,1,0:T(8,128)S(1)}, f32[16,2,256]{2,1,0:T(2,128)}) custom-call(s32[16,128]{1,0:T(8,128)S(1)} %get-tuple-element.22.refs_0_, bf16[512,256]{1,0:T(8,128)(2,1)S(1)} %get-tuple-element.26.refs_1_, f32[2,512,256]{2,1,0:T(8,128)S(1)} %get-tuple-element.27.refs_2_, f32[32,384]{1,0:T(8,128)S(1)} %fusion.1.refs_3_), custom_call_target="tpu_custom_call" | custom-call | tf_op jit(solution)/shard_map/back_x/pallas_call | solution.py:281
  43.0 0.0 copy-done.1
  43.0 2.7 %back_y_own.1.refs_5_ = f32[2,512,256]{2,1,0:T(8,128)} custom-call(s32[16,128]{1,0:T(8,128)S(1)} %get-tuple-element.20.refs_0_, bf16[256,256]{1,0:T(8,128)(2,1)S(1)} %copy-done.1, f32[2,512,256]{2,1,0:T(8,128)S(1)} %get-tuple-element.32.refs_2_, f32[16,768]{1,0:T(8,128)S(1)} %add.65.refs_3_), custom_call_target="tpu_custom_call" | custom-call | tf_op jit(solution)/shard_map/back_y_own/pallas_call | solution.py:358
  45.7 0.0 collective-permute-done.8.refs_4_
  45.7 2.7 %back_y_last.1 = (f32[2,512,256]{2,1,0:T(8,128)}, f32[16,2,512]{2,1,0:T(2,128)}) custom-call(s32[16,128]{1,0:T(8,128)S(1)} %get-tuple-element.20.refs_0_, bf16[256,256]{1,0:T(8,128)(2,1)S(1)} %copy-done.1, f32[2,512,256]{2,1,0:T(8,128)S(1)} %get-tuple-element.32.refs_2_, f32[16,768]{1,0:T(8,128)S(1)} %add.65.refs_3_, ...), custom_call_target="tpu_custom_call", output_to_operand_aliasing={{0}: (5, {})} | custom-call | tf_op jit(solution)/shard_map/back_y_last/pallas_call | solution.py:358
  (24 shorter events, 0.2 us)
Async XLA Ops:
  4.0 0.7 %copy-start = (bf16[256,256]{1,0:T(8,128)(2,1)}, bf16[256,256]{1,0:T(8,128)(2,1)S(1)}, u32[]{:S(2)}) copy-start(bf16[256,256]{1,0:T(8,128)(2,1)S(1)} %get-tuple-element.21.refs_1_) | copy-start | bytes 393220
  4.7 4.1 %collective-permute-start.1 = (f32[32,640]{1,0:T(8,128)S(1)}, f32[32,640]{1,0:T(8,128)S(1)}, u32[]{:S(2)}, u32[]{:S(2)}) collective-permute-start(f32[32,640]{1,0:T(8,128)S(1)} %pad_maximum_fusion.1), channel_id=1, source_target_pairs={{0,32},{32,0},{64,96},{96,64},{128,160},{160,128},{192,224},{224,1... | collective-permute-start | bytes 245768 | tf_op jit(solution)/shard_map/ppermute | solution.py:371
  8.8 4.2 %collective-permute-start.2 = (f32[32,640]{1,0:T(8,128)S(1)}, f32[32,640]{1,0:T(8,128)S(1)}, u32[]{:S(2)}, u32[]{:S(2)}) collective-permute-start(f32[32,640]{1,0:T(8,128)S(1)} %pad_maximum_fusion.2), channel_id=1, source_target_pairs={{0,224},{32,64},{64,32},{96,128},{128,96},{160,192},{192,160},{224... | collective-permute-start | bytes 245768 | tf_op jit(solution)/shard_map/ppermute | solution.py:371
  13.1 3.2 %collective-permute-start.3 = (f32[16,1024]{1,0:T(8,128)S(1)}, f32[16,1024]{1,0:T(8,128)S(1)}, u32[]{:S(2)}, u32[]{:S(2)}) collective-permute-start(f32[16,1024]{1,0:T(8,128)S(1)} %pad_maximum_fusion.3), channel_id=1, source_target_pairs={{0,2},{2,0},{4,6},{6,4},{8,10},{10,8},{12,14},{14,12},{16,18},{18,... | collective-permute-start | bytes 196616 | tf_op jit(solution)/shard_map/ppermute | solution.py:371
  13.2 25.1 %collective-permute-start = (bf16[1,512,256]{2,1,0:T(8,128)(2,1)S(1)}, bf16[1,512,256]{2,1,0:T(8,128)(2,1)S(1)}, u32[]{:S(2)}, u32[]{:S(2)}) collective-permute-start(bf16[1,512,256]{2,1,0:T(8,128)(2,1)S(1)} %get-tuple-element.25), channel_id=1, source_target_pairs={{0,1},{1,0},{2,3},{3,2},{4,5},{5,4},{6,7},{7,6},{8,9},{9,8},{10,11... | collective-permute-start | bytes 786440 | tf_op jit(solution)/shard_map/ppermute | solution.py:407
  16.4 6.4 %collective-permute-start.4 = (f32[16,1024]{1,0:T(8,128)S(1)}, f32[16,1024]{1,0:T(8,128)S(1)}, u32[]{:S(2)}, u32[]{:S(2)}) collective-permute-start(f32[16,1024]{1,0:T(8,128)S(1)} %pad_maximum_fusion.4), channel_id=1, source_target_pairs={{0,16},{2,18},{4,20},{6,22},{8,24},{10,26},{12,28},{14,30},{16,0},... | collective-permute-start | bytes 196616 | tf_op jit(solution)/shard_map/ppermute | solution.py:371
  22.8 6.4 %collective-permute-start.5 = (f32[16,1024]{1,0:T(8,128)S(1)}, f32[16,1024]{1,0:T(8,128)S(1)}, u32[]{:S(2)}, u32[]{:S(2)}) collective-permute-start(f32[16,1024]{1,0:T(8,128)S(1)} %pad_maximum_fusion.5), channel_id=1, source_target_pairs={{0,14},{2,4},{4,2},{6,8},{8,6},{10,12},{12,10},{14,0},{16,30},{18,... | collective-permute-start | bytes 196616 | tf_op jit(solution)/shard_map/ppermute | solution.py:371
  29.2 9.5 %collective-permute-start.7 = (f32[16,768]{1,0:T(8,128)S(1)}, f32[16,768]{1,0:T(8,128)S(1)}, u32[]{:S(2)}, u32[]{:S(2)}) collective-permute-start(f32[16,768]{1,0:T(8,128)S(1)} %slice_add_fusion), channel_id=1, source_target_pairs={{0,6},{2,12},{4,10},{6,0},{8,14},{10,4},{12,2},{14,8},{16,22},{18,... | collective-permute-start | bytes 147464 | tf_op jit(solution)/shard_map/ppermute | solution.py:371
  31.0 9.5 %collective-permute-start.6 = (f32[32,384]{1,0:T(8,128)S(1)}, f32[32,384]{1,0:T(8,128)S(1)}, u32[]{:S(2)}, u32[]{:S(2)}) collective-permute-start(f32[32,384]{1,0:T(8,128)S(1)} %pad_maximum_fusion.6), channel_id=1, source_target_pairs={{0,96},{32,192},{64,160},{96,0},{128,224},{160,64},{192,32},{224,1... | collective-permute-start | bytes 147464 | tf_op jit(solution)/shard_map/ppermute | solution.py:371
  38.8 6.9 %collective-permute-start.8 = (f32[16,768]{1,0:T(8,128)S(1)}, f32[16,768]{1,0:T(8,128)S(1)}, u32[]{:S(2)}, u32[]{:S(2)}) collective-permute-start(f32[16,768]{1,0:T(8,128)S(1)} %add.65.refs_3_), channel_id=1, source_target_pairs={{0,2},{2,0},{4,6},{6,4},{8,10},{10,8},{12,14},{14,12},{16,18},{18,... | collective-permute-start | bytes 147464 | tf_op jit(solution)/shard_map/ppermute | solution.py:371
  40.5 2.5 %copy-start.1 = (bf16[256,256]{1,0:T(8,128)(2,1)S(1)}, bf16[256,256]{1,0:T(8,128)(2,1)}, u32[]{:S(2)}) copy-start(bf16[256,256]{1,0:T(8,128)(2,1)} %copy-done) | copy-start | bytes 393220

commit v5 on v4

--- a/solution.py
+++ b/solution.py
@@ -8,6 +8,8 @@
 
 LEVELS = 16
 RING = 8
+CHUNKS = 2
+LIMIT = pltpu.CompilerParams(vmem_limit_bytes=8 * 1024 * 1024)
 SMEM = pltpu.SMEM
 VMEM = pltpu.VMEM
 F32 = jnp.float32
@@ -35,11 +37,37 @@
     return slopes * (block - blocks // 2) + jnp.minimum(slopes, 0)
 
 
-def barrel(value, amounts, bits):
-    for bit in range(bits):
-        taken = ((amounts >> bit) & 1) == 1
-        value = jnp.where(taken, pltpu.roll(value, 1 << bit, 1), value)
-    return value
+def tiles_of(value):
+    return [value[:, k : k + 128] for k in range(0, value.shape[1], 128)]
+
+
+def shifted(tiles, amount, count):
+    if amount == 0:
+        return tiles[:count]
+    lane = lax.broadcasted_iota(jnp.int32, tiles[0].shape, 1)
+    rolled = [None if tile is None else pltpu.roll(tile, amount, 1) for tile in tiles]
+    out = []
+    for k in range(count):
+        here, before = rolled[k], rolled[k - 1]
+        if here is None and before is None:
+            out.append(None)
+        elif here is None:
+            out.append(jnp.where(lane < amount, before, 0.0))
+        elif before is None:
+            out.append(jnp.where(lane < amount, 0.0, here))
+        else:
+            out.append(jnp.where(lane < amount, before, here))
+    return out
+
+
+def barrel(tiles, amounts):
+    lane = lax.broadcasted_iota(jnp.int32, amounts.shape, 1)
+    low = amounts & 127
+    source = (lane - amounts) & 127
+    zero = jnp.zeros(amounts.shape, F32)
+    turned = [zero if tile is None else jnp.take_along_axis(tile, source, axis=1) for tile in tiles]
+    near = [jnp.where(lane < low, turned[k - 1], turned[k]) for k in range(len(tiles))]
+    return [jnp.where(amounts >= 128, near[k - 1], near[k]) for k in range(len(tiles))]
 
 
 def offsets(slopes, block, blocks, cells):
@@ -59,6 +87,12 @@
     return pltpu.with_memory_space_constraint(value, VMEM)
 
 
+def in_hbm(value):
+    if interpreted():
+        return value
+    return pltpu.with_memory_space_constraint(value, pltpu.HBM)
+
+
 def out_vmem(shape, dtype):
     if interpreted():
         return jax.ShapeDtypeStruct(shape, dtype)
@@ -66,7 +100,7 @@
 
 
 def anywhere():
-    return pl.BlockSpec(memory_space=pl.ANY)
+    return pl.BlockSpec(memory_space=pltpu.HBM)
 
 
 def vmem():
@@ -95,19 +129,22 @@
     bins = volume_ref.shape[2 - family]
     width = out_ref.shape[1]
     first = (block == 0).astype(F32)
-    amounts = tiled(pad - lowest_shift(slopes, block, blocks), width)
-    bits = max(1, (2 * pad).bit_length() - 1)
-    empty = jnp.zeros((views, width - bins), F32)
+    amounts = pad - LEVELS + 1 - lowest_shift(slopes, block, blocks)
+    count = width // 128
+    data = bins // 128
     for plane in range(planes):
         dims = (((1,), (family,)), ((), ()))
         summands = lax.dot_general(table_ref[...], volume_ref[plane], dims, preferred_element_type=F32)
-        total = None
-        for level in reversed(range(LEVELS)):
-            piece = jnp.concatenate([summands[level * views : (level + 1) * views, :], empty], axis=1)
-            total = piece if total is None else pltpu.roll(total, width - 1, 1) + piece
-        total = barrel(total, amounts, bits) * scale
-        known = jnp.concatenate([rows_ref[plane * views : (plane + 1) * views, :] * first, empty], axis=1)
-        total = on_grid(total - pltpu.roll(known, pad, 1))
+        total = [None] * count
+        for level in range(LEVELS):
+            piece = tiles_of(summands[level * views : (level + 1) * views, :]) + [None] * (count - data)
+            piece = shifted(piece, LEVELS - 1 - level, count)
+            total = [p if t is None else t if p is None else t + p for t, p in zip(total, piece)]
+        total = jnp.concatenate(barrel(total, amounts), axis=1) * scale
+        known = tiles_of(rows_ref[plane * views : (plane + 1) * views, :] * first) + [None] * (count - data)
+        known = [None] * (pad // 128) + shifted(known, pad % 128, count - pad // 128)
+        known = jnp.concatenate([jnp.zeros((views, 128), F32) if k is None else k for k in known], axis=1)
+        total = on_grid(total - known)
         out_ref[plane * views : (plane + 1) * views, :] = in_roles(total, odd)
 
 
@@ -192,9 +229,10 @@
             VMEM((planes * views, cells_x), F32),
             pltpu.SemaphoreType.DMA((5,)),
         ],
+        compiler_params=LIMIT,
         interpret=interpreted(),
         name="forward",
-    )(slopes, volume, measured_x, measured_y)
+    )(*(in_hbm(value) for value in (slopes, volume, measured_x, measured_y)))
 
 
 def half_of(index):
@@ -204,20 +242,26 @@
 def spread_into(value, slopes, block, blocks, other, others, pad, scale, spread_ref):
     views, width = value.shape
     bins = width - 2 * pad
-    bits = max(1, (2 * pad).bit_length() - 1)
     place = lax.broadcasted_iota(jnp.int32, (views, width), 1)
     inside = (place >= jnp.where(other == 0, pad, 0)) & (place < jnp.where(other == others - 1, pad + bins, width))
     value = jnp.where(inside, value * scale, 0.0).astype(BF16).astype(F32)
-    amounts = tiled(lowest_shift(slopes, block, blocks) + pad, width)
-    value = pltpu.roll(barrel(value, amounts, bits), width - 2 * pad, 1)
+    tiles = barrel(tiles_of(value), lowest_shift(slopes, block, blocks) + pad)
+    skip = 2 * pad // 128
+    tiles = tiles[skip:] + tiles[:skip]
     for level in range(LEVELS):
-        spread_ref[level * views : (level + 1) * views, :] = value[:, :bins].astype(BF16)
-        value = pltpu.roll(value, 1, 1)
+        piece = jnp.concatenate(shifted(tiles, level, bins // 128), axis=1)
+        spread_ref[level * views : (level + 1) * views, :] = piece.astype(BF16)
 
 
 def middle(value, pad):
-    width = value.shape[1]
-    return pltpu.roll(value, width - pad, 1)[:, : width - 2 * pad]
+    tiles = tiles_of(value)
+    skip = pad // 128
+    tiles = tiles[skip:] + tiles[:skip]
+    count = (value.shape[1] - 2 * pad) // 128
+    if pad % 128 == 0:
+        return jnp.concatenate(tiles[:count], axis=1)
+    tiles = tiles[1:] + tiles[:1]
+    return jnp.concatenate(shifted(tiles, 128 - pad % 128, count), axis=1)
 
 
 def prepare_kernel(lane_ref, volume_ref, beside_ref, table_ref, base_ref, *, blocks):
@@ -247,6 +291,7 @@
         out_shape=(out_vmem((volume.shape[1], lane.shape[1]), BF16), out_vmem(volume.shape, F32)),
         in_specs=[vmem()] * 3,
         out_specs=(vmem(), vmem()),
+        compiler_params=LIMIT,
         interpret=interpreted(),
         name="prepare",
     )(*(in_vmem(value) for value in (lane, volume, beside)))
@@ -289,6 +334,7 @@
             VMEM((views, planes, bins), F32),
             pltpu.SemaphoreType.DMA,
         ],
+        compiler_params=LIMIT,
         interpret=interpreted(),
         name="back_x",
     )(*(in_vmem(value) for value in (column, table, base, residual)))
@@ -310,10 +356,15 @@
     value = from_roles(other_ref[...] if last else half_ref[...], flip)
     spread_into(value, column_ref[...], block, blocks, other, others, pad, scale, spread_ref)
     dims = (((0,), (0,)), ((), ()))
-    back = lax.dot_general(spread_ref[...], table_ref[...], dims, preferred_element_type=F32)
-    sum_ref[...] = partial_ref[pl.ds(plane, 1)] + back[None]
-    store = pltpu.make_async_copy(sum_ref, out_hbm.at[pl.ds(plane, 1)], sems.at[1])
-    store.start()
+    stores = []
+    rows = sum_ref.shape[1] // CHUNKS
+    for c in range(CHUNKS):
+        part = pl.ds(c * rows, rows)
+        back = lax.dot_general(spread_ref[:, c * rows : (c + 1) * rows], table_ref[...], dims, preferred_element_type=F32)
+        sum_ref[:, part, :] = partial_ref[pl.ds(plane, 1), part, :] + back[None]
+        store = pltpu.make_async_copy(sum_ref.at[:, part], out_hbm.at[pl.ds(plane, 1), part], sems.at[1 + c])
+        store.start()
+        stores.append(store)
     if last:
         odd = mine == 1
         rows_ref[:views, :] = middle(from_roles(jnp.where(odd, other_ref[...], half_ref[...]), flip), pad)
@@ -324,7 +375,8 @@
         also = pltpu.make_async_copy(rest_ref, rest_hbm, sems.at[0])
         also.start()
         also.wait()
-    store.wait()
+    for store in stores:
+        store.wait()
 
 
 def back_y(column, table, partial, half, rest, blocks, others, pad, scale):
@@ -351,7 +403,7 @@
         VMEM((1, bins, cells), F32),
         VMEM((LEVELS * views, bins), BF16),
         VMEM((planes * views, bins), F32),
-        pltpu.SemaphoreType.DMA((2,)),
+        pltpu.SemaphoreType.DMA((1 + CHUNKS,)),
     ]
     if last:
         scratch.append(VMEM((views, planes, bins), F32))
@@ -362,6 +414,7 @@
         out_specs=tuple(out_specs),
         scratch_shapes=scratch,
         input_output_aliases=aliases,
+        compiler_params=LIMIT,
         interpret=interpreted(),
         name="back_y_last" if last else "back_y_own",
     )(*operands)

time: 48.5 us -> 42.3 us (0.87)
  Pallas kernels: 11.6 us -> 6.01 us
  local copies, waits for them, and re-layouts: 0.64 us -> 0.02 us
    pallas_call x2, Pallas kernels: 5.43 us -> 2.59 us  [back_y(): pl.pallas_call(body, out_shape=tuple(shapes), in_specs=specs, out_specs=t...]
    pallas_call x1, Pallas kernels: 3.36 us -> 1.92 us  [forward(): pl.pallas_call(body, out_shape=(out_vmem((planes * views, cells_y + 2 * p...]
    pallas_call x1, Pallas kernels: 2.45 us -> 1.09 us  [back_x(): pl.pallas_call(body, out_shape=(out_vmem(base.shape, F32), jax.ShapeDtype...]
    unnamed x4 -> x0, local copies, waits for them, and re-layouts: 0.63 us -> none
  transfers between devices with their start and end apart: 9 -> 9, of which waited for: 5 -> 5; matrix products, arithmetic and copies ran while one was open for 0% -> 0% of each run, Pallas kernels for 11% -> 7%
where the time goes in v5:
time: 42.3 us; the launch traced here: 42.2 us
  starting transfers between devices  21.4 us (51%)
  waiting for transfers between devices  13.8 us (33%)
  Pallas kernels  6.01 us (14%)
  between operations  0.83 us (2%)
    ppermute x8, starting transfers between devices, exchange(): lax.ppermute(value, axis, [(i, partner(i)) for i in range(lax.axis_size(a...  20.3 us
    ppermute x8, waiting for transfers between devices, exchange(): lax.ppermute(value, axis, [(i, partner(i)) for i in range(lax.axis_size(a...  13.8 us
    pallas_call x2, Pallas kernels, back_y(): pl.pallas_call(body, out_shape=tuple(shapes), in_specs=specs, out_specs=t...  2.59 us
    pallas_call x1, Pallas kernels, forward(): pl.pallas_call(body, out_shape=(out_vmem((planes * views, cells_y + 2 * p...  1.92 us
    ppermute x1, starting transfers between devices, steps(): beside = lax.ppermute(near, 'pa', [(0, 1), (1, 0)])  1.13 us
    pallas_call x1, Pallas kernels, back_x(): pl.pallas_call(body, out_shape=(out_vmem(base.shape, F32), jax.ShapeDtype...  1.09 us
  transfers between devices with their start and end apart: 9, of which 5 were waited for; matrix products, arithmetic and copies ran while one was open for 0% of the time, Pallas kernels for 7%

profile of v5, /device:TPU:1, one launch (start us, length us, event | category | flops | bytes accessed | tf_op | source)
XLA Modules:
  0.0 42.2 jit_solution(11608785390274817052)
XLA Ops:
  0.6 1.9 %forward.1 = (f32[32,384]{1,0:T(8,128)S(1)}, f32[32,768]{1,0:T(8,128)S(1)}, bf16[256,256]{1,0:T(8,128)(2,1)S(1)}, bf16[1,512,256]{2,1,0:T(8,128)(2,1)S(1)}, bf16...) custom-call(s32[2,16]{1,0:T(2,128)} %refs_0_.1, ...), custom_call_target="tpu_custom_call" | custom-call | tf_op jit(solution)/shard_map/forward/pallas_call | solution.py:209
  2.6 3.3 %collective-permute-start.1 = (f32[32,640]{1,0:T(8,128)S(1)}, f32[32,640]{1,0:T(8,128)S(1)}, u32[]{:S(2)}, u32[]{:S(2)}) collective-permute-start(f32[32,640]{1,0:T(8,128)S(1)} %pad_maximum_fusion.1), channel_id=1, source_target_pairs={{0,32},{32,0},{64,96},{96,64},{128,160},{160,128},{192,224},{224,1... | collective-permute-start | bytes 245768 | tf_op jit(solution)/shard_map/ppermute | solution.py:424
  5.9 0.9 %collective-permute-done.1 = f32[32,640]{1,0:T(8,128)S(1)} collective-permute-done((f32[32,640]{1,0:T(8,128)S(1)}, f32[32,640]{1,0:T(8,128)S(1)}, u32[]{:S(2)}, u32[]{:S(2)}) %collective-permute-start.1) | collective-permute-done | bytes 81952 | tf_op jit(solution)/shard_map/ppermute | solution.py:424
  6.8 0.1 collective-permute-start.2
  7.0 4.1 %collective-permute-done.2 = f32[32,640]{1,0:T(8,128)S(1)} collective-permute-done((f32[32,640]{1,0:T(8,128)S(1)}, f32[32,640]{1,0:T(8,128)S(1)}, u32[]{:S(2)}, u32[]{:S(2)}) %collective-permute-start.2) | collective-permute-done | bytes 81952 | tf_op jit(solution)/shard_map/ppermute | solution.py:424
  11.2 0.1 collective-permute-start.3
  11.3 1.1 %collective-permute-start = (bf16[1,512,256]{2,1,0:T(8,128)(2,1)S(1)}, bf16[1,512,256]{2,1,0:T(8,128)(2,1)S(1)}, u32[]{:S(2)}, u32[]{:S(2)}) collective-permute-start(bf16[1,512,256]{2,1,0:T(8,128)(2,1)S(1)} %get-tuple-element.25), channel_id=1, source_target_pairs={{0,1},{1,0},{2,3},{3,2},{4,5},{5,4},{6,7},{7,6},{8,9},{9,8},{10,11... | collective-permute-start | bytes 786440 | tf_op jit(solution)/shard_map/ppermute | solution.py:460
  12.4 2.0 %collective-permute-done.3 = f32[16,1024]{1,0:T(8,128)S(1)} collective-permute-done((f32[16,1024]{1,0:T(8,128)S(1)}, f32[16,1024]{1,0:T(8,128)S(1)}, u32[]{:S(2)}, u32[]{:S(2)}) %collective-permute-start.3) | collective-permute-done | bytes 65568 | tf_op jit(solution)/shard_map/ppermute | solution.py:424
  14.4 1.3 %collective-permute-start.4 = (f32[16,1024]{1,0:T(8,128)S(1)}, f32[16,1024]{1,0:T(8,128)S(1)}, u32[]{:S(2)}, u32[]{:S(2)}) collective-permute-start(f32[16,1024]{1,0:T(8,128)S(1)} %pad_maximum_fusion.4), channel_id=1, source_target_pairs={{0,16},{2,18},{4,20},{6,22},{8,24},{10,26},{12,28},{14,30},{16,0},... | collective-permute-start | bytes 196616 | tf_op jit(solution)/shard_map/ppermute | solution.py:424
  15.7 5.1 %collective-permute-done.4 = f32[16,1024]{1,0:T(8,128)S(1)} collective-permute-done((f32[16,1024]{1,0:T(8,128)S(1)}, f32[16,1024]{1,0:T(8,128)S(1)}, u32[]{:S(2)}, u32[]{:S(2)}) %collective-permute-start.4) | collective-permute-done | bytes 65568 | tf_op jit(solution)/shard_map/ppermute | solution.py:424
  20.8 4.8 %collective-permute-start.5 = (f32[16,1024]{1,0:T(8,128)S(1)}, f32[16,1024]{1,0:T(8,128)S(1)}, u32[]{:S(2)}, u32[]{:S(2)}) collective-permute-start(f32[16,1024]{1,0:T(8,128)S(1)} %pad_maximum_fusion.5), channel_id=1, source_target_pairs={{0,14},{2,4},{4,2},{6,8},{8,6},{10,12},{12,10},{14,0},{16,30},{18,... | collective-permute-start | bytes 196616 | tf_op jit(solution)/shard_map/ppermute | solution.py:424
  25.6 1.6 %collective-permute-done.5 = f32[16,1024]{1,0:T(8,128)S(1)} collective-permute-done((f32[16,1024]{1,0:T(8,128)S(1)}, f32[16,1024]{1,0:T(8,128)S(1)}, u32[]{:S(2)}, u32[]{:S(2)}) %collective-permute-start.5) | collective-permute-done | bytes 65568 | tf_op jit(solution)/shard_map/ppermute | solution.py:424
  27.3 1.7 %collective-permute-start.7 = (f32[16,768]{1,0:T(8,128)S(1)}, f32[16,768]{1,0:T(8,128)S(1)}, u32[]{:S(2)}, u32[]{:S(2)}) collective-permute-start(f32[16,768]{1,0:T(8,128)S(1)} %slice_add_fusion), channel_id=1, source_target_pairs={{0,6},{2,12},{4,10},{6,0},{8,14},{10,4},{12,2},{14,8},{16,22},{18,... | collective-permute-start | bytes 147464 | tf_op jit(solution)/shard_map/ppermute | solution.py:424
  29.0 7.4 %collective-permute-start.6 = (f32[32,384]{1,0:T(8,128)S(1)}, f32[32,384]{1,0:T(8,128)S(1)}, u32[]{:S(2)}, u32[]{:S(2)}) collective-permute-start(f32[32,384]{1,0:T(8,128)S(1)} %pad_maximum_fusion.6), channel_id=1, source_target_pairs={{0,96},{32,192},{64,160},{96,0},{128,224},{160,64},{192,32},{224,1... | collective-permute-start | bytes 147464 | tf_op jit(solution)/shard_map/ppermute | solution.py:424
  36.4 0.0 collective-permute-done.refs_2_
  36.4 0.4 prepare.1
  36.8 0.0 collective-permute-done.7
  36.8 1.7 %collective-permute-start.8 = (f32[16,768]{1,0:T(8,128)S(1)}, f32[16,768]{1,0:T(8,128)S(1)}, u32[]{:S(2)}, u32[]{:S(2)}) collective-permute-start(f32[16,768]{1,0:T(8,128)S(1)} %add.65.refs_3_), channel_id=1, source_target_pairs={{0,2},{2,0},{4,6},{6,4},{8,10},{10,8},{12,14},{14,12},{16,18},{18,... | collective-permute-start | bytes 147464 | tf_op jit(solution)/shard_map/ppermute | solution.py:424
  38.5 0.0 collective-permute-done.6
  38.5 1.1 %back_x.1 = (f32[2,512,256]{2,1,0:T(8,128)S(1)}, f32[16,2,256]{2,1,0:T(2,128)}) custom-call(s32[16,128]{1,0:T(8,128)S(1)} %get-tuple-element.22.refs_0_, bf16[512,256]{1,0:T(8,128)(2,1)S(1)} %get-tuple-element.26.refs_1_, f32[2,512,256]{2,1,0:T(8,128)S(1)} %get-tuple-element.27.refs_2_, f32[32,384]{1,0:T(8,128)S(1)} %fusion.1.refs_3_), custom_call_target="tpu_custom_call" | custom-call | tf_op jit(solution)/shard_map/back_x/pallas_call | solution.py:326
  39.6 1.3 %back_y_own.1.refs_5_ = f32[2,512,256]{2,1,0:T(8,128)} custom-call(s32[16,128]{1,0:T(8,128)S(1)} %get-tuple-element.20.refs_0_, bf16[256,256]{1,0:T(8,128)(2,1)S(1)} %get-tuple-element.21.refs_1_, f32[2,512,256]{2,1,0:T(8,128)S(1)} %get-tuple-element.32.refs_2_, f32[16,768]{1,0:T(8,128)S(1)} %add.65.refs_3_), custom_call_target="tpu_custom_call" | custom-call | tf_op jit(solution)/shard_map/back_y_own/pallas_call | solution.py:410
  40.9 0.0 collective-permute-done.8.refs_4_
  40.9 1.3 %back_y_last.1 = (f32[2,512,256]{2,1,0:T(8,128)}, f32[16,2,512]{2,1,0:T(2,128)}) custom-call(s32[16,128]{1,0:T(8,128)S(1)} %get-tuple-element.20.refs_0_, bf16[256,256]{1,0:T(8,128)(2,1)S(1)} %get-tuple-element.21.refs_1_, f32[2,512,256]{2,1,0:T(8,128)S(1)} %get-tuple-element.32.refs_2_, ...), custom_call_target="tpu_custom_call", output_to_operand_aliasing={{0}: (5, {})} | custom-call | tf_op jit(solution)/shard_map/back_y_last/pallas_call | solution.py:410
  (24 shorter events, 0.2 us)
Async XLA Ops:
  2.6 4.2 %collective-permute-start.1 = (f32[32,640]{1,0:T(8,128)S(1)}, f32[32,640]{1,0:T(8,128)S(1)}, u32[]{:S(2)}, u32[]{:S(2)}) collective-permute-start(f32[32,640]{1,0:T(8,128)S(1)} %pad_maximum_fusion.1), channel_id=1, source_target_pairs={{0,32},{32,0},{64,96},{96,64},{128,160},{160,128},{192,224},{224,1... | collective-permute-start | bytes 245768 | tf_op jit(solution)/shard_map/ppermute | solution.py:424
  6.8 4.2 %collective-permute-start.2 = (f32[32,640]{1,0:T(8,128)S(1)}, f32[32,640]{1,0:T(8,128)S(1)}, u32[]{:S(2)}, u32[]{:S(2)}) collective-permute-start(f32[32,640]{1,0:T(8,128)S(1)} %pad_maximum_fusion.2), channel_id=1, source_target_pairs={{0,224},{32,64},{64,32},{96,128},{128,96},{160,192},{192,160},{224... | collective-permute-start | bytes 245768 | tf_op jit(solution)/shard_map/ppermute | solution.py:424
  11.2 3.2 %collective-permute-start.3 = (f32[16,1024]{1,0:T(8,128)S(1)}, f32[16,1024]{1,0:T(8,128)S(1)}, u32[]{:S(2)}, u32[]{:S(2)}) collective-permute-start(f32[16,1024]{1,0:T(8,128)S(1)} %pad_maximum_fusion.3), channel_id=1, source_target_pairs={{0,2},{2,0},{4,6},{6,4},{8,10},{10,8},{12,14},{14,12},{16,18},{18,... | collective-permute-start | bytes 196616 | tf_op jit(solution)/shard_map/ppermute | solution.py:424
  11.3 25.1 %collective-permute-start = (bf16[1,512,256]{2,1,0:T(8,128)(2,1)S(1)}, bf16[1,512,256]{2,1,0:T(8,128)(2,1)S(1)}, u32[]{:S(2)}, u32[]{:S(2)}) collective-permute-start(bf16[1,512,256]{2,1,0:T(8,128)(2,1)S(1)} %get-tuple-element.25), channel_id=1, source_target_pairs={{0,1},{1,0},{2,3},{3,2},{4,5},{5,4},{6,7},{7,6},{8,9},{9,8},{10,11... | collective-permute-start | bytes 786440 | tf_op jit(solution)/shard_map/ppermute | solution.py:460
  14.4 6.4 %collective-permute-start.4 = (f32[16,1024]{1,0:T(8,128)S(1)}, f32[16,1024]{1,0:T(8,128)S(1)}, u32[]{:S(2)}, u32[]{:S(2)}) collective-permute-start(f32[16,1024]{1,0:T(8,128)S(1)} %pad_maximum_fusion.4), channel_id=1, source_target_pairs={{0,16},{2,18},{4,20},{6,22},{8,24},{10,26},{12,28},{14,30},{16,0},... | collective-permute-start | bytes 196616 | tf_op jit(solution)/shard_map/ppermute | solution.py:424
  20.8 6.4 %collective-permute-start.5 = (f32[16,1024]{1,0:T(8,128)S(1)}, f32[16,1024]{1,0:T(8,128)S(1)}, u32[]{:S(2)}, u32[]{:S(2)}) collective-permute-start(f32[16,1024]{1,0:T(8,128)S(1)} %pad_maximum_fusion.5), channel_id=1, source_target_pairs={{0,14},{2,4},{4,2},{6,8},{8,6},{10,12},{12,10},{14,0},{16,30},{18,... | collective-permute-start | bytes 196616 | tf_op jit(solution)/shard_map/ppermute | solution.py:424
  27.3 9.5 %collective-permute-start.7 = (f32[16,768]{1,0:T(8,128)S(1)}, f32[16,768]{1,0:T(8,128)S(1)}, u32[]{:S(2)}, u32[]{:S(2)}) collective-permute-start(f32[16,768]{1,0:T(8,128)S(1)} %slice_add_fusion), channel_id=1, source_target_pairs={{0,6},{2,12},{4,10},{6,0},{8,14},{10,4},{12,2},{14,8},{16,22},{18,... | collective-permute-start | bytes 147464 | tf_op jit(solution)/shard_map/ppermute | solution.py:424
  29.0 9.5 %collective-permute-start.6 = (f32[32,384]{1,0:T(8,128)S(1)}, f32[32,384]{1,0:T(8,128)S(1)}, u32[]{:S(2)}, u32[]{:S(2)}) collective-permute-start(f32[32,384]{1,0:T(8,128)S(1)} %pad_maximum_fusion.6), channel_id=1, source_target_pairs={{0,96},{32,192},{64,160},{96,0},{128,224},{160,64},{192,32},{224,1... | collective-permute-start | bytes 147464 | tf_op jit(solution)/shard_map/ppermute | solution.py:424
  36.8 4.1 %collective-permute-start.8 = (f32[16,768]{1,0:T(8,128)S(1)}, f32[16,768]{1,0:T(8,128)S(1)}, u32[]{:S(2)}, u32[]{:S(2)}) collective-permute-start(f32[16,768]{1,0:T(8,128)S(1)} %add.65.refs_3_), channel_id=1, source_target_pairs={{0,2},{2,0},{4,6},{6,4},{8,10},{10,8},{12,14},{14,12},{16,18},{18,... | collective-permute-start | bytes 147464 | tf_op jit(solution)/shard_map/ppermute | solution.py:424

commit v6 on v5

--- a/solution.py
+++ b/solution.py
@@ -297,27 +297,78 @@
     )(*(in_vmem(value) for value in (lane, volume, beside)))
 
 
-def back_x_kernel(column_ref, table_ref, base_ref, residual_ref, out_ref, rest_hbm, spread_ref, rows_ref, rest_ref, sem, *, blocks, others, pad, scale):
-    planes, _, _ = base_ref.shape
+def store_rows(values, rest_ref, rows_ref):
+    planes, views = len(values), rest_ref.shape[0]
+    for plane in range(planes):
+        rows_ref[plane * views : (plane + 1) * views, :] = values[plane]
+    for plane in range(planes):
+        for v in range(views):
+            rest_ref[v, plane : plane + 1, :] = rows_ref[plane * views + v : plane * views + v + 1, :]
+
+
+def back_own_kernel(column_ref, table_ref, half_ref, out_ref, spread_ref, *, blocks, others, pad, scale):
+    block, other = lax.axis_index("gy"), lax.axis_index("gx")
+    value = from_roles(half_ref[...], other % 2 == 1)
+    spread_into(value, column_ref[...], block, blocks, other, others, pad, scale, spread_ref)
+    dims = (((0,), (0,)), ((), ()))
+    out_ref[...] = lax.dot_general(spread_ref[...], table_ref[...], dims, preferred_element_type=F32)
+
+
+def back_own(column, table, half, bins, blocks, others, pad, scale):
+    def body(*refs):
+        back_own_kernel(*refs, blocks=blocks, others=others, pad=pad, scale=scale)
+
+    return pl.pallas_call(
+        body,
+        out_shape=out_vmem((bins, table.shape[1]), F32),
+        in_specs=[vmem()] * 3,
+        out_specs=vmem(),
+        scratch_shapes=[VMEM((table.shape[0], bins), BF16)],
+        compiler_params=LIMIT,
+        interpret=interpreted(),
+        name="back_own",
+    )(*(in_vmem(value) for value in (column, table, half)))
+
+
+def back_x_kernel(
+    column_ref, table_ref, base_ref, residual_ref, own_ref, out_hbm, rest_hbm, partial_ref,
+    spread_ref, sum_ref, rows_ref, rest_ref, sems, *, blocks, others, pad, scale,
+):
+    planes, cells, _ = base_ref.shape
     views = column_ref.shape[0]
     block, other = lax.axis_index("gx"), lax.axis_index("gy")
     column = column_ref[...]
-    residuals = [from_roles(residual_ref[p * views : (p + 1) * views, :], other % 2 == 1) for p in range(planes)]
-    for plane in range(planes):
-        rows_ref[plane * views : (plane + 1) * views, :] = middle(residuals[plane], pad)
-    for plane in range(planes):
-        for v in range(views):
-            rest_ref[v, plane : plane + 1, :] = rows_ref[plane * views + v : plane * views + v + 1, :]
-    store = pltpu.make_async_copy(rest_ref, rest_hbm, sem)
-    store.start()
-    for plane in range(planes):
-        spread_into(residuals[plane], column, block, blocks, other, others, pad, scale, spread_ref)
-        out_ref[plane] = base_ref[plane] + jnp.dot(table_ref[...], spread_ref[...], preferred_element_type=F32)
-    store.wait()
-
-
-def back_x(column, table, base, residual, blocks, others, pad, scale):
-    planes, _, bins = base.shape
+    flip = other % 2 == 1
+    mine = half_of(other)
+    size = cells // CHUNKS
+    copies = []
+    for last in range(planes):
+        plane = 1 - mine if last else mine
+        start = pl.multiple_of(plane * views, views)
+        residual = from_roles(residual_ref[pl.ds(start, views), :], flip)
+        spread_into(residual, column, block, blocks, other, others, pad, scale, spread_ref)
+        for c in range(CHUNKS):
+            part = pl.ds(c * size, size)
+            value = jnp.dot(table_ref[part, :], spread_ref[...], preferred_element_type=F32)
+            value = base_ref[pl.ds(plane, 1), part, :] + value[None]
+            if last:
+                partial_ref[part, :] = value[0]
+            else:
+                sum_ref[:, part, :] = value + own_ref[part, :][None]
+                copies.append(
+                    pltpu.make_async_copy(sum_ref.at[:, part], out_hbm.at[pl.ds(plane, 1), part], sems.at[1 + c])
+                )
+                copies[-1].start()
+    residuals = [from_roles(residual_ref[p * views : (p + 1) * views, :], flip) for p in range(planes)]
+    store_rows([middle(residual, pad) for residual in residuals], rest_ref, rows_ref)
+    copies.append(pltpu.make_async_copy(rest_ref, rest_hbm, sems.at[0]))
+    copies[-1].start()
+    for copy in copies:
+        copy.wait()
+
+
+def back_x(column, table, base, residual, own, blocks, others, pad, scale):
+    planes, cells, bins = base.shape
     views = column.shape[0]
 
     def body(*refs):
@@ -325,99 +376,83 @@
 
     return pl.pallas_call(
         body,
-        out_shape=(out_vmem(base.shape, F32), jax.ShapeDtypeStruct((views, planes, bins), F32)),
-        in_specs=[vmem()] * 4,
-        out_specs=(vmem(), anywhere()),
+        out_shape=(
+            jax.ShapeDtypeStruct(base.shape, F32),
+            jax.ShapeDtypeStruct((views, planes, bins), F32),
+            out_vmem((cells, bins), F32),
+        ),
+        in_specs=[vmem()] * 5,
+        out_specs=(anywhere(), anywhere(), vmem()),
         scratch_shapes=[
             VMEM((LEVELS * views, bins), BF16),
+            VMEM((1, cells, bins), F32),
             VMEM((planes * views, bins), F32),
             VMEM((views, planes, bins), F32),
-            pltpu.SemaphoreType.DMA,
+            pltpu.SemaphoreType.DMA((1 + CHUNKS,)),
         ],
         compiler_params=LIMIT,
         interpret=interpreted(),
         name="back_x",
-    )(*(in_vmem(value) for value in (column, table, base, residual)))
-
-
-def back_y_kernel(*refs, last, blocks, others, pad, scale, views):
-    column_ref, table_ref, partial_ref, half_ref = refs[:4]
-    rest = list(refs[4:])
-    if last:
-        other_ref = rest.pop(0)
-        rest.pop(0)
-        rest_hbm = rest.pop(1)
-        rest_ref = rest.pop()
-    out_hbm, sum_ref, spread_ref, rows_ref, sems = rest
+    )(*(in_vmem(value) for value in (column, table, base, residual, own)))
+
+
+def back_last_kernel(
+    column_ref, table_ref, partial_ref, half_ref, other_ref, gradient_hbm, out_hbm, rest_hbm,
+    spread_ref, sum_ref, rows_ref, rest_ref, sems, *, blocks, others, pad, scale,
+):
+    bins, _ = partial_ref.shape
     block, other = lax.axis_index("gy"), lax.axis_index("gx")
-    mine = half_of(lax.axis_index("gy"))
     flip = other % 2 == 1
-    plane = 1 - mine if last else mine
-    value = from_roles(other_ref[...] if last else half_ref[...], flip)
+    mine = half_of(block)
+    value = from_roles(other_ref[...], flip)
     spread_into(value, column_ref[...], block, blocks, other, others, pad, scale, spread_ref)
     dims = (((0,), (0,)), ((), ()))
-    stores = []
-    rows = sum_ref.shape[1] // CHUNKS
+    size = bins // CHUNKS
+    copies = []
     for c in range(CHUNKS):
-        part = pl.ds(c * rows, rows)
-        back = lax.dot_general(spread_ref[:, c * rows : (c + 1) * rows], table_ref[...], dims, preferred_element_type=F32)
-        sum_ref[:, part, :] = partial_ref[pl.ds(plane, 1), part, :] + back[None]
-        store = pltpu.make_async_copy(sum_ref.at[:, part], out_hbm.at[pl.ds(plane, 1), part], sems.at[1 + c])
-        store.start()
-        stores.append(store)
-    if last:
-        odd = mine == 1
-        rows_ref[:views, :] = middle(from_roles(jnp.where(odd, other_ref[...], half_ref[...]), flip), pad)
-        rows_ref[views:, :] = middle(from_roles(jnp.where(odd, half_ref[...], other_ref[...]), flip), pad)
-        for p in range(2):
-            for v in range(views):
-                rest_ref[v, p : p + 1, :] = rows_ref[p * views + v : p * views + v + 1, :]
-        also = pltpu.make_async_copy(rest_ref, rest_hbm, sems.at[0])
-        also.start()
-        also.wait()
-    for store in stores:
-        store.wait()
-
-
-def back_y(column, table, partial, half, rest, blocks, others, pad, scale):
-    planes, bins, cells = partial.shape
+        part = pl.ds(c * size, size)
+        back = lax.dot_general(spread_ref[:, c * size : (c + 1) * size], table_ref[...], dims, preferred_element_type=F32)
+        sum_ref[:, part, :] = (partial_ref[part, :] + back)[None]
+        copies.append(pltpu.make_async_copy(sum_ref.at[:, part], out_hbm.at[pl.ds(1 - mine, 1), part], sems.at[1 + c]))
+        copies[-1].start()
+    odd = mine == 1
+    low = from_roles(jnp.where(odd, other_ref[...], half_ref[...]), flip)
+    high = from_roles(jnp.where(odd, half_ref[...], other_ref[...]), flip)
+    store_rows([middle(low, pad), middle(high, pad)], rest_ref, rows_ref)
+    copies.append(pltpu.make_async_copy(rest_ref, rest_hbm, sems.at[0]))
+    copies[-1].start()
+    for copy in copies:
+        copy.wait()
+
+
+def back_last(column, table, partial, half, other, gradient, blocks, others, pad, scale):
+    bins, cells = partial.shape
+    planes = gradient.shape[0]
     views = column.shape[0]
-    last = rest is not None
 
     def body(*refs):
-        back_y_kernel(*refs, last=last, blocks=blocks, others=others, pad=pad, scale=scale, views=views)
-
-    operands = [in_vmem(column), in_vmem(table), in_vmem(partial), in_vmem(half)]
-    specs = [vmem()] * 4
-    shapes = [jax.ShapeDtypeStruct(partial.shape, F32)]
-    out_specs = [anywhere()]
-    aliases = {}
-    if last:
-        other, gradient = rest
-        operands += [in_vmem(other), gradient]
-        specs += [vmem(), anywhere()]
-        shapes.append(jax.ShapeDtypeStruct((views, planes, bins), F32))
-        out_specs.append(anywhere())
-        aliases = {5: 0}
-    scratch = [
-        VMEM((1, bins, cells), F32),
-        VMEM((LEVELS * views, bins), BF16),
-        VMEM((planes * views, bins), F32),
-        pltpu.SemaphoreType.DMA((1 + CHUNKS,)),
-    ]
-    if last:
-        scratch.append(VMEM((views, planes, bins), F32))
+        back_last_kernel(*refs, blocks=blocks, others=others, pad=pad, scale=scale)
+
     return pl.pallas_call(
         body,
-        out_shape=tuple(shapes),
-        in_specs=specs,
-        out_specs=tuple(out_specs),
-        scratch_shapes=scratch,
-        input_output_aliases=aliases,
+        out_shape=(
+            jax.ShapeDtypeStruct(gradient.shape, F32),
+            jax.ShapeDtypeStruct((views, planes, bins), F32),
+        ),
+        in_specs=[vmem()] * 5 + [anywhere()],
+        out_specs=(anywhere(), anywhere()),
+        scratch_shapes=[
+            VMEM((LEVELS * views, bins), BF16),
+            VMEM((1, bins, cells), F32),
+            VMEM((planes * views, bins), F32),
+            VMEM((views, planes, bins), F32),
+            pltpu.SemaphoreType.DMA((1 + CHUNKS,)),
+        ],
+        input_output_aliases={5: 0},
         compiler_params=LIMIT,
         interpret=interpreted(),
-        name="back_y_last" if last else "back_y_own",
-    )(*operands)
+        name="back_last",
+    )(*(in_vmem(value) for value in (column, table, partial, half, other)), gradient)
 
 
 def exchange(value, axis, partner):
@@ -483,13 +518,17 @@
     sum_x = jnp.concatenate([x_a, x_mid, x_b], axis=1)
 
     half = half + exchange(half, "gy", across)
+    other = exchange(half, "gy", twin)
     sum_x = sum_x + exchange(sum_x, "gx", across)
-    other = exchange(half, "gy", twin)
 
     table_x, base = prepare(lane, volume, beside, count_x)
-    partial, residual_x = back_x(column_x, table_x, base, sum_x, count_x, count_y, pad_x, scale_x)
-    (gradient,) = back_y(column_y, table_y, partial, half, None, count_y, count_x, pad_y, scale_y)
-    gradient, residual_y = back_y(column_y, table_y, partial, half, (other, gradient), count_y, count_x, pad_y, scale_y)
+    own = back_own(column_y, table_y, half, cells_x, count_y, count_x, pad_y, scale_y)
+    gradient, residual_x, partial = back_x(
+        column_x, table_x, base, sum_x, own, count_x, count_y, pad_x, scale_x
+    )
+    gradient, residual_y = back_last(
+        column_y, table_y, partial, half, other, gradient, count_y, count_x, pad_y, scale_y
+    )
     return (gradient, residual_x, residual_y)
 
 

time: 42.3 us -> 41.8 us (0.988)
  Pallas kernels: 6.01 us -> 5.41 us
    pallas_call x3, Pallas kernels: 3.68 us -> 3.08 us  [the longest x1 1.3 us: back_last(): pl.pallas_call(body, out_shape=(jax.ShapeDtypeStruct(gradient.shape, F32)...]
  transfers between devices with their start and end apart: 9 -> 9, of which waited for: 5 -> 6; matrix products, arithmetic and copies ran while one was open for 0% -> 0% of each run, Pallas kernels for 7% -> 5%
where the time goes in v6:
time: 41.8 us; the launch traced here: 41.7 us
  starting transfers between devices  21.4 us (51%)
  waiting for transfers between devices  13.9 us (33%)
  Pallas kernels  5.41 us (13%)
  between operations  0.82 us (2%)
    ppermute x8, starting transfers between devices, exchange(): lax.ppermute(value, axis, [(i, partner(i)) for i in range(lax.axis_size(a...  20.3 us
    ppermute x8, waiting for transfers between devices, exchange(): lax.ppermute(value, axis, [(i, partner(i)) for i in range(lax.axis_size(a...  13.9 us
    pallas_call x1, Pallas kernels, forward(): pl.pallas_call(body, out_shape=(out_vmem((planes * views, cells_y + 2 * p...  1.92 us
    pallas_call x1, Pallas kernels, back_last(): pl.pallas_call(body, out_shape=(jax.ShapeDtypeStruct(gradient.shape, F32)...  1.3 us
    pallas_call x1, Pallas kernels, back_x(): pl.pallas_call(body, out_shape=(jax.ShapeDtypeStruct(base.shape, F32), ja...  1.29 us
    ppermute x1, starting transfers between devices, steps(): beside = lax.ppermute(near, 'pa', [(0, 1), (1, 0)])  1.13 us
  transfers between devices with their start and end apart: 9, of which 6 were waited for; matrix products, arithmetic and copies ran while one was open for 0% of the time, Pallas kernels for 5%

profile of v6, /device:TPU:1, one launch (start us, length us, event | category | flops | bytes accessed | tf_op | source)
XLA Modules:
  0.0 41.7 jit_solution(13906683768209241035)
XLA Ops:
  0.6 1.9 %forward.1 = (f32[32,384]{1,0:T(8,128)S(1)}, f32[32,768]{1,0:T(8,128)S(1)}, bf16[256,256]{1,0:T(8,128)(2,1)S(1)}, bf16[1,512,256]{2,1,0:T(8,128)(2,1)S(1)}, bf16...) custom-call(s32[2,16]{1,0:T(2,128)} %refs_0_.1, ...), custom_call_target="tpu_custom_call" | custom-call | tf_op jit(solution)/shard_map/forward/pallas_call | solution.py:209
  2.6 3.3 %collective-permute-start.1 = (f32[32,640]{1,0:T(8,128)S(1)}, f32[32,640]{1,0:T(8,128)S(1)}, u32[]{:S(2)}, u32[]{:S(2)}) collective-permute-start(f32[32,640]{1,0:T(8,128)S(1)} %pad_maximum_fusion.1), channel_id=1, source_target_pairs={{0,32},{32,0},{64,96},{96,64},{128,160},{160,128},{192,224},{224,1... | collective-permute-start | bytes 245768 | tf_op jit(solution)/shard_map/ppermute | solution.py:459
  5.9 0.9 %collective-permute-done.1 = f32[32,640]{1,0:T(8,128)S(1)} collective-permute-done((f32[32,640]{1,0:T(8,128)S(1)}, f32[32,640]{1,0:T(8,128)S(1)}, u32[]{:S(2)}, u32[]{:S(2)}) %collective-permute-start.1) | collective-permute-done | bytes 81952 | tf_op jit(solution)/shard_map/ppermute | solution.py:459
  6.8 0.1 collective-permute-start.2
  7.0 4.1 %collective-permute-done.2 = f32[32,640]{1,0:T(8,128)S(1)} collective-permute-done((f32[32,640]{1,0:T(8,128)S(1)}, f32[32,640]{1,0:T(8,128)S(1)}, u32[]{:S(2)}, u32[]{:S(2)}) %collective-permute-start.2) | collective-permute-done | bytes 81952 | tf_op jit(solution)/shard_map/ppermute | solution.py:459
  11.2 0.1 collective-permute-start.3
  11.3 1.1 %collective-permute-start = (bf16[1,512,256]{2,1,0:T(8,128)(2,1)S(1)}, bf16[1,512,256]{2,1,0:T(8,128)(2,1)S(1)}, u32[]{:S(2)}, u32[]{:S(2)}) collective-permute-start(bf16[1,512,256]{2,1,0:T(8,128)(2,1)S(1)} %get-tuple-element.26), channel_id=1, source_target_pairs={{0,1},{1,0},{2,3},{3,2},{4,5},{5,4},{6,7},{7,6},{8,9},{9,8},{10,11... | collective-permute-start | bytes 786440 | tf_op jit(solution)/shard_map/ppermute | solution.py:495
  12.4 2.0 %collective-permute-done.3 = f32[16,1024]{1,0:T(8,128)S(1)} collective-permute-done((f32[16,1024]{1,0:T(8,128)S(1)}, f32[16,1024]{1,0:T(8,128)S(1)}, u32[]{:S(2)}, u32[]{:S(2)}) %collective-permute-start.3) | collective-permute-done | bytes 65568 | tf_op jit(solution)/shard_map/ppermute | solution.py:459
  14.4 1.3 %collective-permute-start.4 = (f32[16,1024]{1,0:T(8,128)S(1)}, f32[16,1024]{1,0:T(8,128)S(1)}, u32[]{:S(2)}, u32[]{:S(2)}) collective-permute-start(f32[16,1024]{1,0:T(8,128)S(1)} %pad_maximum_fusion.4), channel_id=1, source_target_pairs={{0,16},{2,18},{4,20},{6,22},{8,24},{10,26},{12,28},{14,30},{16,0},... | collective-permute-start | bytes 196616 | tf_op jit(solution)/shard_map/ppermute | solution.py:459
  15.7 5.1 %collective-permute-done.4 = f32[16,1024]{1,0:T(8,128)S(1)} collective-permute-done((f32[16,1024]{1,0:T(8,128)S(1)}, f32[16,1024]{1,0:T(8,128)S(1)}, u32[]{:S(2)}, u32[]{:S(2)}) %collective-permute-start.4) | collective-permute-done | bytes 65568 | tf_op jit(solution)/shard_map/ppermute | solution.py:459
  20.8 4.8 %collective-permute-start.5 = (f32[16,1024]{1,0:T(8,128)S(1)}, f32[16,1024]{1,0:T(8,128)S(1)}, u32[]{:S(2)}, u32[]{:S(2)}) collective-permute-start(f32[16,1024]{1,0:T(8,128)S(1)} %pad_maximum_fusion.5), channel_id=1, source_target_pairs={{0,14},{2,4},{4,2},{6,8},{8,6},{10,12},{12,10},{14,0},{16,30},{18,... | collective-permute-start | bytes 196616 | tf_op jit(solution)/shard_map/ppermute | solution.py:459
  25.6 1.6 %collective-permute-done.5 = f32[16,1024]{1,0:T(8,128)S(1)} collective-permute-done((f32[16,1024]{1,0:T(8,128)S(1)}, f32[16,1024]{1,0:T(8,128)S(1)}, u32[]{:S(2)}, u32[]{:S(2)}) %collective-permute-start.5) | collective-permute-done | bytes 65568 | tf_op jit(solution)/shard_map/ppermute | solution.py:459
  27.3 1.7 %collective-permute-start.7 = (f32[16,768]{1,0:T(8,128)S(1)}, f32[16,768]{1,0:T(8,128)S(1)}, u32[]{:S(2)}, u32[]{:S(2)}) collective-permute-start(f32[16,768]{1,0:T(8,128)S(1)} %slice_add_fusion), channel_id=1, source_target_pairs={{0,6},{2,12},{4,10},{6,0},{8,14},{10,4},{12,2},{14,8},{16,22},{18,... | collective-permute-start | bytes 147464 | tf_op jit(solution)/shard_map/ppermute | solution.py:459
  29.0 7.4 %collective-permute-start.6 = (f32[32,384]{1,0:T(8,128)S(1)}, f32[32,384]{1,0:T(8,128)S(1)}, u32[]{:S(2)}, u32[]{:S(2)}) collective-permute-start(f32[32,384]{1,0:T(8,128)S(1)} %pad_maximum_fusion.6), channel_id=1, source_target_pairs={{0,96},{32,192},{64,160},{96,0},{128,224},{160,64},{192,32},{224,1... | collective-permute-start | bytes 147464 | tf_op jit(solution)/shard_map/ppermute | solution.py:459
  36.4 0.0 collective-permute-done.refs_2_
  36.4 0.4 prepare.1
  36.8 0.0 collective-permute-done.7
  36.8 1.7 %collective-permute-start.8 = (f32[16,768]{1,0:T(8,128)S(1)}, f32[16,768]{1,0:T(8,128)S(1)}, u32[]{:S(2)}, u32[]{:S(2)}) collective-permute-start(f32[16,768]{1,0:T(8,128)S(1)} %add.65.refs_2_.refs_3_), channel_id=1, source_target_pairs={{0,2},{2,0},{4,6},{6,4},{8,10},{10,8},{12,14},{14,12},{16,18},{18,... | collective-permute-start | bytes 147464 | tf_op jit(solution)/shard_map/ppermute | solution.py:459
  38.5 0.0 collective-permute-done.6
  38.5 0.5 %back_own.1.refs_4_ = f32[512,256]{1,0:T(8,128)S(1)} custom-call(s32[16,128]{1,0:T(8,128)S(1)} %get-tuple-element.21.refs_0_, bf16[256,256]{1,0:T(8,128)(2,1)S(1)} %get-tuple-element.22.refs_1_, f32[16,768]{1,0:T(8,128)S(1)} %add.65.refs_2_.refs_3_), custom_call_target="tpu_custom_call" | custom-call | tf_op jit(solution)/shard_map/back_own/pallas_call | solution.py:321
  39.0 1.3 %back_x.1 = (f32[2,512,256]{2,1,0:T(8,128)}, f32[16,2,256]{2,1,0:T(2,128)}, f32[512,256]{1,0:T(8,128)S(1)}) custom-call(s32[16,128]{1,0:T(8,128)S(1)} %get-tuple-element.23.refs_0_, bf16[512,256]{1,0:T(8,128)(2,1)S(1)} %get-tuple-element.27.refs_1_, f32[2,512,256]{2,1,0:T(8,128)S(1)} %get-tuple-element.28.refs_2_, f32[32,384]{1,0:T(8,128)S(1)} %fusion.1.refs_3_, ...), custom_call_target="tpu_custom_call" | custom-call | tf_op jit(solution)/shard_map/back_x/pallas_call | solution.py:377
  40.3 0.1 collective-permute-done.8.refs_4_
  40.4 1.3 %back_last.1 = (f32[2,512,256]{2,1,0:T(8,128)}, f32[16,2,512]{2,1,0:T(2,128)}) custom-call(s32[16,128]{1,0:T(8,128)S(1)} %get-tuple-element.21.refs_0_, bf16[256,256]{1,0:T(8,128)(2,1)S(1)} %get-tuple-element.22.refs_1_, f32[512,256]{1,0:T(8,128)S(1)} %get-tuple-element.34.refs_2_, ...), custom_call_target="tpu_custom_call", output_to_operand_aliasing={{0}: (5, {})} | custom-call | tf_op jit(solution)/shard_map/back_last/pallas_call | solution.py:436
  (24 shorter events, 0.2 us)
Async XLA Ops:
  2.6 4.2 %collective-permute-start.1 = (f32[32,640]{1,0:T(8,128)S(1)}, f32[32,640]{1,0:T(8,128)S(1)}, u32[]{:S(2)}, u32[]{:S(2)}) collective-permute-start(f32[32,640]{1,0:T(8,128)S(1)} %pad_maximum_fusion.1), channel_id=1, source_target_pairs={{0,32},{32,0},{64,96},{96,64},{128,160},{160,128},{192,224},{224,1... | collective-permute-start | bytes 245768 | tf_op jit(solution)/shard_map/ppermute | solution.py:459
  6.8 4.2 %collective-permute-start.2 = (f32[32,640]{1,0:T(8,128)S(1)}, f32[32,640]{1,0:T(8,128)S(1)}, u32[]{:S(2)}, u32[]{:S(2)}) collective-permute-start(f32[32,640]{1,0:T(8,128)S(1)} %pad_maximum_fusion.2), channel_id=1, source_target_pairs={{0,224},{32,64},{64,32},{96,128},{128,96},{160,192},{192,160},{224... | collective-permute-start | bytes 245768 | tf_op jit(solution)/shard_map/ppermute | solution.py:459
  11.2 3.2 %collective-permute-start.3 = (f32[16,1024]{1,0:T(8,128)S(1)}, f32[16,1024]{1,0:T(8,128)S(1)}, u32[]{:S(2)}, u32[]{:S(2)}) collective-permute-start(f32[16,1024]{1,0:T(8,128)S(1)} %pad_maximum_fusion.3), channel_id=1, source_target_pairs={{0,2},{2,0},{4,6},{6,4},{8,10},{10,8},{12,14},{14,12},{16,18},{18,... | collective-permute-start | bytes 196616 | tf_op jit(solution)/shard_map/ppermute | solution.py:459
  11.3 25.1 %collective-permute-start = (bf16[1,512,256]{2,1,0:T(8,128)(2,1)S(1)}, bf16[1,512,256]{2,1,0:T(8,128)(2,1)S(1)}, u32[]{:S(2)}, u32[]{:S(2)}) collective-permute-start(bf16[1,512,256]{2,1,0:T(8,128)(2,1)S(1)} %get-tuple-element.26), channel_id=1, source_target_pairs={{0,1},{1,0},{2,3},{3,2},{4,5},{5,4},{6,7},{7,6},{8,9},{9,8},{10,11... | collective-permute-start | bytes 786440 | tf_op jit(solution)/shard_map/ppermute | solution.py:495
  14.4 6.4 %collective-permute-start.4 = (f32[16,1024]{1,0:T(8,128)S(1)}, f32[16,1024]{1,0:T(8,128)S(1)}, u32[]{:S(2)}, u32[]{:S(2)}) collective-permute-start(f32[16,1024]{1,0:T(8,128)S(1)} %pad_maximum_fusion.4), channel_id=1, source_target_pairs={{0,16},{2,18},{4,20},{6,22},{8,24},{10,26},{12,28},{14,30},{16,0},... | collective-permute-start | bytes 196616 | tf_op jit(solution)/shard_map/ppermute | solution.py:459
  20.8 6.4 %collective-permute-start.5 = (f32[16,1024]{1,0:T(8,128)S(1)}, f32[16,1024]{1,0:T(8,128)S(1)}, u32[]{:S(2)}, u32[]{:S(2)}) collective-permute-start(f32[16,1024]{1,0:T(8,128)S(1)} %pad_maximum_fusion.5), channel_id=1, source_target_pairs={{0,14},{2,4},{4,2},{6,8},{8,6},{10,12},{12,10},{14,0},{16,30},{18,... | collective-permute-start | bytes 196616 | tf_op jit(solution)/shard_map/ppermute | solution.py:459
  27.3 9.5 %collective-permute-start.7 = (f32[16,768]{1,0:T(8,128)S(1)}, f32[16,768]{1,0:T(8,128)S(1)}, u32[]{:S(2)}, u32[]{:S(2)}) collective-permute-start(f32[16,768]{1,0:T(8,128)S(1)} %slice_add_fusion), channel_id=1, source_target_pairs={{0,6},{2,12},{4,10},{6,0},{8,14},{10,4},{12,2},{14,8},{16,22},{18,... | collective-permute-start | bytes 147464 | tf_op jit(solution)/shard_map/ppermute | solution.py:459
  29.0 9.5 %collective-permute-start.6 = (f32[32,384]{1,0:T(8,128)S(1)}, f32[32,384]{1,0:T(8,128)S(1)}, u32[]{:S(2)}, u32[]{:S(2)}) collective-permute-start(f32[32,384]{1,0:T(8,128)S(1)} %pad_maximum_fusion.6), channel_id=1, source_target_pairs={{0,96},{32,192},{64,160},{96,0},{128,224},{160,64},{192,32},{224,1... | collective-permute-start | bytes 147464 | tf_op jit(solution)/shard_map/ppermute | solution.py:459
  36.8 3.6 %collective-permute-start.8 = (f32[16,768]{1,0:T(8,128)S(1)}, f32[16,768]{1,0:T(8,128)S(1)}, u32[]{:S(2)}, u32[]{:S(2)}) collective-permute-start(f32[16,768]{1,0:T(8,128)S(1)} %add.65.refs_2_.refs_3_), channel_id=1, source_target_pairs={{0,2},{2,0},{4,6},{6,4},{8,10},{10,8},{12,14},{14,12},{16,18},{18,... | collective-permute-start | bytes 147464 | tf_op jit(solution)/shard_map/ppermute | solution.py:459

commit v7 on v6

--- a/solution.py
+++ b/solution.py
@@ -9,6 +9,7 @@
 LEVELS = 16
 RING = 8
 CHUNKS = 2
+PIECES = 4
 LIMIT = pltpu.CompilerParams(vmem_limit_bytes=8 * 1024 * 1024)
 SMEM = pltpu.SMEM
 VMEM = pltpu.VMEM
@@ -123,8 +124,7 @@
     return jnp.round(value * 32768.0) * (1.0 / 32768.0)
 
 
-def project(table_ref, volume_ref, rows_ref, slopes, out_ref, family, block, blocks, odd, pad, scale):
-    planes = volume_ref.shape[0]
+def project(table_ref, volume_ref, rows_ref, slopes, out_ref, plane, family, block, blocks, odd, pad, scale):
     views = slopes.shape[0]
     bins = volume_ref.shape[2 - family]
     width = out_ref.shape[1]
@@ -132,20 +132,19 @@
     amounts = pad - LEVELS + 1 - lowest_shift(slopes, block, blocks)
     count = width // 128
     data = bins // 128
-    for plane in range(planes):
-        dims = (((1,), (family,)), ((), ()))
-        summands = lax.dot_general(table_ref[...], volume_ref[plane], dims, preferred_element_type=F32)
-        total = [None] * count
-        for level in range(LEVELS):
-            piece = tiles_of(summands[level * views : (level + 1) * views, :]) + [None] * (count - data)
-            piece = shifted(piece, LEVELS - 1 - level, count)
-            total = [p if t is None else t if p is None else t + p for t, p in zip(total, piece)]
-        total = jnp.concatenate(barrel(total, amounts), axis=1) * scale
-        known = tiles_of(rows_ref[plane * views : (plane + 1) * views, :] * first) + [None] * (count - data)
-        known = [None] * (pad // 128) + shifted(known, pad % 128, count - pad // 128)
-        known = jnp.concatenate([jnp.zeros((views, 128), F32) if k is None else k for k in known], axis=1)
-        total = on_grid(total - known)
-        out_ref[plane * views : (plane + 1) * views, :] = in_roles(total, odd)
+    dims = (((1,), (family,)), ((), ()))
+    summands = lax.dot_general(table_ref[...], volume_ref[plane], dims, preferred_element_type=F32)
+    total = [None] * count
+    for level in range(LEVELS):
+        piece = tiles_of(summands[level * views : (level + 1) * views, :]) + [None] * (count - data)
+        piece = shifted(piece, LEVELS - 1 - level, count)
+        total = [p if t is None else t if p is None else t + p for t, p in zip(total, piece)]
+    total = jnp.concatenate(barrel(total, amounts), axis=1) * scale
+    known = tiles_of(rows_ref[plane * views : (plane + 1) * views, :] * first) + [None] * (count - data)
+    known = [None] * (pad // 128) + shifted(known, pad % 128, count - pad // 128)
+    known = jnp.concatenate([jnp.zeros((views, 128), F32) if k is None else k for k in known], axis=1)
+    total = on_grid(total - known)
+    out_ref[plane * views : (plane + 1) * views, :] = in_roles(total, odd)
 
 
 def build_table(slopes, block, blocks, cells, table_ref):
@@ -168,12 +167,13 @@
     table_x_ref, slopes_ref, mx_ref, my_ref, rows_x_ref, rows_y_ref, sems,
     *, count_x, count_y, pad_x, pad_y, scale_x, scale_y,
 ):
-    _, cells_x, cells_y = volume_ref.shape
+    planes, cells_x, cells_y = volume_ref.shape
     fetches = [
         pltpu.make_async_copy(slopes_hbm, slopes_ref, sems.at[0]),
-        pltpu.make_async_copy(volume_hbm, volume_ref, sems.at[1]),
+        pltpu.make_async_copy(volume_hbm.at[0:1], volume_ref.at[0:1], sems.at[1]),
         pltpu.make_async_copy(mx_hbm, mx_ref, sems.at[2]),
         pltpu.make_async_copy(my_hbm, my_ref, sems.at[3]),
+        pltpu.make_async_copy(volume_hbm.at[1:2], volume_ref.at[1:2], sems.at[5]),
         pltpu.make_async_copy(volume_hbm.at[pl.ds(1 - lax.axis_index("pa"), 1)], near_ref, sems.at[4]),
     ]
     for fetch in fetches:
@@ -191,10 +191,15 @@
     fetches[3].wait()
     gather_rows(mx_ref, rows_x_ref)
     gather_rows(my_ref, rows_y_ref)
-    fetches[1].wait()
-    project(table_y_ref, volume_ref, rows_y_ref, column_y, y_ref, 1, here_y, count_y, here_x % 2 == 1, pad_y, scale_y)
-    project(table_x_ref, volume_ref, rows_x_ref, column_x, x_ref, 0, here_x, count_x, here_y % 2 == 1, pad_x, scale_x)
-    fetches[4].wait()
+    for plane in range(planes):
+        fetches[1 if plane == 0 else 4].wait()
+        project(
+            table_y_ref, volume_ref, rows_y_ref, column_y, y_ref, plane, 1, here_y, count_y, here_x % 2 == 1, pad_y, scale_y
+        )
+        project(
+            table_x_ref, volume_ref, rows_x_ref, column_x, x_ref, plane, 0, here_x, count_x, here_y % 2 == 1, pad_x, scale_x
+        )
+    fetches[5].wait()
 
 
 def forward(slopes, volume, measured_x, measured_y, count_x, count_y, pad_x, pad_y, scale_x, scale_y):
@@ -227,7 +232,7 @@
             VMEM(measured_y.shape, F32),
             VMEM((planes * views, cells_y), F32),
             VMEM((planes * views, cells_x), F32),
-            pltpu.SemaphoreType.DMA((5,)),
+            pltpu.SemaphoreType.DMA((6,)),
         ],
         compiler_params=LIMIT,
         interpret=interpreted(),
@@ -331,22 +336,24 @@
 
 
 def back_x_kernel(
-    column_ref, table_ref, base_ref, residual_ref, own_ref, out_hbm, rest_hbm, partial_ref,
+    column_ref, table_ref, base_ref, half_ref, away_ref, own_ref, out_hbm, rest_hbm, partial_ref,
     spread_ref, sum_ref, rows_ref, rest_ref, sems, *, blocks, others, pad, scale,
 ):
     planes, cells, _ = base_ref.shape
-    views = column_ref.shape[0]
     block, other = lax.axis_index("gx"), lax.axis_index("gy")
     column = column_ref[...]
     flip = other % 2 == 1
     mine = half_of(other)
+    held = half_of(block)
     size = cells // CHUNKS
     copies = []
+
+    def residual_of(plane):
+        return from_roles(jnp.where(plane == held, half_ref[...], away_ref[...]), flip)
+
     for last in range(planes):
         plane = 1 - mine if last else mine
-        start = pl.multiple_of(plane * views, views)
-        residual = from_roles(residual_ref[pl.ds(start, views), :], flip)
-        spread_into(residual, column, block, blocks, other, others, pad, scale, spread_ref)
+        spread_into(residual_of(plane), column, block, blocks, other, others, pad, scale, spread_ref)
         for c in range(CHUNKS):
             part = pl.ds(c * size, size)
             value = jnp.dot(table_ref[part, :], spread_ref[...], preferred_element_type=F32)
@@ -359,15 +366,14 @@
                     pltpu.make_async_copy(sum_ref.at[:, part], out_hbm.at[pl.ds(plane, 1), part], sems.at[1 + c])
                 )
                 copies[-1].start()
-    residuals = [from_roles(residual_ref[p * views : (p + 1) * views, :], flip) for p in range(planes)]
-    store_rows([middle(residual, pad) for residual in residuals], rest_ref, rows_ref)
+    store_rows([middle(residual_of(p), pad) for p in range(planes)], rest_ref, rows_ref)
     copies.append(pltpu.make_async_copy(rest_ref, rest_hbm, sems.at[0]))
     copies[-1].start()
     for copy in copies:
         copy.wait()
 
 
-def back_x(column, table, base, residual, own, blocks, others, pad, scale):
+def back_x(column, table, base, half, away, own, blocks, others, pad, scale):
     planes, cells, bins = base.shape
     views = column.shape[0]
 
@@ -381,7 +387,7 @@
             jax.ShapeDtypeStruct((views, planes, bins), F32),
             out_vmem((cells, bins), F32),
         ),
-        in_specs=[vmem()] * 5,
+        in_specs=[vmem()] * 6,
         out_specs=(anywhere(), anywhere(), vmem()),
         scratch_shapes=[
             VMEM((LEVELS * views, bins), BF16),
@@ -393,7 +399,7 @@
         compiler_params=LIMIT,
         interpret=interpreted(),
         name="back_x",
-    )(*(in_vmem(value) for value in (column, table, base, residual, own)))
+    )(*(in_vmem(value) for value in (column, table, base, half, away, own)))
 
 
 def back_last_kernel(
@@ -407,9 +413,9 @@
     value = from_roles(other_ref[...], flip)
     spread_into(value, column_ref[...], block, blocks, other, others, pad, scale, spread_ref)
     dims = (((0,), (0,)), ((), ()))
-    size = bins // CHUNKS
+    size = bins // PIECES
     copies = []
-    for c in range(CHUNKS):
+    for c in range(PIECES):
         part = pl.ds(c * size, size)
         back = lax.dot_general(spread_ref[:, c * size : (c + 1) * size], table_ref[...], dims, preferred_element_type=F32)
         sum_ref[:, part, :] = (partial_ref[part, :] + back)[None]
@@ -446,7 +452,7 @@
             VMEM((1, bins, cells), F32),
             VMEM((planes * views, bins), F32),
             VMEM((views, planes, bins), F32),
-            pltpu.SemaphoreType.DMA((1 + CHUNKS,)),
+            pltpu.SemaphoreType.DMA((1 + PIECES,)),
         ],
         input_output_aliases={5: 0},
         compiler_params=LIMIT,
@@ -487,44 +493,55 @@
     sum_x, sum_y, table_y, near, volume, column_x, column_y, lane = forward(
         view_slopes, volume, measured_x, measured_y, count_x, count_y, pad_x, pad_y, scale_x, scale_y
     )
-    wide = sum_x.shape[1]
-    edge_x, edge_y = wide // 3, sum_y.shape[1] // 3
+    wide, long = sum_x.shape[1], sum_y.shape[1]
+    edge_x, edge_y = wide // 3, long // 3
+    rows = sum_x.shape[0] // 2
+
+    def side_by_side(value):
+        return jnp.concatenate([value[:rows], value[rows:]], axis=1)
+
+    def one_above(value):
+        return jnp.concatenate([value[:, : value.shape[1] // 2], value[:, value.shape[1] // 2 :]], axis=0)
+
+    def split(value, axis):
+        owns = half_of(lax.axis_index(axis)) == 0
+        low, high = value[:rows], value[rows:]
+        return jnp.where(owns, low, high), jnp.where(owns, high, low)
+
     y_a, y_mid, y_b = sum_y[:, :edge_y], sum_y[:, edge_y : 2 * edge_y], sum_y[:, 2 * edge_y :]
-
-    got = exchange(jnp.concatenate([sum_x, y_a], axis=1), "gx", twin)
+    half_x, sent = split(sum_x, "gx")
+    got = exchange(jnp.concatenate([sent, side_by_side(y_a)], axis=1), "gx", twin)
     beside = lax.ppermute(near, "pa", [(0, 1), (1, 0)])
-    sum_x, y_a = sum_x + got[:, :wide], y_a + got[:, wide:]
-    got = exchange(jnp.concatenate([sum_x, y_b], axis=1), "gx", odd_twin)
-    sum_x, y_b = sum_x + got[:, :wide], y_b + jnp.where(at_end(count_x, "gx"), 0.0, got[:, wide:])
+    half_x, y_a = half_x + got[:, :wide], y_a + one_above(got[:, wide:])
+    got = exchange(jnp.concatenate([half_x, side_by_side(y_b)], axis=1), "gx", odd_twin)
+    half_x = half_x + got[:, :wide]
+    y_b = y_b + jnp.where(at_end(count_x, "gx"), 0.0, one_above(got[:, wide:]))
     sum_y = jnp.concatenate([y_a, y_mid, y_b], axis=1)
-    x_a, x_mid, x_b = sum_x[:, :edge_x], sum_x[:, edge_x : 2 * edge_x], sum_x[:, 2 * edge_x :]
-
-    rows = sum_y.shape[0] // 2
-    long = sum_y.shape[1]
-    owns = half_of(lax.axis_index("gy")) == 0
-    kept = jnp.where(owns, sum_y[:rows], sum_y[rows:])
-    sent = jnp.where(owns, sum_y[rows:], sum_y[:rows])
-    got = exchange(jnp.concatenate([sent, x_a[:rows], x_a[rows:]], axis=1), "gy", twin)
-    half = kept + got[:, :long]
-    x_a = x_a + jnp.concatenate([got[:, long : long + edge_x], got[:, long + edge_x :]], axis=0)
-    got = exchange(jnp.concatenate([half, x_b[:rows], x_b[rows:]], axis=1), "gy", lambda i: i ^ RING)
+    x_a, x_mid, x_b = half_x[:, :edge_x], half_x[:, edge_x : 2 * edge_x], half_x[:, 2 * edge_x :]
+
+    half, sent = split(sum_y, "gy")
+    got = exchange(jnp.concatenate([sent, x_a], axis=1), "gy", twin)
+    half, x_a = half + got[:, :long], x_a + got[:, long:]
+    got = exchange(jnp.concatenate([half, x_b], axis=1), "gy", lambda i: i ^ RING)
     half = half + got[:, :long]
-    sent_b = jnp.where(at_end(RING, "gy"), got[:, long:], jnp.concatenate([x_b[:rows], x_b[rows:]], axis=1))
+    sent_b = jnp.where(at_end(RING, "gy"), got[:, long:], x_b)
     got = exchange(jnp.concatenate([half, sent_b], axis=1), "gy", odd_twin)
     half = half + got[:, :long]
-    got = jnp.where(at_end(count_y, "gy"), 0.0, got)
+    got = jnp.where(at_end(count_y, "gy"), 0.0, got[:, long:])
     half, x_b, got = lax.optimization_barrier((half, x_b, got))
-    x_b = x_b + jnp.concatenate([got[:, long : long + edge_x], got[:, long + edge_x :]], axis=0)
-    sum_x = jnp.concatenate([x_a, x_mid, x_b], axis=1)
+    half_x = jnp.concatenate([x_a, x_mid, x_b + got], axis=1)
 
     half = half + exchange(half, "gy", across)
+    got = exchange(half_x, "gx", across)
     other = exchange(half, "gy", twin)
-    sum_x = sum_x + exchange(sum_x, "gx", across)
+    half_x, half = lax.optimization_barrier((half_x, half))
+    half_x = half_x + got
+    away_x = exchange(half_x, "gx", twin)
 
     table_x, base = prepare(lane, volume, beside, count_x)
     own = back_own(column_y, table_y, half, cells_x, count_y, count_x, pad_y, scale_y)
     gradient, residual_x, partial = back_x(
-        column_x, table_x, base, sum_x, own, count_x, count_y, pad_x, scale_x
+        column_x, table_x, base, half_x, away_x, own, count_x, count_y, pad_x, scale_x
     )
     gradient, residual_y = back_last(
         column_y, table_y, partial, half, other, gradient, count_y, count_x, pad_y, scale_y

time: 41.8 us -> 40 us (0.957)
  the two profiles are of different devices: /device:TPU:1 before, /device:TPU:6 now
where the time goes in v7:
time: 40 us; the launch traced here: 39.9 us
  waiting for transfers between devices  17.3 us (43%)
  starting transfers between devices  16 us (40%)
  Pallas kernels  5.59 us (14%)
  between operations  0.87 us (2%)
    ppermute x9, waiting for transfers between devices, exchange(): lax.ppermute(value, axis, [(i, partner(i)) for i in range(lax.axis_size(a...  17.3 us
    ppermute x9, starting transfers between devices, exchange(): lax.ppermute(value, axis, [(i, partner(i)) for i in range(lax.axis_size(a...  15.2 us
    pallas_call x1, Pallas kernels, forward(): pl.pallas_call(body, out_shape=(out_vmem((planes * views, cells_y + 2 * p...  2.14 us
    pallas_call x1, Pallas kernels, back_last(): pl.pallas_call(body, out_shape=(jax.ShapeDtypeStruct(gradient.shape, F32)...  1.29 us
    pallas_call x1, Pallas kernels, back_x(): pl.pallas_call(body, out_shape=(jax.ShapeDtypeStruct(base.shape, F32), ja...  1.27 us
  transfers between devices with their start and end apart: 10, of which 8 were waited for; matrix products, arithmetic and copies ran while one was open for 0% of the time, Pallas kernels for 5%

profile of v7, /device:TPU:6, one launch (start us, length us, event | category | flops | bytes accessed | tf_op | source)
XLA Modules:
  0.0 39.9 jit_solution(5925609370225170773)
XLA Ops:
  0.7 2.1 %forward.1 = (f32[32,384]{1,0:T(8,128)S(1)}, f32[32,768]{1,0:T(8,128)S(1)}, bf16[256,256]{1,0:T(8,128)(2,1)S(1)}, bf16[1,512,256]{2,1,0:T(8,128)(2,1)S(1)}, bf16...) custom-call(s32[2,16]{1,0:T(2,128)} %refs_0_.1, ...), custom_call_target="tpu_custom_call" | custom-call | tf_op jit(solution)/shard_map/forward/pallas_call | solution.py:214
  2.8 0.1 collective-permute-start.1
  3.0 1.2 %collective-permute-done.1 = f32[16,896]{1,0:T(8,128)S(1)} collective-permute-done((f32[16,896]{1,0:T(8,128)S(1)}, f32[16,896]{1,0:T(8,128)S(1)}, u32[]{:S(2)}, u32[]{:S(2)}) %collective-permute-start.1) | collective-permute-done | bytes 57376 | tf_op jit(solution)/shard_map/ppermute | solution.py:465
  4.2 2.9 %collective-permute-start.2 = (f32[16,896]{1,0:T(8,128)S(1)}, f32[16,896]{1,0:T(8,128)S(1)}, u32[]{:S(2)}, u32[]{:S(2)}) collective-permute-start(f32[16,896]{1,0:T(8,128)S(1)} %pad_maximum_fusion.2), channel_id=1, source_target_pairs={{0,224},{32,64},{64,32},{96,128},{128,96},{160,192},{192,160},{224... | collective-permute-start | bytes 172040 | tf_op jit(solution)/shard_map/ppermute | solution.py:465
  7.1 2.0 %collective-permute-done.2 = f32[16,896]{1,0:T(8,128)S(1)} collective-permute-done((f32[16,896]{1,0:T(8,128)S(1)}, f32[16,896]{1,0:T(8,128)S(1)}, u32[]{:S(2)}, u32[]{:S(2)}) %collective-permute-start.2) | collective-permute-done | bytes 57376 | tf_op jit(solution)/shard_map/ppermute | solution.py:465
  9.2 2.0 %collective-permute-start.3 = (f32[16,896]{1,0:T(8,128)S(1)}, f32[16,896]{1,0:T(8,128)S(1)}, u32[]{:S(2)}, u32[]{:S(2)}) collective-permute-start(f32[16,896]{1,0:T(8,128)S(1)} %pad_maximum_fusion.3), channel_id=1, source_target_pairs={{0,2},{2,0},{4,6},{6,4},{8,10},{10,8},{12,14},{14,12},{16,18},{18,... | collective-permute-start | bytes 172040 | tf_op jit(solution)/shard_map/ppermute | solution.py:465
  11.2 2.3 %collective-permute-done.3 = f32[16,896]{1,0:T(8,128)S(1)} collective-permute-done((f32[16,896]{1,0:T(8,128)S(1)}, f32[16,896]{1,0:T(8,128)S(1)}, u32[]{:S(2)}, u32[]{:S(2)}) %collective-permute-start.3) | collective-permute-done | bytes 57376 | tf_op jit(solution)/shard_map/ppermute | solution.py:465
  13.5 1.5 %collective-permute-start.4 = (f32[16,896]{1,0:T(8,128)S(1)}, f32[16,896]{1,0:T(8,128)S(1)}, u32[]{:S(2)}, u32[]{:S(2)}) collective-permute-start(f32[16,896]{1,0:T(8,128)S(1)} %pad_maximum_fusion.4), channel_id=1, source_target_pairs={{0,16},{2,18},{4,20},{6,22},{8,24},{10,26},{12,28},{14,30},{16,0},... | collective-permute-start | bytes 172040 | tf_op jit(solution)/shard_map/ppermute | solution.py:465
  15.0 4.3 %collective-permute-done.4 = f32[16,896]{1,0:T(8,128)S(1)} collective-permute-done((f32[16,896]{1,0:T(8,128)S(1)}, f32[16,896]{1,0:T(8,128)S(1)}, u32[]{:S(2)}, u32[]{:S(2)}) %collective-permute-start.4) | collective-permute-done | bytes 57376 | tf_op jit(solution)/shard_map/ppermute | solution.py:465
  19.3 6.6 %collective-permute-start.5 = (f32[16,896]{1,0:T(8,128)S(1)}, f32[16,896]{1,0:T(8,128)S(1)}, u32[]{:S(2)}, u32[]{:S(2)}) collective-permute-start(f32[16,896]{1,0:T(8,128)S(1)} %pad_maximum_fusion.5), channel_id=1, source_target_pairs={{0,14},{2,4},{4,2},{6,8},{8,6},{10,12},{12,10},{14,0},{16,30},{18,... | collective-permute-start | bytes 172040 | tf_op jit(solution)/shard_map/ppermute | solution.py:465
  25.8 0.8 %collective-permute-start = (bf16[1,512,256]{2,1,0:T(8,128)(2,1)S(1)}, bf16[1,512,256]{2,1,0:T(8,128)(2,1)S(1)}, u32[]{:S(2)}, u32[]{:S(2)}) collective-permute-start(bf16[1,512,256]{2,1,0:T(8,128)(2,1)S(1)} %get-tuple-element.28), channel_id=1, source_target_pairs={{0,1},{1,0},{2,3},{3,2},{4,5},{5,4},{6,7},{7,6},{8,9},{9,8},{10,11... | collective-permute-start | bytes 786440 | tf_op jit(solution)/shard_map/ppermute | solution.py:514
  26.6 1.5 %collective-permute-done.5 = f32[16,896]{1,0:T(8,128)S(1)} collective-permute-done((f32[16,896]{1,0:T(8,128)S(1)}, f32[16,896]{1,0:T(8,128)S(1)}, u32[]{:S(2)}, u32[]{:S(2)}) %collective-permute-start.5) | collective-permute-done | bytes 57376 | tf_op jit(solution)/shard_map/ppermute | solution.py:465
  28.1 2.0 %collective-permute-start.6 = (f32[16,768]{1,0:T(8,128)S(1)}, f32[16,768]{1,0:T(8,128)S(1)}, u32[]{:S(2)}, u32[]{:S(2)}) collective-permute-start(f32[16,768]{1,0:T(8,128)S(1)} %slice_add_fusion), channel_id=1, source_target_pairs={{0,6},{2,12},{4,10},{6,0},{8,14},{10,4},{12,2},{14,8},{16,22},{18,... | collective-permute-start | bytes 147464 | tf_op jit(solution)/shard_map/ppermute | solution.py:465
  30.1 0.0 collective-permute-start.7
  30.1 4.3 %collective-permute-done.6 = f32[16,768]{1,0:T(8,128)S(1)} collective-permute-done((f32[16,768]{1,0:T(8,128)S(1)}, f32[16,768]{1,0:T(8,128)S(1)}, u32[]{:S(2)}, u32[]{:S(2)}) %collective-permute-start.6) | collective-permute-done | bytes 49184 | tf_op jit(solution)/shard_map/ppermute | solution.py:465
  34.4 0.1 collective-permute-start.9
  34.5 0.0 collective-permute-done.7
  34.6 0.1 collective-permute-start.8
  34.7 0.0 collective-permute-done.refs_2_
  34.7 0.4 %prepare.1 = (bf16[512,256]{1,0:T(8,128)(2,1)S(1)}, f32[2,512,256]{2,1,0:T(8,128)S(1)}) custom-call(s32[8,256]{1,0:T(8,128)S(1)} %get-tuple-element.26.refs_0_, bf16[2,512,256]{2,1,0:T(8,128)(2,1)S(1)} %get-tuple-element.27.refs_1_, bf16[1,512,256]{2,1,0:T(8,128)(2,1)S(1)} %collective-permute-done.refs_2_), custom_call_target="tpu_custom_call" | custom-call | tf_op jit(solution)/shard_map/prepare/pallas_call | solution.py:294
  35.1 0.5 %back_own.1.refs_5_ = f32[512,256]{1,0:T(8,128)S(1)} custom-call(s32[16,128]{1,0:T(8,128)S(1)} %get-tuple-element.23.refs_0_, bf16[256,256]{1,0:T(8,128)(2,1)S(1)} %get-tuple-element.24.refs_1_, f32[16,768]{1,0:T(8,128)S(1)} %add.73.refs_2_.refs_3_), custom_call_target="tpu_custom_call" | custom-call | tf_op jit(solution)/shard_map/back_own/pallas_call | solution.py:326
  35.6 0.3 collective-permute-done.8.refs_4_
  35.8 1.3 %back_x.1 = (f32[2,512,256]{2,1,0:T(8,128)}, f32[16,2,256]{2,1,0:T(2,128)}, f32[512,256]{1,0:T(8,128)S(1)}) custom-call(s32[16,128]{1,0:T(8,128)S(1)} %get-tuple-element.25.refs_0_, bf16[512,256]{1,0:T(8,128)(2,1)S(1)} %get-tuple-element.29.refs_1_, f32[2,512,256]{2,1,0:T(8,128)S(1)} %get-tuple-element.30.refs_2_, f32[16,384]{1,0:T(8,128)S(1)} %add.74.refs_3_, ...), custom_call_target="tpu_custom_call" | custom-call | tf_op jit(solution)/shard_map/back_x/pallas_call | solution.py:383
  37.1 1.5 %collective-permute-done.9.refs_4_ = f32[16,768]{1,0:T(8,128)S(1)} collective-permute-done((f32[16,768]{1,0:T(8,128)S(1)}, f32[16,768]{1,0:T(8,128)S(1)}, u32[]{:S(2)}, u32[]{:S(2)}) %collective-permute-start.9) | collective-permute-done | bytes 49184 | tf_op jit(solution)/shard_map/ppermute | solution.py:465
  38.6 1.3 %back_last.1 = (f32[2,512,256]{2,1,0:T(8,128)}, f32[16,2,512]{2,1,0:T(2,128)}) custom-call(s32[16,128]{1,0:T(8,128)S(1)} %get-tuple-element.23.refs_0_, bf16[256,256]{1,0:T(8,128)(2,1)S(1)} %get-tuple-element.24.refs_1_, f32[512,256]{1,0:T(8,128)S(1)} %get-tuple-element.38.refs_2_, ...), custom_call_target="tpu_custom_call", output_to_operand_aliasing={{0}: (5, {})} | custom-call | tf_op jit(solution)/shard_map/back_last/pallas_call | solution.py:442
  (24 shorter events, 0.2 us)
Async XLA Ops:
  2.8 1.3 %collective-permute-start.1 = (f32[16,896]{1,0:T(8,128)S(1)}, f32[16,896]{1,0:T(8,128)S(1)}, u32[]{:S(2)}, u32[]{:S(2)}) collective-permute-start(f32[16,896]{1,0:T(8,128)S(1)} %pad_maximum_fusion.1), channel_id=1, source_target_pairs={{0,32},{32,0},{64,96},{96,64},{128,160},{160,128},{192,224},{224,1... | collective-permute-start | bytes 172040 | tf_op jit(solution)/shard_map/ppermute | solution.py:465
  4.2 4.9 %collective-permute-start.2 = (f32[16,896]{1,0:T(8,128)S(1)}, f32[16,896]{1,0:T(8,128)S(1)}, u32[]{:S(2)}, u32[]{:S(2)}) collective-permute-start(f32[16,896]{1,0:T(8,128)S(1)} %pad_maximum_fusion.2), channel_id=1, source_target_pairs={{0,224},{32,64},{64,32},{96,128},{128,96},{160,192},{192,160},{224... | collective-permute-start | bytes 172040 | tf_op jit(solution)/shard_map/ppermute | solution.py:465
  9.2 4.3 %collective-permute-start.3 = (f32[16,896]{1,0:T(8,128)S(1)}, f32[16,896]{1,0:T(8,128)S(1)}, u32[]{:S(2)}, u32[]{:S(2)}) collective-permute-start(f32[16,896]{1,0:T(8,128)S(1)} %pad_maximum_fusion.3), channel_id=1, source_target_pairs={{0,2},{2,0},{4,6},{6,4},{8,10},{10,8},{12,14},{14,12},{16,18},{18,... | collective-permute-start | bytes 172040 | tf_op jit(solution)/shard_map/ppermute | solution.py:465
  13.5 5.8 %collective-permute-start.4 = (f32[16,896]{1,0:T(8,128)S(1)}, f32[16,896]{1,0:T(8,128)S(1)}, u32[]{:S(2)}, u32[]{:S(2)}) collective-permute-start(f32[16,896]{1,0:T(8,128)S(1)} %pad_maximum_fusion.4), channel_id=1, source_target_pairs={{0,16},{2,18},{4,20},{6,22},{8,24},{10,26},{12,28},{14,30},{16,0},... | collective-permute-start | bytes 172040 | tf_op jit(solution)/shard_map/ppermute | solution.py:465
  19.3 8.8 %collective-permute-start.5 = (f32[16,896]{1,0:T(8,128)S(1)}, f32[16,896]{1,0:T(8,128)S(1)}, u32[]{:S(2)}, u32[]{:S(2)}) collective-permute-start(f32[16,896]{1,0:T(8,128)S(1)} %pad_maximum_fusion.5), channel_id=1, source_target_pairs={{0,14},{2,4},{4,2},{6,8},{8,6},{10,12},{12,10},{14,0},{16,30},{18,... | collective-permute-start | bytes 172040 | tf_op jit(solution)/shard_map/ppermute | solution.py:465
  25.8 8.8 %collective-permute-start = (bf16[1,512,256]{2,1,0:T(8,128)(2,1)S(1)}, bf16[1,512,256]{2,1,0:T(8,128)(2,1)S(1)}, u32[]{:S(2)}, u32[]{:S(2)}) collective-permute-start(bf16[1,512,256]{2,1,0:T(8,128)(2,1)S(1)} %get-tuple-element.28), channel_id=1, source_target_pairs={{0,1},{1,0},{2,3},{3,2},{4,5},{5,4},{6,7},{7,6},{8,9},{9,8},{10,11... | collective-permute-start | bytes 786440 | tf_op jit(solution)/shard_map/ppermute | solution.py:514
  28.1 6.3 %collective-permute-start.6 = (f32[16,768]{1,0:T(8,128)S(1)}, f32[16,768]{1,0:T(8,128)S(1)}, u32[]{:S(2)}, u32[]{:S(2)}) collective-permute-start(f32[16,768]{1,0:T(8,128)S(1)} %slice_add_fusion), channel_id=1, source_target_pairs={{0,6},{2,12},{4,10},{6,0},{8,14},{10,4},{12,2},{14,8},{16,22},{18,... | collective-permute-start | bytes 147464 | tf_op jit(solution)/shard_map/ppermute | solution.py:465
  30.1 4.4 %collective-permute-start.7 = (f32[16,384]{1,0:T(8,128)S(1)}, f32[16,384]{1,0:T(8,128)S(1)}, u32[]{:S(2)}, u32[]{:S(2)}) collective-permute-start(f32[16,384]{1,0:T(8,128)S(1)} %pad_maximum_fusion.6), channel_id=1, source_target_pairs={{0,96},{32,192},{64,160},{96,0},{128,224},{160,64},{192,32},{224,1... | collective-permute-start | bytes 73736 | tf_op jit(solution)/shard_map/ppermute | solution.py:465
  34.4 4.2 %collective-permute-start.9 = (f32[16,768]{1,0:T(8,128)S(1)}, f32[16,768]{1,0:T(8,128)S(1)}, u32[]{:S(2)}, u32[]{:S(2)}) collective-permute-start(f32[16,768]{1,0:T(8,128)S(1)} %add.73.refs_2_.refs_3_), channel_id=1, source_target_pairs={{0,2},{2,0},{4,6},{6,4},{8,10},{10,8},{12,14},{14,12},{16,18},{18,... | collective-permute-start | bytes 147464 | tf_op jit(solution)/shard_map/ppermute | solution.py:465
  34.6 1.3 %collective-permute-start.8 = (f32[16,384]{1,0:T(8,128)S(1)}, f32[16,384]{1,0:T(8,128)S(1)}, u32[]{:S(2)}, u32[]{:S(2)}) collective-permute-start(f32[16,384]{1,0:T(8,128)S(1)} %add.74.refs_3_), channel_id=1, source_target_pairs={{0,32},{32,0},{64,96},{96,64},{128,160},{160,128},{192,224},{224,1... | collective-permute-start | bytes 73736 | tf_op jit(solution)/shard_map/ppermute | solution.py:465

commit v8 on v7

--- a/solution.py
+++ b/solution.py
@@ -170,10 +170,9 @@
     planes, cells_x, cells_y = volume_ref.shape
     fetches = [
         pltpu.make_async_copy(slopes_hbm, slopes_ref, sems.at[0]),
-        pltpu.make_async_copy(volume_hbm.at[0:1], volume_ref.at[0:1], sems.at[1]),
+        pltpu.make_async_copy(volume_hbm, volume_ref, sems.at[1]),
         pltpu.make_async_copy(mx_hbm, mx_ref, sems.at[2]),
         pltpu.make_async_copy(my_hbm, my_ref, sems.at[3]),
-        pltpu.make_async_copy(volume_hbm.at[1:2], volume_ref.at[1:2], sems.at[5]),
         pltpu.make_async_copy(volume_hbm.at[pl.ds(1 - lax.axis_index("pa"), 1)], near_ref, sems.at[4]),
     ]
     for fetch in fetches:
@@ -191,15 +190,16 @@
     fetches[3].wait()
     gather_rows(mx_ref, rows_x_ref)
     gather_rows(my_ref, rows_y_ref)
+    fetches[1].wait()
     for plane in range(planes):
-        fetches[1 if plane == 0 else 4].wait()
         project(
             table_y_ref, volume_ref, rows_y_ref, column_y, y_ref, plane, 1, here_y, count_y, here_x % 2 == 1, pad_y, scale_y
         )
+    for plane in range(planes):
         project(
             table_x_ref, volume_ref, rows_x_ref, column_x, x_ref, plane, 0, here_x, count_x, here_y % 2 == 1, pad_x, scale_x
         )
-    fetches[5].wait()
+    fetches[4].wait()
 
 
 def forward(slopes, volume, measured_x, measured_y, count_x, count_y, pad_x, pad_y, scale_x, scale_y):
@@ -232,7 +232,7 @@
             VMEM(measured_y.shape, F32),
             VMEM((planes * views, cells_y), F32),
             VMEM((planes * views, cells_x), F32),
-            pltpu.SemaphoreType.DMA((6,)),
+            pltpu.SemaphoreType.DMA((5,)),
         ],
         compiler_params=LIMIT,
         interpret=interpreted(),
@@ -462,7 +462,7 @@
 
 
 def exchange(value, axis, partner):
-    return lax.ppermute(value, axis, [(i, partner(i)) for i in range(lax.axis_size(axis))])
+    return lax.ppermute(value, axis, [(i, partner(i)) for i in range(lax.axis_size(axis)) if partner(i) != i])
 
 
 def twin(i):
@@ -471,6 +471,14 @@
 
 def odd_twin(i):
     return i - i % RING + (i + (1 if i % 2 else -1)) % RING
+
+
+def next_twin(i):
+    return odd_twin(i) if abs(odd_twin(i) - i) == 1 else i
+
+
+def end_twin(i):
+    return i if abs(odd_twin(i) - i) == 1 else odd_twin(i)
 
 
 def across(i):
@@ -513,9 +521,8 @@
     got = exchange(jnp.concatenate([sent, side_by_side(y_a)], axis=1), "gx", twin)
     beside = lax.ppermute(near, "pa", [(0, 1), (1, 0)])
     half_x, y_a = half_x + got[:, :wide], y_a + one_above(got[:, wide:])
-    got = exchange(jnp.concatenate([half_x, side_by_side(y_b)], axis=1), "gx", odd_twin)
-    half_x = half_x + got[:, :wide]
-    y_b = y_b + jnp.where(at_end(count_x, "gx"), 0.0, one_above(got[:, wide:]))
+    got = exchange(jnp.concatenate([half_x, side_by_side(y_b)], axis=1), "gx", next_twin)
+    half_x, y_b = half_x + got[:, :wide], y_b + one_above(got[:, wide:])
     sum_y = jnp.concatenate([y_a, y_mid, y_b], axis=1)
     x_a, x_mid, x_b = half_x[:, :edge_x], half_x[:, edge_x : 2 * edge_x], half_x[:, 2 * edge_x :]
 
@@ -532,6 +539,7 @@
     half_x = jnp.concatenate([x_a, x_mid, x_b + got], axis=1)
 
     half = half + exchange(half, "gy", across)
+    half_x = half_x + exchange(half_x, "gx", end_twin)
     got = exchange(half_x, "gx", across)
     other = exchange(half, "gy", twin)
     half_x, half = lax.optimization_barrier((half_x, half))

time: 40 us -> 42.2 us (1.055)
  the two profiles are of different devices: /device:TPU:6 before, /device:TPU:16 now
where the time goes in v8:
time: 42.2 us; the launch traced here: 42 us
  starting transfers between devices  17.8 us (42%)
  waiting for transfers between devices  17.8 us (42%)
  Pallas kernels  5.38 us (13%)
  between operations  0.91 us (2%)
    ppermute x10, waiting for transfers between devices, exchange(): lax.ppermute(value, axis, [(i, partner(i)) for i in range(lax.axis_size(a...  17.8 us
    ppermute x10, starting transfers between devices, exchange(): lax.ppermute(value, axis, [(i, partner(i)) for i in range(lax.axis_size(a...  16.2 us
    pallas_call x1, Pallas kernels, forward(): pl.pallas_call(body, out_shape=(out_vmem((planes * views, cells_y + 2 * p...  1.92 us
    ppermute x1, starting transfers between devices, steps(): beside = lax.ppermute(near, 'pa', [(0, 1), (1, 0)])  1.58 us
    pallas_call x1, Pallas kernels, back_last(): pl.pallas_call(body, out_shape=(jax.ShapeDtypeStruct(gradient.shape, F32)...  1.29 us
    pallas_call x1, Pallas kernels, back_x(): pl.pallas_call(body, out_shape=(jax.ShapeDtypeStruct(base.shape, F32), ja...  1.27 us
  transfers between devices with their start and end apart: 11, of which 8 were waited for; matrix products, arithmetic and copies ran while one was open for 0% of the time, Pallas kernels for 5%

profile of v8, /device:TPU:16, one launch (start us, length us, event | category | flops | bytes accessed | tf_op | source)
XLA Modules:
  0.0 42.0 jit_solution(1397963350196762757)
XLA Ops:
  0.7 1.9 %forward.1 = (f32[32,384]{1,0:T(8,128)S(1)}, f32[32,768]{1,0:T(8,128)S(1)}, bf16[256,256]{1,0:T(8,128)(2,1)S(1)}, bf16[1,512,256]{2,1,0:T(8,128)(2,1)S(1)}, bf16...) custom-call(s32[2,16]{1,0:T(2,128)} %refs_0_.1, ...), custom_call_target="tpu_custom_call" | custom-call | tf_op jit(solution)/shard_map/forward/pallas_call | solution.py:214
  2.6 0.1 collective-permute-start.1
  2.7 1.2 %collective-permute-done.1 = f32[16,896]{1,0:T(8,128)S(1)} collective-permute-done((f32[16,896]{1,0:T(8,128)S(1)}, f32[16,896]{1,0:T(8,128)S(1)}, u32[]{:S(2)}, u32[]{:S(2)}) %collective-permute-start.1) | collective-permute-done | bytes 57376 | tf_op jit(solution)/shard_map/ppermute | solution.py:465
  4.0 2.1 %collective-permute-start.2 = (f32[16,896]{1,0:T(8,128)S(1)}, f32[16,896]{1,0:T(8,128)S(1)}, u32[]{:S(2)}, u32[]{:S(2)}) collective-permute-start(f32[16,896]{1,0:T(8,128)S(1)} %pad_maximum_fusion.2), channel_id=1, source_target_pairs={{32,64},{64,32},{96,128},{128,96},{160,192},{192,160},{33,65},{65,... | collective-permute-start | bytes 172040 | tf_op jit(solution)/shard_map/ppermute | solution.py:465
  6.1 3.4 %collective-permute-done.2 = f32[16,896]{1,0:T(8,128)S(1)} collective-permute-done((f32[16,896]{1,0:T(8,128)S(1)}, f32[16,896]{1,0:T(8,128)S(1)}, u32[]{:S(2)}, u32[]{:S(2)}) %collective-permute-start.2) | collective-permute-done | bytes 57376 | tf_op jit(solution)/shard_map/ppermute | solution.py:465
  9.6 2.0 %collective-permute-start.3 = (f32[16,896]{1,0:T(8,128)S(1)}, f32[16,896]{1,0:T(8,128)S(1)}, u32[]{:S(2)}, u32[]{:S(2)}) collective-permute-start(f32[16,896]{1,0:T(8,128)S(1)} %pad_maximum_fusion.3), channel_id=1, source_target_pairs={{0,2},{2,0},{4,6},{6,4},{8,10},{10,8},{12,14},{14,12},{16,18},{18,... | collective-permute-start | bytes 172040 | tf_op jit(solution)/shard_map/ppermute | solution.py:465
  11.6 2.3 %collective-permute-done.3 = f32[16,896]{1,0:T(8,128)S(1)} collective-permute-done((f32[16,896]{1,0:T(8,128)S(1)}, f32[16,896]{1,0:T(8,128)S(1)}, u32[]{:S(2)}, u32[]{:S(2)}) %collective-permute-start.3) | collective-permute-done | bytes 57376 | tf_op jit(solution)/shard_map/ppermute | solution.py:465
  13.9 3.1 %collective-permute-start.4 = (f32[16,896]{1,0:T(8,128)S(1)}, f32[16,896]{1,0:T(8,128)S(1)}, u32[]{:S(2)}, u32[]{:S(2)}) collective-permute-start(f32[16,896]{1,0:T(8,128)S(1)} %pad_maximum_fusion.4), channel_id=1, source_target_pairs={{0,16},{2,18},{4,20},{6,22},{8,24},{10,26},{12,28},{14,30},{16,0},... | collective-permute-start | bytes 172040 | tf_op jit(solution)/shard_map/ppermute | solution.py:465
  17.0 2.7 %collective-permute-done.4 = f32[16,896]{1,0:T(8,128)S(1)} collective-permute-done((f32[16,896]{1,0:T(8,128)S(1)}, f32[16,896]{1,0:T(8,128)S(1)}, u32[]{:S(2)}, u32[]{:S(2)}) %collective-permute-start.4) | collective-permute-done | bytes 57376 | tf_op jit(solution)/shard_map/ppermute | solution.py:465
  19.7 5.9 %collective-permute-start.5 = (f32[16,896]{1,0:T(8,128)S(1)}, f32[16,896]{1,0:T(8,128)S(1)}, u32[]{:S(2)}, u32[]{:S(2)}) collective-permute-start(f32[16,896]{1,0:T(8,128)S(1)} %pad_maximum_fusion.5), channel_id=1, source_target_pairs={{0,14},{2,4},{4,2},{6,8},{8,6},{10,12},{12,10},{14,0},{16,30},{18,... | collective-permute-start | bytes 172040 | tf_op jit(solution)/shard_map/ppermute | solution.py:465
  25.6 2.2 %collective-permute-done.5 = f32[16,896]{1,0:T(8,128)S(1)} collective-permute-done((f32[16,896]{1,0:T(8,128)S(1)}, f32[16,896]{1,0:T(8,128)S(1)}, u32[]{:S(2)}, u32[]{:S(2)}) %collective-permute-start.5) | collective-permute-done | bytes 57376 | tf_op jit(solution)/shard_map/ppermute | solution.py:465
  27.8 0.7 %collective-permute-start.6 = (f32[16,384]{1,0:T(8,128)S(1)}, f32[16,384]{1,0:T(8,128)S(1)}, u32[]{:S(2)}, u32[]{:S(2)}) collective-permute-start(f32[16,384]{1,0:T(8,128)S(1)} %pad_maximum_fusion.6), channel_id=1, source_target_pairs={{0,224},{224,0},{1,225},{225,1},{2,226},{226,2},{3,227},{227,3},{4... | collective-permute-start | bytes 73736 | tf_op jit(solution)/shard_map/ppermute | solution.py:465
  28.5 1.6 %collective-permute-start = (bf16[1,512,256]{2,1,0:T(8,128)(2,1)S(1)}, bf16[1,512,256]{2,1,0:T(8,128)(2,1)S(1)}, u32[]{:S(2)}, u32[]{:S(2)}) collective-permute-start(bf16[1,512,256]{2,1,0:T(8,128)(2,1)S(1)} %get-tuple-element.28), channel_id=1, source_target_pairs={{0,1},{1,0},{2,3},{3,2},{4,5},{5,4},{6,7},{7,6},{8,9},{9,8},{10,11... | collective-permute-start | bytes 786440 | tf_op jit(solution)/shard_map/ppermute | solution.py:522
  30.0 2.0 %collective-permute-start.7 = (f32[16,768]{1,0:T(8,128)S(1)}, f32[16,768]{1,0:T(8,128)S(1)}, u32[]{:S(2)}, u32[]{:S(2)}) collective-permute-start(f32[16,768]{1,0:T(8,128)S(1)} %slice_add_fusion), channel_id=1, source_target_pairs={{0,6},{2,12},{4,10},{6,0},{8,14},{10,4},{12,2},{14,8},{16,22},{18,... | collective-permute-start | bytes 147464 | tf_op jit(solution)/shard_map/ppermute | solution.py:465
  32.0 0.0 collective-permute-done.6
  32.1 0.1 collective-permute-start.8
  32.2 4.4 %collective-permute-done.7 = f32[16,768]{1,0:T(8,128)S(1)} collective-permute-done((f32[16,768]{1,0:T(8,128)S(1)}, f32[16,768]{1,0:T(8,128)S(1)}, u32[]{:S(2)}, u32[]{:S(2)}) %collective-permute-start.7) | collective-permute-done | bytes 49184 | tf_op jit(solution)/shard_map/ppermute | solution.py:465
  36.6 0.1 collective-permute-start.10
  36.7 0.0 collective-permute-done.8
  36.7 0.1 collective-permute-start.9
  36.8 0.0 collective-permute-done.refs_2_
  36.8 0.4 prepare.1
  37.2 0.5 %back_own.1.refs_5_ = f32[512,256]{1,0:T(8,128)S(1)} custom-call(s32[16,128]{1,0:T(8,128)S(1)} %get-tuple-element.23.refs_0_, bf16[256,256]{1,0:T(8,128)(2,1)S(1)} %get-tuple-element.24.refs_1_, f32[16,768]{1,0:T(8,128)S(1)} %add.73.refs_2_.refs_3_), custom_call_target="tpu_custom_call" | custom-call | tf_op jit(solution)/shard_map/back_own/pallas_call | solution.py:326
  37.7 0.3 collective-permute-done.9.refs_4_
  38.0 1.3 %back_x.1 = (f32[2,512,256]{2,1,0:T(8,128)}, f32[16,2,256]{2,1,0:T(2,128)}, f32[512,256]{1,0:T(8,128)S(1)}) custom-call(s32[16,128]{1,0:T(8,128)S(1)} %get-tuple-element.25.refs_0_, bf16[512,256]{1,0:T(8,128)(2,1)S(1)} %get-tuple-element.29.refs_1_, f32[2,512,256]{2,1,0:T(8,128)S(1)} %get-tuple-element.30.refs_2_, f32[16,384]{1,0:T(8,128)S(1)} %add.74.refs_3_, ...), custom_call_target="tpu_custom_call" | custom-call | tf_op jit(solution)/shard_map/back_x/pallas_call | solution.py:383
  39.2 1.5 %collective-permute-done.10.refs_4_ = f32[16,768]{1,0:T(8,128)S(1)} collective-permute-done((f32[16,768]{1,0:T(8,128)S(1)}, f32[16,768]{1,0:T(8,128)S(1)}, u32[]{:S(2)}, u32[]{:S(2)}) %collective-permute-start.10) | collective-permute-done | bytes 49184 | tf_op jit(solution)/shard_map/ppermute | solution.py:465
  40.7 1.3 %back_last.1 = (f32[2,512,256]{2,1,0:T(8,128)}, f32[16,2,512]{2,1,0:T(2,128)}) custom-call(s32[16,128]{1,0:T(8,128)S(1)} %get-tuple-element.23.refs_0_, bf16[256,256]{1,0:T(8,128)(2,1)S(1)} %get-tuple-element.24.refs_1_, f32[512,256]{1,0:T(8,128)S(1)} %get-tuple-element.38.refs_2_, ...), custom_call_target="tpu_custom_call", output_to_operand_aliasing={{0}: (5, {})} | custom-call | tf_op jit(solution)/shard_map/back_last/pallas_call | solution.py:442
  (25 shorter events, 0.2 us)
Async XLA Ops:
  2.6 1.3 %collective-permute-start.1 = (f32[16,896]{1,0:T(8,128)S(1)}, f32[16,896]{1,0:T(8,128)S(1)}, u32[]{:S(2)}, u32[]{:S(2)}) collective-permute-start(f32[16,896]{1,0:T(8,128)S(1)} %pad_maximum_fusion.1), channel_id=1, source_target_pairs={{0,32},{32,0},{64,96},{96,64},{128,160},{160,128},{192,224},{224,1... | collective-permute-start | bytes 172040 | tf_op jit(solution)/shard_map/ppermute | solution.py:465
  4.0 5.5 %collective-permute-start.2 = (f32[16,896]{1,0:T(8,128)S(1)}, f32[16,896]{1,0:T(8,128)S(1)}, u32[]{:S(2)}, u32[]{:S(2)}) collective-permute-start(f32[16,896]{1,0:T(8,128)S(1)} %pad_maximum_fusion.2), channel_id=1, source_target_pairs={{32,64},{64,32},{96,128},{128,96},{160,192},{192,160},{33,65},{65,... | collective-permute-start | bytes 172040 | tf_op jit(solution)/shard_map/ppermute | solution.py:465
  9.6 4.3 %collective-permute-start.3 = (f32[16,896]{1,0:T(8,128)S(1)}, f32[16,896]{1,0:T(8,128)S(1)}, u32[]{:S(2)}, u32[]{:S(2)}) collective-permute-start(f32[16,896]{1,0:T(8,128)S(1)} %pad_maximum_fusion.3), channel_id=1, source_target_pairs={{0,2},{2,0},{4,6},{6,4},{8,10},{10,8},{12,14},{14,12},{16,18},{18,... | collective-permute-start | bytes 172040 | tf_op jit(solution)/shard_map/ppermute | solution.py:465
  13.9 5.8 %collective-permute-start.4 = (f32[16,896]{1,0:T(8,128)S(1)}, f32[16,896]{1,0:T(8,128)S(1)}, u32[]{:S(2)}, u32[]{:S(2)}) collective-permute-start(f32[16,896]{1,0:T(8,128)S(1)} %pad_maximum_fusion.4), channel_id=1, source_target_pairs={{0,16},{2,18},{4,20},{6,22},{8,24},{10,26},{12,28},{14,30},{16,0},... | collective-permute-start | bytes 172040 | tf_op jit(solution)/shard_map/ppermute | solution.py:465
  19.7 8.1 %collective-permute-start.5 = (f32[16,896]{1,0:T(8,128)S(1)}, f32[16,896]{1,0:T(8,128)S(1)}, u32[]{:S(2)}, u32[]{:S(2)}) collective-permute-start(f32[16,896]{1,0:T(8,128)S(1)} %pad_maximum_fusion.5), channel_id=1, source_target_pairs={{0,14},{2,4},{4,2},{6,8},{8,6},{10,12},{12,10},{14,0},{16,30},{18,... | collective-permute-start | bytes 172040 | tf_op jit(solution)/shard_map/ppermute | solution.py:465
  27.8 4.3 %collective-permute-start.6 = (f32[16,384]{1,0:T(8,128)S(1)}, f32[16,384]{1,0:T(8,128)S(1)}, u32[]{:S(2)}, u32[]{:S(2)}) collective-permute-start(f32[16,384]{1,0:T(8,128)S(1)} %pad_maximum_fusion.6), channel_id=1, source_target_pairs={{0,224},{224,0},{1,225},{225,1},{2,226},{226,2},{3,227},{227,3},{4... | collective-permute-start | bytes 73736 | tf_op jit(solution)/shard_map/ppermute | solution.py:465
  28.5 8.3 %collective-permute-start = (bf16[1,512,256]{2,1,0:T(8,128)(2,1)S(1)}, bf16[1,512,256]{2,1,0:T(8,128)(2,1)S(1)}, u32[]{:S(2)}, u32[]{:S(2)}) collective-permute-start(bf16[1,512,256]{2,1,0:T(8,128)(2,1)S(1)} %get-tuple-element.28), channel_id=1, source_target_pairs={{0,1},{1,0},{2,3},{3,2},{4,5},{5,4},{6,7},{7,6},{8,9},{9,8},{10,11... | collective-permute-start | bytes 786440 | tf_op jit(solution)/shard_map/ppermute | solution.py:522
  30.0 6.5 %collective-permute-start.7 = (f32[16,768]{1,0:T(8,128)S(1)}, f32[16,768]{1,0:T(8,128)S(1)}, u32[]{:S(2)}, u32[]{:S(2)}) collective-permute-start(f32[16,768]{1,0:T(8,128)S(1)} %slice_add_fusion), channel_id=1, source_target_pairs={{0,6},{2,12},{4,10},{6,0},{8,14},{10,4},{12,2},{14,8},{16,22},{18,... | collective-permute-start | bytes 147464 | tf_op jit(solution)/shard_map/ppermute | solution.py:465
  32.1 4.6 %collective-permute-start.8 = (f32[16,384]{1,0:T(8,128)S(1)}, f32[16,384]{1,0:T(8,128)S(1)}, u32[]{:S(2)}, u32[]{:S(2)}) collective-permute-start(f32[16,384]{1,0:T(8,128)S(1)} %fusion), channel_id=1, source_target_pairs={{0,96},{32,192},{64,160},{96,0},{128,224},{160,64},{192,32},{224,1... | collective-permute-start | bytes 73736 | tf_op jit(solution)/shard_map/ppermute | solution.py:465
  36.6 4.2 %collective-permute-start.10 = (f32[16,768]{1,0:T(8,128)S(1)}, f32[16,768]{1,0:T(8,128)S(1)}, u32[]{:S(2)}, u32[]{:S(2)}) collective-permute-start(f32[16,768]{1,0:T(8,128)S(1)} %add.73.refs_2_.refs_3_), channel_id=1, source_target_pairs={{0,2},{2,0},{4,6},{6,4},{8,10},{10,8},{12,14},{14,12},{16,18},{18,... | collective-permute-start | bytes 147464 | tf_op jit(solution)/shard_map/ppermute | solution.py:465
  36.7 1.3 %collective-permute-start.9 = (f32[16,384]{1,0:T(8,128)S(1)}, f32[16,384]{1,0:T(8,128)S(1)}, u32[]{:S(2)}, u32[]{:S(2)}) collective-permute-start(f32[16,384]{1,0:T(8,128)S(1)} %add.74.refs_3_), channel_id=1, source_target_pairs={{0,32},{32,0},{64,96},{96,64},{128,160},{160,128},{192,224},{224,1... | collective-permute-start | bytes 73736 | tf_op jit(solution)/shard_map/ppermute | solution.py:465

commit v9 on v8

--- a/solution.py
+++ b/solution.py
@@ -344,7 +344,7 @@
     column = column_ref[...]
     flip = other % 2 == 1
     mine = half_of(other)
-    held = half_of(block)
+    held = block % 2
     size = cells // CHUNKS
     copies = []
 
@@ -477,10 +477,6 @@
     return odd_twin(i) if abs(odd_twin(i) - i) == 1 else i
 
 
-def end_twin(i):
-    return i if abs(odd_twin(i) - i) == 1 else odd_twin(i)
-
-
 def across(i):
     return i - i % RING + (i + (-3 if i % 2 else 3)) % RING
 
@@ -511,22 +507,22 @@
     def one_above(value):
         return jnp.concatenate([value[:, : value.shape[1] // 2], value[:, value.shape[1] // 2 :]], axis=0)
 
-    def split(value, axis):
-        owns = half_of(lax.axis_index(axis)) == 0
+    def split(value, held):
+        owns = held == 0
         low, high = value[:rows], value[rows:]
         return jnp.where(owns, low, high), jnp.where(owns, high, low)
 
     y_a, y_mid, y_b = sum_y[:, :edge_y], sum_y[:, edge_y : 2 * edge_y], sum_y[:, 2 * edge_y :]
-    half_x, sent = split(sum_x, "gx")
+    half_x, sent = split(sum_x, lax.axis_index("gx") % 2)
     got = exchange(jnp.concatenate([sent, side_by_side(y_a)], axis=1), "gx", twin)
+    got_b = exchange(y_b, "gx", next_twin)
     beside = lax.ppermute(near, "pa", [(0, 1), (1, 0)])
     half_x, y_a = half_x + got[:, :wide], y_a + one_above(got[:, wide:])
-    got = exchange(jnp.concatenate([half_x, side_by_side(y_b)], axis=1), "gx", next_twin)
-    half_x, y_b = half_x + got[:, :wide], y_b + one_above(got[:, wide:])
+    y_b = y_b + got_b
     sum_y = jnp.concatenate([y_a, y_mid, y_b], axis=1)
     x_a, x_mid, x_b = half_x[:, :edge_x], half_x[:, edge_x : 2 * edge_x], half_x[:, 2 * edge_x :]
 
-    half, sent = split(sum_y, "gy")
+    half, sent = split(sum_y, half_of(lax.axis_index("gy")))
     got = exchange(jnp.concatenate([sent, x_a], axis=1), "gy", twin)
     half, x_a = half + got[:, :long], x_a + got[:, long:]
     got = exchange(jnp.concatenate([half, x_b], axis=1), "gy", lambda i: i ^ RING)
@@ -539,11 +535,10 @@
     half_x = jnp.concatenate([x_a, x_mid, x_b + got], axis=1)
 
     half = half + exchange(half, "gy", across)
-    half_x = half_x + exchange(half_x, "gx", end_twin)
-    got = exchange(half_x, "gx", across)
+    got = [exchange(half_x, "gx", lambda i: i ^ bit) for bit in (2, 6, 4)]
     other = exchange(half, "gy", twin)
     half_x, half = lax.optimization_barrier((half_x, half))
-    half_x = half_x + got
+    half_x = half_x + got[0] + got[1] + got[2]
     away_x = exchange(half_x, "gx", twin)
 
     table_x, base = prepare(lane, volume, beside, count_x)

time: 42.2 us -> 42.8 us (1.014)
  the two profiles are of different devices: /device:TPU:16 before, /device:TPU:10 now
where the time goes in v9:
time: 42.8 us; the launch traced here: 42.4 us
  starting transfers between devices  21.3 us (50%)
  waiting for transfers between devices  14.7 us (34%)
  Pallas kernels  5.4 us (13%)
  between operations  0.87 us (2%)
    ppermute x11, starting transfers between devices, exchange(): lax.ppermute(value, axis, [(i, partner(i)) for i in range(lax.axis_size(a...  20.8 us
    ppermute x11, waiting for transfers between devices, exchange(): lax.ppermute(value, axis, [(i, partner(i)) for i in range(lax.axis_size(a...  12.4 us
    ppermute x1, waiting for transfers between devices, steps(): beside = lax.ppermute(near, 'pa', [(0, 1), (1, 0)])  2.28 us
    pallas_call x1, Pallas kernels, forward(): pl.pallas_call(body, out_shape=(out_vmem((planes * views, cells_y + 2 * p...  1.92 us
    pallas_call x1, Pallas kernels, back_last(): pl.pallas_call(body, out_shape=(jax.ShapeDtypeStruct(gradient.shape, F32)...  1.31 us
    pallas_call x1, Pallas kernels, back_x(): pl.pallas_call(body, out_shape=(jax.ShapeDtypeStruct(base.shape, F32), ja...  1.28 us
  transfers between devices with their start and end apart: 12, of which 6 were waited for; matrix products, arithmetic and copies ran while one was open for 0% of the time, Pallas kernels for 5%

profile of v9, /device:TPU:10, one launch (start us, length us, event | category | flops | bytes accessed | tf_op | source)
XLA Modules:
  0.0 42.4 jit_solution(14995533394095330194)
XLA Ops:
  0.6 1.9 %forward.1 = (f32[32,384]{1,0:T(8,128)S(1)}, f32[32,768]{1,0:T(8,128)S(1)}, bf16[256,256]{1,0:T(8,128)(2,1)S(1)}, bf16[1,512,256]{2,1,0:T(8,128)(2,1)S(1)}, bf16...) custom-call(s32[2,16]{1,0:T(2,128)} %refs_0_.1, ...), custom_call_target="tpu_custom_call" | custom-call | tf_op jit(solution)/shard_map/forward/pallas_call | solution.py:214
  2.6 0.1 collective-permute-start.1
  2.7 2.4 %collective-permute-start.2 = (f32[32,256]{1,0:T(8,128)S(1)}, f32[32,256]{1,0:T(8,128)S(1)}, u32[]{:S(2)}, u32[]{:S(2)}) collective-permute-start(f32[32,256]{1,0:T(8,128)S(1)} %slice.78), channel_id=1, source_target_pairs={{32,64},{64,32},{96,128},{128,96},{160,192},{192,160},{33,65},{65,... | collective-permute-start | bytes 98312 | tf_op jit(solution)/shard_map/ppermute | solution.py:465
  5.2 0.0 collective-permute-done.1
  5.2 2.7 %collective-permute-done.2 = f32[32,256]{1,0:T(8,128)S(1)} collective-permute-done((f32[32,256]{1,0:T(8,128)S(1)}, f32[32,256]{1,0:T(8,128)S(1)}, u32[]{:S(2)}, u32[]{:S(2)}) %collective-permute-start.2) | collective-permute-done | bytes 32800 | tf_op jit(solution)/shard_map/ppermute | solution.py:465
  8.0 2.0 %collective-permute-start.3 = (f32[16,896]{1,0:T(8,128)S(1)}, f32[16,896]{1,0:T(8,128)S(1)}, u32[]{:S(2)}, u32[]{:S(2)}) collective-permute-start(f32[16,896]{1,0:T(8,128)S(1)} %pad_maximum_fusion.2), channel_id=1, source_target_pairs={{0,2},{2,0},{4,6},{6,4},{8,10},{10,8},{12,14},{14,12},{16,18},{18,... | collective-permute-start | bytes 172040 | tf_op jit(solution)/shard_map/ppermute | solution.py:465
  10.0 2.6 %collective-permute-done.3 = f32[16,896]{1,0:T(8,128)S(1)} collective-permute-done((f32[16,896]{1,0:T(8,128)S(1)}, f32[16,896]{1,0:T(8,128)S(1)}, u32[]{:S(2)}, u32[]{:S(2)}) %collective-permute-start.3) | collective-permute-done | bytes 57376 | tf_op jit(solution)/shard_map/ppermute | solution.py:465
  12.6 2.2 %collective-permute-start.4 = (f32[16,896]{1,0:T(8,128)S(1)}, f32[16,896]{1,0:T(8,128)S(1)}, u32[]{:S(2)}, u32[]{:S(2)}) collective-permute-start(f32[16,896]{1,0:T(8,128)S(1)} %pad_maximum_fusion.3), channel_id=1, source_target_pairs={{0,16},{2,18},{4,20},{6,22},{8,24},{10,26},{12,28},{14,30},{16,0},... | collective-permute-start | bytes 172040 | tf_op jit(solution)/shard_map/ppermute | solution.py:465
  14.8 3.6 %collective-permute-done.4 = f32[16,896]{1,0:T(8,128)S(1)} collective-permute-done((f32[16,896]{1,0:T(8,128)S(1)}, f32[16,896]{1,0:T(8,128)S(1)}, u32[]{:S(2)}, u32[]{:S(2)}) %collective-permute-start.4) | collective-permute-done | bytes 57376 | tf_op jit(solution)/shard_map/ppermute | solution.py:465
  18.4 5.8 %collective-permute-start.5 = (f32[16,896]{1,0:T(8,128)S(1)}, f32[16,896]{1,0:T(8,128)S(1)}, u32[]{:S(2)}, u32[]{:S(2)}) collective-permute-start(f32[16,896]{1,0:T(8,128)S(1)} %pad_maximum_fusion.4), channel_id=1, source_target_pairs={{0,14},{2,4},{4,2},{6,8},{8,6},{10,12},{12,10},{14,0},{16,30},{18,... | collective-permute-start | bytes 172040 | tf_op jit(solution)/shard_map/ppermute | solution.py:465
  24.2 2.2 %collective-permute-done.5 = f32[16,896]{1,0:T(8,128)S(1)} collective-permute-done((f32[16,896]{1,0:T(8,128)S(1)}, f32[16,896]{1,0:T(8,128)S(1)}, u32[]{:S(2)}, u32[]{:S(2)}) %collective-permute-start.5) | collective-permute-done | bytes 57376 | tf_op jit(solution)/shard_map/ppermute | solution.py:465
  26.4 2.1 %collective-permute-start.6 = (f32[16,768]{1,0:T(8,128)S(1)}, f32[16,768]{1,0:T(8,128)S(1)}, u32[]{:S(2)}, u32[]{:S(2)}) collective-permute-start(f32[16,768]{1,0:T(8,128)S(1)} %slice_add_fusion), channel_id=1, source_target_pairs={{0,6},{2,12},{4,10},{6,0},{8,14},{10,4},{12,2},{14,8},{16,22},{18,... | collective-permute-start | bytes 147464 | tf_op jit(solution)/shard_map/ppermute | solution.py:465
  28.5 0.0 collective-permute-start.7
  28.5 2.7 %collective-permute-start.8 = (f32[16,384]{1,0:T(8,128)S(1)}, f32[16,384]{1,0:T(8,128)S(1)}, u32[]{:S(2)}, u32[]{:S(2)}) collective-permute-start(f32[16,384]{1,0:T(8,128)S(1)} %pad_maximum_fusion.5), channel_id=1, source_target_pairs={{0,192},{32,224},{64,128},{96,160},{128,64},{160,96},{192,0},{224,... | collective-permute-start | bytes 73736 | tf_op jit(solution)/shard_map/ppermute | solution.py:465
  31.2 1.4 %collective-permute-start.9 = (f32[16,384]{1,0:T(8,128)S(1)}, f32[16,384]{1,0:T(8,128)S(1)}, u32[]{:S(2)}, u32[]{:S(2)}) collective-permute-start(f32[16,384]{1,0:T(8,128)S(1)} %pad_maximum_fusion.5), channel_id=1, source_target_pairs={{0,128},{32,160},{64,192},{96,224},{128,0},{160,32},{192,64},{224,... | collective-permute-start | bytes 73736 | tf_op jit(solution)/shard_map/ppermute | solution.py:465
  32.5 0.5 %collective-permute-start = (bf16[1,512,256]{2,1,0:T(8,128)(2,1)S(1)}, bf16[1,512,256]{2,1,0:T(8,128)(2,1)S(1)}, u32[]{:S(2)}, u32[]{:S(2)}) collective-permute-start(bf16[1,512,256]{2,1,0:T(8,128)(2,1)S(1)} %get-tuple-element.28), channel_id=1, source_target_pairs={{0,1},{1,0},{2,3},{3,2},{4,5},{5,4},{6,7},{7,6},{8,9},{9,8},{10,11... | collective-permute-start | bytes 786440 | tf_op jit(solution)/shard_map/ppermute | solution.py:519
  33.1 0.0 collective-permute-done.6
  33.1 2.0 %collective-permute-start.11 = (f32[16,768]{1,0:T(8,128)S(1)}, f32[16,768]{1,0:T(8,128)S(1)}, u32[]{:S(2)}, u32[]{:S(2)}) collective-permute-start(f32[16,768]{1,0:T(8,128)S(1)} %add.66.refs_2_.refs_3_), channel_id=1, source_target_pairs={{0,2},{2,0},{4,6},{6,4},{8,10},{10,8},{12,14},{14,12},{16,18},{18,... | collective-permute-start | bytes 147464 | tf_op jit(solution)/shard_map/ppermute | solution.py:465
  35.1 0.0 collective-permute-done.7
  35.1 0.0 collective-permute-done.8
  35.1 1.4 %collective-permute-done.9 = f32[16,384]{1,0:T(8,128)S(1)} collective-permute-done((f32[16,384]{1,0:T(8,128)S(1)}, f32[16,384]{1,0:T(8,128)S(1)}, u32[]{:S(2)}, u32[]{:S(2)}) %collective-permute-start.9) | collective-permute-done | bytes 24608 | tf_op jit(solution)/shard_map/ppermute | solution.py:465
  36.5 0.1 collective-permute-start.10
  36.6 2.3 %collective-permute-done.refs_2_ = bf16[1,512,256]{2,1,0:T(8,128)(2,1)S(1)} collective-permute-done((bf16[1,512,256]{2,1,0:T(8,128)(2,1)S(1)}, bf16[1,512,256]{2,1,0:T(8,128)(2,1)S(1)}, u32[]{:S(2)}, u32[]{:S(2)}) %collective-permute-start) | collective-permute-done | bytes 262176 | tf_op jit(solution)/shard_map/ppermute | solution.py:519
  38.9 0.4 prepare.1
  39.3 0.5 %back_own.1.refs_5_ = f32[512,256]{1,0:T(8,128)S(1)} custom-call(s32[16,128]{1,0:T(8,128)S(1)} %get-tuple-element.23.refs_0_, bf16[256,256]{1,0:T(8,128)(2,1)S(1)} %get-tuple-element.24.refs_1_, f32[16,768]{1,0:T(8,128)S(1)} %add.66.refs_2_.refs_3_), custom_call_target="tpu_custom_call" | custom-call | tf_op jit(solution)/shard_map/back_own/pallas_call | solution.py:326
  39.8 0.0 collective-permute-done.10.refs_4_
  39.8 1.3 %back_x.1 = (f32[2,512,256]{2,1,0:T(8,128)}, f32[16,2,256]{2,1,0:T(2,128)}, f32[512,256]{1,0:T(8,128)S(1)}) custom-call(s32[16,128]{1,0:T(8,128)S(1)} %get-tuple-element.25.refs_0_, bf16[512,256]{1,0:T(8,128)(2,1)S(1)} %get-tuple-element.29.refs_1_, f32[2,512,256]{2,1,0:T(8,128)S(1)} %get-tuple-element.30.refs_2_, f32[16,384]{1,0:T(8,128)S(1)} %add_add_fusion.refs_3_, ...), custom_call_target="tpu_custom_call" | custom-call | tf_op jit(solution)/shard_map/back_x/pallas_call | solution.py:383
  41.1 0.0 collective-permute-done.11.refs_4_
  41.1 1.3 %back_last.1 = (f32[2,512,256]{2,1,0:T(8,128)}, f32[16,2,512]{2,1,0:T(2,128)}) custom-call(s32[16,128]{1,0:T(8,128)S(1)} %get-tuple-element.23.refs_0_, bf16[256,256]{1,0:T(8,128)(2,1)S(1)} %get-tuple-element.24.refs_1_, f32[512,256]{1,0:T(8,128)S(1)} %get-tuple-element.38.refs_2_, ...), custom_call_target="tpu_custom_call", output_to_operand_aliasing={{0}: (5, {})} | custom-call | tf_op jit(solution)/shard_map/back_last/pallas_call | solution.py:442
  (22 shorter events, 0.1 us)
Async XLA Ops:
  2.6 2.6 %collective-permute-start.1 = (f32[16,896]{1,0:T(8,128)S(1)}, f32[16,896]{1,0:T(8,128)S(1)}, u32[]{:S(2)}, u32[]{:S(2)}) collective-permute-start(f32[16,896]{1,0:T(8,128)S(1)} %pad_maximum_fusion.1), channel_id=1, source_target_pairs={{0,32},{32,0},{64,96},{96,64},{128,160},{160,128},{192,224},{224,1... | collective-permute-start | bytes 172040 | tf_op jit(solution)/shard_map/ppermute | solution.py:465
  2.7 5.2 %collective-permute-start.2 = (f32[32,256]{1,0:T(8,128)S(1)}, f32[32,256]{1,0:T(8,128)S(1)}, u32[]{:S(2)}, u32[]{:S(2)}) collective-permute-start(f32[32,256]{1,0:T(8,128)S(1)} %slice.78), channel_id=1, source_target_pairs={{32,64},{64,32},{96,128},{128,96},{160,192},{192,160},{33,65},{65,... | collective-permute-start | bytes 98312 | tf_op jit(solution)/shard_map/ppermute | solution.py:465
  8.0 4.6 %collective-permute-start.3 = (f32[16,896]{1,0:T(8,128)S(1)}, f32[16,896]{1,0:T(8,128)S(1)}, u32[]{:S(2)}, u32[]{:S(2)}) collective-permute-start(f32[16,896]{1,0:T(8,128)S(1)} %pad_maximum_fusion.2), channel_id=1, source_target_pairs={{0,2},{2,0},{4,6},{6,4},{8,10},{10,8},{12,14},{14,12},{16,18},{18,... | collective-permute-start | bytes 172040 | tf_op jit(solution)/shard_map/ppermute | solution.py:465
  12.6 5.8 %collective-permute-start.4 = (f32[16,896]{1,0:T(8,128)S(1)}, f32[16,896]{1,0:T(8,128)S(1)}, u32[]{:S(2)}, u32[]{:S(2)}) collective-permute-start(f32[16,896]{1,0:T(8,128)S(1)} %pad_maximum_fusion.3), channel_id=1, source_target_pairs={{0,16},{2,18},{4,20},{6,22},{8,24},{10,26},{12,28},{14,30},{16,0},... | collective-permute-start | bytes 172040 | tf_op jit(solution)/shard_map/ppermute | solution.py:465
  18.4 7.9 %collective-permute-start.5 = (f32[16,896]{1,0:T(8,128)S(1)}, f32[16,896]{1,0:T(8,128)S(1)}, u32[]{:S(2)}, u32[]{:S(2)}) collective-permute-start(f32[16,896]{1,0:T(8,128)S(1)} %pad_maximum_fusion.4), channel_id=1, source_target_pairs={{0,14},{2,4},{4,2},{6,8},{8,6},{10,12},{12,10},{14,0},{16,30},{18,... | collective-permute-start | bytes 172040 | tf_op jit(solution)/shard_map/ppermute | solution.py:465
  26.4 6.7 %collective-permute-start.6 = (f32[16,768]{1,0:T(8,128)S(1)}, f32[16,768]{1,0:T(8,128)S(1)}, u32[]{:S(2)}, u32[]{:S(2)}) collective-permute-start(f32[16,768]{1,0:T(8,128)S(1)} %slice_add_fusion), channel_id=1, source_target_pairs={{0,6},{2,12},{4,10},{6,0},{8,14},{10,4},{12,2},{14,8},{16,22},{18,... | collective-permute-start | bytes 147464 | tf_op jit(solution)/shard_map/ppermute | solution.py:465
  28.5 6.7 %collective-permute-start.7 = (f32[16,384]{1,0:T(8,128)S(1)}, f32[16,384]{1,0:T(8,128)S(1)}, u32[]{:S(2)}, u32[]{:S(2)}) collective-permute-start(f32[16,384]{1,0:T(8,128)S(1)} %pad_maximum_fusion.5), channel_id=1, source_target_pairs={{0,64},{32,96},{64,0},{96,32},{128,192},{160,224},{192,128},{224,1... | collective-permute-start | bytes 73736 | tf_op jit(solution)/shard_map/ppermute | solution.py:465
  28.5 6.7 %collective-permute-start.8 = (f32[16,384]{1,0:T(8,128)S(1)}, f32[16,384]{1,0:T(8,128)S(1)}, u32[]{:S(2)}, u32[]{:S(2)}) collective-permute-start(f32[16,384]{1,0:T(8,128)S(1)} %pad_maximum_fusion.5), channel_id=1, source_target_pairs={{0,192},{32,224},{64,128},{96,160},{128,64},{160,96},{192,0},{224,... | collective-permute-start | bytes 73736 | tf_op jit(solution)/shard_map/ppermute | solution.py:465
  31.2 5.3 %collective-permute-start.9 = (f32[16,384]{1,0:T(8,128)S(1)}, f32[16,384]{1,0:T(8,128)S(1)}, u32[]{:S(2)}, u32[]{:S(2)}) collective-permute-start(f32[16,384]{1,0:T(8,128)S(1)} %pad_maximum_fusion.5), channel_id=1, source_target_pairs={{0,128},{32,160},{64,192},{96,224},{128,0},{160,32},{192,64},{224,... | collective-permute-start | bytes 73736 | tf_op jit(solution)/shard_map/ppermute | solution.py:465
  32.5 6.4 %collective-permute-start = (bf16[1,512,256]{2,1,0:T(8,128)(2,1)S(1)}, bf16[1,512,256]{2,1,0:T(8,128)(2,1)S(1)}, u32[]{:S(2)}, u32[]{:S(2)}) collective-permute-start(bf16[1,512,256]{2,1,0:T(8,128)(2,1)S(1)} %get-tuple-element.28), channel_id=1, source_target_pairs={{0,1},{1,0},{2,3},{3,2},{4,5},{5,4},{6,7},{7,6},{8,9},{9,8},{10,11... | collective-permute-start | bytes 786440 | tf_op jit(solution)/shard_map/ppermute | solution.py:519
  33.1 8.0 %collective-permute-start.11 = (f32[16,768]{1,0:T(8,128)S(1)}, f32[16,768]{1,0:T(8,128)S(1)}, u32[]{:S(2)}, u32[]{:S(2)}) collective-permute-start(f32[16,768]{1,0:T(8,128)S(1)} %add.66.refs_2_.refs_3_), channel_id=1, source_target_pairs={{0,2},{2,0},{4,6},{6,4},{8,10},{10,8},{12,14},{14,12},{16,18},{18,... | collective-permute-start | bytes 147464 | tf_op jit(solution)/shard_map/ppermute | solution.py:465
  36.5 3.3 %collective-permute-start.10 = (f32[16,384]{1,0:T(8,128)S(1)}, f32[16,384]{1,0:T(8,128)S(1)}, u32[]{:S(2)}, u32[]{:S(2)}) collective-permute-start(f32[16,384]{1,0:T(8,128)S(1)} %add_add_fusion.refs_3_), channel_id=1, source_target_pairs={{0,32},{32,0},{64,96},{96,64},{128,160},{160,128},{192,224},{224,1... | collective-permute-start | bytes 73736 | tf_op jit(solution)/shard_map/ppermute | solution.py:465

commit v10 on v9

--- a/solution.py
+++ b/solution.py
@@ -481,6 +481,12 @@
     return i - i % RING + (i + (-3 if i % 2 else 3)) % RING
 
 
+def seam(value, axis):
+    ends = range(RING, lax.axis_size(axis), RING)
+    pairs = [(i - 1, i) for i in ends] + [(i, i - 1) for i in ends]
+    return lax.ppermute(value, axis, pairs)
+
+
 def at_end(size, axis):
     index = lax.axis_index(axis) % size
     return (index == 0) | (index == size - 1)
@@ -520,25 +526,28 @@
     half_x, y_a = half_x + got[:, :wide], y_a + one_above(got[:, wide:])
     y_b = y_b + got_b
     sum_y = jnp.concatenate([y_a, y_mid, y_b], axis=1)
+    half, sent = split(sum_y, half_of(lax.axis_index("gy")))
+    got_y = exchange(sent, "gy", twin)
+    got_x = exchange(half_x, "gx", lambda i: i ^ 2)
+    half = half + got_y
+    half_x, half = lax.optimization_barrier((half_x, half))
+    half_x = half_x + got_x
+    got_y = exchange(half, "gy", lambda i: i ^ RING)
+    got_x = exchange(half_x, "gx", lambda i: i ^ 6)
+    half, half_x = half + got_y, half_x + got_x
     x_a, x_mid, x_b = half_x[:, :edge_x], half_x[:, edge_x : 2 * edge_x], half_x[:, 2 * edge_x :]
 
-    half, sent = split(sum_y, half_of(lax.axis_index("gy")))
-    got = exchange(jnp.concatenate([sent, x_a], axis=1), "gy", twin)
-    half, x_a = half + got[:, :long], x_a + got[:, long:]
-    got = exchange(jnp.concatenate([half, x_b], axis=1), "gy", lambda i: i ^ RING)
+    got = exchange(jnp.concatenate([half, x_b], axis=1), "gy", odd_twin)
+    got_b = seam(x_b, "gy")
     half = half + got[:, :long]
-    sent_b = jnp.where(at_end(RING, "gy"), got[:, long:], x_b)
-    got = exchange(jnp.concatenate([half, sent_b], axis=1), "gy", odd_twin)
-    half = half + got[:, :long]
-    got = jnp.where(at_end(count_y, "gy"), 0.0, got[:, long:])
-    half, x_b, got = lax.optimization_barrier((half, x_b, got))
-    half_x = jnp.concatenate([x_a, x_mid, x_b + got], axis=1)
-
-    half = half + exchange(half, "gy", across)
-    got = [exchange(half_x, "gx", lambda i: i ^ bit) for bit in (2, 6, 4)]
+    x_a, half = lax.optimization_barrier((x_a, half))
+    got_y = exchange(half, "gy", across)
+    got_a = exchange(x_a, "gy", twin)
+    half = half + got_y
     other = exchange(half, "gy", twin)
-    half_x, half = lax.optimization_barrier((half_x, half))
-    half_x = half_x + got[0] + got[1] + got[2]
+    x_a, half, got = lax.optimization_barrier((x_a, half, got))
+    x_b = x_b + jnp.where(at_end(RING, "gy"), 0.0, got[:, long:]) + got_b
+    half_x = jnp.concatenate([x_a + got_a, x_mid, x_b], axis=1)
     away_x = exchange(half_x, "gx", twin)
 
     table_x, base = prepare(lane, volume, beside, count_x)

time: 42.8 us -> 47.3 us (1.11)
  the two profiles are of different devices: /device:TPU:10 before, /device:TPU:6 now
where the time goes in v10:
time: 47.3 us; the launch traced here: 47.1 us
  starting transfers between devices  26.2 us (55%)
  waiting for transfers between devices  14.6 us (31%)
  Pallas kernels  5.4 us (11%)
  between operations  0.87 us (2%)
    ppermute x11, starting transfers between devices, exchange(): lax.ppermute(value, axis, [(i, partner(i)) for i in range(lax.axis_size(a...  22.1 us
    ppermute x11, waiting for transfers between devices, exchange(): lax.ppermute(value, axis, [(i, partner(i)) for i in range(lax.axis_size(a...  8.98 us
    ppermute x1, waiting for transfers between devices, seam(): return lax.ppermute(value, axis, pairs)  4.91 us
    ppermute x1, starting transfers between devices, seam(): return lax.ppermute(value, axis, pairs)  3.96 us
    pallas_call x1, Pallas kernels, forward(): pl.pallas_call(body, out_shape=(out_vmem((planes * views, cells_y + 2 * p...  1.92 us
    pallas_call x1, Pallas kernels, back_last(): pl.pallas_call(body, out_shape=(jax.ShapeDtypeStruct(gradient.shape, F32)...  1.31 us
    pallas_call x1, Pallas kernels, back_x(): pl.pallas_call(body, out_shape=(jax.ShapeDtypeStruct(base.shape, F32), ja...  1.28 us
  transfers between devices with their start and end apart: 13, of which 7 were waited for; matrix products, arithmetic and copies ran while one was open for 0% of the time, Pallas kernels for 5%

profile of v10, /device:TPU:6, one launch (start us, length us, event | category | flops | bytes accessed | tf_op | source)
XLA Modules:
  0.0 47.1 jit_solution(16768341142964573344)
XLA Ops:
  0.6 1.9 %forward.1 = (f32[32,384]{1,0:T(8,128)S(1)}, f32[32,768]{1,0:T(8,128)S(1)}, bf16[256,256]{1,0:T(8,128)(2,1)S(1)}, bf16[1,512,256]{2,1,0:T(8,128)(2,1)S(1)}, bf16...) custom-call(s32[2,16]{1,0:T(2,128)} %refs_0_.1, ...), custom_call_target="tpu_custom_call" | custom-call | tf_op jit(solution)/shard_map/forward/pallas_call | solution.py:214
  2.6 0.1 collective-permute-start.1
  2.7 0.7 %collective-permute-start.2 = (f32[32,256]{1,0:T(8,128)S(1)}, f32[32,256]{1,0:T(8,128)S(1)}, u32[]{:S(2)}, u32[]{:S(2)}) collective-permute-start(f32[32,256]{1,0:T(8,128)S(1)} %slice.65), channel_id=1, source_target_pairs={{32,64},{64,32},{96,128},{128,96},{160,192},{192,160},{33,65},{65,... | collective-permute-start | bytes 98312 | tf_op jit(solution)/shard_map/ppermute | solution.py:465
  3.4 0.5 %collective-permute-done.1 = f32[16,896]{1,0:T(8,128)S(1)} collective-permute-done((f32[16,896]{1,0:T(8,128)S(1)}, f32[16,896]{1,0:T(8,128)S(1)}, u32[]{:S(2)}, u32[]{:S(2)}) %collective-permute-start.1) | collective-permute-done | bytes 57376 | tf_op jit(solution)/shard_map/ppermute | solution.py:465
  3.9 0.0 collective-permute-done.2
  4.0 2.0 %collective-permute-start.3 = (f32[16,768]{1,0:T(8,128)S(1)}, f32[16,768]{1,0:T(8,128)S(1)}, u32[]{:S(2)}, u32[]{:S(2)}) collective-permute-start(f32[16,768]{1,0:T(8,128)S(1)} %slice_select_fusion), channel_id=1, source_target_pairs={{0,2},{2,0},{4,6},{6,4},{8,10},{10,8},{12,14},{14,12},{16,18},{18,... | collective-permute-start | bytes 147464 | tf_op jit(solution)/shard_map/ppermute | solution.py:465
  6.0 5.6 %collective-permute-start.4 = (f32[16,384]{1,0:T(8,128)S(1)}, f32[16,384]{1,0:T(8,128)S(1)}, u32[]{:S(2)}, u32[]{:S(2)}) collective-permute-start(f32[16,384]{1,0:T(8,128)S(1)} %slice_add_fusion.1), channel_id=1, source_target_pairs={{0,64},{32,96},{64,0},{96,32},{128,192},{160,224},{192,128},{224,1... | collective-permute-start | bytes 73736 | tf_op jit(solution)/shard_map/ppermute | solution.py:465
  11.6 0.0 collective-permute-done.3
  11.6 1.8 %collective-permute-done.4 = f32[16,384]{1,0:T(8,128)S(1)} collective-permute-done((f32[16,384]{1,0:T(8,128)S(1)}, f32[16,384]{1,0:T(8,128)S(1)}, u32[]{:S(2)}, u32[]{:S(2)}) %collective-permute-start.4) | collective-permute-done | bytes 24608 | tf_op jit(solution)/shard_map/ppermute | solution.py:465
  13.4 3.5 %collective-permute-start.5 = (f32[16,384]{1,0:T(8,128)S(1)}, f32[16,384]{1,0:T(8,128)S(1)}, u32[]{:S(2)}, u32[]{:S(2)}) collective-permute-start(f32[16,384]{1,0:T(8,128)S(1)} %add.57), channel_id=1, source_target_pairs={{0,192},{32,224},{64,128},{96,160},{128,64},{160,96},{192,0},{224,... | collective-permute-start | bytes 73736 | tf_op jit(solution)/shard_map/ppermute | solution.py:465
  16.9 1.4 %collective-permute-start.6 = (f32[16,768]{1,0:T(8,128)S(1)}, f32[16,768]{1,0:T(8,128)S(1)}, u32[]{:S(2)}, u32[]{:S(2)}) collective-permute-start(f32[16,768]{1,0:T(8,128)S(1)} %select_add_fusion), channel_id=1, source_target_pairs={{0,16},{2,18},{4,20},{6,22},{8,24},{10,26},{12,28},{14,30},{16,0},... | collective-permute-start | bytes 147464 | tf_op jit(solution)/shard_map/ppermute | solution.py:465
  18.3 0.4 collective-permute-done.5
  18.7 3.8 %collective-permute-done.6 = f32[16,768]{1,0:T(8,128)S(1)} collective-permute-done((f32[16,768]{1,0:T(8,128)S(1)}, f32[16,768]{1,0:T(8,128)S(1)}, u32[]{:S(2)}, u32[]{:S(2)}) %collective-permute-start.6) | collective-permute-done | bytes 49184 | tf_op jit(solution)/shard_map/ppermute | solution.py:465
  22.5 5.0 %collective-permute-start.7 = (f32[16,896]{1,0:T(8,128)S(1)}, f32[16,896]{1,0:T(8,128)S(1)}, u32[]{:S(2)}, u32[]{:S(2)}) collective-permute-start(f32[16,896]{1,0:T(8,128)S(1)} %pad_maximum_fusion.2), channel_id=1, source_target_pairs={{0,14},{2,4},{4,2},{6,8},{8,6},{10,12},{12,10},{14,0},{16,30},{18,... | collective-permute-start | bytes 172040 | tf_op jit(solution)/shard_map/ppermute | solution.py:465
  27.5 2.5 %collective-permute-done.7 = f32[16,896]{1,0:T(8,128)S(1)} collective-permute-done((f32[16,896]{1,0:T(8,128)S(1)}, f32[16,896]{1,0:T(8,128)S(1)}, u32[]{:S(2)}, u32[]{:S(2)}) %collective-permute-start.7) | collective-permute-done | bytes 57376 | tf_op jit(solution)/shard_map/ppermute | solution.py:465
  30.0 1.7 %collective-permute-start.8 = (f32[16,768]{1,0:T(8,128)S(1)}, f32[16,768]{1,0:T(8,128)S(1)}, u32[]{:S(2)}, u32[]{:S(2)}) collective-permute-start(f32[16,768]{1,0:T(8,128)S(1)} %slice_add_fusion), channel_id=1, source_target_pairs={{0,6},{2,12},{4,10},{6,0},{8,14},{10,4},{12,2},{14,8},{16,22},{18,... | collective-permute-start | bytes 147464 | tf_op jit(solution)/shard_map/ppermute | solution.py:465
  31.7 2.0 %collective-permute-start.9 = (f32[16,128]{1,0:T(8,128)S(1)}, f32[16,128]{1,0:T(8,128)S(1)}, u32[]{:S(2)}, u32[]{:S(2)}) collective-permute-start(f32[16,128]{1,0:T(8,128)S(1)} %get-tuple-element.39), channel_id=1, source_target_pairs={{0,2},{2,0},{4,6},{6,4},{8,10},{10,8},{12,14},{14,12},{16,18},{18,... | collective-permute-start | bytes 24584 | tf_op jit(solution)/shard_map/ppermute | solution.py:465
  33.7 4.0 %collective-permute-start.10 = (f32[16,128]{1,0:T(8,128)S(1)}, f32[16,128]{1,0:T(8,128)S(1)}, u32[]{:S(2)}, u32[]{:S(2)}) collective-permute-start(f32[16,128]{1,0:T(8,128)S(1)} %get-tuple-element.57), channel_id=1, source_target_pairs={{14,16},{16,14},{15,17},{17,15},{46,48},{48,46},{47,49},{49,47},{7... | collective-permute-start | bytes 24584 | tf_op jit(solution)/shard_map/ppermute | solution.py:487
  37.7 0.1 collective-permute-start
  37.8 0.0 collective-permute-done.8
  37.8 0.1 collective-permute-start.12
  37.9 0.0 collective-permute-done.9
  37.9 4.9 %collective-permute-done.10 = f32[16,128]{1,0:T(8,128)S(1)} collective-permute-done((f32[16,128]{1,0:T(8,128)S(1)}, f32[16,128]{1,0:T(8,128)S(1)}, u32[]{:S(2)}, u32[]{:S(2)}) %collective-permute-start.10) | collective-permute-done | bytes 8224 | tf_op jit(solution)/shard_map/ppermute | solution.py:487
  42.9 0.1 collective-permute-start.11
  43.0 0.5 %back_own.1.refs_5_ = f32[512,256]{1,0:T(8,128)S(1)} custom-call(s32[16,128]{1,0:T(8,128)S(1)} %get-tuple-element.25.refs_0_, bf16[256,256]{1,0:T(8,128)(2,1)S(1)} %get-tuple-element.26.refs_1_, f32[16,768]{1,0:T(8,128)S(1)} %add.61.refs_2_.refs_3_), custom_call_target="tpu_custom_call" | custom-call | tf_op jit(solution)/shard_map/back_own/pallas_call | solution.py:326
  43.4 0.7 %collective-permute-done.refs_2_ = bf16[1,512,256]{2,1,0:T(8,128)(2,1)S(1)} collective-permute-done((bf16[1,512,256]{2,1,0:T(8,128)(2,1)S(1)}, bf16[1,512,256]{2,1,0:T(8,128)(2,1)S(1)}, u32[]{:S(2)}, u32[]{:S(2)}) %collective-permute-start) | collective-permute-done | bytes 262176 | tf_op jit(solution)/shard_map/ppermute | solution.py:525
  44.1 0.4 prepare.1
  44.5 0.0 collective-permute-done.11.refs_4_
  44.5 1.3 %back_x.1 = (f32[2,512,256]{2,1,0:T(8,128)}, f32[16,2,256]{2,1,0:T(2,128)}, f32[512,256]{1,0:T(8,128)S(1)}) custom-call(s32[16,128]{1,0:T(8,128)S(1)} %get-tuple-element.27.refs_0_, bf16[512,256]{1,0:T(8,128)(2,1)S(1)} %get-tuple-element.31.refs_1_, f32[2,512,256]{2,1,0:T(8,128)S(1)} %get-tuple-element.32.refs_2_, f32[16,384]{1,0:T(8,128)S(1)} %pad_maximum_fusion.3.refs_3_, ...), custom_call_target="tpu_custom_call" | custom-call | tf_op jit(solution)/shard_map/back_x/pallas_call | solution.py:383
  45.8 0.0 collective-permute-done.12.refs_4_
  45.8 1.3 %back_last.1 = (f32[2,512,256]{2,1,0:T(8,128)}, f32[16,2,512]{2,1,0:T(2,128)}) custom-call(s32[16,128]{1,0:T(8,128)S(1)} %get-tuple-element.25.refs_0_, bf16[256,256]{1,0:T(8,128)(2,1)S(1)} %get-tuple-element.26.refs_1_, f32[512,256]{1,0:T(8,128)S(1)} %get-tuple-element.42.refs_2_, ...), custom_call_target="tpu_custom_call", output_to_operand_aliasing={{0}: (5, {})} | custom-call | tf_op jit(solution)/shard_map/back_last/pallas_call | solution.py:442
  (20 shorter events, 0.1 us)
Async XLA Ops:
  2.6 1.3 %collective-permute-start.1 = (f32[16,896]{1,0:T(8,128)S(1)}, f32[16,896]{1,0:T(8,128)S(1)}, u32[]{:S(2)}, u32[]{:S(2)}) collective-permute-start(f32[16,896]{1,0:T(8,128)S(1)} %pad_maximum_fusion.1), channel_id=1, source_target_pairs={{0,32},{32,0},{64,96},{96,64},{128,160},{160,128},{192,224},{224,1... | collective-permute-start | bytes 172040 | tf_op jit(solution)/shard_map/ppermute | solution.py:465
  2.7 1.2 %collective-permute-start.2 = (f32[32,256]{1,0:T(8,128)S(1)}, f32[32,256]{1,0:T(8,128)S(1)}, u32[]{:S(2)}, u32[]{:S(2)}) collective-permute-start(f32[32,256]{1,0:T(8,128)S(1)} %slice.65), channel_id=1, source_target_pairs={{32,64},{64,32},{96,128},{128,96},{160,192},{192,160},{33,65},{65,... | collective-permute-start | bytes 98312 | tf_op jit(solution)/shard_map/ppermute | solution.py:465
  4.0 7.6 %collective-permute-start.3 = (f32[16,768]{1,0:T(8,128)S(1)}, f32[16,768]{1,0:T(8,128)S(1)}, u32[]{:S(2)}, u32[]{:S(2)}) collective-permute-start(f32[16,768]{1,0:T(8,128)S(1)} %slice_select_fusion), channel_id=1, source_target_pairs={{0,2},{2,0},{4,6},{6,4},{8,10},{10,8},{12,14},{14,12},{16,18},{18,... | collective-permute-start | bytes 147464 | tf_op jit(solution)/shard_map/ppermute | solution.py:465
  6.0 7.4 %collective-permute-start.4 = (f32[16,384]{1,0:T(8,128)S(1)}, f32[16,384]{1,0:T(8,128)S(1)}, u32[]{:S(2)}, u32[]{:S(2)}) collective-permute-start(f32[16,384]{1,0:T(8,128)S(1)} %slice_add_fusion.1), channel_id=1, source_target_pairs={{0,64},{32,96},{64,0},{96,32},{128,192},{160,224},{192,128},{224,1... | collective-permute-start | bytes 73736 | tf_op jit(solution)/shard_map/ppermute | solution.py:465
  13.4 5.3 %collective-permute-start.5 = (f32[16,384]{1,0:T(8,128)S(1)}, f32[16,384]{1,0:T(8,128)S(1)}, u32[]{:S(2)}, u32[]{:S(2)}) collective-permute-start(f32[16,384]{1,0:T(8,128)S(1)} %add.57), channel_id=1, source_target_pairs={{0,192},{32,224},{64,128},{96,160},{128,64},{160,96},{192,0},{224,... | collective-permute-start | bytes 73736 | tf_op jit(solution)/shard_map/ppermute | solution.py:465
  16.9 5.6 %collective-permute-start.6 = (f32[16,768]{1,0:T(8,128)S(1)}, f32[16,768]{1,0:T(8,128)S(1)}, u32[]{:S(2)}, u32[]{:S(2)}) collective-permute-start(f32[16,768]{1,0:T(8,128)S(1)} %select_add_fusion), channel_id=1, source_target_pairs={{0,16},{2,18},{4,20},{6,22},{8,24},{10,26},{12,28},{14,30},{16,0},... | collective-permute-start | bytes 147464 | tf_op jit(solution)/shard_map/ppermute | solution.py:465
  22.5 7.5 %collective-permute-start.7 = (f32[16,896]{1,0:T(8,128)S(1)}, f32[16,896]{1,0:T(8,128)S(1)}, u32[]{:S(2)}, u32[]{:S(2)}) collective-permute-start(f32[16,896]{1,0:T(8,128)S(1)} %pad_maximum_fusion.2), channel_id=1, source_target_pairs={{0,14},{2,4},{4,2},{6,8},{8,6},{10,12},{12,10},{14,0},{16,30},{18,... | collective-permute-start | bytes 172040 | tf_op jit(solution)/shard_map/ppermute | solution.py:465
  30.0 7.8 %collective-permute-start.8 = (f32[16,768]{1,0:T(8,128)S(1)}, f32[16,768]{1,0:T(8,128)S(1)}, u32[]{:S(2)}, u32[]{:S(2)}) collective-permute-start(f32[16,768]{1,0:T(8,128)S(1)} %slice_add_fusion), channel_id=1, source_target_pairs={{0,6},{2,12},{4,10},{6,0},{8,14},{10,4},{12,2},{14,8},{16,22},{18,... | collective-permute-start | bytes 147464 | tf_op jit(solution)/shard_map/ppermute | solution.py:465
  31.7 6.2 %collective-permute-start.9 = (f32[16,128]{1,0:T(8,128)S(1)}, f32[16,128]{1,0:T(8,128)S(1)}, u32[]{:S(2)}, u32[]{:S(2)}) collective-permute-start(f32[16,128]{1,0:T(8,128)S(1)} %get-tuple-element.39), channel_id=1, source_target_pairs={{0,2},{2,0},{4,6},{6,4},{8,10},{10,8},{12,14},{14,12},{16,18},{18,... | collective-permute-start | bytes 24584 | tf_op jit(solution)/shard_map/ppermute | solution.py:465
  33.7 9.1 %collective-permute-start.10 = (f32[16,128]{1,0:T(8,128)S(1)}, f32[16,128]{1,0:T(8,128)S(1)}, u32[]{:S(2)}, u32[]{:S(2)}) collective-permute-start(f32[16,128]{1,0:T(8,128)S(1)} %get-tuple-element.57), channel_id=1, source_target_pairs={{14,16},{16,14},{15,17},{17,15},{46,48},{48,46},{47,49},{49,47},{7... | collective-permute-start | bytes 24584 | tf_op jit(solution)/shard_map/ppermute | solution.py:487
  37.7 6.5 %collective-permute-start = (bf16[1,512,256]{2,1,0:T(8,128)(2,1)S(1)}, bf16[1,512,256]{2,1,0:T(8,128)(2,1)S(1)}, u32[]{:S(2)}, u32[]{:S(2)}) collective-permute-start(bf16[1,512,256]{2,1,0:T(8,128)(2,1)S(1)} %get-tuple-element.30), channel_id=1, source_target_pairs={{0,1},{1,0},{2,3},{3,2},{4,5},{5,4},{6,7},{7,6},{8,9},{9,8},{10,11... | collective-permute-start | bytes 786440 | tf_op jit(solution)/shard_map/ppermute | solution.py:525
  37.8 8.0 %collective-permute-start.12 = (f32[16,768]{1,0:T(8,128)S(1)}, f32[16,768]{1,0:T(8,128)S(1)}, u32[]{:S(2)}, u32[]{:S(2)}) collective-permute-start(f32[16,768]{1,0:T(8,128)S(1)} %add.61.refs_2_.refs_3_), channel_id=1, source_target_pairs={{0,2},{2,0},{4,6},{6,4},{8,10},{10,8},{12,14},{14,12},{16,18},{18,... | collective-permute-start | bytes 147464 | tf_op jit(solution)/shard_map/ppermute | solution.py:465
  42.9 1.7 %collective-permute-start.11 = (f32[16,384]{1,0:T(8,128)S(1)}, f32[16,384]{1,0:T(8,128)S(1)}, u32[]{:S(2)}, u32[]{:S(2)}) collective-permute-start(f32[16,384]{1,0:T(8,128)S(1)} %pad_maximum_fusion.3.refs_3_), channel_id=1, source_target_pairs={{0,32},{32,0},{64,96},{96,64},{128,160},{160,128},{192,224},{224,1... | collective-permute-start | bytes 73736 | tf_op jit(solution)/shard_map/ppermute | solution.py:465

commit v11 on v7

--- a/solution.py
+++ b/solution.py
@@ -170,10 +170,9 @@
     planes, cells_x, cells_y = volume_ref.shape
     fetches = [
         pltpu.make_async_copy(slopes_hbm, slopes_ref, sems.at[0]),
-        pltpu.make_async_copy(volume_hbm.at[0:1], volume_ref.at[0:1], sems.at[1]),
+        pltpu.make_async_copy(volume_hbm, volume_ref, sems.at[1]),
         pltpu.make_async_copy(mx_hbm, mx_ref, sems.at[2]),
         pltpu.make_async_copy(my_hbm, my_ref, sems.at[3]),
-        pltpu.make_async_copy(volume_hbm.at[1:2], volume_ref.at[1:2], sems.at[5]),
         pltpu.make_async_copy(volume_hbm.at[pl.ds(1 - lax.axis_index("pa"), 1)], near_ref, sems.at[4]),
     ]
     for fetch in fetches:
@@ -191,15 +190,16 @@
     fetches[3].wait()
     gather_rows(mx_ref, rows_x_ref)
     gather_rows(my_ref, rows_y_ref)
+    fetches[1].wait()
     for plane in range(planes):
-        fetches[1 if plane == 0 else 4].wait()
         project(
             table_y_ref, volume_ref, rows_y_ref, column_y, y_ref, plane, 1, here_y, count_y, here_x % 2 == 1, pad_y, scale_y
         )
+    for plane in range(planes):
         project(
             table_x_ref, volume_ref, rows_x_ref, column_x, x_ref, plane, 0, here_x, count_x, here_y % 2 == 1, pad_x, scale_x
         )
-    fetches[5].wait()
+    fetches[4].wait()
 
 
 def forward(slopes, volume, measured_x, measured_y, count_x, count_y, pad_x, pad_y, scale_x, scale_y):
@@ -232,7 +232,7 @@
             VMEM(measured_y.shape, F32),
             VMEM((planes * views, cells_y), F32),
             VMEM((planes * views, cells_x), F32),
-            pltpu.SemaphoreType.DMA((6,)),
+            pltpu.SemaphoreType.DMA((5,)),
         ],
         compiler_params=LIMIT,
         interpret=interpreted(),

time: 40 us -> 39.8 us (level)
  no operation moved by 1% of the time
where the time goes in v11:
time: 39.8 us; the launch traced here: 39.7 us
  waiting for transfers between devices  17.3 us (43%)
  starting transfers between devices  15.9 us (40%)
  Pallas kernels  5.38 us (14%)
  between operations  0.87 us (2%)
    ppermute x9, waiting for transfers between devices, exchange(): lax.ppermute(value, axis, [(i, partner(i)) for i in range(lax.axis_size(a...  17.3 us
    ppermute x9, starting transfers between devices, exchange(): lax.ppermute(value, axis, [(i, partner(i)) for i in range(lax.axis_size(a...  15.2 us
    pallas_call x1, Pallas kernels, forward(): pl.pallas_call(body, out_shape=(out_vmem((planes * views, cells_y + 2 * p...  1.92 us
    pallas_call x1, Pallas kernels, back_last(): pl.pallas_call(body, out_shape=(jax.ShapeDtypeStruct(gradient.shape, F32)...  1.29 us
    pallas_call x1, Pallas kernels, back_x(): pl.pallas_call(body, out_shape=(jax.ShapeDtypeStruct(base.shape, F32), ja...  1.27 us
  transfers between devices with their start and end apart: 10, of which 8 were waited for; matrix products, arithmetic and copies ran while one was open for 0% of the time, Pallas kernels for 5%

profile of v11, /device:TPU:6, one launch (start us, length us, event | category | flops | bytes accessed | tf_op | source)
XLA Modules:
  0.0 39.7 jit_solution(8439030514382117227)
XLA Ops:
  0.7 1.9 %forward.1 = (f32[32,384]{1,0:T(8,128)S(1)}, f32[32,768]{1,0:T(8,128)S(1)}, bf16[256,256]{1,0:T(8,128)(2,1)S(1)}, bf16[1,512,256]{2,1,0:T(8,128)(2,1)S(1)}, bf16...) custom-call(s32[2,16]{1,0:T(2,128)} %refs_0_.1, ...), custom_call_target="tpu_custom_call" | custom-call | tf_op jit(solution)/shard_map/forward/pallas_call | solution.py:214
  2.6 0.1 collective-permute-start.1
  2.8 1.2 %collective-permute-done.1 = f32[16,896]{1,0:T(8,128)S(1)} collective-permute-done((f32[16,896]{1,0:T(8,128)S(1)}, f32[16,896]{1,0:T(8,128)S(1)}, u32[]{:S(2)}, u32[]{:S(2)}) %collective-permute-start.1) | collective-permute-done | bytes 57376 | tf_op jit(solution)/shard_map/ppermute | solution.py:465
  4.0 2.9 %collective-permute-start.2 = (f32[16,896]{1,0:T(8,128)S(1)}, f32[16,896]{1,0:T(8,128)S(1)}, u32[]{:S(2)}, u32[]{:S(2)}) collective-permute-start(f32[16,896]{1,0:T(8,128)S(1)} %pad_maximum_fusion.2), channel_id=1, source_target_pairs={{0,224},{32,64},{64,32},{96,128},{128,96},{160,192},{192,160},{224... | collective-permute-start | bytes 172040 | tf_op jit(solution)/shard_map/ppermute | solution.py:465
  6.8 2.0 %collective-permute-done.2 = f32[16,896]{1,0:T(8,128)S(1)} collective-permute-done((f32[16,896]{1,0:T(8,128)S(1)}, f32[16,896]{1,0:T(8,128)S(1)}, u32[]{:S(2)}, u32[]{:S(2)}) %collective-permute-start.2) | collective-permute-done | bytes 57376 | tf_op jit(solution)/shard_map/ppermute | solution.py:465
  9.0 2.0 %collective-permute-start.3 = (f32[16,896]{1,0:T(8,128)S(1)}, f32[16,896]{1,0:T(8,128)S(1)}, u32[]{:S(2)}, u32[]{:S(2)}) collective-permute-start(f32[16,896]{1,0:T(8,128)S(1)} %pad_maximum_fusion.3), channel_id=1, source_target_pairs={{0,2},{2,0},{4,6},{6,4},{8,10},{10,8},{12,14},{14,12},{16,18},{18,... | collective-permute-start | bytes 172040 | tf_op jit(solution)/shard_map/ppermute | solution.py:465
  11.0 2.3 %collective-permute-done.3 = f32[16,896]{1,0:T(8,128)S(1)} collective-permute-done((f32[16,896]{1,0:T(8,128)S(1)}, f32[16,896]{1,0:T(8,128)S(1)}, u32[]{:S(2)}, u32[]{:S(2)}) %collective-permute-start.3) | collective-permute-done | bytes 57376 | tf_op jit(solution)/shard_map/ppermute | solution.py:465
  13.3 1.5 %collective-permute-start.4 = (f32[16,896]{1,0:T(8,128)S(1)}, f32[16,896]{1,0:T(8,128)S(1)}, u32[]{:S(2)}, u32[]{:S(2)}) collective-permute-start(f32[16,896]{1,0:T(8,128)S(1)} %pad_maximum_fusion.4), channel_id=1, source_target_pairs={{0,16},{2,18},{4,20},{6,22},{8,24},{10,26},{12,28},{14,30},{16,0},... | collective-permute-start | bytes 172040 | tf_op jit(solution)/shard_map/ppermute | solution.py:465
  14.8 4.3 %collective-permute-done.4 = f32[16,896]{1,0:T(8,128)S(1)} collective-permute-done((f32[16,896]{1,0:T(8,128)S(1)}, f32[16,896]{1,0:T(8,128)S(1)}, u32[]{:S(2)}, u32[]{:S(2)}) %collective-permute-start.4) | collective-permute-done | bytes 57376 | tf_op jit(solution)/shard_map/ppermute | solution.py:465
  19.1 6.6 %collective-permute-start.5 = (f32[16,896]{1,0:T(8,128)S(1)}, f32[16,896]{1,0:T(8,128)S(1)}, u32[]{:S(2)}, u32[]{:S(2)}) collective-permute-start(f32[16,896]{1,0:T(8,128)S(1)} %pad_maximum_fusion.5), channel_id=1, source_target_pairs={{0,14},{2,4},{4,2},{6,8},{8,6},{10,12},{12,10},{14,0},{16,30},{18,... | collective-permute-start | bytes 172040 | tf_op jit(solution)/shard_map/ppermute | solution.py:465
  25.6 0.8 %collective-permute-start = (bf16[1,512,256]{2,1,0:T(8,128)(2,1)S(1)}, bf16[1,512,256]{2,1,0:T(8,128)(2,1)S(1)}, u32[]{:S(2)}, u32[]{:S(2)}) collective-permute-start(bf16[1,512,256]{2,1,0:T(8,128)(2,1)S(1)} %get-tuple-element.28), channel_id=1, source_target_pairs={{0,1},{1,0},{2,3},{3,2},{4,5},{5,4},{6,7},{7,6},{8,9},{9,8},{10,11... | collective-permute-start | bytes 786440 | tf_op jit(solution)/shard_map/ppermute | solution.py:514
  26.4 1.5 %collective-permute-done.5 = f32[16,896]{1,0:T(8,128)S(1)} collective-permute-done((f32[16,896]{1,0:T(8,128)S(1)}, f32[16,896]{1,0:T(8,128)S(1)}, u32[]{:S(2)}, u32[]{:S(2)}) %collective-permute-start.5) | collective-permute-done | bytes 57376 | tf_op jit(solution)/shard_map/ppermute | solution.py:465
  27.9 2.0 %collective-permute-start.6 = (f32[16,768]{1,0:T(8,128)S(1)}, f32[16,768]{1,0:T(8,128)S(1)}, u32[]{:S(2)}, u32[]{:S(2)}) collective-permute-start(f32[16,768]{1,0:T(8,128)S(1)} %slice_add_fusion), channel_id=1, source_target_pairs={{0,6},{2,12},{4,10},{6,0},{8,14},{10,4},{12,2},{14,8},{16,22},{18,... | collective-permute-start | bytes 147464 | tf_op jit(solution)/shard_map/ppermute | solution.py:465
  29.9 0.0 collective-permute-start.7
  29.9 4.3 %collective-permute-done.6 = f32[16,768]{1,0:T(8,128)S(1)} collective-permute-done((f32[16,768]{1,0:T(8,128)S(1)}, f32[16,768]{1,0:T(8,128)S(1)}, u32[]{:S(2)}, u32[]{:S(2)}) %collective-permute-start.6) | collective-permute-done | bytes 49184 | tf_op jit(solution)/shard_map/ppermute | solution.py:465
  34.2 0.1 collective-permute-start.9
  34.3 0.0 collective-permute-done.7
  34.3 0.1 collective-permute-start.8
  34.4 0.0 collective-permute-done.refs_2_
  34.5 0.4 %prepare.1 = (bf16[512,256]{1,0:T(8,128)(2,1)S(1)}, f32[2,512,256]{2,1,0:T(8,128)S(1)}) custom-call(s32[8,256]{1,0:T(8,128)S(1)} %get-tuple-element.26.refs_0_, bf16[2,512,256]{2,1,0:T(8,128)(2,1)S(1)} %get-tuple-element.27.refs_1_, bf16[1,512,256]{2,1,0:T(8,128)(2,1)S(1)} %collective-permute-done.refs_2_), custom_call_target="tpu_custom_call" | custom-call | tf_op jit(solution)/shard_map/prepare/pallas_call | solution.py:294
  34.9 0.5 %back_own.1.refs_5_ = f32[512,256]{1,0:T(8,128)S(1)} custom-call(s32[16,128]{1,0:T(8,128)S(1)} %get-tuple-element.23.refs_0_, bf16[256,256]{1,0:T(8,128)(2,1)S(1)} %get-tuple-element.24.refs_1_, f32[16,768]{1,0:T(8,128)S(1)} %add.73.refs_2_.refs_3_), custom_call_target="tpu_custom_call" | custom-call | tf_op jit(solution)/shard_map/back_own/pallas_call | solution.py:326
  35.4 0.3 collective-permute-done.8.refs_4_
  35.6 1.3 %back_x.1 = (f32[2,512,256]{2,1,0:T(8,128)}, f32[16,2,256]{2,1,0:T(2,128)}, f32[512,256]{1,0:T(8,128)S(1)}) custom-call(s32[16,128]{1,0:T(8,128)S(1)} %get-tuple-element.25.refs_0_, bf16[512,256]{1,0:T(8,128)(2,1)S(1)} %get-tuple-element.29.refs_1_, f32[2,512,256]{2,1,0:T(8,128)S(1)} %get-tuple-element.30.refs_2_, f32[16,384]{1,0:T(8,128)S(1)} %add.74.refs_3_, ...), custom_call_target="tpu_custom_call" | custom-call | tf_op jit(solution)/shard_map/back_x/pallas_call | solution.py:383
  36.9 1.5 %collective-permute-done.9.refs_4_ = f32[16,768]{1,0:T(8,128)S(1)} collective-permute-done((f32[16,768]{1,0:T(8,128)S(1)}, f32[16,768]{1,0:T(8,128)S(1)}, u32[]{:S(2)}, u32[]{:S(2)}) %collective-permute-start.9) | collective-permute-done | bytes 49184 | tf_op jit(solution)/shard_map/ppermute | solution.py:465
  38.4 1.3 %back_last.1 = (f32[2,512,256]{2,1,0:T(8,128)}, f32[16,2,512]{2,1,0:T(2,128)}) custom-call(s32[16,128]{1,0:T(8,128)S(1)} %get-tuple-element.23.refs_0_, bf16[256,256]{1,0:T(8,128)(2,1)S(1)} %get-tuple-element.24.refs_1_, f32[512,256]{1,0:T(8,128)S(1)} %get-tuple-element.38.refs_2_, ...), custom_call_target="tpu_custom_call", output_to_operand_aliasing={{0}: (5, {})} | custom-call | tf_op jit(solution)/shard_map/back_last/pallas_call | solution.py:442
  (24 shorter events, 0.2 us)
Async XLA Ops:
  2.6 1.3 %collective-permute-start.1 = (f32[16,896]{1,0:T(8,128)S(1)}, f32[16,896]{1,0:T(8,128)S(1)}, u32[]{:S(2)}, u32[]{:S(2)}) collective-permute-start(f32[16,896]{1,0:T(8,128)S(1)} %pad_maximum_fusion.1), channel_id=1, source_target_pairs={{0,32},{32,0},{64,96},{96,64},{128,160},{160,128},{192,224},{224,1... | collective-permute-start | bytes 172040 | tf_op jit(solution)/shard_map/ppermute | solution.py:465
  4.0 4.9 %collective-permute-start.2 = (f32[16,896]{1,0:T(8,128)S(1)}, f32[16,896]{1,0:T(8,128)S(1)}, u32[]{:S(2)}, u32[]{:S(2)}) collective-permute-start(f32[16,896]{1,0:T(8,128)S(1)} %pad_maximum_fusion.2), channel_id=1, source_target_pairs={{0,224},{32,64},{64,32},{96,128},{128,96},{160,192},{192,160},{224... | collective-permute-start | bytes 172040 | tf_op jit(solution)/shard_map/ppermute | solution.py:465
  9.0 4.3 %collective-permute-start.3 = (f32[16,896]{1,0:T(8,128)S(1)}, f32[16,896]{1,0:T(8,128)S(1)}, u32[]{:S(2)}, u32[]{:S(2)}) collective-permute-start(f32[16,896]{1,0:T(8,128)S(1)} %pad_maximum_fusion.3), channel_id=1, source_target_pairs={{0,2},{2,0},{4,6},{6,4},{8,10},{10,8},{12,14},{14,12},{16,18},{18,... | collective-permute-start | bytes 172040 | tf_op jit(solution)/shard_map/ppermute | solution.py:465
  13.3 5.8 %collective-permute-start.4 = (f32[16,896]{1,0:T(8,128)S(1)}, f32[16,896]{1,0:T(8,128)S(1)}, u32[]{:S(2)}, u32[]{:S(2)}) collective-permute-start(f32[16,896]{1,0:T(8,128)S(1)} %pad_maximum_fusion.4), channel_id=1, source_target_pairs={{0,16},{2,18},{4,20},{6,22},{8,24},{10,26},{12,28},{14,30},{16,0},... | collective-permute-start | bytes 172040 | tf_op jit(solution)/shard_map/ppermute | solution.py:465
  19.1 8.8 %collective-permute-start.5 = (f32[16,896]{1,0:T(8,128)S(1)}, f32[16,896]{1,0:T(8,128)S(1)}, u32[]{:S(2)}, u32[]{:S(2)}) collective-permute-start(f32[16,896]{1,0:T(8,128)S(1)} %pad_maximum_fusion.5), channel_id=1, source_target_pairs={{0,14},{2,4},{4,2},{6,8},{8,6},{10,12},{12,10},{14,0},{16,30},{18,... | collective-permute-start | bytes 172040 | tf_op jit(solution)/shard_map/ppermute | solution.py:465
  25.6 8.8 %collective-permute-start = (bf16[1,512,256]{2,1,0:T(8,128)(2,1)S(1)}, bf16[1,512,256]{2,1,0:T(8,128)(2,1)S(1)}, u32[]{:S(2)}, u32[]{:S(2)}) collective-permute-start(bf16[1,512,256]{2,1,0:T(8,128)(2,1)S(1)} %get-tuple-element.28), channel_id=1, source_target_pairs={{0,1},{1,0},{2,3},{3,2},{4,5},{5,4},{6,7},{7,6},{8,9},{9,8},{10,11... | collective-permute-start | bytes 786440 | tf_op jit(solution)/shard_map/ppermute | solution.py:514
  27.9 6.3 %collective-permute-start.6 = (f32[16,768]{1,0:T(8,128)S(1)}, f32[16,768]{1,0:T(8,128)S(1)}, u32[]{:S(2)}, u32[]{:S(2)}) collective-permute-start(f32[16,768]{1,0:T(8,128)S(1)} %slice_add_fusion), channel_id=1, source_target_pairs={{0,6},{2,12},{4,10},{6,0},{8,14},{10,4},{12,2},{14,8},{16,22},{18,... | collective-permute-start | bytes 147464 | tf_op jit(solution)/shard_map/ppermute | solution.py:465
  29.9 4.4 %collective-permute-start.7 = (f32[16,384]{1,0:T(8,128)S(1)}, f32[16,384]{1,0:T(8,128)S(1)}, u32[]{:S(2)}, u32[]{:S(2)}) collective-permute-start(f32[16,384]{1,0:T(8,128)S(1)} %pad_maximum_fusion.6), channel_id=1, source_target_pairs={{0,96},{32,192},{64,160},{96,0},{128,224},{160,64},{192,32},{224,1... | collective-permute-start | bytes 73736 | tf_op jit(solution)/shard_map/ppermute | solution.py:465
  34.2 4.2 %collective-permute-start.9 = (f32[16,768]{1,0:T(8,128)S(1)}, f32[16,768]{1,0:T(8,128)S(1)}, u32[]{:S(2)}, u32[]{:S(2)}) collective-permute-start(f32[16,768]{1,0:T(8,128)S(1)} %add.73.refs_2_.refs_3_), channel_id=1, source_target_pairs={{0,2},{2,0},{4,6},{6,4},{8,10},{10,8},{12,14},{14,12},{16,18},{18,... | collective-permute-start | bytes 147464 | tf_op jit(solution)/shard_map/ppermute | solution.py:465
  34.3 1.3 %collective-permute-start.8 = (f32[16,384]{1,0:T(8,128)S(1)}, f32[16,384]{1,0:T(8,128)S(1)}, u32[]{:S(2)}, u32[]{:S(2)}) collective-permute-start(f32[16,384]{1,0:T(8,128)S(1)} %add.74.refs_3_), channel_id=1, source_target_pairs={{0,32},{32,0},{64,96},{96,64},{128,160},{160,128},{192,224},{224,1... | collective-permute-start | bytes 73736 | tf_op jit(solution)/shard_map/ppermute | solution.py:465

commit v12 on v10

--- a/solution.py
+++ b/solution.py
@@ -462,7 +462,9 @@
 
 
 def exchange(value, axis, partner):
-    return lax.ppermute(value, axis, [(i, partner(i)) for i in range(lax.axis_size(axis)) if partner(i) != i])
+    size = lax.axis_size(axis)
+    pairs = [(i, partner(i)) for i in range(size) if partner(i) != i and 0 <= partner(i) < size]
+    return lax.ppermute(value, axis, pairs)
 
 
 def twin(i):
@@ -481,15 +483,8 @@
     return i - i % RING + (i + (-3 if i % 2 else 3)) % RING
 
 
-def seam(value, axis):
-    ends = range(RING, lax.axis_size(axis), RING)
-    pairs = [(i - 1, i) for i in ends] + [(i, i - 1) for i in ends]
-    return lax.ppermute(value, axis, pairs)
-
-
-def at_end(size, axis):
-    index = lax.axis_index(axis) % size
-    return (index == 0) | (index == size - 1)
+def border(i):
+    return i + (1 if i % 2 else -1)
 
 
 def steps(volume, view_slopes, measured_x, measured_y):
@@ -534,19 +529,19 @@
     half_x = half_x + got_x
     got_y = exchange(half, "gy", lambda i: i ^ RING)
     got_x = exchange(half_x, "gx", lambda i: i ^ 6)
-    half, half_x = half + got_y, half_x + got_x
+    half = half + got_y
+    got_y = exchange(half, "gy", odd_twin)
+    half = half + got_y
+    half_x, half = lax.optimization_barrier((half_x, half))
+    half_x = half_x + got_x
     x_a, x_mid, x_b = half_x[:, :edge_x], half_x[:, edge_x : 2 * edge_x], half_x[:, 2 * edge_x :]
-
-    got = exchange(jnp.concatenate([half, x_b], axis=1), "gy", odd_twin)
-    got_b = seam(x_b, "gy")
-    half = half + got[:, :long]
-    x_a, half = lax.optimization_barrier((x_a, half))
     got_y = exchange(half, "gy", across)
     got_a = exchange(x_a, "gy", twin)
+    got_b = exchange(x_b, "gy", border)
     half = half + got_y
     other = exchange(half, "gy", twin)
-    x_a, half, got = lax.optimization_barrier((x_a, half, got))
-    x_b = x_b + jnp.where(at_end(RING, "gy"), 0.0, got[:, long:]) + got_b
+    x_a, x_b, half = lax.optimization_barrier((x_a, x_b, half))
+    x_b = x_b + got_b
     half_x = jnp.concatenate([x_a + got_a, x_mid, x_b], axis=1)
     away_x = exchange(half_x, "gx", twin)
 

time: 47.3 us -> 48.5 us (1.025)
  the two profiles are of different devices: /device:TPU:6 before, /device:TPU:5 now
where the time goes in v12:
time: 48.5 us; the launch traced here: 48.4 us
  starting transfers between devices  29.7 us (61%)
  waiting for transfers between devices  12.3 us (25%)
  Pallas kernels  5.39 us (11%)
  between operations  0.82 us (2%)
    ppermute x12, starting transfers between devices, exchange(): return lax.ppermute(value, axis, pairs)  28.8 us
    ppermute x12, waiting for transfers between devices, exchange(): return lax.ppermute(value, axis, pairs)  12.3 us
    pallas_call x1, Pallas kernels, forward(): pl.pallas_call(body, out_shape=(out_vmem((planes * views, cells_y + 2 * p...  1.92 us
    pallas_call x1, Pallas kernels, back_last(): pl.pallas_call(body, out_shape=(jax.ShapeDtypeStruct(gradient.shape, F32)...  1.31 us
    pallas_call x1, Pallas kernels, back_x(): pl.pallas_call(body, out_shape=(jax.ShapeDtypeStruct(base.shape, F32), ja...  1.28 us
  transfers between devices with their start and end apart: 13, of which 6 were waited for; matrix products, arithmetic and copies ran while one was open for 0% of the time, Pallas kernels for 4%

profile of v12, /device:TPU:5, one launch (start us, length us, event | category | flops | bytes accessed | tf_op | source)
XLA Modules:
  0.0 48.4 jit_solution(13121252887173052701)
XLA Ops:
  0.6 1.9 %forward.1 = (f32[32,384]{1,0:T(8,128)S(1)}, f32[32,768]{1,0:T(8,128)S(1)}, bf16[256,256]{1,0:T(8,128)(2,1)S(1)}, bf16[1,512,256]{2,1,0:T(8,128)(2,1)S(1)}, bf16...) custom-call(s32[2,16]{1,0:T(2,128)} %refs_0_.1, ...), custom_call_target="tpu_custom_call" | custom-call | tf_op jit(solution)/shard_map/forward/pallas_call | solution.py:214
  2.6 0.8 %collective-permute-start.1 = (f32[16,896]{1,0:T(8,128)S(1)}, f32[16,896]{1,0:T(8,128)S(1)}, u32[]{:S(2)}, u32[]{:S(2)}) collective-permute-start(f32[16,896]{1,0:T(8,128)S(1)} %pad_maximum_fusion.1), channel_id=1, source_target_pairs={{0,32},{32,0},{64,96},{96,64},{128,160},{160,128},{192,224},{224,1... | collective-permute-start | bytes 172040 | tf_op jit(solution)/shard_map/ppermute | solution.py:467
  3.4 3.1 %collective-permute-start.2 = (f32[32,256]{1,0:T(8,128)S(1)}, f32[32,256]{1,0:T(8,128)S(1)}, u32[]{:S(2)}, u32[]{:S(2)}) collective-permute-start(f32[32,256]{1,0:T(8,128)S(1)} %slice.59), channel_id=1, source_target_pairs={{32,64},{64,32},{96,128},{128,96},{160,192},{192,160},{33,65},{65,... | collective-permute-start | bytes 98312 | tf_op jit(solution)/shard_map/ppermute | solution.py:467
  6.5 0.0 collective-permute-done.1
  6.5 2.1 %collective-permute-done.2 = f32[32,256]{1,0:T(8,128)S(1)} collective-permute-done((f32[32,256]{1,0:T(8,128)S(1)}, f32[32,256]{1,0:T(8,128)S(1)}, u32[]{:S(2)}, u32[]{:S(2)}) %collective-permute-start.2) | collective-permute-done | bytes 32800 | tf_op jit(solution)/shard_map/ppermute | solution.py:467
  8.6 1.7 %collective-permute-start.3 = (f32[16,768]{1,0:T(8,128)S(1)}, f32[16,768]{1,0:T(8,128)S(1)}, u32[]{:S(2)}, u32[]{:S(2)}) collective-permute-start(f32[16,768]{1,0:T(8,128)S(1)} %slice_select_fusion), channel_id=1, source_target_pairs={{0,2},{2,0},{4,6},{6,4},{8,10},{10,8},{12,14},{14,12},{16,18},{18,... | collective-permute-start | bytes 147464 | tf_op jit(solution)/shard_map/ppermute | solution.py:467
  10.4 1.5 %collective-permute-done.3 = f32[16,768]{1,0:T(8,128)S(1)} collective-permute-done((f32[16,768]{1,0:T(8,128)S(1)}, f32[16,768]{1,0:T(8,128)S(1)}, u32[]{:S(2)}, u32[]{:S(2)}) %collective-permute-start.3) | collective-permute-done | bytes 49184 | tf_op jit(solution)/shard_map/ppermute | solution.py:467
  11.9 1.8 %collective-permute-start.5 = (f32[16,768]{1,0:T(8,128)S(1)}, f32[16,768]{1,0:T(8,128)S(1)}, u32[]{:S(2)}, u32[]{:S(2)}) collective-permute-start(f32[16,768]{1,0:T(8,128)S(1)} %select_add_fusion), channel_id=1, source_target_pairs={{0,16},{2,18},{4,20},{6,22},{8,24},{10,26},{12,28},{14,30},{16,0},... | collective-permute-start | bytes 147464 | tf_op jit(solution)/shard_map/ppermute | solution.py:467
  13.7 2.7 %collective-permute-done.5 = f32[16,768]{1,0:T(8,128)S(1)} collective-permute-done((f32[16,768]{1,0:T(8,128)S(1)}, f32[16,768]{1,0:T(8,128)S(1)}, u32[]{:S(2)}, u32[]{:S(2)}) %collective-permute-start.5) | collective-permute-done | bytes 49184 | tf_op jit(solution)/shard_map/ppermute | solution.py:467
  16.4 5.5 %collective-permute-start.6 = (f32[16,768]{1,0:T(8,128)S(1)}, f32[16,768]{1,0:T(8,128)S(1)}, u32[]{:S(2)}, u32[]{:S(2)}) collective-permute-start(f32[16,768]{1,0:T(8,128)S(1)} %add.52), channel_id=1, source_target_pairs={{0,14},{2,4},{4,2},{6,8},{8,6},{10,12},{12,10},{14,0},{16,30},{18,... | collective-permute-start | bytes 147464 | tf_op jit(solution)/shard_map/ppermute | solution.py:467
  21.9 1.6 %collective-permute-start.4 = (f32[16,384]{1,0:T(8,128)S(1)}, f32[16,384]{1,0:T(8,128)S(1)}, u32[]{:S(2)}, u32[]{:S(2)}) collective-permute-start(f32[16,384]{1,0:T(8,128)S(1)} %slice_add_fusion), channel_id=1, source_target_pairs={{0,64},{32,96},{64,0},{96,32},{128,192},{160,224},{192,128},{224,1... | collective-permute-start | bytes 73736 | tf_op jit(solution)/shard_map/ppermute | solution.py:467
  23.5 1.2 %collective-permute-done.4 = f32[16,384]{1,0:T(8,128)S(1)} collective-permute-done((f32[16,384]{1,0:T(8,128)S(1)}, f32[16,384]{1,0:T(8,128)S(1)}, u32[]{:S(2)}, u32[]{:S(2)}) %collective-permute-start.4) | collective-permute-done | bytes 24608 | tf_op jit(solution)/shard_map/ppermute | solution.py:467
  24.7 1.9 %collective-permute-start.7 = (f32[16,384]{1,0:T(8,128)S(1)}, f32[16,384]{1,0:T(8,128)S(1)}, u32[]{:S(2)}, u32[]{:S(2)}) collective-permute-start(f32[16,384]{1,0:T(8,128)S(1)} %add.51), channel_id=1, source_target_pairs={{0,192},{32,224},{64,128},{96,160},{128,64},{160,96},{192,0},{224,... | collective-permute-start | bytes 73736 | tf_op jit(solution)/shard_map/ppermute | solution.py:467
  26.6 0.9 %collective-permute-start = (bf16[1,512,256]{2,1,0:T(8,128)(2,1)S(1)}, bf16[1,512,256]{2,1,0:T(8,128)(2,1)S(1)}, u32[]{:S(2)}, u32[]{:S(2)}) collective-permute-start(bf16[1,512,256]{2,1,0:T(8,128)(2,1)S(1)} %get-tuple-element.30), channel_id=1, source_target_pairs={{0,1},{1,0},{2,3},{3,2},{4,5},{5,4},{6,7},{7,6},{8,9},{9,8},{10,11... | collective-permute-start | bytes 786440 | tf_op jit(solution)/shard_map/ppermute | solution.py:520
  27.6 0.0 collective-permute-done.6
  27.6 1.7 %collective-permute-start.8 = (f32[16,768]{1,0:T(8,128)S(1)}, f32[16,768]{1,0:T(8,128)S(1)}, u32[]{:S(2)}, u32[]{:S(2)}) collective-permute-start(f32[16,768]{1,0:T(8,128)S(1)} %add.53), channel_id=1, source_target_pairs={{0,6},{2,12},{4,10},{6,0},{8,14},{10,4},{12,2},{14,8},{16,22},{18,... | collective-permute-start | bytes 147464 | tf_op jit(solution)/shard_map/ppermute | solution.py:467
  29.3 0.0 collective-permute-done.7
  29.3 0.8 %collective-permute-start.9 = (f32[16,128]{1,0:T(8,128)S(1)}, f32[16,128]{1,0:T(8,128)S(1)}, u32[]{:S(2)}, u32[]{:S(2)}) collective-permute-start(f32[16,128]{1,0:T(8,128)S(1)} %get-tuple-element.39), channel_id=1, source_target_pairs={{0,2},{2,0},{4,6},{6,4},{8,10},{10,8},{12,14},{14,12},{16,18},{18,... | collective-permute-start | bytes 24584 | tf_op jit(solution)/shard_map/ppermute | solution.py:467
  30.1 1.9 %collective-permute-start.10 = (f32[16,128]{1,0:T(8,128)S(1)}, f32[16,128]{1,0:T(8,128)S(1)}, u32[]{:S(2)}, u32[]{:S(2)}) collective-permute-start(f32[16,128]{1,0:T(8,128)S(1)} %get-tuple-element.40), channel_id=1, source_target_pairs={{2,4},{4,2},{6,8},{8,6},{10,12},{12,10},{14,16},{16,14},{18,20},{2... | collective-permute-start | bytes 24584 | tf_op jit(solution)/shard_map/ppermute | solution.py:467
  32.0 0.4 collective-permute-done.8
  32.4 1.2 %collective-permute-start.12 = (f32[16,768]{1,0:T(8,128)S(1)}, f32[16,768]{1,0:T(8,128)S(1)}, u32[]{:S(2)}, u32[]{:S(2)}) collective-permute-start(f32[16,768]{1,0:T(8,128)S(1)} %add.55.refs_2_.refs_3_), channel_id=1, source_target_pairs={{0,2},{2,0},{4,6},{6,4},{8,10},{10,8},{12,14},{14,12},{16,18},{18,... | collective-permute-start | bytes 147464 | tf_op jit(solution)/shard_map/ppermute | solution.py:467
  33.6 0.0 collective-permute-done.9
  33.6 4.5 %collective-permute-done.10 = f32[16,128]{1,0:T(8,128)S(1)} collective-permute-done((f32[16,128]{1,0:T(8,128)S(1)}, f32[16,128]{1,0:T(8,128)S(1)}, u32[]{:S(2)}, u32[]{:S(2)}) %collective-permute-start.10) | collective-permute-done | bytes 8224 | tf_op jit(solution)/shard_map/ppermute | solution.py:467
  38.1 6.7 %collective-permute-start.11 = (f32[16,384]{1,0:T(8,128)S(1)}, f32[16,384]{1,0:T(8,128)S(1)}, u32[]{:S(2)}, u32[]{:S(2)}) collective-permute-start(f32[16,384]{1,0:T(8,128)S(1)} %pad_maximum_fusion.2.refs_3_), channel_id=1, source_target_pairs={{0,32},{32,0},{64,96},{96,64},{128,160},{160,128},{192,224},{224,1... | collective-permute-start | bytes 73736 | tf_op jit(solution)/shard_map/ppermute | solution.py:467
  44.8 0.5 back_own.1.refs_5_
  45.3 0.0 collective-permute-done.refs_2_
  45.3 0.4 prepare.1
  45.7 0.0 collective-permute-done.11.refs_4_
  45.7 1.3 %back_x.1 = (f32[2,512,256]{2,1,0:T(8,128)}, f32[16,2,256]{2,1,0:T(2,128)}, f32[512,256]{1,0:T(8,128)S(1)}) custom-call(s32[16,128]{1,0:T(8,128)S(1)} %get-tuple-element.27.refs_0_, bf16[512,256]{1,0:T(8,128)(2,1)S(1)} %get-tuple-element.31.refs_1_, f32[2,512,256]{2,1,0:T(8,128)S(1)} %get-tuple-element.32.refs_2_, f32[16,384]{1,0:T(8,128)S(1)} %pad_maximum_fusion.2.refs_3_, ...), custom_call_target="tpu_custom_call" | custom-call | tf_op jit(solution)/shard_map/back_x/pallas_call | solution.py:383
  47.0 0.0 collective-permute-done.12.refs_4_
  47.0 1.3 %back_last.1 = (f32[2,512,256]{2,1,0:T(8,128)}, f32[16,2,512]{2,1,0:T(2,128)}) custom-call(s32[16,128]{1,0:T(8,128)S(1)} %get-tuple-element.25.refs_0_, bf16[256,256]{1,0:T(8,128)(2,1)S(1)} %get-tuple-element.26.refs_1_, f32[512,256]{1,0:T(8,128)S(1)} %get-tuple-element.42.refs_2_, ...), custom_call_target="tpu_custom_call", output_to_operand_aliasing={{0}: (5, {})} | custom-call | tf_op jit(solution)/shard_map/back_last/pallas_call | solution.py:442
  (19 shorter events, 0.1 us)
Async XLA Ops:
  2.6 3.9 %collective-permute-start.1 = (f32[16,896]{1,0:T(8,128)S(1)}, f32[16,896]{1,0:T(8,128)S(1)}, u32[]{:S(2)}, u32[]{:S(2)}) collective-permute-start(f32[16,896]{1,0:T(8,128)S(1)} %pad_maximum_fusion.1), channel_id=1, source_target_pairs={{0,32},{32,0},{64,96},{96,64},{128,160},{160,128},{192,224},{224,1... | collective-permute-start | bytes 172040 | tf_op jit(solution)/shard_map/ppermute | solution.py:467
  3.4 5.2 %collective-permute-start.2 = (f32[32,256]{1,0:T(8,128)S(1)}, f32[32,256]{1,0:T(8,128)S(1)}, u32[]{:S(2)}, u32[]{:S(2)}) collective-permute-start(f32[32,256]{1,0:T(8,128)S(1)} %slice.59), channel_id=1, source_target_pairs={{32,64},{64,32},{96,128},{128,96},{160,192},{192,160},{33,65},{65,... | collective-permute-start | bytes 98312 | tf_op jit(solution)/shard_map/ppermute | solution.py:467
  8.6 3.2 %collective-permute-start.3 = (f32[16,768]{1,0:T(8,128)S(1)}, f32[16,768]{1,0:T(8,128)S(1)}, u32[]{:S(2)}, u32[]{:S(2)}) collective-permute-start(f32[16,768]{1,0:T(8,128)S(1)} %slice_select_fusion), channel_id=1, source_target_pairs={{0,2},{2,0},{4,6},{6,4},{8,10},{10,8},{12,14},{14,12},{16,18},{18,... | collective-permute-start | bytes 147464 | tf_op jit(solution)/shard_map/ppermute | solution.py:467
  11.9 4.5 %collective-permute-start.5 = (f32[16,768]{1,0:T(8,128)S(1)}, f32[16,768]{1,0:T(8,128)S(1)}, u32[]{:S(2)}, u32[]{:S(2)}) collective-permute-start(f32[16,768]{1,0:T(8,128)S(1)} %select_add_fusion), channel_id=1, source_target_pairs={{0,16},{2,18},{4,20},{6,22},{8,24},{10,26},{12,28},{14,30},{16,0},... | collective-permute-start | bytes 147464 | tf_op jit(solution)/shard_map/ppermute | solution.py:467
  16.4 11.1 %collective-permute-start.6 = (f32[16,768]{1,0:T(8,128)S(1)}, f32[16,768]{1,0:T(8,128)S(1)}, u32[]{:S(2)}, u32[]{:S(2)}) collective-permute-start(f32[16,768]{1,0:T(8,128)S(1)} %add.52), channel_id=1, source_target_pairs={{0,14},{2,4},{4,2},{6,8},{8,6},{10,12},{12,10},{14,0},{16,30},{18,... | collective-permute-start | bytes 147464 | tf_op jit(solution)/shard_map/ppermute | solution.py:467
  21.9 2.8 %collective-permute-start.4 = (f32[16,384]{1,0:T(8,128)S(1)}, f32[16,384]{1,0:T(8,128)S(1)}, u32[]{:S(2)}, u32[]{:S(2)}) collective-permute-start(f32[16,384]{1,0:T(8,128)S(1)} %slice_add_fusion), channel_id=1, source_target_pairs={{0,64},{32,96},{64,0},{96,32},{128,192},{160,224},{192,128},{224,1... | collective-permute-start | bytes 73736 | tf_op jit(solution)/shard_map/ppermute | solution.py:467
  24.7 4.5 %collective-permute-start.7 = (f32[16,384]{1,0:T(8,128)S(1)}, f32[16,384]{1,0:T(8,128)S(1)}, u32[]{:S(2)}, u32[]{:S(2)}) collective-permute-start(f32[16,384]{1,0:T(8,128)S(1)} %add.51), channel_id=1, source_target_pairs={{0,192},{32,224},{64,128},{96,160},{128,64},{160,96},{192,0},{224,... | collective-permute-start | bytes 73736 | tf_op jit(solution)/shard_map/ppermute | solution.py:467
  26.6 18.7 %collective-permute-start = (bf16[1,512,256]{2,1,0:T(8,128)(2,1)S(1)}, bf16[1,512,256]{2,1,0:T(8,128)(2,1)S(1)}, u32[]{:S(2)}, u32[]{:S(2)}) collective-permute-start(bf16[1,512,256]{2,1,0:T(8,128)(2,1)S(1)} %get-tuple-element.30), channel_id=1, source_target_pairs={{0,1},{1,0},{2,3},{3,2},{4,5},{5,4},{6,7},{7,6},{8,9},{9,8},{10,11... | collective-permute-start | bytes 786440 | tf_op jit(solution)/shard_map/ppermute | solution.py:520
  27.6 4.8 %collective-permute-start.8 = (f32[16,768]{1,0:T(8,128)S(1)}, f32[16,768]{1,0:T(8,128)S(1)}, u32[]{:S(2)}, u32[]{:S(2)}) collective-permute-start(f32[16,768]{1,0:T(8,128)S(1)} %add.53), channel_id=1, source_target_pairs={{0,6},{2,12},{4,10},{6,0},{8,14},{10,4},{12,2},{14,8},{16,22},{18,... | collective-permute-start | bytes 147464 | tf_op jit(solution)/shard_map/ppermute | solution.py:467
  29.3 4.3 %collective-permute-start.9 = (f32[16,128]{1,0:T(8,128)S(1)}, f32[16,128]{1,0:T(8,128)S(1)}, u32[]{:S(2)}, u32[]{:S(2)}) collective-permute-start(f32[16,128]{1,0:T(8,128)S(1)} %get-tuple-element.39), channel_id=1, source_target_pairs={{0,2},{2,0},{4,6},{6,4},{8,10},{10,8},{12,14},{14,12},{16,18},{18,... | collective-permute-start | bytes 24584 | tf_op jit(solution)/shard_map/ppermute | solution.py:467
  30.1 8.0 %collective-permute-start.10 = (f32[16,128]{1,0:T(8,128)S(1)}, f32[16,128]{1,0:T(8,128)S(1)}, u32[]{:S(2)}, u32[]{:S(2)}) collective-permute-start(f32[16,128]{1,0:T(8,128)S(1)} %get-tuple-element.40), channel_id=1, source_target_pairs={{2,4},{4,2},{6,8},{8,6},{10,12},{12,10},{14,16},{16,14},{18,20},{2... | collective-permute-start | bytes 24584 | tf_op jit(solution)/shard_map/ppermute | solution.py:467
  32.4 14.6 %collective-permute-start.12 = (f32[16,768]{1,0:T(8,128)S(1)}, f32[16,768]{1,0:T(8,128)S(1)}, u32[]{:S(2)}, u32[]{:S(2)}) collective-permute-start(f32[16,768]{1,0:T(8,128)S(1)} %add.55.refs_2_.refs_3_), channel_id=1, source_target_pairs={{0,2},{2,0},{4,6},{6,4},{8,10},{10,8},{12,14},{14,12},{16,18},{18,... | collective-permute-start | bytes 147464 | tf_op jit(solution)/shard_map/ppermute | solution.py:467
  38.1 7.6 %collective-permute-start.11 = (f32[16,384]{1,0:T(8,128)S(1)}, f32[16,384]{1,0:T(8,128)S(1)}, u32[]{:S(2)}, u32[]{:S(2)}) collective-permute-start(f32[16,384]{1,0:T(8,128)S(1)} %pad_maximum_fusion.2.refs_3_), channel_id=1, source_target_pairs={{0,32},{32,0},{64,96},{96,64},{128,160},{160,128},{192,224},{224,1... | collective-permute-start | bytes 73736 | tf_op jit(solution)/shard_map/ppermute | solution.py:467

commit v13 on v8

--- a/solution.py
+++ b/solution.py
@@ -477,10 +477,6 @@
     return odd_twin(i) if abs(odd_twin(i) - i) == 1 else i
 
 
-def end_twin(i):
-    return i if abs(odd_twin(i) - i) == 1 else odd_twin(i)
-
-
 def across(i):
     return i - i % RING + (i + (-3 if i % 2 else 3)) % RING
 
@@ -519,10 +515,11 @@
     y_a, y_mid, y_b = sum_y[:, :edge_y], sum_y[:, edge_y : 2 * edge_y], sum_y[:, 2 * edge_y :]
     half_x, sent = split(sum_x, "gx")
     got = exchange(jnp.concatenate([sent, side_by_side(y_a)], axis=1), "gx", twin)
+    got_b = exchange(y_b, "gx", next_twin)
     beside = lax.ppermute(near, "pa", [(0, 1), (1, 0)])
     half_x, y_a = half_x + got[:, :wide], y_a + one_above(got[:, wide:])
-    got = exchange(jnp.concatenate([half_x, side_by_side(y_b)], axis=1), "gx", next_twin)
-    half_x, y_b = half_x + got[:, :wide], y_b + one_above(got[:, wide:])
+    half_x = half_x + exchange(half_x, "gx", odd_twin)
+    y_b = y_b + got_b
     sum_y = jnp.concatenate([y_a, y_mid, y_b], axis=1)
     x_a, x_mid, x_b = half_x[:, :edge_x], half_x[:, edge_x : 2 * edge_x], half_x[:, 2 * edge_x :]
 
@@ -539,7 +536,6 @@
     half_x = jnp.concatenate([x_a, x_mid, x_b + got], axis=1)
 
     half = half + exchange(half, "gy", across)
-    half_x = half_x + exchange(half_x, "gx", end_twin)
     got = exchange(half_x, "gx", across)
     other = exchange(half, "gy", twin)
     half_x, half = lax.optimization_barrier((half_x, half))

time: 42.2 us -> 39.4 us (0.934)
  the two profiles are of different devices: /device:TPU:16 before, /device:TPU:10 now
where the time goes in v13:
time: 39.4 us; the launch traced here: 39.3 us
  starting transfers between devices  17 us (43%)
  waiting for transfers between devices  15.9 us (40%)
  Pallas kernels  5.38 us (14%)
  between operations  0.88 us (2%)
    ppermute x10, starting transfers between devices, exchange(): lax.ppermute(value, axis, [(i, partner(i)) for i in range(lax.axis_size(a...  16.4 us
    ppermute x10, waiting for transfers between devices, exchange(): lax.ppermute(value, axis, [(i, partner(i)) for i in range(lax.axis_size(a...  15.9 us
    pallas_call x1, Pallas kernels, forward(): pl.pallas_call(body, out_shape=(out_vmem((planes * views, cells_y + 2 * p...  1.92 us
    pallas_call x1, Pallas kernels, back_last(): pl.pallas_call(body, out_shape=(jax.ShapeDtypeStruct(gradient.shape, F32)...  1.29 us
    pallas_call x1, Pallas kernels, back_x(): pl.pallas_call(body, out_shape=(jax.ShapeDtypeStruct(base.shape, F32), ja...  1.27 us
  transfers between devices with their start and end apart: 11, of which 8 were waited for; matrix products, arithmetic and copies ran while one was open for 0% of the time, Pallas kernels for 6%

profile of v13, /device:TPU:10, one launch (start us, length us, event | category | flops | bytes accessed | tf_op | source)
XLA Modules:
  0.0 39.3 jit_solution(16610519206283211647)
XLA Ops:
  0.7 1.9 %forward.1 = (f32[32,384]{1,0:T(8,128)S(1)}, f32[32,768]{1,0:T(8,128)S(1)}, bf16[256,256]{1,0:T(8,128)(2,1)S(1)}, bf16[1,512,256]{2,1,0:T(8,128)(2,1)S(1)}, bf16...) custom-call(s32[2,16]{1,0:T(2,128)} %refs_0_.1, ...), custom_call_target="tpu_custom_call" | custom-call | tf_op jit(solution)/shard_map/forward/pallas_call | solution.py:214
  2.6 0.1 collective-permute-start.1
  2.7 2.4 %collective-permute-start.3 = (f32[32,256]{1,0:T(8,128)S(1)}, f32[32,256]{1,0:T(8,128)S(1)}, u32[]{:S(2)}, u32[]{:S(2)}) collective-permute-start(f32[32,256]{1,0:T(8,128)S(1)} %slice.78), channel_id=1, source_target_pairs={{32,64},{64,32},{96,128},{128,96},{160,192},{192,160},{33,65},{65,... | collective-permute-start | bytes 98312 | tf_op jit(solution)/shard_map/ppermute | solution.py:465
  5.2 0.0 collective-permute-done.1
  5.2 1.3 %collective-permute-start.2 = (f32[16,384]{1,0:T(8,128)S(1)}, f32[16,384]{1,0:T(8,128)S(1)}, u32[]{:S(2)}, u32[]{:S(2)}) collective-permute-start(f32[16,384]{1,0:T(8,128)S(1)} %slice_add_fusion.3), channel_id=1, source_target_pairs={{0,224},{32,64},{64,32},{96,128},{128,96},{160,192},{192,160},{224... | collective-permute-start | bytes 73736 | tf_op jit(solution)/shard_map/ppermute | solution.py:465
  6.5 1.4 %collective-permute-done.3 = f32[32,256]{1,0:T(8,128)S(1)} collective-permute-done((f32[32,256]{1,0:T(8,128)S(1)}, f32[32,256]{1,0:T(8,128)S(1)}, u32[]{:S(2)}, u32[]{:S(2)}) %collective-permute-start.3) | collective-permute-done | bytes 32800 | tf_op jit(solution)/shard_map/ppermute | solution.py:465
  8.0 0.6 %collective-permute-done.2 = f32[16,384]{1,0:T(8,128)S(1)} collective-permute-done((f32[16,384]{1,0:T(8,128)S(1)}, f32[16,384]{1,0:T(8,128)S(1)}, u32[]{:S(2)}, u32[]{:S(2)}) %collective-permute-start.2) | collective-permute-done | bytes 24608 | tf_op jit(solution)/shard_map/ppermute | solution.py:465
  8.6 2.0 %collective-permute-start.4 = (f32[16,896]{1,0:T(8,128)S(1)}, f32[16,896]{1,0:T(8,128)S(1)}, u32[]{:S(2)}, u32[]{:S(2)}) collective-permute-start(f32[16,896]{1,0:T(8,128)S(1)} %pad_maximum_fusion.2), channel_id=1, source_target_pairs={{0,2},{2,0},{4,6},{6,4},{8,10},{10,8},{12,14},{14,12},{16,18},{18,... | collective-permute-start | bytes 172040 | tf_op jit(solution)/shard_map/ppermute | solution.py:465
  10.6 2.5 %collective-permute-done.4 = f32[16,896]{1,0:T(8,128)S(1)} collective-permute-done((f32[16,896]{1,0:T(8,128)S(1)}, f32[16,896]{1,0:T(8,128)S(1)}, u32[]{:S(2)}, u32[]{:S(2)}) %collective-permute-start.4) | collective-permute-done | bytes 57376 | tf_op jit(solution)/shard_map/ppermute | solution.py:465
  13.1 2.2 %collective-permute-start.5 = (f32[16,896]{1,0:T(8,128)S(1)}, f32[16,896]{1,0:T(8,128)S(1)}, u32[]{:S(2)}, u32[]{:S(2)}) collective-permute-start(f32[16,896]{1,0:T(8,128)S(1)} %pad_maximum_fusion.3), channel_id=1, source_target_pairs={{0,16},{2,18},{4,20},{6,22},{8,24},{10,26},{12,28},{14,30},{16,0},... | collective-permute-start | bytes 172040 | tf_op jit(solution)/shard_map/ppermute | solution.py:465
  15.3 3.6 %collective-permute-done.5 = f32[16,896]{1,0:T(8,128)S(1)} collective-permute-done((f32[16,896]{1,0:T(8,128)S(1)}, f32[16,896]{1,0:T(8,128)S(1)}, u32[]{:S(2)}, u32[]{:S(2)}) %collective-permute-start.5) | collective-permute-done | bytes 57376 | tf_op jit(solution)/shard_map/ppermute | solution.py:465
  18.9 6.1 %collective-permute-start.6 = (f32[16,896]{1,0:T(8,128)S(1)}, f32[16,896]{1,0:T(8,128)S(1)}, u32[]{:S(2)}, u32[]{:S(2)}) collective-permute-start(f32[16,896]{1,0:T(8,128)S(1)} %pad_maximum_fusion.4), channel_id=1, source_target_pairs={{0,14},{2,4},{4,2},{6,8},{8,6},{10,12},{12,10},{14,0},{16,30},{18,... | collective-permute-start | bytes 172040 | tf_op jit(solution)/shard_map/ppermute | solution.py:465
  25.1 0.5 %collective-permute-start = (bf16[1,512,256]{2,1,0:T(8,128)(2,1)S(1)}, bf16[1,512,256]{2,1,0:T(8,128)(2,1)S(1)}, u32[]{:S(2)}, u32[]{:S(2)}) collective-permute-start(bf16[1,512,256]{2,1,0:T(8,128)(2,1)S(1)} %get-tuple-element.28), channel_id=1, source_target_pairs={{0,1},{1,0},{2,3},{3,2},{4,5},{5,4},{6,7},{7,6},{8,9},{9,8},{10,11... | collective-permute-start | bytes 786440 | tf_op jit(solution)/shard_map/ppermute | solution.py:519
  25.6 1.6 %collective-permute-done.6 = f32[16,896]{1,0:T(8,128)S(1)} collective-permute-done((f32[16,896]{1,0:T(8,128)S(1)}, f32[16,896]{1,0:T(8,128)S(1)}, u32[]{:S(2)}, u32[]{:S(2)}) %collective-permute-start.6) | collective-permute-done | bytes 57376 | tf_op jit(solution)/shard_map/ppermute | solution.py:465
  27.2 2.1 %collective-permute-start.7 = (f32[16,768]{1,0:T(8,128)S(1)}, f32[16,768]{1,0:T(8,128)S(1)}, u32[]{:S(2)}, u32[]{:S(2)}) collective-permute-start(f32[16,768]{1,0:T(8,128)S(1)} %slice_add_fusion), channel_id=1, source_target_pairs={{0,6},{2,12},{4,10},{6,0},{8,14},{10,4},{12,2},{14,8},{16,22},{18,... | collective-permute-start | bytes 147464 | tf_op jit(solution)/shard_map/ppermute | solution.py:465
  29.3 0.0 collective-permute-start.8
  29.3 4.5 %collective-permute-done.7 = f32[16,768]{1,0:T(8,128)S(1)} collective-permute-done((f32[16,768]{1,0:T(8,128)S(1)}, f32[16,768]{1,0:T(8,128)S(1)}, u32[]{:S(2)}, u32[]{:S(2)}) %collective-permute-start.7) | collective-permute-done | bytes 49184 | tf_op jit(solution)/shard_map/ppermute | solution.py:465
  33.8 0.1 collective-permute-start.10
  33.9 0.0 collective-permute-done.8
  34.0 0.1 collective-permute-start.9
  34.1 0.0 collective-permute-done.refs_2_
  34.1 0.4 %prepare.1 = (bf16[512,256]{1,0:T(8,128)(2,1)S(1)}, f32[2,512,256]{2,1,0:T(8,128)S(1)}) custom-call(s32[8,256]{1,0:T(8,128)S(1)} %get-tuple-element.26.refs_0_, bf16[2,512,256]{2,1,0:T(8,128)(2,1)S(1)} %get-tuple-element.27.refs_1_, bf16[1,512,256]{2,1,0:T(8,128)(2,1)S(1)} %collective-permute-done.refs_2_), custom_call_target="tpu_custom_call" | custom-call | tf_op jit(solution)/shard_map/prepare/pallas_call | solution.py:294
  34.5 0.5 %back_own.1.refs_5_ = f32[512,256]{1,0:T(8,128)S(1)} custom-call(s32[16,128]{1,0:T(8,128)S(1)} %get-tuple-element.23.refs_0_, bf16[256,256]{1,0:T(8,128)(2,1)S(1)} %get-tuple-element.24.refs_1_, f32[16,768]{1,0:T(8,128)S(1)} %add.69.refs_2_.refs_3_), custom_call_target="tpu_custom_call" | custom-call | tf_op jit(solution)/shard_map/back_own/pallas_call | solution.py:326
  35.0 0.3 collective-permute-done.9.refs_4_
  35.2 1.3 %back_x.1 = (f32[2,512,256]{2,1,0:T(8,128)}, f32[16,2,256]{2,1,0:T(2,128)}, f32[512,256]{1,0:T(8,128)S(1)}) custom-call(s32[16,128]{1,0:T(8,128)S(1)} %get-tuple-element.25.refs_0_, bf16[512,256]{1,0:T(8,128)(2,1)S(1)} %get-tuple-element.29.refs_1_, f32[2,512,256]{2,1,0:T(8,128)S(1)} %get-tuple-element.30.refs_2_, f32[16,384]{1,0:T(8,128)S(1)} %add.70.refs_3_, ...), custom_call_target="tpu_custom_call" | custom-call | tf_op jit(solution)/shard_map/back_x/pallas_call | solution.py:383
  36.5 1.5 %collective-permute-done.10.refs_4_ = f32[16,768]{1,0:T(8,128)S(1)} collective-permute-done((f32[16,768]{1,0:T(8,128)S(1)}, f32[16,768]{1,0:T(8,128)S(1)}, u32[]{:S(2)}, u32[]{:S(2)}) %collective-permute-start.10) | collective-permute-done | bytes 49184 | tf_op jit(solution)/shard_map/ppermute | solution.py:465
  38.0 1.3 %back_last.1 = (f32[2,512,256]{2,1,0:T(8,128)}, f32[16,2,512]{2,1,0:T(2,128)}) custom-call(s32[16,128]{1,0:T(8,128)S(1)} %get-tuple-element.23.refs_0_, bf16[256,256]{1,0:T(8,128)(2,1)S(1)} %get-tuple-element.24.refs_1_, f32[512,256]{1,0:T(8,128)S(1)} %get-tuple-element.38.refs_2_, ...), custom_call_target="tpu_custom_call", output_to_operand_aliasing={{0}: (5, {})} | custom-call | tf_op jit(solution)/shard_map/back_last/pallas_call | solution.py:442
  (23 shorter events, 0.2 us)
Async XLA Ops:
  2.6 2.6 %collective-permute-start.1 = (f32[16,896]{1,0:T(8,128)S(1)}, f32[16,896]{1,0:T(8,128)S(1)}, u32[]{:S(2)}, u32[]{:S(2)}) collective-permute-start(f32[16,896]{1,0:T(8,128)S(1)} %pad_maximum_fusion.1), channel_id=1, source_target_pairs={{0,32},{32,0},{64,96},{96,64},{128,160},{160,128},{192,224},{224,1... | collective-permute-start | bytes 172040 | tf_op jit(solution)/shard_map/ppermute | solution.py:465
  2.7 5.2 %collective-permute-start.3 = (f32[32,256]{1,0:T(8,128)S(1)}, f32[32,256]{1,0:T(8,128)S(1)}, u32[]{:S(2)}, u32[]{:S(2)}) collective-permute-start(f32[32,256]{1,0:T(8,128)S(1)} %slice.78), channel_id=1, source_target_pairs={{32,64},{64,32},{96,128},{128,96},{160,192},{192,160},{33,65},{65,... | collective-permute-start | bytes 98312 | tf_op jit(solution)/shard_map/ppermute | solution.py:465
  5.2 3.3 %collective-permute-start.2 = (f32[16,384]{1,0:T(8,128)S(1)}, f32[16,384]{1,0:T(8,128)S(1)}, u32[]{:S(2)}, u32[]{:S(2)}) collective-permute-start(f32[16,384]{1,0:T(8,128)S(1)} %slice_add_fusion.3), channel_id=1, source_target_pairs={{0,224},{32,64},{64,32},{96,128},{128,96},{160,192},{192,160},{224... | collective-permute-start | bytes 73736 | tf_op jit(solution)/shard_map/ppermute | solution.py:465
  8.6 4.5 %collective-permute-start.4 = (f32[16,896]{1,0:T(8,128)S(1)}, f32[16,896]{1,0:T(8,128)S(1)}, u32[]{:S(2)}, u32[]{:S(2)}) collective-permute-start(f32[16,896]{1,0:T(8,128)S(1)} %pad_maximum_fusion.2), channel_id=1, source_target_pairs={{0,2},{2,0},{4,6},{6,4},{8,10},{10,8},{12,14},{14,12},{16,18},{18,... | collective-permute-start | bytes 172040 | tf_op jit(solution)/shard_map/ppermute | solution.py:465
  13.1 5.8 %collective-permute-start.5 = (f32[16,896]{1,0:T(8,128)S(1)}, f32[16,896]{1,0:T(8,128)S(1)}, u32[]{:S(2)}, u32[]{:S(2)}) collective-permute-start(f32[16,896]{1,0:T(8,128)S(1)} %pad_maximum_fusion.3), channel_id=1, source_target_pairs={{0,16},{2,18},{4,20},{6,22},{8,24},{10,26},{12,28},{14,30},{16,0},... | collective-permute-start | bytes 172040 | tf_op jit(solution)/shard_map/ppermute | solution.py:465
  18.9 8.3 %collective-permute-start.6 = (f32[16,896]{1,0:T(8,128)S(1)}, f32[16,896]{1,0:T(8,128)S(1)}, u32[]{:S(2)}, u32[]{:S(2)}) collective-permute-start(f32[16,896]{1,0:T(8,128)S(1)} %pad_maximum_fusion.4), channel_id=1, source_target_pairs={{0,14},{2,4},{4,2},{6,8},{8,6},{10,12},{12,10},{14,0},{16,30},{18,... | collective-permute-start | bytes 172040 | tf_op jit(solution)/shard_map/ppermute | solution.py:465
  25.1 9.0 %collective-permute-start = (bf16[1,512,256]{2,1,0:T(8,128)(2,1)S(1)}, bf16[1,512,256]{2,1,0:T(8,128)(2,1)S(1)}, u32[]{:S(2)}, u32[]{:S(2)}) collective-permute-start(bf16[1,512,256]{2,1,0:T(8,128)(2,1)S(1)} %get-tuple-element.28), channel_id=1, source_target_pairs={{0,1},{1,0},{2,3},{3,2},{4,5},{5,4},{6,7},{7,6},{8,9},{9,8},{10,11... | collective-permute-start | bytes 786440 | tf_op jit(solution)/shard_map/ppermute | solution.py:519
  27.2 6.6 %collective-permute-start.7 = (f32[16,768]{1,0:T(8,128)S(1)}, f32[16,768]{1,0:T(8,128)S(1)}, u32[]{:S(2)}, u32[]{:S(2)}) collective-permute-start(f32[16,768]{1,0:T(8,128)S(1)} %slice_add_fusion), channel_id=1, source_target_pairs={{0,6},{2,12},{4,10},{6,0},{8,14},{10,4},{12,2},{14,8},{16,22},{18,... | collective-permute-start | bytes 147464 | tf_op jit(solution)/shard_map/ppermute | solution.py:465
  29.3 4.6 %collective-permute-start.8 = (f32[16,384]{1,0:T(8,128)S(1)}, f32[16,384]{1,0:T(8,128)S(1)}, u32[]{:S(2)}, u32[]{:S(2)}) collective-permute-start(f32[16,384]{1,0:T(8,128)S(1)} %pad_maximum_fusion.5), channel_id=1, source_target_pairs={{0,96},{32,192},{64,160},{96,0},{128,224},{160,64},{192,32},{224,1... | collective-permute-start | bytes 73736 | tf_op jit(solution)/shard_map/ppermute | solution.py:465
  33.8 4.2 %collective-permute-start.10 = (f32[16,768]{1,0:T(8,128)S(1)}, f32[16,768]{1,0:T(8,128)S(1)}, u32[]{:S(2)}, u32[]{:S(2)}) collective-permute-start(f32[16,768]{1,0:T(8,128)S(1)} %add.69.refs_2_.refs_3_), channel_id=1, source_target_pairs={{0,2},{2,0},{4,6},{6,4},{8,10},{10,8},{12,14},{14,12},{16,18},{18,... | collective-permute-start | bytes 147464 | tf_op jit(solution)/shard_map/ppermute | solution.py:465
  34.0 1.3 %collective-permute-start.9 = (f32[16,384]{1,0:T(8,128)S(1)}, f32[16,384]{1,0:T(8,128)S(1)}, u32[]{:S(2)}, u32[]{:S(2)}) collective-permute-start(f32[16,384]{1,0:T(8,128)S(1)} %add.70.refs_3_), channel_id=1, source_target_pairs={{0,32},{32,0},{64,96},{96,64},{128,160},{160,128},{192,224},{224,1... | collective-permute-start | bytes 73736 | tf_op jit(solution)/shard_map/ppermute | solution.py:465
